TPU v7x, 32 devices: a whole 2x2x4 slice. The times are simulated.
32 devices in a mesh: rep: 8 (over y, x, core), shard: 4 (over z).
Axes of the slice: x: 2, y: 2, z: 4, core: 2. Of those that a mesh axis runs over, the one named last changes fastest.
Arguments:
- tokens: bfloat16 [3, 4096, 1472], P(None, ('rep', 'shard')), may hold values from -6 to 6
- cotangent: bfloat16 [3, 4096, 1472], P(None, ('rep', 'shard')), may hold values from -6 to 6
- gate_cotangent: bfloat16 [3, 4096], P(None, ('rep', 'shard')), may hold values from -6 to 6
- slot_of: int32 [3, 8, 512], P(None, 'rep'), may hold values from 0 to 511, as said below
- seq_lengths: int32 [3, 8, 2], P(None, 'rep'), may hold values from 256 to 256, as said below
- buckets: int32 [1023], replicated, may hold values from 0 to 31
- gain_attn: bfloat16 [1472], P('shard'), may hold values from 0.099609375 to 1.8984375
- w_query: bfloat16 [1472, 384], P('shard'), may hold values from -0.078125 to 0.078125
- w_key: bfloat16 [1472, 384], P('shard'), may hold values from -0.078125 to 0.078125
- w_value: bfloat16 [1472, 384], P('shard'), may hold values from -0.15625 to 0.15625
- w_out: bfloat16 [384, 1472], P('shard'), may hold values from -1.75 to 1.75
- rel_bias: bfloat16 [32, 6], P('shard'), may hold values from -4 to 4
- gain_ffn: bfloat16 [1472], P('shard'), may hold values from 0.099609375 to 1.8984375
- w_gate: bfloat16 [1472, 3584], P('shard'), may hold values from -0.15625 to 0.15625
- w_up: bfloat16 [1472, 3584], P('shard'), may hold values from -0.15625 to 0.15625
- w_down: bfloat16 [3584, 1472], P('shard'), may hold values from -0.09375 to 0.09375
- gain_delete: bfloat16 [1472], P('shard'), may hold values from 0.099609375 to 1.8984375
- w_delete: bfloat16 [1472], P('shard'), may hold values from -0.15625 to 0.15625
Outputs:
- states: float32 [3, 4096, 1472], P(None, ('rep', 'shard'))
- delete_gate: float32 [3, 4096], P(None, ('rep', 'shard'))
- grad_tokens: bfloat16 [3, 4096, 1472], P(None, ('rep', 'shard'))
- grad_gain_attn: float32 [1472], P('shard')
- grad_w_query: float32 [1472, 384], P('shard')
- grad_w_key: float32 [1472, 384], P('shard')
- grad_w_value: float32 [1472, 384], P('shard')
- grad_w_out: float32 [384, 1472], P('shard')
- grad_rel_bias: float32 [32, 6], P('shard')
- grad_gain_ffn: float32 [1472], P('shard')
- grad_w_gate: float32 [1472, 3584], P('shard')
- grad_w_up: float32 [1472, 3584], P('shard')
- grad_w_down: float32 [3584, 1472], P('shard')
- grad_gain_delete: float32 [1472], P('shard')
- grad_w_delete: float32 [1472], P('shard')
Inputs may be any that keep to these rules, and one draw needn't show every extreme that they name: `slot_of`: each row is a permutation of the 512 slots of a group; of the 128 tokens that arrive on one device, exactly 32 have slots in each block of 128 consecutive slots. `seq_lengths`: the two lengths of a group sum to 512; the first sequence takes the first slots.
All inputs are finite; a program needn't handle non-finite values.
Results may differ from a plain program's by a relative error of at most 0.02.
Values may be sent and summed in bfloat16 or wider, within the bound.
No kernel may reach another device: no remote copies, remote signals or barrier semaphores. Data moves between devices by JAX's collectives and lax.ppermute only.
A program may use at most 256 MiB of HBM per device.

v0:
```python
import jax
import jax.numpy as jnp
from jax import lax
from jax.sharding import PartitionSpec as P

EPSILON = 1e-06
HIGHEST = lax.Precision.HIGHEST
MASKED = -1000000000.0


def gelu_tanh(value):
    return jax.nn.gelu(value, approximate=True)


def rms_scale(hidden):
    return lax.rsqrt(jnp.mean(hidden * hidden, axis=-1, keepdims=True) + EPSILON)


def rms_back(hidden, scale_row, gain, upstream):
    scaled = upstream * gain
    return scale_row * scaled - hidden * (scale_row * scale_row * scale_row) * jnp.mean(
        hidden * scaled, axis=-1, keepdims=True
    )


def routing(slot_row, shard_rank, local_rows, shards):
    per_peer = local_rows // shards
    blocks = slot_row.reshape(shards, local_rows)
    target = blocks // local_rows
    orders = jnp.argsort(target, axis=1, stable=True)
    sorted_slots = jnp.take_along_axis(blocks, orders, axis=1)
    incoming = (
        lax.dynamic_slice_in_dim(sorted_slots, shard_rank * per_peer, per_peer, 1).reshape(-1)
        - shard_rank * local_rows
    )
    send_order = lax.dynamic_index_in_dim(orders, shard_rank, 0, keepdims=False)
    counting = jnp.arange(local_rows, dtype=jnp.int32)
    arrange = jnp.zeros((local_rows,), jnp.int32).at[incoming].set(counting)
    restore = jnp.zeros((local_rows,), jnp.int32).at[send_order].set(counting)
    return (send_order, incoming, arrange, restore)


def bias_block(bias_rows, start_row, block_rows, group_rows):
    head_count = bias_rows.shape[0]
    width = group_rows + block_rows - 1
    window = lax.dynamic_slice_in_dim(bias_rows, group_rows - start_row - block_rows, width, 1)
    padded = jnp.pad(window, ((0, 0), (0, 1)))
    tiled = jnp.broadcast_to(padded[:, None, :], (head_count, block_rows, width + 1)).reshape(
        head_count, block_rows * (width + 1)
    )
    skewed = tiled[:, : block_rows * width].reshape(head_count, block_rows, width)
    return skewed[:, :, block_rows - 1 :]


def bias_fold(grad_rows, block_rows):
    head_count, rows_here, key_count = grad_rows.shape
    width = key_count + block_rows - 1
    placed = jnp.pad(grad_rows, ((0, 0), (0, 0), (block_rows - 1, 0))).reshape(
        head_count, block_rows * width
    )
    placed = jnp.pad(placed, ((0, 0), (0, block_rows)))
    return jnp.sum(placed.reshape(head_count, block_rows, width + 1), axis=1)[:, :width]


def score_block(queries, key_heads, bias_rows, query_seg, key_seg, start_row, group_rows):
    block_rows = queries.shape[0]
    scores = jnp.einsum("qhd,khd->hqk", queries, key_heads, preferred_element_type=jnp.float32)
    biased = scores + bias_block(bias_rows, start_row, block_rows, group_rows)
    same_seq = (query_seg[:, None] == key_seg[None, :])[None]
    return jnp.where(same_seq, biased, MASKED)


def on_device(
    tokens,
    cotangent,
    gate_cotangent,
    slot_of,
    seq_lengths,
    buckets,
    gain_attn,
    w_query,
    w_key,
    w_value,
    w_out,
    rel_bias,
    gain_ffn,
    w_gate,
    w_up,
    w_down,
    gain_delete,
    w_delete,
):
    shards = lax.axis_size("shard")
    shard_rank = lax.axis_index("shard")
    micro_count, local_rows, model_width = tokens.shape
    group_rows = local_rows * shards
    per_peer = local_rows // shards
    head_count = rel_bias.shape[1]
    head_size = w_query.shape[1] // head_count
    block_rows = min(512, local_rows)
    blocks = local_rows // block_rows
    offsets = 2 * group_rows - 1
    width = group_rows + block_rows - 1
    bucket_count = rel_bias.shape[0] * shards
    shard_params = (
        gain_attn,
        w_query,
        w_key,
        w_value,
        w_out,
        rel_bias,
        gain_ffn,
        w_gate,
        w_up,
        w_down,
        gain_delete,
        w_delete,
    )
    onehot = (buckets[:, None] == jnp.arange(bucket_count, dtype=jnp.int32)[None, :]).astype(
        jnp.float32
    )
    totals = [
        jnp.zeros((weight.shape[0] * shards,) + weight.shape[1:], jnp.float32)
        for weight in shard_params
    ]
    block_starts = jnp.arange(blocks, dtype=jnp.int32) * block_rows + shard_rank * local_rows
    outs_states = []
    outs_delete = []
    outs_grad = []
    saved = []
    full_params = (
        lax.all_gather(gain_attn, "shard", axis=0, tiled=True),
        lax.all_gather(w_query, "shard", axis=0, tiled=True),
        lax.all_gather(w_key, "shard", axis=0, tiled=True),
        lax.all_gather(w_value, "shard", axis=0, tiled=True),
        lax.all_gather(w_out, "shard", axis=0, tiled=True),
        lax.all_gather(rel_bias, "shard", axis=0, tiled=True),
        lax.all_gather(gain_ffn, "shard", axis=0, tiled=True),
        lax.all_gather(w_gate, "shard", axis=0, tiled=True),
        lax.all_gather(w_up, "shard", axis=0, tiled=True),
        lax.all_gather(w_down, "shard", axis=0, tiled=True),
        lax.all_gather(gain_delete, "shard", axis=0, tiled=True),
        lax.all_gather(w_delete, "shard", axis=0, tiled=True),
    )
    attn_gain = full_params[0].astype(jnp.float32)
    ffn_gain = full_params[6].astype(jnp.float32)
    delete_gain = full_params[10].astype(jnp.float32)
    delete_vec = full_params[11].astype(jnp.float32)
    bias_rows = jnp.dot(onehot, full_params[5].astype(jnp.float32), precision=HIGHEST).T
    for micro_step in range(micro_count):
        slot_row = slot_of[micro_step, 0]
        send_order, incoming, arrange, restore = routing(slot_row, shard_rank, local_rows, shards)
        arrived = (
            lax.all_to_all(
                tokens[micro_step][send_order].reshape(shards, per_peer, model_width),
                "shard",
                split_axis=0,
                concat_axis=0,
                tiled=True,
            ),
            lax.all_to_all(
                cotangent[micro_step][send_order].reshape(shards, per_peer, model_width),
                "shard",
                split_axis=0,
                concat_axis=0,
                tiled=True,
            ),
            lax.all_to_all(
                gate_cotangent[micro_step][send_order].reshape(shards, per_peer),
                "shard",
                split_axis=0,
                concat_axis=0,
                tiled=True,
            ),
        )
        inputs = arrived[0].reshape(local_rows, model_width)[arrange]
        upstream = arrived[1].reshape(local_rows, model_width)[arrange].astype(jnp.float32)
        gate_upstream = arrived[2].reshape(local_rows)[arrange].astype(jnp.float32)
        first_len = seq_lengths[micro_step, 0, 0]
        group_index = jnp.arange(group_rows, dtype=jnp.int32)
        key_seg = (group_index >= first_len).astype(jnp.int32)
        query_seg = lax.dynamic_slice_in_dim(key_seg, shard_rank * local_rows, local_rows).reshape(
            blocks, block_rows
        )
        hidden_in = inputs.astype(jnp.float32)
        scale_one = rms_scale(hidden_in)
        normed_one = (hidden_in * scale_one * attn_gain).astype(jnp.bfloat16)
        queries = jnp.dot(normed_one, full_params[1], preferred_element_type=jnp.float32).astype(
            jnp.bfloat16
        )
        key_local = jnp.dot(normed_one, full_params[2], preferred_element_type=jnp.float32).astype(
            jnp.bfloat16
        )
        value_local = jnp.dot(
            normed_one, full_params[3], preferred_element_type=jnp.float32
        ).astype(jnp.bfloat16)
        key_all, value_all = (
            lax.all_gather(key_local, "shard", axis=0, tiled=True),
            lax.all_gather(value_local, "shard", axis=0, tiled=True),
        )
        key_heads = key_all.reshape(group_rows, head_count, head_size)
        value_heads = value_all.reshape(group_rows, head_count, head_size)
        query_blocks = queries.reshape(blocks, block_rows, head_count, head_size)

        def forward_block(members):
            query_block, seg_block, start_row = members
            scores = score_block(
                query_block, key_heads, bias_rows, seg_block, key_seg, start_row, group_rows
            )
            row_peak = jnp.max(scores, axis=-1, keepdims=True)
            weights = jnp.exp(scores - row_peak)
            denominator = jnp.sum(weights, axis=-1, keepdims=True)
            probabilities = (weights / denominator).astype(jnp.bfloat16)
            context_block = jnp.einsum(
                "hqk,khd->qhd", probabilities, value_heads, preferred_element_type=jnp.float32
            )
            return (context_block, row_peak[..., 0] + jnp.log(denominator[..., 0]))

        context, log_total = lax.map(forward_block, (query_blocks, query_seg, block_starts))
        context = context.reshape(local_rows, head_count * head_size).astype(jnp.bfloat16)
        hidden_mid = hidden_in + jnp.dot(
            context, full_params[4], preferred_element_type=jnp.float32
        )
        scale_two = rms_scale(hidden_mid)
        normed_two = (hidden_mid * scale_two * ffn_gain).astype(jnp.bfloat16)
        gate_pre = jnp.dot(normed_two, full_params[7], preferred_element_type=jnp.float32)
        up_pre = jnp.dot(normed_two, full_params[8], preferred_element_type=jnp.float32)
        activated = gelu_tanh(gate_pre)
        inner_act = (activated * up_pre).astype(jnp.bfloat16)
        hidden_out = hidden_mid + jnp.dot(
            inner_act, full_params[9], preferred_element_type=jnp.float32
        )
        scale_three = rms_scale(hidden_out)
        delete_norm = hidden_out * scale_three * delete_gain
        delete_logit = jnp.sum(delete_norm * delete_vec, axis=-1)
        sigmoid_val = jax.nn.sigmoid(delete_logit)
        deleted = -30.0 * sigmoid_val
        returned = (
            lax.all_to_all(
                hidden_out[incoming].reshape(shards, per_peer, model_width).astype(jnp.bfloat16),
                "shard",
                split_axis=0,
                concat_axis=0,
                tiled=True,
            ).astype(jnp.float32),
            lax.all_to_all(
                deleted[incoming].reshape(shards, per_peer).astype(jnp.bfloat16),
                "shard",
                split_axis=0,
                concat_axis=0,
                tiled=True,
            ).astype(jnp.float32),
        )
        outs_states.append(returned[0].reshape(local_rows, model_width)[restore])
        outs_delete.append(returned[1].reshape(local_rows)[restore])
        saved.append(
            (
                incoming,
                restore,
                upstream,
                gate_upstream,
                key_seg,
                query_seg,
                hidden_in,
                scale_one,
                normed_one,
                query_blocks,
                key_local,
                value_local,
                key_heads,
                value_heads,
                log_total,
                context,
                hidden_mid,
                scale_two,
                normed_two,
                gate_pre,
                up_pre,
                inner_act,
                hidden_out,
                scale_three,
                delete_norm,
                sigmoid_val,
            )
        )
    back_params = (
        lax.all_gather(gain_attn, "shard", axis=0, tiled=True),
        lax.all_gather(w_query, "shard", axis=0, tiled=True),
        lax.all_gather(w_key, "shard", axis=0, tiled=True),
        lax.all_gather(w_value, "shard", axis=0, tiled=True),
        lax.all_gather(w_out, "shard", axis=0, tiled=True),
        lax.all_gather(rel_bias, "shard", axis=0, tiled=True),
        lax.all_gather(gain_ffn, "shard", axis=0, tiled=True),
        lax.all_gather(w_gate, "shard", axis=0, tiled=True),
        lax.all_gather(w_up, "shard", axis=0, tiled=True),
        lax.all_gather(w_down, "shard", axis=0, tiled=True),
        lax.all_gather(gain_delete, "shard", axis=0, tiled=True),
        lax.all_gather(w_delete, "shard", axis=0, tiled=True),
    )
    for micro_step in range(micro_count):
        (
            incoming,
            restore,
            upstream,
            gate_upstream,
            key_seg,
            query_seg,
            hidden_in,
            scale_one,
            normed_one,
            query_blocks,
            key_local,
            value_local,
            key_heads,
            value_heads,
            log_total,
            context,
            hidden_mid,
            scale_two,
            normed_two,
            gate_pre,
            up_pre,
            inner_act,
            hidden_out,
            scale_three,
            delete_norm,
            sigmoid_val,
        ) = saved[micro_step]
        key_again, value_again = (
            lax.all_gather(key_local, "shard", axis=0, tiled=True),
            lax.all_gather(value_local, "shard", axis=0, tiled=True),
        )
        key_back = key_again.reshape(group_rows, head_count, head_size)
        value_back = value_again.reshape(group_rows, head_count, head_size)
        gate_slope = gate_upstream * -30.0 * sigmoid_val * (1.0 - sigmoid_val)
        totals[11] = totals[11] + jnp.sum(gate_slope[:, None] * delete_norm, axis=0)
        delete_up = gate_slope[:, None] * back_params[11].astype(jnp.float32)
        totals[10] = totals[10] + jnp.sum(delete_up * hidden_out * scale_three, axis=0)
        grad_out = upstream + rms_back(
            hidden_out, scale_three, back_params[10].astype(jnp.float32), delete_up
        )
        down_grad = grad_out.astype(jnp.bfloat16)
        totals[9] = totals[9] + jnp.einsum(
            "tf,td->fd", inner_act, down_grad, preferred_element_type=jnp.float32
        )
        inner_grad = jnp.einsum(
            "td,fd->tf", down_grad, back_params[9], preferred_element_type=jnp.float32
        )
        activated, gelu_pull = jax.vjp(gelu_tanh, gate_pre)
        gate_grad = gelu_pull(inner_grad * up_pre)[0].astype(jnp.bfloat16)
        up_grad = (inner_grad * activated).astype(jnp.bfloat16)
        totals[7] = totals[7] + jnp.einsum(
            "td,tf->df", normed_two, gate_grad, preferred_element_type=jnp.float32
        )
        totals[8] = totals[8] + jnp.einsum(
            "td,tf->df", normed_two, up_grad, preferred_element_type=jnp.float32
        )
        normed_two_grad = jnp.einsum(
            "tf,df->td", gate_grad, back_params[7], preferred_element_type=jnp.float32
        ) + jnp.einsum("tf,df->td", up_grad, back_params[8], preferred_element_type=jnp.float32)
        totals[6] = totals[6] + jnp.sum(normed_two_grad * hidden_mid * scale_two, axis=0)
        grad_mid = grad_out + rms_back(
            hidden_mid, scale_two, back_params[6].astype(jnp.float32), normed_two_grad
        )
        out_grad = grad_mid.astype(jnp.bfloat16)
        totals[4] = totals[4] + jnp.einsum(
            "th,td->hd", context, out_grad, preferred_element_type=jnp.float32
        )
        context_grad = jnp.einsum(
            "td,hd->th", out_grad, back_params[4], preferred_element_type=jnp.float32
        ).astype(jnp.bfloat16)
        context_grad = context_grad.reshape(blocks, block_rows, head_count, head_size)

        def backward_block(carried, members):
            key_acc, value_acc, bias_acc = carried
            query_block, grad_block, lse_block, seg_block, start_row = members
            scores = score_block(
                query_block, key_back, bias_rows, seg_block, key_seg, start_row, group_rows
            )
            probabilities = jnp.exp(scores - lse_block[..., None])
            prob_grad = jnp.einsum(
                "qhd,khd->hqk", grad_block, value_back, preferred_element_type=jnp.float32
            )
            inner_sum = jnp.sum(probabilities * prob_grad, axis=-1, keepdims=True)
            score_grad = (probabilities * (prob_grad - inner_sum)).astype(jnp.bfloat16)
            query_grad = jnp.einsum(
                "hqk,khd->qhd", score_grad, key_back, preferred_element_type=jnp.float32
            )
            key_acc = key_acc + jnp.einsum(
                "hqk,qhd->khd", score_grad, query_block, preferred_element_type=jnp.float32
            )
            value_acc = value_acc + jnp.einsum(
                "hqk,qhd->khd",
                probabilities.astype(jnp.bfloat16),
                grad_block,
                preferred_element_type=jnp.float32,
            )
            folded = bias_fold(score_grad.astype(jnp.float32), block_rows)
            window_start = group_rows - start_row - block_rows
            current = lax.dynamic_slice_in_dim(bias_acc, window_start, width, 1)
            bias_acc = lax.dynamic_update_slice_in_dim(bias_acc, current + folded, window_start, 1)
            return ((key_acc, value_acc, bias_acc), query_grad)

        start_carry = (
            jnp.zeros((group_rows, head_count, head_size), jnp.float32),
            jnp.zeros((group_rows, head_count, head_size), jnp.float32),
            jnp.zeros((head_count, offsets), jnp.float32),
        )
        (key_acc, value_acc, bias_acc), query_grads = lax.scan(
            backward_block,
            start_carry,
            (query_blocks, context_grad, log_total, query_seg, block_starts),
        )
        key_sum, value_sum = (
            lax.psum_scatter(
                key_acc.reshape(group_rows, head_count * head_size),
                "shard",
                scatter_dimension=0,
                tiled=True,
            ),
            lax.psum_scatter(
                value_acc.reshape(group_rows, head_count * head_size),
                "shard",
                scatter_dimension=0,
                tiled=True,
            ),
        )
        key_grad = key_sum.astype(jnp.bfloat16)
        value_grad = value_sum.astype(jnp.bfloat16)
        query_grad = query_grads.reshape(local_rows, head_count * head_size).astype(jnp.bfloat16)
        totals[5] = totals[5] + jnp.einsum("ob,ho->bh", onehot, bias_acc, precision=HIGHEST)
        totals[1] = totals[1] + jnp.einsum(
            "td,th->dh", normed_one, query_grad, preferred_element_type=jnp.float32
        )
        totals[2] = totals[2] + jnp.einsum(
            "td,th->dh", normed_one, key_grad, preferred_element_type=jnp.float32
        )
        totals[3] = totals[3] + jnp.einsum(
            "td,th->dh", normed_one, value_grad, preferred_element_type=jnp.float32
        )
        normed_one_grad = jnp.einsum(
            "th,dh->td", query_grad, back_params[1], preferred_element_type=jnp.float32
        )
        normed_one_grad = normed_one_grad + jnp.einsum(
            "th,dh->td", key_grad, back_params[2], preferred_element_type=jnp.float32
        )
        normed_one_grad = normed_one_grad + jnp.einsum(
            "th,dh->td", value_grad, back_params[3], preferred_element_type=jnp.float32
        )
        totals[0] = totals[0] + jnp.sum(normed_one_grad * hidden_in * scale_one, axis=0)
        grad_in = grad_mid + rms_back(
            hidden_in, scale_one, back_params[0].astype(jnp.float32), normed_one_grad
        )
        sent_back = lax.all_to_all(
            grad_in[incoming].astype(jnp.bfloat16).reshape(shards, per_peer, model_width),
            "shard",
            split_axis=0,
            concat_axis=0,
            tiled=True,
        )
        outs_grad.append(sent_back.reshape(local_rows, model_width)[restore])
    share_list = list(
        (
            lax.psum_scatter(
                totals[0].astype(jnp.bfloat16), "shard", scatter_dimension=0, tiled=True
            ).astype(jnp.float32),
            lax.psum_scatter(
                totals[1].astype(jnp.bfloat16), "shard", scatter_dimension=0, tiled=True
            ).astype(jnp.float32),
            lax.psum_scatter(
                totals[2].astype(jnp.bfloat16), "shard", scatter_dimension=0, tiled=True
            ).astype(jnp.float32),
            lax.psum_scatter(
                totals[3].astype(jnp.bfloat16), "shard", scatter_dimension=0, tiled=True
            ).astype(jnp.float32),
            lax.psum_scatter(
                totals[4].astype(jnp.bfloat16), "shard", scatter_dimension=0, tiled=True
            ).astype(jnp.float32),
            lax.psum_scatter(
                totals[5].astype(jnp.bfloat16), "shard", scatter_dimension=0, tiled=True
            ).astype(jnp.float32),
            lax.psum_scatter(
                totals[6].astype(jnp.bfloat16), "shard", scatter_dimension=0, tiled=True
            ).astype(jnp.float32),
            lax.psum_scatter(
                totals[7].astype(jnp.bfloat16), "shard", scatter_dimension=0, tiled=True
            ).astype(jnp.float32),
            lax.psum_scatter(
                totals[8].astype(jnp.bfloat16), "shard", scatter_dimension=0, tiled=True
            ).astype(jnp.float32),
            lax.psum_scatter(
                totals[9].astype(jnp.bfloat16), "shard", scatter_dimension=0, tiled=True
            ).astype(jnp.float32),
            lax.psum_scatter(
                totals[10].astype(jnp.bfloat16), "shard", scatter_dimension=0, tiled=True
            ).astype(jnp.float32),
            lax.psum_scatter(
                totals[11].astype(jnp.bfloat16), "shard", scatter_dimension=0, tiled=True
            ).astype(jnp.float32),
        )
    )
    summed = (
        lax.psum(share_list[0].astype(jnp.bfloat16), "rep").astype(jnp.float32),
        lax.psum(share_list[1].astype(jnp.bfloat16), "rep").astype(jnp.float32),
        lax.psum(share_list[2].astype(jnp.bfloat16), "rep").astype(jnp.float32),
        lax.psum(share_list[3].astype(jnp.bfloat16), "rep").astype(jnp.float32),
        lax.psum(share_list[4].astype(jnp.bfloat16), "rep").astype(jnp.float32),
        lax.psum(share_list[5].astype(jnp.bfloat16), "rep").astype(jnp.float32),
        lax.psum(share_list[6].astype(jnp.bfloat16), "rep").astype(jnp.float32),
        lax.psum(share_list[7].astype(jnp.bfloat16), "rep").astype(jnp.float32),
        lax.psum(share_list[8].astype(jnp.bfloat16), "rep").astype(jnp.float32),
        lax.psum(share_list[9].astype(jnp.bfloat16), "rep").astype(jnp.float32),
        lax.psum(share_list[10].astype(jnp.bfloat16), "rep").astype(jnp.float32),
        lax.psum(share_list[11].astype(jnp.bfloat16), "rep").astype(jnp.float32),
    )
    return (
        jnp.stack(outs_states),
        jnp.stack(outs_delete),
        jnp.stack(outs_grad),
        summed[0],
        summed[1],
        summed[2],
        summed[3],
        summed[4],
        summed[5],
        summed[6],
        summed[7],
        summed[8],
        summed[9],
        summed[10],
        summed[11],
    )


def solution(mesh):
    in_specs = (
        P(None, ("rep", "shard"), None),
        P(None, ("rep", "shard"), None),
        P(None, ("rep", "shard")),
        P(None, "rep", None),
        P(None, "rep", None),
        P(),
        P("shard"),
        P("shard", None),
        P("shard", None),
        P("shard", None),
        P("shard", None),
        P("shard", None),
        P("shard"),
        P("shard", None),
        P("shard", None),
        P("shard", None),
        P("shard"),
        P("shard"),
    )
    out_specs = (
        P(None, ("rep", "shard"), None),
        P(None, ("rep", "shard")),
        P(None, ("rep", "shard"), None),
        P("shard"),
        P("shard", None),
        P("shard", None),
        P("shard", None),
        P("shard", None),
        P("shard", None),
        P("shard"),
        P("shard", None),
        P("shard", None),
        P("shard", None),
        P("shard"),
        P("shard"),
    )
    return jax.shard_map(
        on_device, mesh=mesh, in_specs=in_specs, out_specs=out_specs, check_vma=False
    )
```

profile of v0, /device:TPU:0, one launch (start us, length us, event | category | flops | bytes accessed | tf_op | source)
XLA Modules:
  0.0 1839.6 jit_solution(3698980436760434024)
XLA Ops:
  18.1 13.6 all_gather.77
  38.7 17.5 all-reduce.19
  99.9 10.2 all-to-all-done.4
  132.9 16.5 all-to-all-done.2
  169.4 20.5 %all-to-all-done.9 = bf16[4,32,1472]{2,1,0:T(8,128)(2,1)S(1)} async-done(((bf16[4,32,1472]{2,1,0:T(8,128)(2,1)}), bf16[4,32,1472]{2,1,0:T(8,128)(2,1)S(1)}, u32[]{:S(2)}, u32[]{:S(2)}) %all-to-all-start.9) | async-done | bytes 376864 | tf_op jit(solution)/shard_map/all_to_all | solution.py:161
  215.5 20.8 %all_gather.85 = bf16[512,384]{1,0:T(8,128)(2,1)S(1)} all-gather(bf16[128,384]{1,0:T(8,128)(2,1)S(1)} %convolution_convert_fusion.11), channel_id=1, replica_groups=mesh['rep'=8,'shard'=4] {'shard'}, dimensions={0}, use_global_device_ids=true | all-gather | bytes 491520 | tf_op jit(solution)/shard_map/all_gather | solution.py:199
  242.0 25.8 %all_gather.86 = bf16[512,384]{1,0:T(8,128)(2,1)S(1)} all-gather(bf16[128,384]{1,0:T(8,128)(2,1)S(1)} %convolution_convert_fusion.9), channel_id=1, replica_groups=mesh['rep'=8,'shard'=4] {'shard'}, dimensions={0}, use_global_device_ids=true | all-gather | bytes 491520 | tf_op jit(solution)/shard_map/all_gather | solution.py:198
  269.5 23.0 %all_gather.73 = bf16[512,384]{1,0:T(8,128)(2,1)} all-gather(bf16[128,384]{1,0:T(8,128)(2,1)S(1)} %convolution_convert_fusion.17), channel_id=1, replica_groups=mesh['rep'=8,'shard'=4] {'shard'}, dimensions={0}, use_global_device_ids=true | all-gather | bytes 491520 | tf_op jit(solution)/shard_map/all_gather | solution.py:199
  299.4 23.9 %all_gather.76 = bf16[512,384]{1,0:T(8,128)(2,1)} all-gather(bf16[128,384]{1,0:T(8,128)(2,1)S(1)} %convolution_convert_fusion.15), channel_id=1, replica_groups=mesh['rep'=8,'shard'=4] {'shard'}, dimensions={0}, use_global_device_ids=true | all-gather | bytes 491520 | tf_op jit(solution)/shard_map/all_gather | solution.py:198
  325.9 20.9 %all_gather.83 = bf16[512,384]{1,0:T(8,128)(2,1)S(1)} all-gather(bf16[128,384]{1,0:T(8,128)(2,1)S(1)} %convolution_convert_fusion.14), channel_id=1, replica_groups=mesh['rep'=8,'shard'=4] {'shard'}, dimensions={0}, use_global_device_ids=true | all-gather | bytes 491520 | tf_op jit(solution)/shard_map/all_gather | solution.py:199
  351.3 23.6 %all_gather.84 = bf16[512,384]{1,0:T(8,128)(2,1)S(1)} all-gather(bf16[128,384]{1,0:T(8,128)(2,1)S(1)} %convolution_convert_fusion.12), channel_id=1, replica_groups=mesh['rep'=8,'shard'=4] {'shard'}, dimensions={0}, use_global_device_ids=true | all-gather | bytes 491520 | tf_op jit(solution)/shard_map/all_gather | solution.py:198
  390.6 6.8 fusion.197
  397.4 177.8 %all-gather.18.cloned.1.call-done = bf16[1472,3584]{1,0:T(8,128)(2,1)} async-done(((bf16[368,3584]{1,0:T(8,128)(2,1)}), bf16[1472,3584]{1,0:T(8,128)(2,1)}) %all-gather.18.cloned.1.call-update) | async-done | bytes 10551312 | tf_op jit(solution)/shard_map/all_gather | solution.py:140
  575.3 8.1 multiply_convert_fusion.5
  583.4 176.5 %all-gather.20.cloned.1.call-done = bf16[3584,1472]{0,1:T(8,128)(2,1)} async-done(((bf16[896,1472]{0,1:T(8,128)(2,1)}), bf16[3584,1472]{0,1:T(8,128)(2,1)}) %all-gather.20.cloned.1.call-update) | async-done | bytes 10551312 | tf_op jit(solution)/shard_map/all_gather | solution.py:141
  759.9 6.6 multiply_reduce_fusion.17
  774.0 6.1 multiply_reduce_fusion.15
  785.0 6.0 multiply_reduce_fusion.13
  796.3 7.5 multiply_convert_fusion.1
  811.5 8.5 multiply_convert_fusion.2
  823.8 6.6 multiply_reduce_fusion.8
  830.5 7.5 multiply_convert_fusion
  873.1 10.4 fusion.113
  883.5 9.1 fusion.106
  892.7 18.9 %add_convert_fusion = bf16[3584,1472]{0,1:T(8,128)(2,1)} fusion(f32[3584,1472]{0,1:T(8,128)} %fusion.113, f32[3584,1472]{0,1:T(8,128)} %fusion.106, bf16[128,3584]{1,0:T(8,128)(2,1)S(1)} %copy-done.61, f32[128,1472]{0,1:T(8,128)S(1)} %copy-done.23, bf16[128,1472]{0,1:T(8,128)(2,1)S(1)} %copy-done.76, f32[128]{0:T(128)S(1)} %broadcast_multiply_fusion.5, ...), kind=kOutput, calls=%fused_computation.45 | convolution fusion | flops 1368088576 | bytes 54818304 | tf_op jit(solution)/shard_map/tf,td->fd/dot_general | solution.py:343
  911.6 14.6 copy.185
  947.8 10.0 fusion.206
  960.6 11.9 reduce-scatter.22.cloned.1.call-done
  976.1 21.1 %reduce-scatter.26.cloned.1.call-done = f32[128,384]{0,1:T(8,128)} async-done(((f32[512,384]{0,1:T(8,128)}), f32[128,384]{0,1:T(8,128)}) %reduce-scatter.26.cloned.1.call-update) | async-done | bytes 196624 | tf_op jit(solution)/shard_map/reduce_scatter | solution.py:421
  1000.7 10.5 fusion.207
  1011.2 18.9 %add_convert_fusion.2 = bf16[1472,3584]{1,0:T(8,128)(2,1)} fusion(f32[1472,3584]{1,0:T(8,128)} %fusion.206, f32[1472,3584]{1,0:T(8,128)} %fusion.207, bf16[128,1472]{0,1:T(8,128)(2,1)S(1)} %copy-done.36, bf16[128,3584]{1,0:T(8,128)(2,1)S(1)} %copy-done.70), kind=kOutput, calls=%fused_computation.47 | convolution fusion | flops 1366392832 | bytes 54050816 | tf_op jit(solution)/shard_map/td,tf->df/dot_general | solution.py:352
  1066.0 10.2 fusion.208
  1076.2 9.0 fusion.209
  1085.2 19.3 %add_convert_fusion.1 = bf16[1472,3584]{1,0:T(8,128)(2,1)} fusion(f32[1472,3584]{1,0:T(8,128)} %fusion.208, f32[1472,3584]{1,0:T(8,128)} %fusion.209, bf16[128,1472]{0,1:T(8,128)(2,1)S(1)} %copy-done.37, bf16[128,3584]{1,0:T(8,128)(2,1)S(1)} %copy-done.68), kind=kOutput, calls=%fused_computation.46 | convolution fusion | flops 1366392832 | bytes 54050816 | tf_op jit(solution)/shard_map/td,tf->df/dot_general | solution.py:355
  1137.9 5.8 all-to-all-done.7
  1147.1 6.8 all-to-all-done.6
  1167.1 24.9 %reduce-scatter.40.cloned.1.call-done = bf16[896,1472]{1,0:T(8,128)(2,1)} async-done(((bf16[3584,1472]{1,0:T(8,128)(2,1)}), bf16[896,1472]{1,0:T(8,128)(2,1)}) %reduce-scatter.40.cloned.1.call-update) | async-done | bytes 2637840
  1196.5 28.5 %reduce-scatter.28.cloned.1.call-done = bf16[368,384]{1,0:T(8,128)(2,1)} async-done(((bf16[1472,384]{1,0:T(8,128)(2,1)}), bf16[368,384]{1,0:T(8,128)(2,1)}) %reduce-scatter.28.cloned.1.call-update) | async-done | bytes 282640 | tf_op jit(solution)/shard_map/reduce_scatter | solution.py:467
  1225.0 30.8 %reduce-scatter.34.cloned.1.call-done = bf16[96,1472]{1,0:T(8,128)(2,1)} async-done(((bf16[384,1472]{1,0:T(8,128)(2,1)}), bf16[96,1472]{1,0:T(8,128)(2,1)}) %reduce-scatter.34.cloned.1.call-update) | async-done | bytes 282640 | tf_op jit(solution)/shard_map/reduce_scatter | solution.py:476
  1255.8 29.7 %reduce-scatter.30.cloned.1.call-done = bf16[368,384]{1,0:T(8,128)(2,1)} async-done(((bf16[1472,384]{1,0:T(8,128)(2,1)}), bf16[368,384]{1,0:T(8,128)(2,1)}) %reduce-scatter.30.cloned.1.call-update) | async-done | bytes 282640 | tf_op jit(solution)/shard_map/reduce_scatter | solution.py:470
  1285.4 29.6 %reduce-scatter.32.cloned.1.call-done = bf16[368,384]{1,0:T(8,128)(2,1)} async-done(((bf16[1472,384]{1,0:T(8,128)(2,1)}), bf16[368,384]{1,0:T(8,128)(2,1)}) %reduce-scatter.32.cloned.1.call-update) | async-done | bytes 282640 | tf_op jit(solution)/shard_map/reduce_scatter | solution.py:473
  1315.1 179.9 %reduce-scatter.36.cloned.1.call-done = bf16[368,3584]{1,0:T(8,128)(2,1)} async-done(((bf16[1472,3584]{1,0:T(8,128)(2,1)}), bf16[368,3584]{1,0:T(8,128)(2,1)}) %reduce-scatter.36.cloned.1.call-update) | async-done | bytes 2637840 | tf_op jit(solution)/shard_map/reduce_scatter | solution.py:485
  1495.0 182.5 %reduce-scatter.38.cloned.1.call-done = bf16[368,3584]{1,0:T(8,128)(2,1)} async-done(((bf16[1472,3584]{1,0:T(8,128)(2,1)}), bf16[368,3584]{1,0:T(8,128)(2,1)}) %reduce-scatter.38.cloned.1.call-update) | async-done | bytes 2637840 | tf_op jit(solution)/shard_map/reduce_scatter | solution.py:488
  1687.3 12.2 all-to-all-done.3
  1722.5 7.2 all-to-all-done.17
  1753.1 19.4 %all-reduce.18 = (bf16[1472]{0:T(1024)(128)(2,1)S(1)}, bf16[32,6]{1,0:T(8,128)(2,1)S(1)}, bf16[1472]{0:T(1024)(128)(2,1)S(1)}, bf16[1472]{0:T(1024)(128)(2,1)S(1)}, bf16[1472]{0:T(1024)(128)(2,1)S(1)}) all-reduce(bf16[1472]{0:T(1024)(128)(2,1)S(1)} %add_convert_fusion.6, ...), channel_id=8, replica_groups=mesh['rep'=8,'shard'=4] {'shard'}, use_global_device_ids=true, to_apply=%region_48.50.clone | all-reduce | flops 6080 | bytes 24320
  1772.9 12.8 all-reduce.16
  1793.2 22.9 %all-reduce.22.cloned.1.call-done = (bf16[368,384]{1,0:T(8,128)(2,1)}, bf16[368,384]{1,0:T(8,128)(2,1)}, bf16[368,384]{1,0:T(8,128)(2,1)}, bf16[96,1472]{1,0:T(8...) async-done(((bf16[368,384]{1,0:T(8,128)(2,1)}, bf16[368,384]{1,0:T(8,128)(2,1)}, bf16[368,384]{1,0:T(8,128)(2,1)}, ...) | async-done | bytes 9043984 | tf_op jit(solution)/shard_map/psum | solution.py:504
  (782 shorter events, 427.9 us)
Async XLA Ops:
  12.0 201.6 %all-gather.8.cloned.1.call-start = ((), (), s32[]{:S(2)}) async-start(), calls=%async_computation.31 | async-start | bytes 1413120 | tf_op jit(solution)/shard_map/all_gather | solution.py:135
  12.5 224.7 %all-gather.10.cloned.1.call-start = ((), (), s32[]{:S(2)}) async-start(), calls=%async_computation.32 | async-start | bytes 1413120 | tf_op jit(solution)/shard_map/all_gather | solution.py:133
  13.1 226.9 %all-gather.12.cloned.1.call-start = ((), (), s32[]{:S(2)}) async-start(), calls=%async_computation.33 | async-start | bytes 1413120 | tf_op jit(solution)/shard_map/all_gather | solution.py:134
  13.7 368.8 %all-gather.14.cloned.1.call-start = ((), (), s32[]{:S(2)}) async-start(), calls=%async_computation.34 | async-start | bytes 1474560 | tf_op jit(solution)/shard_map/all_gather | solution.py:136
  14.5 376.1 %all-gather.16.cloned.1.call-start = ((), (), s32[]{:S(2)}) async-start(), calls=%async_computation.35 | async-start | bytes 13189120 | tf_op jit(solution)/shard_map/all_gather | solution.py:139
  15.2 560.1 %all-gather.18.cloned.1.call-start = ((), (), s32[]{:S(2)}) async-start(), calls=%async_computation.36 | async-start | bytes 13189120 | tf_op jit(solution)/shard_map/all_gather | solution.py:140
  16.0 743.9 %all-gather.20.cloned.1.call-start = ((), (), s32[]{:S(2)}) async-start(), calls=%async_computation.37 | async-start | bytes 13189120 | tf_op jit(solution)/shard_map/all_gather | solution.py:141
  59.3 8.7 all-to-all-start.16
  68.0 8.7 all-to-all-start.13
  76.6 8.8 all-to-all-start.10
  85.4 24.7 %all-to-all-start.4 = ((bf16[4,32,1472]{2,1,0:T(8,128)(2,1)}), bf16[4,32,1472]{2,1,0:T(8,128)(2,1)S(1)}, u32[]{:S(2)}, u32[]{:S(2)}) async-start(bf16[4,32,1472]{2,1,0:T(8,128)(2,1)} %bitcast.44), calls=%async_computation.4 | async-start | bytes 786432 | tf_op jit(solution)/shard_map/all_to_all | solution.py:154
  88.9 261.6 %copy-start.77 = (f32[1472]{0:T(1024)}, f32[1472]{0:T(1024)S(1)}, u32[]{:S(2)}) copy-start(f32[1472]{0:T(1024)S(1)} %convert_element_type.519) | copy-start | bytes 17668
  110.1 12.3 all-to-all-start
  122.4 27.0 %all-to-all-start.2 = ((bf16[4,32,1472]{2,1,0:T(8,128)(2,1)}), bf16[4,32,1472]{2,1,0:T(8,128)(2,1)S(1)}, u32[]{:S(2)}, u32[]{:S(2)}) async-start(bf16[4,32,1472]{2,1,0:T(8,128)(2,1)} %bitcast.25), calls=%async_computation.2 | async-start | bytes 786432 | tf_op jit(solution)/shard_map/all_to_all | solution.py:154
  149.4 15.5 all-to-all-start.12
  164.9 25.0 %all-to-all-start.9 = ((bf16[4,32,1472]{2,1,0:T(8,128)(2,1)}), bf16[4,32,1472]{2,1,0:T(8,128)(2,1)S(1)}, u32[]{:S(2)}, u32[]{:S(2)}) async-start(bf16[4,32,1472]{2,1,0:T(8,128)(2,1)} %bitcast.63), calls=%async_computation.9 | async-start | bytes 786432 | tf_op jit(solution)/shard_map/all_to_all | solution.py:161
  189.9 19.6 %all-to-all-start.15 = ((bf16[4,32,1472]{2,1,0:T(8,128)(2,1)}), bf16[4,32,1472]{2,1,0:T(8,128)(2,1)S(1)}, u32[]{:S(2)}, u32[]{:S(2)}) async-start(bf16[4,32,1472]{2,1,0:T(8,128)(2,1)} %bitcast.91), calls=%async_computation.19 | async-start | bytes 786432 | tf_op jit(solution)/shard_map/all_to_all | solution.py:161
  193.3 744.5 %reduce-scatter.16.cloned.1.call-start = ((), (), s32[]{:S(2)}) async-start(), calls=%async_computation.38 | async-start | bytes 983040 | tf_op jit(solution)/shard_map/reduce_scatter | solution.py:415
  199.7 188.2 %copy-start = (bf16[128,1472]{0,1:T(8,128)(2,1)}, bf16[128,1472]{0,1:T(8,128)(2,1)S(1)}, u32[]{:S(2)}) copy-start(bf16[128,1472]{0,1:T(8,128)(2,1)S(1)} %copy.160) | copy-start | bytes 1130500
  200.8 181.7 %copy-start.2 = (bf16[128,1472]{0,1:T(8,128)(2,1)}, bf16[128,1472]{0,1:T(8,128)(2,1)S(1)}, u32[]{:S(2)}) copy-start(bf16[128,1472]{0,1:T(8,128)(2,1)S(1)} %copy.148) | copy-start | bytes 1130500
  202.0 183.8 %copy-start.4 = (bf16[128,1472]{0,1:T(8,128)(2,1)}, bf16[128,1472]{0,1:T(8,128)(2,1)S(1)}, u32[]{:S(2)}) copy-start(bf16[128,1472]{0,1:T(8,128)(2,1)S(1)} %copy.154) | copy-start | bytes 1130500
  213.0 85.6 %copy-start.131 = (f32[128]{0:T(128)}, f32[128]{0:T(128)S(1)}, u32[]{:S(2)}) copy-start(f32[128]{0:T(128)S(1)} %get-tuple-element.391) | copy-start | bytes 1540
  213.5 137.0 %copy-start.142 = (f32[128]{0:T(128)}, f32[128]{0:T(128)S(1)}, u32[]{:S(2)}) copy-start(f32[128]{0:T(128)S(1)} %get-tuple-element.397) | copy-start | bytes 1540
  390.2 391.5 %copy-start.35 = (bf16[128,1472]{0,1:T(8,128)(2,1)}, bf16[128,1472]{0,1:T(8,128)(2,1)S(1)}, u32[]{:S(2)}) copy-start(bf16[128,1472]{0,1:T(8,128)(2,1)S(1)} %get-tuple-element.378) | copy-start | bytes 1130500
  575.3 184.6 %copy-start.33 = (f32[128,1472]{0,1:T(8,128)S(1)}, f32[128,1472]{0,1:T(8,128)}, u32[]{:S(2)}) copy-start(f32[128,1472]{0,1:T(8,128)} %copy-done.32) | copy-start | bytes 2260996
  766.5 74.5 %copy-start.24 = (f32[128,1472]{0,1:T(8,128)}, f32[128,1472]{0,1:T(8,128)S(1)}, u32[]{:S(2)}) copy-start(f32[128,1472]{0,1:T(8,128)S(1)} %get-tuple-element.427) | copy-start | bytes 2260996
  851.7 89.0 %reduce-scatter.20.cloned.1.call-start = ((), (), s32[]{:S(2)}) async-start(), calls=%async_computation.40 | async-start | bytes 983040 | tf_op jit(solution)/shard_map/reduce_scatter | solution.py:415
  859.7 84.6 %reduce-scatter.24.cloned.1.call-start = ((), (), s32[]{:S(2)}) async-start(), calls=%async_computation.42 | async-start | bytes 983040 | tf_op jit(solution)/shard_map/reduce_scatter | solution.py:415
  868.4 89.4 %reduce-scatter.18.cloned.1.call-start = ((), (), s32[]{:S(2)}) async-start(), calls=%async_computation.39 | async-start | bytes 983040 | tf_op jit(solution)/shard_map/reduce_scatter | solution.py:421
  870.2 102.3 %reduce-scatter.22.cloned.1.call-start = ((), (), s32[]{:S(2)}) async-start(), calls=%async_computation.41 | async-start | bytes 983040 | tf_op jit(solution)/shard_map/reduce_scatter | solution.py:421
  873.0 124.2 %reduce-scatter.26.cloned.1.call-start = ((), (), s32[]{:S(2)}) async-start(), calls=%async_computation.43 | async-start | bytes 983040 | tf_op jit(solution)/shard_map/reduce_scatter | solution.py:421
  892.6 299.4 %reduce-scatter.40.cloned.1.call-start = ((), (), s32[]{:S(2)}) async-start(), calls=%async_computation.50 | async-start | bytes 13762560
  926.3 298.7 %reduce-scatter.28.cloned.1.call-start = ((), (), s32[]{:S(2)}) async-start(), calls=%async_computation.44 | async-start | bytes 1413120 | tf_op jit(solution)/shard_map/reduce_scatter | solution.py:467
  933.4 322.4 %reduce-scatter.34.cloned.1.call-start = ((), (), s32[]{:S(2)}) async-start(), calls=%async_computation.47 | async-start | bytes 1474560 | tf_op jit(solution)/shard_map/reduce_scatter | solution.py:476
  937.8 347.7 %reduce-scatter.30.cloned.1.call-start = ((), (), s32[]{:S(2)}) async-start(), calls=%async_computation.45 | async-start | bytes 1413120 | tf_op jit(solution)/shard_map/reduce_scatter | solution.py:470
  947.7 367.3 %reduce-scatter.32.cloned.1.call-start = ((), (), s32[]{:S(2)}) async-start(), calls=%async_computation.46 | async-start | bytes 1413120 | tf_op jit(solution)/shard_map/reduce_scatter | solution.py:473
  1000.6 494.4 %reduce-scatter.36.cloned.1.call-start = ((), (), s32[]{:S(2)}) async-start(), calls=%async_computation.48 | async-start | bytes 13189120 | tf_op jit(solution)/shard_map/reduce_scatter | solution.py:485
  1041.4 91.2 %all-to-all-start.8 = ((bf16[4,1,32]{2,1,0:T(2,128)(2,1)}), bf16[4,1,32]{2,1,0:T(2,128)(2,1)S(1)}, u32[]{:S(2)}, u32[]{:S(2)}) async-start(bf16[4,1,32]{2,1,0:T(2,128)(2,1)} %convert_element_type.653), calls=%async_computation.8 | async-start | bytes 4096 | tf_op jit(solution)/shard_map/all_to_all | solution.py:246
  1044.6 632.9 %reduce-scatter.38.cloned.1.call-start = ((), (), s32[]{:S(2)}) async-start(), calls=%async_computation.49 | async-start | bytes 13189120 | tf_op jit(solution)/shard_map/reduce_scatter | solution.py:488
  1132.6 11.1 all-to-all-start.7
  1143.7 10.2 all-to-all-start.6
  1154.0 528.5 %all-to-all-start.5 = ((bf16[4,32,1472]{2,1,0:T(8,128)(2,1)}), bf16[4,32,1472]{2,1,0:T(8,128)(2,1)}, u32[]{:S(2)}, u32[]{:S(2)}) async-start(bf16[4,32,1472]{2,1,0:T(8,128)(2,1)} %bitcast.56), calls=%async_computation.5 | async-start | bytes 786432 | tf_op jit(solution)/shard_map/all_to_all | solution.py:239
  1158.1 658.0 %all-reduce.22.cloned.1.call-start = ((), (), s32[]{:S(2)}) async-start(), calls=%async_computation.51 | async-start | bytes 18112512 | tf_op jit(solution)/shard_map/psum | solution.py:504
  1682.4 17.1 all-to-all-start.3
  1699.5 15.9 all-to-all-start.1
  1715.4 14.3 all-to-all-start.17
  1729.7 13.3 all-to-all-start.14
  1743.0 47.6 %all-to-all-start.11 = ((bf16[4,32,1472]{2,1,0:T(8,128)(2,1)}), bf16[4,32,1472]{2,1,0:T(8,128)(2,1)S(1)}, u32[]{:S(2)}, u32[]{:S(2)}) async-start(bf16[4,32,1472]{2,1,0:T(8,128)(2,1)} %bitcast.73), calls=%async_computation.13 | async-start | bytes 786432 | tf_op jit(solution)/shard_map/all_to_all | solution.py:454
  (175 other events, 1276.9 us)
Sparse Core Ops, SparseCore 0:
  11.7 2.0 sort.51.cloned.1.call-done
  17.5 2.0 sort.49.cloned.1.call-done
  23.3 2.0 sort.47.cloned.1.call-done
  1677.7 138.3 all-reduce.21
  (3 shorter events, 0.0 us)
Sparse Core Ops, SparseCore 1:
  14.0 32.2 all-gather.7
  47.7 28.9 all-gather.9
  78.2 37.3 all-gather.11
  117.3 37.7 all-gather.13
  156.7 233.8 all-gather.15
  392.3 183.0 all-gather.17
  576.8 183.0 all-gather.19
  851.8 21.2 reduce-scatter.15
  875.3 22.4 reduce-scatter.19
  900.2 22.5 reduce-scatter.23
  925.0 22.5 reduce-scatter.17
  950.0 22.5 reduce-scatter.21
  974.8 22.5 reduce-scatter.25
  999.8 192.2 reduce-scatter.39
  1195.1 29.8 reduce-scatter.27
  1228.0 27.7 reduce-scatter.33
  1258.2 27.2 reduce-scatter.29
  1287.9 27.1 reduce-scatter.31
  1317.4 177.5 reduce-scatter.35
  1497.5 180.0 reduce-scatter.37
where the time goes:
time: 1850 us; the launch traced here: 1840 us
  waiting for transfers between devices  1020 us (55%)
  matrix products  295 us (16%)
  blocking collectives  201 us (11%)
  local copies, waits for them, and re-layouts  169 us (9%)
  starting transfers between devices  68.8 us (4%)
  other arithmetic  61.8 us (3%)
  between operations  20.5 us (1%)
    reduce_scatter x1, waiting for transfers between devices, on_device(): lax.psum_scatter(totals[8].astype(jnp.bfloat16), 'shard', scatter_dimensi...  183 us
    reduce_scatter x1, waiting for transfers between devices, on_device(): lax.psum_scatter(totals[7].astype(jnp.bfloat16), 'shard', scatter_dimensi...  180 us
    all_gather x1, waiting for transfers between devices, on_device(): lax.all_gather(w_up, 'shard', axis=0, tiled=True)  178 us
    all_gather x1, waiting for transfers between devices, on_device(): lax.all_gather(w_down, 'shard', axis=0, tiled=True)  176 us
    all_gather x3, blocking collectives, on_device(): lax.all_gather(key_local, 'shard', axis=0, tiled=True)  73.3 us
    all_gather x3, blocking collectives, on_device(): lax.all_gather(value_local, 'shard', axis=0, tiled=True)  64.7 us
    unnamed x391, local copies, waits for them, and re-layouts  44.3 us
    dot_general x3, matrix products, on_device(): jnp.einsum('td,tf->df', normed_two, gate_grad, preferred_element_type=jnp...  39.3 us
  transfers between devices with their start and end apart: 39, of which 28 were waited for; matrix products, arithmetic and copies ran while one was open for 22% of the time, Pallas kernels for 0%

commit v1 on v0

v1 whole, which is shorter than its diff:
```python
import functools

import jax
import jax.numpy as jnp
from jax import lax
from jax.experimental import pallas as pl
from jax.experimental.pallas import tpu as pltpu
from jax.sharding import PartitionSpec as P

EPSILON = 1e-06
HIGHEST = lax.Precision.HIGHEST
MASKED = -1000000000.0
BF16 = jnp.bfloat16
F32 = jnp.float32


def gelu_tanh(value):
    return jax.nn.gelu(value, approximate=True)


def rms_scale(hidden):
    return lax.rsqrt(jnp.mean(hidden * hidden, axis=-1, keepdims=True) + EPSILON)


def rms_back(hidden, scale_row, gain, upstream):
    scaled = upstream * gain
    return scale_row * scaled - hidden * (scale_row * scale_row * scale_row) * jnp.mean(
        hidden * scaled, axis=-1, keepdims=True
    )


def dot(left, right, kind=F32):
    return jnp.dot(left, right, preferred_element_type=F32).astype(kind)


def bias_kernel(rows_ref, slots_ref, out_ref):
    group = out_ref.shape[2]
    row = jnp.broadcast_to(rows_ref[0], (group, rows_ref.shape[2]))
    grid = pltpu.roll(row, group + 1, 1, stride=1, stride_axis=0)[:, :group].astype(BF16)
    tokens = slots_ref.shape[0]
    pick = (slots_ref[...] == lax.broadcasted_iota(jnp.int32, (tokens, group), 1)).astype(BF16)
    out_ref[0] = jnp.dot(pick, grid, preferred_element_type=F32)


def bias_of_queries(bias_rows, slots, group):
    heads, width = bias_rows.shape
    tokens = slots.shape[0]
    return pl.pallas_call(
        bias_kernel,
        grid=(heads,),
        in_specs=[
            pl.BlockSpec((1, 1, width), lambda h: (h, 0, 0)),
            pl.BlockSpec((tokens, 1), lambda h: (0, 0)),
        ],
        out_specs=pl.BlockSpec((1, tokens, group), lambda h: (h, 0, 0)),
        out_shape=jax.ShapeDtypeStruct((heads, tokens, group), F32),
    )(bias_rows.reshape(heads, 1, width), slots.reshape(tokens, 1))


def fold_kernel(grad_ref, slots_ref, out_ref):
    tokens, group = grad_ref.shape[1:]
    place = (
        lax.broadcasted_iota(jnp.int32, (group, tokens), 0) == (group - 1) - slots_ref[...]
    ).astype(BF16)
    square = jnp.dot(place, grad_ref[0], preferred_element_type=F32)
    wide = jnp.concatenate([square, jnp.zeros_like(square)], axis=1)
    rolled = pltpu.roll(wide, 0, 1, stride=1, stride_axis=0)
    out_ref[0] = jnp.sum(rolled, axis=0, keepdims=True)


def bias_fold(score_grad, slots):
    heads, tokens, group = score_grad.shape
    return pl.pallas_call(
        fold_kernel,
        grid=(heads,),
        in_specs=[
            pl.BlockSpec((1, tokens, group), lambda h: (h, 0, 0)),
            pl.BlockSpec((1, tokens), lambda h: (0, 0)),
        ],
        out_specs=pl.BlockSpec((1, 1, 2 * group), lambda h: (h, 0, 0)),
        out_shape=jax.ShapeDtypeStruct((heads, 1, 2 * group), F32),
    )(score_grad, slots.reshape(1, tokens)).reshape(heads, 2 * group)


def on_device(
    tokens,
    cotangent,
    gate_cotangent,
    slot_of,
    seq_lengths,
    buckets,
    gain_attn,
    w_query,
    w_key,
    w_value,
    w_out,
    rel_bias,
    gain_ffn,
    w_gate,
    w_up,
    w_down,
    gain_delete,
    w_delete,
):
    shards = lax.axis_size("shard")
    reps = lax.axis_size("rep")
    chips = reps // 2
    rank = lax.axis_index("shard")
    rep_rank = lax.axis_index("rep")
    core = rep_rank % 2
    chip = rep_rank // 2
    micro_count, local_rows, width = tokens.shape
    group = local_rows * shards
    rows = micro_count * local_rows
    heads = rel_bias.shape[1]
    bucket_rows = rel_bias.shape[0]
    bucket_count = bucket_rows * shards
    proj = w_query.shape[1]
    head_size = proj // heads
    block = gain_attn.shape[0]
    inner = w_gate.shape[1]
    half_inner = inner // 2
    col_piece = inner // chips
    down_block = w_down.shape[0]
    down_half = down_block // 2
    down_piece = down_half // chips
    half_shards = shards // 2

    def swap(value, mask):
        return lax.ppermute(value, "rep", [(i, i ^ mask) for i in range(reps)])

    def shift(value):
        return lax.ppermute(value, "shard", [(i, (i + 1) % shards) for i in range(shards)])

    def cut(count):
        half = count // 2
        return half // 16 * 16 if half >= 16 else half

    def plane_gather(piece):
        if chips == 1:
            return []
        near = swap(piece, 2)
        found = [(1, 0, near)]
        if chips >= 4:
            far = swap(piece, 4)
            middle = cut(piece.shape[0])
            found += [
                (2, 0, far),
                (3, 0, swap(far[:middle], 2)),
                (3, middle, swap(near[middle:], 4)),
            ]
        bit = 4
        while bit < chips:
            found += [
                (mask ^ bit, start, swap(part, 2 * bit))
                for mask, start, part in [(0, 0, piece)] + found
            ]
            bit *= 2
        return found

    def plane_reduce(take):
        def reduce_level(get, level):
            if level == 1:
                return get(0)
            if level == 2:
                return (get(0).astype(F32) + swap(get(1), 2).astype(F32)).astype(BF16)
            if level == 4:
                diagonal = get(3)
                middle = cut(diagonal.shape[0])
                top = swap(diagonal[:middle], 2)
                low = swap(diagonal[middle:], 4)
                far, near = get(2), get(1)
                far = jnp.concatenate(
                    [(far[:middle].astype(F32) + top.astype(F32)).astype(BF16), far[middle:]]
                )
                near = jnp.concatenate(
                    [near[:middle], (near[middle:].astype(F32) + low.astype(F32)).astype(BF16)]
                )
                return (
                    get(0).astype(F32) + swap(far, 4).astype(F32) + swap(near, 2).astype(F32)
                ).astype(BF16)
            bit = level // 2
            return reduce_level(
                lambda mask: (
                    get(mask).astype(F32) + swap(get(mask ^ bit), 2 * bit).astype(F32)
                ).astype(BF16),
                bit,
            )

        return reduce_level(take, chips)

    def ring_reduce(block_of):
        total = block_of(1)
        for step in range(2, shards + 1):
            arrived = shift(total)
            total = (arrived.astype(F32) + block_of(step % shards).astype(F32)).astype(BF16)
        return total

    def source(step):
        return (rank - step) % shards

    vector_pack = jnp.concatenate(
        [gain_attn, gain_ffn, gain_delete, w_delete, rel_bias.reshape(-1)]
    ).reshape(1, -1)
    vectors = jnp.zeros((shards, vector_pack.shape[1]), BF16)
    moving = vector_pack
    vectors = lax.dynamic_update_slice(vectors, moving, (rank, 0))
    for step in range(1, shards):
        moving = shift(moving)
        vectors = lax.dynamic_update_slice(vectors, moving, (source(step), 0))
    attn_gain = vectors[:, :block].reshape(width).astype(F32)
    ffn_gain = vectors[:, block : 2 * block].reshape(width).astype(F32)
    delete_gain = vectors[:, 2 * block : 3 * block].reshape(width).astype(F32)
    delete_vec = vectors[:, 3 * block : 4 * block].reshape(width).astype(F32)
    bias_table = vectors[:, 4 * block :].reshape(bucket_count, heads)

    attn_rows = 4 * block // reps
    per_matrix = reps // 4
    attn_own = jnp.stack([w_query, w_key, w_value, w_out.reshape(block, proj)]).reshape(
        4, per_matrix, attn_rows, proj
    )
    attn_full = jnp.zeros((4, shards, per_matrix, attn_rows, proj), BF16)
    attn_full = lax.dynamic_update_slice(attn_full, attn_own[:, None], (0, rank, 0, 0, 0))
    attn_piece = lax.dynamic_index_in_dim(
        attn_own.reshape(reps, attn_rows, proj), rep_rank, 0, keepdims=False
    )
    attn_moving = attn_piece
    attn_foreign = []
    for step in range(1, shards):
        attn_moving = shift(attn_moving)
        attn_foreign.append(attn_moving)
    stacked = jnp.stack(attn_foreign)
    attn_found = [(0, 0, stacked)] + plane_gather_stack(plane_gather, stacked)
    attn_found = [(2 * mask, start, part) for mask, start, part in attn_found]
    attn_found = attn_found + [(mask ^ 1, start, swap(part, 1)) for mask, start, part in attn_found]
    for mask, start, part in attn_found:
        owner = rep_rank ^ mask
        for index in range(part.shape[0]):
            attn_full = lax.dynamic_update_slice(
                attn_full,
                part[index][None, None, None],
                (owner // per_matrix, source(start + index + 1), owner % per_matrix, 0, 0),
            )
    query_full = attn_full[0].reshape(width, proj)
    key_full = attn_full[1].reshape(width, proj)
    value_full = attn_full[2].reshape(width, proj)
    out_full = attn_full[3].reshape(proj, width)

    column = core * half_inner
    gate_up_own = jnp.concatenate(
        [
            lax.dynamic_slice_in_dim(w_gate, column, half_inner, 1),
            lax.dynamic_slice_in_dim(w_up, column, half_inner, 1),
        ],
        axis=1,
    )
    gate_up = jnp.zeros((width, inner), BF16)
    gate_up = lax.dynamic_update_slice(gate_up, gate_up_own, (rank * block, 0))
    moving = lax.dynamic_slice_in_dim(gate_up_own, chip * col_piece, col_piece, 1)
    for step in range(1, shards):
        moving = shift(moving)
        for mask, start, part in [(0, 0, moving)] + plane_gather(moving):
            gate_up = lax.dynamic_update_slice(
                gate_up, part, (source(step) * block + start, (chip ^ mask) * col_piece)
            )

    down_own = lax.dynamic_slice_in_dim(w_down, core * down_half, down_half, 0)
    carried = jnp.zeros((shards, down_half, width), BF16)
    carried = lax.dynamic_update_slice(carried, down_own[None], (rank, 0, 0))
    moving = lax.dynamic_slice_in_dim(down_own, chip * down_piece, down_piece, 0)
    for step in range(1, shards):
        moving = shift(moving)
        for mask, start, part in [(0, 0, moving)] + plane_gather(moving):
            carried = lax.dynamic_update_slice(
                carried, part[None], (source(step), (chip ^ mask) * down_piece + start, 0)
            )
    kept = lax.dynamic_slice_in_dim(carried, core * half_shards, half_shards, 0)
    given = swap(lax.dynamic_slice_in_dim(carried, (1 - core) * half_shards, half_shards, 0), 1)
    down = jnp.stack(
        [jnp.where(core == 0, kept, given), jnp.where(core == 0, given, kept)], axis=1
    ).reshape(half_inner, width)

    slots = slot_of[:, 0]
    own_slots = lax.dynamic_slice_in_dim(slots, rank * local_rows, local_rows, 1)
    order = (rank - jnp.arange(shards, dtype=jnp.int32)) % shards
    key_slots = jnp.take(slots.reshape(micro_count, shards, local_rows), order, axis=1)
    key_slots = key_slots.reshape(micro_count, group)
    to_slots = (
        key_slots[:, None, :] == jnp.arange(group, dtype=jnp.int32)[None, :, None]
    ).astype(BF16)
    onehot = (buckets[:, None] == jnp.arange(bucket_count, dtype=jnp.int32)[None, :]).astype(F32)
    onehot = jnp.pad(onehot, ((0, 1), (0, 0)))
    bias_rows = jnp.dot(onehot, bias_table.astype(F32), precision=HIGHEST).T
    bias = bias_of_queries(bias_rows, own_slots.reshape(rows), group).reshape(
        heads, micro_count, local_rows, group
    )
    first_len = seq_lengths[:, 0, 0]
    query_seg = own_slots >= first_len[:, None]
    key_seg = jnp.arange(group, dtype=jnp.int32)[None, :] >= first_len[:, None]
    same_seq = (query_seg[:, :, None] == key_seg[:, None, :])[None]

    hidden_in = tokens.reshape(rows, width).astype(F32)
    scale_one = rms_scale(hidden_in)
    normed_one = (hidden_in * scale_one * attn_gain).astype(BF16)
    queries = dot(normed_one, query_full, BF16)
    moving = jnp.concatenate(
        [dot(normed_one, key_full, BF16), dot(normed_one, value_full, BF16)], axis=1
    )
    arrived = [moving]
    for step in range(1, shards):
        moving = shift(moving)
        arrived.append(moving)
    pairs = jnp.stack([part.reshape(micro_count, local_rows, 2 * proj) for part in arrived], axis=1)
    pairs = pairs.reshape(micro_count, group, 2 * proj)
    packed = jnp.einsum("msj,mjc->msc", to_slots, pairs, preferred_element_type=F32).astype(BF16)
    packed = packed.reshape(micro_count, group, 2, heads, head_size)
    keys, values = packed[:, :, 0], packed[:, :, 1]
    queries = queries.reshape(micro_count, local_rows, heads, head_size)
    scores = jnp.einsum("mqhd,mkhd->hmqk", queries, keys, preferred_element_type=F32) + bias
    scores = jnp.where(same_seq, scores, MASKED)
    weights = jnp.exp(scores - jnp.max(scores, axis=-1, keepdims=True))
    probabilities = weights / jnp.sum(weights, axis=-1, keepdims=True)
    rounded = probabilities.astype(BF16)
    context = jnp.einsum("hmqk,mkhd->mqhd", rounded, values, preferred_element_type=F32)
    context = context.astype(BF16).reshape(rows, proj)
    hidden_mid = hidden_in + dot(context, out_full)

    scale_two = rms_scale(hidden_mid)
    normed_two = (hidden_mid * scale_two * ffn_gain).astype(BF16)
    normed_pair = jnp.concatenate([normed_two, swap(normed_two, 1)])
    both = dot(normed_pair, gate_up)
    gate_pre, up_pre = both[:, :half_inner], both[:, half_inner:]
    inner_act = (gelu_tanh(gate_pre) * up_pre).astype(BF16)
    partial = dot(inner_act, down)
    hidden_out = hidden_mid + partial[:rows] + swap(partial[rows:].astype(BF16), 1).astype(F32)
    scale_three = rms_scale(hidden_out)
    delete_norm = hidden_out * scale_three * delete_gain
    sigmoid_val = jax.nn.sigmoid(jnp.sum(delete_norm * delete_vec, axis=-1))
    deleted = -30.0 * sigmoid_val

    gate_upstream = gate_cotangent.reshape(rows).astype(F32)
    gate_slope = gate_upstream * -30.0 * sigmoid_val * (1.0 - sigmoid_val)
    grad_delete_vec = jnp.sum(gate_slope[:, None] * delete_norm, axis=0)
    delete_up = gate_slope[:, None] * delete_vec
    grad_delete_gain = jnp.sum(delete_up * hidden_out * scale_three, axis=0)
    grad_out = cotangent.reshape(rows, width).astype(F32) + rms_back(
        hidden_out, scale_three, delete_gain, delete_up
    )
    down_up = grad_out.astype(BF16)
    down_up_pair = jnp.concatenate([down_up, swap(down_up, 1)])

    grad_down = jnp.einsum("tf,td->fd", inner_act, down_up_pair, preferred_element_type=F32)
    grad_down = grad_down.astype(BF16).reshape(half_shards, 2, down_half, width)
    kept = lax.dynamic_index_in_dim(grad_down, core, 1, keepdims=False)
    given = swap(lax.dynamic_index_in_dim(grad_down, 1 - core, 1, keepdims=False), 1)
    carried = jnp.concatenate(
        [jnp.where(core == 0, kept, given), jnp.where(core == 0, given, kept)]
    )

    def down_block_of(step):
        return plane_reduce(
            lambda mask: lax.dynamic_slice(
                carried,
                (source(step), (chip ^ mask) * down_piece, 0),
                (1, down_piece, width),
            )[0]
        )

    down_sum = ring_reduce(down_block_of)

    inner_grad = jnp.einsum("td,fd->tf", down_up_pair, down, preferred_element_type=F32)
    activated, gelu_pull = jax.vjp(gelu_tanh, gate_pre)
    both_grad = jnp.concatenate(
        [
            gelu_pull(inner_grad * up_pre)[0].astype(BF16),
            (inner_grad * activated).astype(BF16),
        ],
        axis=1,
    )
    grad_gate_up = jnp.einsum("td,tf->df", normed_pair, both_grad, preferred_element_type=F32)
    grad_gate_up = grad_gate_up.astype(BF16)

    def gate_up_block_of(step):
        return plane_reduce(
            lambda mask: lax.dynamic_slice(
                grad_gate_up,
                (source(step) * block, (chip ^ mask) * col_piece),
                (block, col_piece),
            )
        )

    gate_up_sum = ring_reduce(gate_up_block_of)

    partial = jnp.einsum("tf,df->td", both_grad, gate_up, preferred_element_type=F32)
    normed_two_grad = partial[:rows] + swap(partial[rows:].astype(BF16), 1).astype(F32)
    grad_ffn_gain = jnp.sum(normed_two_grad * hidden_mid * scale_two, axis=0)
    grad_mid = grad_out + rms_back(hidden_mid, scale_two, ffn_gain, normed_two_grad)
    out_grad = grad_mid.astype(BF16)
    grad_w_out = jnp.einsum("th,td->hd", context, out_grad, preferred_element_type=F32)
    context_grad = jnp.einsum("td,hd->th", out_grad, out_full, preferred_element_type=F32)
    context_grad = context_grad.astype(BF16).reshape(micro_count, local_rows, heads, head_size)
    prob_grad = jnp.einsum("mqhd,mkhd->hmqk", context_grad, values, preferred_element_type=F32)
    inner_sum = jnp.sum(probabilities * prob_grad, axis=-1, keepdims=True)
    score_grad = (probabilities * (prob_grad - inner_sum)).astype(BF16)
    query_grad = jnp.einsum("hmqk,mkhd->mqhd", score_grad, keys, preferred_element_type=F32)
    query_grad = query_grad.astype(BF16).reshape(rows, proj)
    key_part = jnp.einsum("hmqk,mqhd->mkhd", score_grad, queries, preferred_element_type=F32)
    value_part = jnp.einsum("hmqk,mqhd->mkhd", rounded, context_grad, preferred_element_type=F32)
    pair_part = jnp.concatenate(
        [key_part.reshape(micro_count, group, proj), value_part.reshape(micro_count, group, proj)],
        axis=2,
    ).astype(BF16)
    pair_part = jnp.einsum("msj,msc->mjc", to_slots, pair_part, preferred_element_type=F32)
    pair_part = pair_part.astype(BF16).reshape(micro_count, shards, local_rows, 2 * proj)
    pair_sum = ring_reduce(lambda step: pair_part[:, step].reshape(rows, 2 * proj))
    grad_bias_rows = bias_fold(
        score_grad.reshape(heads, rows, group), own_slots.reshape(rows)
    )
    grad_bias = jnp.einsum("ob,ho->bh", onehot, grad_bias_rows, precision=HIGHEST)

    projected = jnp.concatenate([query_grad, pair_sum], axis=1)
    grad_proj = jnp.einsum("td,th->dh", normed_one, projected, preferred_element_type=F32)
    grad_proj = grad_proj.astype(BF16)
    normed_one_grad = (
        jnp.einsum("th,dh->td", query_grad, query_full, preferred_element_type=F32)
        + jnp.einsum("th,dh->td", pair_sum[:, :proj], key_full, preferred_element_type=F32)
        + jnp.einsum("th,dh->td", pair_sum[:, proj:], value_full, preferred_element_type=F32)
    )
    grad_attn_gain = jnp.sum(normed_one_grad * hidden_in * scale_one, axis=0)
    grad_in = grad_mid + rms_back(hidden_in, scale_one, attn_gain, normed_one_grad)

    attn_grads = jnp.stack(
        [
            grad_proj[:, :proj].reshape(shards, block, proj),
            grad_proj[:, proj : 2 * proj].reshape(shards, block, proj),
            grad_proj[:, 2 * proj :].reshape(shards, block, proj),
            grad_w_out.astype(BF16).reshape(shards, block, proj),
        ],
        axis=1,
    ).reshape(shards, chips, 2, attn_rows, proj)
    attn_grads = jnp.take(attn_grads, order, axis=0)
    kept = lax.dynamic_index_in_dim(attn_grads, core, 2, keepdims=False)
    given = swap(lax.dynamic_index_in_dim(attn_grads, 1 - core, 2, keepdims=False), 1)
    attn_grads = (kept.astype(F32) + given.astype(F32)).astype(BF16)
    attn_sum = plane_reduce(
        lambda mask: lax.dynamic_index_in_dim(attn_grads, chip ^ mask, 1, keepdims=False)
    )
    attn_sum = ring_reduce(lambda step: attn_sum[step])

    gate_up_half = jnp.zeros((block, inner), BF16)
    for mask, start, part in [(0, 0, gate_up_sum)] + plane_gather(gate_up_sum):
        gate_up_half = lax.dynamic_update_slice(
            gate_up_half, part, (start, (chip ^ mask) * col_piece)
        )
    gate_up_other = swap(gate_up_half, 1)
    low = jnp.where(core == 0, gate_up_half, gate_up_other).astype(F32)
    high = jnp.where(core == 0, gate_up_other, gate_up_half).astype(F32)
    grad_gate = jnp.concatenate([low[:, :half_inner], high[:, :half_inner]], axis=1)
    grad_up = jnp.concatenate([low[:, half_inner:], high[:, half_inner:]], axis=1)

    down_half_sum = jnp.zeros((down_half, width), BF16)
    for mask, start, part in [(0, 0, down_sum)] + plane_gather(down_sum):
        down_half_sum = lax.dynamic_update_slice(
            down_half_sum, part, ((chip ^ mask) * down_piece + start, 0)
        )
    down_other = swap(down_half_sum, 1)
    grad_down_out = jnp.concatenate(
        [jnp.where(core == 0, down_half_sum, down_other), jnp.where(core == 0, down_other, down_half_sum)]
    ).astype(F32)

    attn_half = jnp.zeros((chips, attn_rows, proj), BF16)
    for mask, start, part in [(0, 0, attn_sum)] + plane_gather(attn_sum):
        attn_half = lax.dynamic_update_slice(attn_half, part[None], (chip ^ mask, start, 0))
    attn_other = swap(attn_half, 1)
    attn_shard = jnp.stack(
        [jnp.where(core == 0, attn_half, attn_other), jnp.where(core == 0, attn_other, attn_half)],
        axis=1,
    ).reshape(4, block, proj).astype(F32)

    small = jnp.concatenate(
        [
            grad_attn_gain.reshape(shards, block),
            grad_ffn_gain.reshape(shards, block),
            grad_delete_gain.reshape(shards, block),
            grad_delete_vec.reshape(shards, block),
            grad_bias.reshape(shards, bucket_rows * heads),
        ],
        axis=1,
    )
    small = jnp.take(small, order, axis=0)
    bit = 1
    while bit < reps:
        small = small + swap(small, bit)
        bit *= 2
    total = small[1:2]
    for step in range(2, shards + 1):
        total = shift(total) + small[step % shards : step % shards + 1]
    total = total.reshape(-1)

    return (
        hidden_out.reshape(micro_count, local_rows, width),
        deleted.reshape(micro_count, local_rows),
        grad_in.astype(BF16).reshape(micro_count, local_rows, width),
        total[:block],
        attn_shard[0],
        attn_shard[1],
        attn_shard[2],
        attn_shard[3].reshape(proj // shards, width),
        total[4 * block :].reshape(bucket_rows, heads),
        total[block : 2 * block],
        grad_gate,
        grad_up,
        grad_down_out,
        total[2 * block : 3 * block],
        total[3 * block : 4 * block],
    )


def plane_gather_stack(plane_gather, stacked):
    return plane_gather(stacked)


def solution(mesh):
    rows = P(None, ("rep", "shard"), None)
    flat = P(None, ("rep", "shard"))
    by_rep = P(None, "rep", None)
    vector = P("shard")
    matrix = P("shard", None)
    in_specs = (
        (rows, rows, flat, by_rep, by_rep, P(), vector)
        + (matrix,) * 5
        + (vector,)
        + (matrix,) * 3
        + (vector, vector)
    )
    out_specs = (
        (rows, flat, rows, vector) + (matrix,) * 5 + (vector,) + (matrix,) * 3 + (vector, vector)
    )
    return jax.shard_map(
        on_device, mesh=mesh, in_specs=in_specs, out_specs=out_specs, check_vma=False
    )
```

time: 1850 us -> 846 us (0.46)
  waiting for transfers between devices: 1020 us -> 194 us
  blocking collectives: 201 us -> 0 us
  matrix products: 295 us -> 100 us
  local copies, waits for them, and re-layouts: 169 us -> 279 us
  other arithmetic: 61.8 us -> 118 us
  starting transfers between devices: 68.8 us -> 123 us
    reduce_scatter x12 -> x0, waiting for transfers between devices: 514 us -> none  [the longest x1 183 us: on_device(): lax.psum_scatter(totals[8].astype(jnp.bfloat16), 'shard', scatter_dimensi...]
    all_gather x7 -> x0, waiting for transfers between devices: 355 us -> none  [the longest x1 178 us: on_device(): lax.all_gather(w_up, 'shard', axis=0, tiled=True)]
    dot_general x85 -> x25, matrix products: 295 us -> 93.3 us  [the longest x6 23.3 us: dot(): return jnp.dot(left, right, preferred_element_type=F32).astype(kind)]
    ppermute x0 -> x124, waiting for transfers between devices: none -> 194 us  [the longest x94 135 us: swap(): return lax.ppermute(value, 'rep', [(i, i ^ mask) for i in range(reps)])]
    all_gather x7 -> x0, blocking collectives: 152 us -> none  [the longest x3 73.3 us: on_device(): lax.all_gather(key_local, 'shard', axis=0, tiled=True)]
    dynamic_update_slice x3 -> x71, local copies, waits for them, and re-layouts: 3.36 us -> 127 us  [the longest x15 87.6 us: on_device(): lax.dynamic_update_slice(gate_up, part, (source(step) * block + start, (c...]
    ppermute x0 -> x124, starting transfers between devices: none -> 123 us  [the longest x94 88 us: swap(): return lax.ppermute(value, 'rep', [(i, i ^ mask) for i in range(reps)])]
    all_to_all x18 -> x0, waiting for transfers between devices: 103 us -> none  [the longest x3 28.5 us: on_device(): lax.all_to_all(tokens[micro_step][send_order].reshape(shards, per_peer, m...]
  transfers between devices with their start and end apart: 39 -> 124, of which waited for: 28 -> 46; matrix products, arithmetic and copies ran while one was open for 22% -> 50% of each run, Pallas kernels for 0% -> 1%
where the time goes in v1:
time: 846 us; the launch traced here: 830 us
  local copies, waits for them, and re-layouts  279 us (33%)
  waiting for transfers between devices  194 us (23%)
  starting transfers between devices  123 us (15%)
  other arithmetic  118 us (14%)
  matrix products  100 us (12%)
  Pallas kernels  12.3 us (1%)
    ppermute x94, waiting for transfers between devices, swap(): return lax.ppermute(value, 'rep', [(i, i ^ mask) for i in range(reps)])  135 us
    ppermute x94, starting transfers between devices, swap(): return lax.ppermute(value, 'rep', [(i, i ^ mask) for i in range(reps)])  88 us
    dynamic_update_slice x15, local copies, waits for them, and re-layouts, on_device(): lax.dynamic_update_slice(gate_up, part, (source(step) * block + start, (c...  87.6 us
    ppermute x30, waiting for transfers between devices, shift(): lax.ppermute(value, 'shard', [(i, (i + 1) % shards) for i in range(shards)])  58.3 us
    ppermute x30, starting transfers between devices, shift(): lax.ppermute(value, 'shard', [(i, (i + 1) % shards) for i in range(shards)])  35.1 us
    unnamed x213, local copies, waits for them, and re-layouts  31.5 us
    dot_general x6, matrix products, dot(): return jnp.dot(left, right, preferred_element_type=F32).astype(kind)  23.3 us
    dynamic_update_slice x24, local copies, waits for them, and re-layouts, on_device(): lax.dynamic_update_slice(attn_full, part[index][None, None, None], (owner...  17.1 us
  transfers between devices with their start and end apart: 124, of which 46 were waited for; matrix products, arithmetic and copies ran while one was open for 50% of the time, Pallas kernels for 1%

profile of v1, /device:TPU:0, one launch (start us, length us, event | category | flops | bytes accessed | tf_op | source)
XLA Modules:
  0.0 829.6 jit_solution(7068604878358462016)
XLA Ops:
  25.4 4.5 broadcast_in_dim.164
  60.1 6.0 shard_map.289
  67.9 5.3 collective-permute-done.4
  89.8 7.1 dynamic_update_slice.258
  109.4 12.9 %collective-permute-done.40 = bf16[112,1472]{1,0:T(8,128)(2,1)S(1)} collective-permute-done((bf16[112,1472]{1,0:T(8,128)(2,1)S(1)}, bf16[112,1472]{1,0:T(8,128)(2,1)S(1)}, u32[]{:S(2)}, u32[]{:S(2)}) %collective-permute-start.40) | collective-permute-done | bytes 329760 | tf_op jit(solution)/shard_map/ppermute | solution.py:130
  174.6 6.8 dynamic_update_slice.259
  181.4 6.8 dynamic_update_slice.260
  232.6 7.1 dynamic_update_slice.263
  239.7 7.1 dynamic_update_slice.264
  246.8 7.1 dynamic_update_slice.265
  260.2 4.1 dynamic_update_slice.267
  264.3 7.2 dynamic_update_slice.268
  273.6 7.1 dynamic_update_slice.269
  280.7 7.1 dynamic_update_slice.270
  287.8 4.1 dynamic_update_slice.271
  291.9 4.1 dynamic_update_slice.272
  303.7 4.5 copy.175
  311.5 6.9 fusion.177
  332.7 13.0 %fusion.49 = f32[768,3584]{1,0:T(8,128)S(1)} fusion(bf16[1472,3584]{1,0:T(8,128)(2,1)} %dynamic_update_slice.272, bf16[384,1472]{0,1:T(8,128)(2,1)S(1)} %collective-permute-done.18, bf16[384,1472]{0,1:T(8,128)(2,1)S(1)} %multiply_convert_fusion.4), kind=kOutput, calls=%fused_computation.137 | convolution fusion | flops 8107917312 | bytes 23822336 | tf_op jit(solution)/shard_map/dot_general | solution.py:33
  349.8 4.8 fusion.180
  377.6 12.9 %fusion.8 = (bf16[768,1792]{1,0:T(8,128)(2,1)S(1)}, bf16[768,1792]{1,0:T(8,128)(2,1)S(1)}) fusion(f32[768,3584]{1,0:T(8,128)} %copy-done.20, bf16[1792,1472]{1,0:T(8,128)(2,1)} %bitcast.446, bf16[384,1472]{0,1:T(8,128)(2,1)} %collective-permute-done.51, bf16[384,1472]{0,1:T(8,128)(2,1)} %fusion.165), kind=kOutput, calls=%fused_computation.48 | convolution fusion | flops 4089249792 | bytes 24051712 | tf_op jit(solution)/shard_map/td,fd->tf/dot_general | solution.py:371
  390.5 13.1 %fusion.11 = f32[768,1472]{0,1:T(8,128)S(1)} fusion(bf16[1472,3584]{1,0:T(8,128)(2,1)} %dynamic_update_slice.272, bf16[768,1792]{1,0:T(8,128)(2,1)S(1)} %get-tuple-element.95, bf16[768,1792]{1,0:T(8,128)(2,1)S(1)} %get-tuple-element.94), kind=kOutput, calls=%fused_computation.65 | convolution fusion | flops 8114405376 | bytes 20578304 | tf_op jit(solution)/shard_map/tf,df->td/dot_general | solution.py:394
  406.5 11.2 %convolution_convert_fusion = bf16[1472,3584]{1,0:T(8,128)(2,1)S(1)} fusion(bf16[768,1792]{1,0:T(8,128)(2,1)} %copy-done.99, bf16[768,1792]{1,0:T(8,128)(2,1)} %copy-done.98, bf16[384,1472]{0,1:T(8,128)(2,1)S(1)} %copy-done.96, bf16[384,1472]{0,1:T(8,128)(2,1)S(1)} %copy-done.63), kind=kOutput, calls=%fused_computation.37 | convolution fusion | flops 8124203008 | bytes 18317312 | tf_op jit(solution)/shard_map/td,tf->df/dot_general | solution.py:380
  428.3 8.6 %convolution_convert_fusion.1 = bf16[1792,1472]{0,1:T(8,128)(2,1)} fusion(bf16[768,1792]{1,0:T(8,128)(2,1)S(1)} %copy-done.38, bf16[384,1472]{0,1:T(8,128)(2,1)} %collective-permute-done.51, bf16[384,1472]{0,1:T(8,128)(2,1)} %fusion.165), kind=kOutput, calls=%fused_computation.40 | convolution fusion | flops 4058857472 | bytes 10289152 | tf_op jit(solution)/shard_map/tf,td->fd/dot_general | solution.py:352
  436.9 8.2 copy.215
  461.4 7.4 collective-permute-done.92
  470.7 5.3 collective-permute-done.82
  476.1 7.4 collective-permute-done.77
  516.5 16.9 %multiply_convert_fusion.2 = bf16[6,3,128,512]{3,2,1,0:T(8,128)(2,1)S(1)} fusion(f32[6,3,128,512]{3,2,1,0:T(8,128)S(1)} %fusion.60, f32[6,3,128,512]{3,2,1,0:T(8,128)} %get-tuple-element.181, f32[6,3,128]{2,1,0:T(4,128)S(1)} %get-tuple-element.180), kind=kOutput, calls=%fused_computation.56 | output fusion | flops 7080703 | bytes 11805696 | tf_op jit(solution)/shard_map/sub | solution.py:404
  544.4 6.3 shard_map.290
  571.5 5.3 collective-permute-done.54
  579.5 11.4 %collective-permute-done.84 = bf16[368,896]{1,0:T(8,128)(2,1)} collective-permute-done((bf16[368,896]{1,0:T(8,128)(2,1)}, bf16[368,896]{1,0:T(8,128)(2,1)}, u32[]{:S(2)}, u32[]{:S(2)}) %collective-permute-start.84) | collective-permute-done | bytes 659488 | tf_op jit(solution)/shard_map/ppermute | solution.py:133
  600.5 4.4 collective-permute-done.115
  621.7 6.0 collective-permute-done.117
  629.2 4.2 collective-permute-done.102
  634.9 4.2 collective-permute-done.107
  640.6 4.2 collective-permute-done.112
  661.3 5.8 gather_fusion.2
  672.7 4.8 collective-permute-done.103
  705.1 7.8 collective-permute-done.109
  718.3 12.3 %collective-permute-done.94 = bf16[368,896]{1,0:T(8,128)(2,1)S(1)} collective-permute-done((bf16[368,896]{1,0:T(8,128)(2,1)S(1)}, bf16[368,896]{1,0:T(8,128)(2,1)S(1)}, u32[]{:S(2)}, u32[]{:S(2)}) %collective-permute-start.94) | collective-permute-done | bytes 659488 | tf_op jit(solution)/shard_map/ppermute | solution.py:130
  733.2 4.8 collective-permute-done.118
  752.8 6.7 collective-permute-done.63
  764.4 13.3 %collective-permute-done.122 = bf16[64,1472]{1,0:T(8,128)(2,1)S(1)} collective-permute-done((bf16[64,1472]{1,0:T(8,128)(2,1)S(1)}, bf16[64,1472]{1,0:T(8,128)(2,1)S(1)}, u32[]{:S(2)}, u32[]{:S(2)}) %collective-permute-start.122) | collective-permute-done | bytes 188448 | tf_op jit(solution)/shard_map/ppermute | solution.py:130
  779.6 8.1 collective-permute-done.67
  789.3 5.9 collective-permute-done.68
  797.2 4.9 collective-permute-done.69
  808.5 6.1 copy.218
  (743 shorter events, 475.5 us)
Async XLA Ops:
  4.9 84.8 %collective-permute-start.19 = (bf16[368,896]{1,0:T(8,128)(2,1)}, bf16[368,896]{1,0:T(8,128)(2,1)}, u32[]{:S(2)}, u32[]{:S(2)}) collective-permute-start(bf16[368,896]{1,0:T(8,128)(2,1)} %fusion.85), channel_id=1, source_target_pairs={{0,1},{1,2},{2,3},{3,0},{4,5},{5,6},{6,7},{7,4},{8,9},{9,10},{10,1... | collective-permute-start | bytes 1978376 | tf_op jit(solution)/shard_map/ppermute | solution.py:133
  11.2 55.0 %collective-permute-start.3 = (bf16[184,384]{1,0:T(8,128)(2,1)}, bf16[184,384]{1,0:T(8,128)(2,1)}, u32[]{:S(2)}, u32[]{:S(2)}) collective-permute-start(bf16[184,384]{1,0:T(8,128)(2,1)} %dynamic-slice_bitcast_fusion.8), channel_id=1, source_target_pairs={{0,1},{1,2},{2,3},{3,0},{4,5},{5,6},{6,7},{7,4},{8,9},{9,10},{10,1... | collective-permute-start | bytes 423944 | tf_op jit(solution)/shard_map/ppermute | solution.py:133
  13.0 28.4 %collective-permute-start = (bf16[1,1520]{1,0:T(2,128)(2,1)S(1)}, bf16[1,1520]{1,0:T(2,128)(2,1)S(1)}, u32[]{:S(2)}, u32[]{:S(2)}) collective-permute-start(bf16[1,1520]{1,0:T(2,128)(2,1)S(1)} %reshape.498), channel_id=1, source_target_pairs={{0,1},{1,2},{2,3},{3,0},{4,5},{5,6},{6,7},{7,4},{8,9},{9,10},{10,1... | collective-permute-start | bytes 9128 | tf_op jit(solution)/shard_map/ppermute | solution.py:133
  15.7 58.2 %collective-permute-start.34 = (bf16[112,1472]{1,0:T(8,128)(2,1)}, bf16[112,1472]{1,0:T(8,128)(2,1)}, u32[]{:S(2)}, u32[]{:S(2)}) collective-permute-start(bf16[112,1472]{1,0:T(8,128)(2,1)} %copy.225), channel_id=1, source_target_pairs={{0,1},{1,2},{2,3},{3,0},{4,5},{5,6},{6,7},{7,4},{8,9},{9,10},{10,1... | collective-permute-start | bytes 989192 | tf_op jit(solution)/shard_map/ppermute | solution.py:133
  77.1 23.9 %collective-permute-start.39 = (bf16[112,1472]{1,0:T(8,128)(2,1)}, bf16[112,1472]{1,0:T(8,128)(2,1)S(1)}, u32[]{:S(2)}, u32[]{:S(2)}) collective-permute-start(bf16[112,1472]{1,0:T(8,128)(2,1)} %collective-permute-done.34), channel_id=1, source_target_pairs={{0,1},{1,2},{2,3},{3,0},{4,5},{5,6},{6,7},{7,4},{8,9},{9,10},{10,1... | collective-permute-start | bytes 989192 | tf_op jit(solution)/shard_map/ppermute | solution.py:133
  86.0 21.1 %collective-permute-start.7 = (bf16[3,184,384]{2,1,0:T(8,128)(2,1)S(1)}, bf16[3,184,384]{2,1,0:T(8,128)(2,1)S(1)}, u32[]{:S(2)}, u32[]{:S(2)}) collective-permute-start(bf16[3,184,384]{2,1,0:T(8,128)(2,1)S(1)} %pad_maximum_fusion.27), channel_id=1, source_target_pairs={{0,16},{4,20},{8,24},{12,28},{16,0},{20,4},{24,8},{28,12},{1,17},{... | collective-permute-start | bytes 1271816 | tf_op jit(solution)/shard_map/ppermute | solution.py:130
  89.7 48.8 %collective-permute-start.10 = (bf16[3,184,384]{2,1,0:T(8,128)(2,1)S(1)}, bf16[3,184,384]{2,1,0:T(8,128)(2,1)S(1)}, u32[]{:S(2)}, u32[]{:S(2)}) collective-permute-start(bf16[3,184,384]{2,1,0:T(8,128)(2,1)S(1)} %pad_maximum_fusion.27), channel_id=1, source_target_pairs={{0,4},{4,0},{8,12},{12,8},{16,20},{20,16},{24,28},{28,24},{1,5},{5... | collective-permute-start | bytes 1271816 | tf_op jit(solution)/shard_map/ppermute | solution.py:130
  97.7 75.3 %collective-permute-start.20 = (bf16[368,896]{1,0:T(8,128)(2,1)}, bf16[368,896]{1,0:T(8,128)(2,1)S(1)}, u32[]{:S(2)}, u32[]{:S(2)}) collective-permute-start(bf16[368,896]{1,0:T(8,128)(2,1)} %collective-permute-done.19), channel_id=1, source_target_pairs={{0,8},{4,12},{8,0},{12,4},{16,24},{20,28},{24,16},{28,20},{1,9},{5... | collective-permute-start | bytes 1978376 | tf_op jit(solution)/shard_map/ppermute | solution.py:130
  101.0 54.9 %collective-permute-start.24 = (bf16[368,896]{1,0:T(8,128)(2,1)}, bf16[368,896]{1,0:T(8,128)(2,1)}, u32[]{:S(2)}, u32[]{:S(2)}) collective-permute-start(bf16[368,896]{1,0:T(8,128)(2,1)} %collective-permute-done.19), channel_id=1, source_target_pairs={{0,1},{1,2},{2,3},{3,0},{4,5},{5,6},{6,7},{7,4},{8,9},{9,10},{10,1... | collective-permute-start | bytes 1978376 | tf_op jit(solution)/shard_map/ppermute | solution.py:133
  155.9 32.9 %collective-permute-start.47 = (bf16[48,1472]{1,0:T(8,128)(2,1)S(1)}, bf16[48,1472]{1,0:T(8,128)(2,1)S(1)}, u32[]{:S(2)}, u32[]{:S(2)}) collective-permute-start(bf16[48,1472]{1,0:T(8,128)(2,1)S(1)} %slice.721), channel_id=1, source_target_pairs={{0,8},{4,12},{8,0},{12,4},{16,24},{20,28},{24,16},{28,20},{1,9},{5... | collective-permute-start | bytes 423944 | tf_op jit(solution)/shard_map/ppermute | solution.py:130
  157.6 30.6 %collective-permute-start.29 = (bf16[368,896]{1,0:T(8,128)(2,1)}, bf16[368,896]{1,0:T(8,128)(2,1)}, u32[]{:S(2)}, u32[]{:S(2)}) collective-permute-start(bf16[368,896]{1,0:T(8,128)(2,1)} %collective-permute-done.24), channel_id=1, source_target_pairs={{0,1},{1,2},{2,3},{3,0},{4,5},{5,6},{6,7},{7,4},{8,9},{9,10},{10,1... | collective-permute-start | bytes 1978376 | tf_op jit(solution)/shard_map/ppermute | solution.py:133
  166.2 24.5 %collective-permute-start.15 = (bf16[384,768]{0,1:T(8,128)(2,1)S(1)}, bf16[384,768]{0,1:T(8,128)(2,1)}, u32[]{:S(2)}, u32[]{:S(2)}) collective-permute-start(bf16[384,768]{0,1:T(8,128)(2,1)S(1)} %pad_maximum_fusion.24), channel_id=1, source_target_pairs={{0,1},{1,2},{2,3},{3,0},{4,5},{5,6},{6,7},{7,4},{8,9},{9,10},{10,1... | collective-permute-start | bytes 1769480 | tf_op jit(solution)/shard_map/ppermute | solution.py:133
  170.1 31.6 %collective-permute-start.25 = (bf16[368,896]{1,0:T(8,128)(2,1)}, bf16[368,896]{1,0:T(8,128)(2,1)}, u32[]{:S(2)}, u32[]{:S(2)}) collective-permute-start(bf16[368,896]{1,0:T(8,128)(2,1)} %collective-permute-done.24), channel_id=1, source_target_pairs={{0,8},{4,12},{8,0},{12,4},{16,24},{20,28},{24,16},{28,20},{1,9},{5... | collective-permute-start | bytes 1978376 | tf_op jit(solution)/shard_map/ppermute | solution.py:130
  172.9 37.4 %collective-permute-start.26 = (bf16[368,896]{1,0:T(8,128)(2,1)}, bf16[368,896]{1,0:T(8,128)(2,1)}, u32[]{:S(2)}, u32[]{:S(2)}) collective-permute-start(bf16[368,896]{1,0:T(8,128)(2,1)} %collective-permute-done.24), channel_id=1, source_target_pairs={{0,16},{4,20},{8,24},{12,28},{16,0},{20,4},{24,8},{28,12},{1,17},{... | collective-permute-start | bytes 1978376 | tf_op jit(solution)/shard_map/ppermute | solution.py:130
  188.9 23.8 %collective-permute-start.31 = (bf16[368,896]{1,0:T(8,128)(2,1)}, bf16[368,896]{1,0:T(8,128)(2,1)}, u32[]{:S(2)}, u32[]{:S(2)}) collective-permute-start(bf16[368,896]{1,0:T(8,128)(2,1)} %collective-permute-done.29), channel_id=1, source_target_pairs={{0,16},{4,20},{8,24},{12,28},{16,0},{20,4},{24,8},{28,12},{1,17},{... | collective-permute-start | bytes 1978376 | tf_op jit(solution)/shard_map/ppermute | solution.py:130
  210.3 49.9 %collective-permute-start.28 = (bf16[192,896]{1,0:T(8,128)(2,1)}, bf16[192,896]{1,0:T(8,128)(2,1)}, u32[]{:S(2)}, u32[]{:S(2)}) collective-permute-start(bf16[192,896]{1,0:T(8,128)(2,1)} %slice.712), channel_id=1, source_target_pairs={{0,16},{4,20},{8,24},{12,28},{16,0},{20,4},{24,8},{28,12},{1,17},{... | collective-permute-start | bytes 1032200 | tf_op jit(solution)/shard_map/ppermute | solution.py:130
  210.6 85.4 %collective-permute-start.17 = (bf16[384,768]{0,1:T(8,128)(2,1)}, bf16[384,768]{0,1:T(8,128)(2,1)}, u32[]{:S(2)}, u32[]{:S(2)}) collective-permute-start(bf16[384,768]{0,1:T(8,128)(2,1)} %collective-permute-done.16), channel_id=1, source_target_pairs={{0,1},{1,2},{2,3},{3,0},{4,5},{5,6},{6,7},{7,4},{8,9},{9,10},{10,1... | collective-permute-start | bytes 1769480 | tf_op jit(solution)/shard_map/ppermute | solution.py:133
  212.6 79.3 %collective-permute-start.33 = (bf16[192,896]{1,0:T(8,128)(2,1)}, bf16[192,896]{1,0:T(8,128)(2,1)}, u32[]{:S(2)}, u32[]{:S(2)}) collective-permute-start(bf16[192,896]{1,0:T(8,128)(2,1)} %slice.714), channel_id=1, source_target_pairs={{0,16},{4,20},{8,24},{12,28},{16,0},{20,4},{24,8},{28,12},{1,17},{... | collective-permute-start | bytes 1032200 | tf_op jit(solution)/shard_map/ppermute | solution.py:130
  218.3 37.8 %collective-permute-start.27 = (bf16[176,896]{1,0:T(8,128)(2,1)}, bf16[176,896]{1,0:T(8,128)(2,1)}, u32[]{:S(2)}, u32[]{:S(2)}) collective-permute-start(bf16[176,896]{1,0:T(8,128)(2,1)} %slice.711), channel_id=1, source_target_pairs={{0,8},{4,12},{8,0},{12,4},{16,24},{20,28},{24,16},{28,20},{1,9},{5... | collective-permute-start | bytes 946184 | tf_op jit(solution)/shard_map/ppermute | solution.py:130
  219.8 68.0 %collective-permute-start.32 = (bf16[176,896]{1,0:T(8,128)(2,1)}, bf16[176,896]{1,0:T(8,128)(2,1)}, u32[]{:S(2)}, u32[]{:S(2)}) collective-permute-start(bf16[176,896]{1,0:T(8,128)(2,1)} %slice.713), channel_id=1, source_target_pairs={{0,8},{4,12},{8,0},{12,4},{16,24},{20,28},{24,16},{28,20},{1,9},{5... | collective-permute-start | bytes 946184 | tf_op jit(solution)/shard_map/ppermute | solution.py:130
  256.1 71.7 %collective-permute-start.49 = (bf16[2,448,1472]{2,1,0:T(8,128)(2,1)}, bf16[2,448,1472]{2,1,0:T(8,128)(2,1)}, u32[]{:S(2)}, u32[]{:S(2)}) collective-permute-start(bf16[2,448,1472]{2,1,0:T(8,128)(2,1)} %constant_dynamic-slice_fusion), channel_id=1, source_target_pairs={{0,4},{4,0},{8,12},{12,8},{16,20},{20,16},{24,28},{28,24},{1,5},{5... | collective-permute-start | bytes 7913480 | tf_op jit(solution)/shard_map/ppermute | solution.py:130
  406.1 98.4 %collective-permute-start.52 = (bf16[384,1472]{0,1:T(8,128)(2,1)}, bf16[384,1472]{0,1:T(8,128)(2,1)}, u32[]{:S(2)}, u32[]{:S(2)}) collective-permute-start(bf16[384,1472]{0,1:T(8,128)(2,1)} %slice.944), channel_id=1, source_target_pairs={{0,4},{4,0},{8,12},{12,8},{16,20},{20,16},{24,28},{28,24},{1,5},{5... | collective-permute-start | bytes 3391496 | tf_op jit(solution)/shard_map/ppermute | solution.py:130
  423.2 27.1 %collective-permute-start.85 = (bf16[176,896]{1,0:T(8,128)(2,1)}, bf16[176,896]{1,0:T(8,128)(2,1)}, u32[]{:S(2)}, u32[]{:S(2)}) collective-permute-start(bf16[176,896]{1,0:T(8,128)(2,1)} %get-tuple-element.100), channel_id=1, source_target_pairs={{0,8},{4,12},{8,0},{12,4},{16,24},{20,28},{24,16},{28,20},{1,9},{5... | collective-permute-start | bytes 946184 | tf_op jit(solution)/shard_map/ppermute | solution.py:130
  426.3 26.1 %collective-permute-start.90 = (bf16[176,896]{1,0:T(8,128)(2,1)}, bf16[176,896]{1,0:T(8,128)(2,1)}, u32[]{:S(2)}, u32[]{:S(2)}) collective-permute-start(bf16[176,896]{1,0:T(8,128)(2,1)} %get-tuple-element.102), channel_id=1, source_target_pairs={{0,8},{4,12},{8,0},{12,4},{16,24},{20,28},{24,16},{28,20},{1,9},{5... | collective-permute-start | bytes 946184 | tf_op jit(solution)/shard_map/ppermute | solution.py:130
  426.3 26.1 %collective-permute-start.80 = (bf16[176,896]{1,0:T(8,128)(2,1)}, bf16[176,896]{1,0:T(8,128)(2,1)}, u32[]{:S(2)}, u32[]{:S(2)}) collective-permute-start(bf16[176,896]{1,0:T(8,128)(2,1)} %get-tuple-element.105), channel_id=1, source_target_pairs={{0,8},{4,12},{8,0},{12,4},{16,24},{20,28},{24,16},{28,20},{1,9},{5... | collective-permute-start | bytes 946184 | tf_op jit(solution)/shard_map/ppermute | solution.py:130
  428.3 26.3 %collective-permute-start.75 = (bf16[176,896]{1,0:T(8,128)(2,1)}, bf16[176,896]{1,0:T(8,128)(2,1)}, u32[]{:S(2)}, u32[]{:S(2)}) collective-permute-start(bf16[176,896]{1,0:T(8,128)(2,1)} %get-tuple-element.107), channel_id=1, source_target_pairs={{0,8},{4,12},{8,0},{12,4},{16,24},{20,28},{24,16},{28,20},{1,9},{5... | collective-permute-start | bytes 946184 | tf_op jit(solution)/shard_map/ppermute | solution.py:130
  452.4 23.6 %collective-permute-start.82 = (bf16[192,896]{1,0:T(8,128)(2,1)S(1)}, bf16[192,896]{1,0:T(8,128)(2,1)S(1)}, u32[]{:S(2)}, u32[]{:S(2)}) collective-permute-start(bf16[192,896]{1,0:T(8,128)(2,1)S(1)} %get-tuple-element.112), channel_id=1, source_target_pairs={{0,16},{4,20},{8,24},{12,28},{16,0},{20,4},{24,8},{28,12},{1,17},{... | collective-permute-start | bytes 1032200 | tf_op jit(solution)/shard_map/ppermute | solution.py:130
  454.6 28.8 %collective-permute-start.77 = (bf16[192,896]{1,0:T(8,128)(2,1)S(1)}, bf16[192,896]{1,0:T(8,128)(2,1)S(1)}, u32[]{:S(2)}, u32[]{:S(2)}) collective-permute-start(bf16[192,896]{1,0:T(8,128)(2,1)S(1)} %get-tuple-element.114), channel_id=1, source_target_pairs={{0,16},{4,20},{8,24},{12,28},{16,0},{20,4},{24,8},{28,12},{1,17},{... | collective-permute-start | bytes 1032200 | tf_op jit(solution)/shard_map/ppermute | solution.py:130
  461.3 132.9 %collective-permute-start.99 = (bf16[2,448,1472]{2,1,0:T(8,128)(2,1)}, bf16[2,448,1472]{2,1,0:T(8,128)(2,1)}, u32[]{:S(2)}, u32[]{:S(2)}) collective-permute-start(bf16[2,448,1472]{2,1,0:T(8,128)(2,1)} %dynamic-slice_bitcast_fusion), channel_id=1, source_target_pairs={{0,4},{4,0},{8,12},{12,8},{16,20},{20,16},{24,28},{28,24},{1,5},{5... | collective-permute-start | bytes 7913480 | tf_op jit(solution)/shard_map/ppermute | solution.py:130
  468.7 28.9 %collective-permute-start.76 = (bf16[368,896]{1,0:T(8,128)(2,1)S(1)}, bf16[368,896]{1,0:T(8,128)(2,1)S(1)}, u32[]{:S(2)}, u32[]{:S(2)}) collective-permute-start(bf16[368,896]{1,0:T(8,128)(2,1)S(1)} %pad_maximum_fusion.16), channel_id=1, source_target_pairs={{0,16},{4,20},{8,24},{12,28},{16,0},{20,4},{24,8},{28,12},{1,17},{... | collective-permute-start | bytes 1978376 | tf_op jit(solution)/shard_map/ppermute | solution.py:130
  488.2 69.0 %collective-permute-start.81 = (bf16[368,896]{1,0:T(8,128)(2,1)}, bf16[368,896]{1,0:T(8,128)(2,1)}, u32[]{:S(2)}, u32[]{:S(2)}) collective-permute-start(bf16[368,896]{1,0:T(8,128)(2,1)} %pad_maximum_fusion.18), channel_id=1, source_target_pairs={{0,16},{4,20},{8,24},{12,28},{16,0},{20,4},{24,8},{28,12},{1,17},{... | collective-permute-start | bytes 1978376 | tf_op jit(solution)/shard_map/ppermute | solution.py:130
  497.6 60.8 %collective-permute-start.83 = (bf16[368,896]{1,0:T(8,128)(2,1)}, bf16[368,896]{1,0:T(8,128)(2,1)}, u32[]{:S(2)}, u32[]{:S(2)}) collective-permute-start(bf16[368,896]{1,0:T(8,128)(2,1)} %pad_maximum_fusion.19), channel_id=1, source_target_pairs={{0,8},{4,12},{8,0},{12,4},{16,24},{20,28},{24,16},{28,20},{1,9},{5... | collective-permute-start | bytes 1978376 | tf_op jit(solution)/shard_map/ppermute | solution.py:130
  502.7 57.8 %collective-permute-start.79 = (bf16[368,896]{1,0:T(8,128)(2,1)}, bf16[368,896]{1,0:T(8,128)(2,1)}, u32[]{:S(2)}, u32[]{:S(2)}) collective-permute-start(bf16[368,896]{1,0:T(8,128)(2,1)} %add_convert_fusion.7), channel_id=1, source_target_pairs={{0,1},{1,2},{2,3},{3,0},{4,5},{5,6},{6,7},{7,4},{8,9},{9,10},{10,1... | collective-permute-start | bytes 1978376 | tf_op jit(solution)/shard_map/ppermute | solution.py:133
  553.7 24.9 %collective-permute-start.86 = (bf16[368,896]{1,0:T(8,128)(2,1)}, bf16[368,896]{1,0:T(8,128)(2,1)}, u32[]{:S(2)}, u32[]{:S(2)}) collective-permute-start(bf16[368,896]{1,0:T(8,128)(2,1)} %pad_maximum_fusion.20), channel_id=1, source_target_pairs={{0,16},{4,20},{8,24},{12,28},{16,0},{20,4},{24,8},{28,12},{1,17},{... | collective-permute-start | bytes 1978376 | tf_op jit(solution)/shard_map/ppermute | solution.py:130
  557.2 22.3 %collective-permute-start.88 = (bf16[368,896]{1,0:T(8,128)(2,1)}, bf16[368,896]{1,0:T(8,128)(2,1)}, u32[]{:S(2)}, u32[]{:S(2)}) collective-permute-start(bf16[368,896]{1,0:T(8,128)(2,1)} %pad_maximum_fusion.21), channel_id=1, source_target_pairs={{0,8},{4,12},{8,0},{12,4},{16,24},{20,28},{24,16},{28,20},{1,9},{5... | collective-permute-start | bytes 1978376 | tf_op jit(solution)/shard_map/ppermute | solution.py:130
  563.3 27.6 %collective-permute-start.84 = (bf16[368,896]{1,0:T(8,128)(2,1)}, bf16[368,896]{1,0:T(8,128)(2,1)}, u32[]{:S(2)}, u32[]{:S(2)}) collective-permute-start(bf16[368,896]{1,0:T(8,128)(2,1)} %add_convert_fusion.5), channel_id=1, source_target_pairs={{0,1},{1,2},{2,3},{3,0},{4,5},{5,6},{6,7},{7,4},{8,9},{9,10},{10,1... | collective-permute-start | bytes 1978376 | tf_op jit(solution)/shard_map/ppermute | solution.py:133
  576.8 104.0 %collective-permute-start.91 = (bf16[368,896]{1,0:T(8,128)(2,1)}, bf16[368,896]{1,0:T(8,128)(2,1)}, u32[]{:S(2)}, u32[]{:S(2)}) collective-permute-start(bf16[368,896]{1,0:T(8,128)(2,1)} %pad_maximum_fusion.22), channel_id=1, source_target_pairs={{0,16},{4,20},{8,24},{12,28},{16,0},{20,4},{24,8},{28,12},{1,17},{... | collective-permute-start | bytes 1978376 | tf_op jit(solution)/shard_map/ppermute | solution.py:130
  578.6 110.5 %collective-permute-start.93 = (bf16[368,896]{1,0:T(8,128)(2,1)}, bf16[368,896]{1,0:T(8,128)(2,1)}, u32[]{:S(2)}, u32[]{:S(2)}) collective-permute-start(bf16[368,896]{1,0:T(8,128)(2,1)} %pad_maximum_fusion.23), channel_id=1, source_target_pairs={{0,8},{4,12},{8,0},{12,4},{16,24},{20,28},{24,16},{28,20},{1,9},{5... | collective-permute-start | bytes 1978376 | tf_op jit(solution)/shard_map/ppermute | solution.py:130
  579.5 66.7 %collective-permute-start.55 = (bf16[384,768]{1,0:T(8,128)(2,1)S(1)}, bf16[384,768]{1,0:T(8,128)(2,1)S(1)}, u32[]{:S(2)}, u32[]{:S(2)}) collective-permute-start(bf16[384,768]{1,0:T(8,128)(2,1)S(1)} %fusion.58), channel_id=1, source_target_pairs={{0,1},{1,2},{2,3},{3,0},{4,5},{5,6},{6,7},{7,4},{8,9},{9,10},{10,1... | collective-permute-start | bytes 1769480 | tf_op jit(solution)/shard_map/ppermute | solution.py:133
  593.8 96.8 %collective-permute-start.89 = (bf16[368,896]{1,0:T(8,128)(2,1)}, bf16[368,896]{1,0:T(8,128)(2,1)}, u32[]{:S(2)}, u32[]{:S(2)}) collective-permute-start(bf16[368,896]{1,0:T(8,128)(2,1)} %add_convert_fusion.3), channel_id=1, source_target_pairs={{0,1},{1,2},{2,3},{3,0},{4,5},{5,6},{6,7},{7,4},{8,9},{9,10},{10,1... | collective-permute-start | bytes 1978376 | tf_op jit(solution)/shard_map/ppermute | solution.py:133
  644.8 26.5 %collective-permute-start.101 = (bf16[112,1472]{1,0:T(8,128)(2,1)}, bf16[112,1472]{1,0:T(8,128)(2,1)}, u32[]{:S(2)}, u32[]{:S(2)}) collective-permute-start(bf16[112,1472]{1,0:T(8,128)(2,1)} %pad_maximum_fusion.28), channel_id=1, source_target_pairs={{0,16},{4,20},{8,24},{12,28},{16,0},{20,4},{24,8},{28,12},{1,17},{... | collective-permute-start | bytes 989192 | tf_op jit(solution)/shard_map/ppermute | solution.py:130
  671.2 25.0 %collective-permute-start.106 = (bf16[112,1472]{1,0:T(8,128)(2,1)S(1)}, bf16[112,1472]{1,0:T(8,128)(2,1)}, u32[]{:S(2)}, u32[]{:S(2)}) collective-permute-start(bf16[112,1472]{1,0:T(8,128)(2,1)S(1)} %copy-done.68), channel_id=1, source_target_pairs={{0,16},{4,20},{8,24},{12,28},{16,0},{20,4},{24,8},{28,12},{1,17},{... | collective-permute-start | bytes 989192 | tf_op jit(solution)/shard_map/ppermute | solution.py:130
  696.2 54.1 %collective-permute-start.62 = (bf16[4,4,184,384]{3,2,1,0:T(8,128)(2,1)S(1)}, bf16[4,4,184,384]{3,2,1,0:T(8,128)(2,1)S(1)}, u32[]{:S(2)}, u32[]{:S(2)}) collective-permute-start(bf16[4,4,184,384]{3,2,1,0:T(8,128)(2,1)S(1)} %copy-done.46), channel_id=1, source_target_pairs={{0,4},{4,0},{8,12},{12,8},{16,20},{20,16},{24,28},{28,24},{1,5},{5... | collective-permute-start | bytes 6782984 | tf_op jit(solution)/shard_map/ppermute | solution.py:130
  702.9 29.7 %collective-permute-start.116 = (bf16[112,1472]{1,0:T(8,128)(2,1)S(1)}, bf16[112,1472]{1,0:T(8,128)(2,1)S(1)}, u32[]{:S(2)}, u32[]{:S(2)}) collective-permute-start(bf16[112,1472]{1,0:T(8,128)(2,1)S(1)} %copy-done.65), channel_id=1, source_target_pairs={{0,16},{4,20},{8,24},{12,28},{16,0},{20,4},{24,8},{28,12},{1,17},{... | collective-permute-start | bytes 989192 | tf_op jit(solution)/shard_map/ppermute | solution.py:130
  714.3 23.7 %collective-permute-start.118 = (bf16[112,1472]{1,0:T(8,128)(2,1)S(1)}, bf16[112,1472]{1,0:T(8,128)(2,1)S(1)}, u32[]{:S(2)}, u32[]{:S(2)}) collective-permute-start(bf16[112,1472]{1,0:T(8,128)(2,1)S(1)} %copy-done.66), channel_id=1, source_target_pairs={{0,8},{4,12},{8,0},{12,4},{16,24},{20,28},{24,16},{28,20},{1,9},{5... | collective-permute-start | bytes 989192 | tf_op jit(solution)/shard_map/ppermute | solution.py:130
  715.3 22.7 %collective-permute-start.114 = (bf16[112,1472]{1,0:T(8,128)(2,1)S(1)}, bf16[112,1472]{1,0:T(8,128)(2,1)S(1)}, u32[]{:S(2)}, u32[]{:S(2)}) collective-permute-start(bf16[112,1472]{1,0:T(8,128)(2,1)S(1)} %add_convert_fusion.9), channel_id=1, source_target_pairs={{0,1},{1,2},{2,3},{3,0},{4,5},{5,6},{6,7},{7,4},{8,9},{9,10},{10,1... | collective-permute-start | bytes 989192 | tf_op jit(solution)/shard_map/ppermute | solution.py:133
  744.7 34.9 %collective-permute-start.61 = (f32[1,1520]{1,0:T(1,128)S(1)}, f32[1,1520]{1,0:T(1,128)S(1)}, u32[]{:S(2)}, u32[]{:S(2)}) collective-permute-start(f32[1,1520]{1,0:T(1,128)S(1)} %slice_add_fusion.3), channel_id=1, source_target_pairs={{0,1},{1,2},{2,3},{3,0},{4,5},{5,6},{6,7},{7,4},{8,9},{9,10},{10,1... | collective-permute-start | bytes 18248 | tf_op jit(solution)/shard_map/ppermute | solution.py:133
  746.2 71.0 %collective-permute-start.98 = (bf16[368,3584]{1,0:T(8,128)(2,1)}, bf16[368,3584]{1,0:T(8,128)(2,1)S(1)}, u32[]{:S(2)}, u32[]{:S(2)}) collective-permute-start(bf16[368,3584]{1,0:T(8,128)(2,1)} %constant_dynamic-update-slice_fusion.9), channel_id=1, source_target_pairs={{0,4},{4,0},{8,12},{12,8},{16,20},{20,16},{24,28},{28,24},{1,5},{5... | collective-permute-start | bytes 7913480 | tf_op jit(solution)/shard_map/ppermute | solution.py:130
  (180 other events, 1841.2 us)

commit v2 on v1

--- a/solution.py
+++ b/solution.py
@@ -1,4 +1,6 @@
 import functools
+
+import math
 
 import jax
 import jax.numpy as jnp
@@ -80,6 +82,297 @@
         out_specs=pl.BlockSpec((1, 1, 2 * group), lambda h: (h, 0, 0)),
         out_shape=jax.ShapeDtypeStruct((heads, 1, 2 * group), F32),
     )(score_grad, slots.reshape(1, tokens)).reshape(heads, 2 * group)
+
+
+def axis_ranks():
+    return lax.axis_index("shard"), lax.axis_index("rep") // 2
+
+
+def gelu_parts(value):
+    inner = math.sqrt(2.0 / math.pi)
+    square = value * value
+    bend = jnp.tanh(inner * value * (1.0 + 0.044715 * square))
+    outside = 0.5 * (1.0 + bend)
+    slope = outside + 0.5 * value * (1.0 - bend * bend) * (inner * (1.0 + 0.134145 * square))
+    return value * outside, slope
+
+
+def run_copies(copies, sems):
+    started = [pltpu.make_async_copy(src, dst, sems.at[i]) for i, (src, dst) in enumerate(copies)]
+    for copy in started:
+        copy.start()
+    return started
+
+
+ANY = pl.BlockSpec(memory_space=pl.ANY)
+VMEM = pl.BlockSpec(memory_space=pltpu.VMEM)
+
+
+def pick_kernel(gate_ref, up_ref, out_ref):
+    core = lax.axis_index("rep") % 2
+    inner = gate_ref.shape[1]
+    shards = lax.axis_size("shard")
+    unit = inner // shards
+    half = unit // 2
+    for index, ref in enumerate((gate_ref, up_ref)):
+        parts = []
+        for shard in range(shards):
+            low = ref[:, shard * unit : shard * unit + half]
+            high = ref[:, shard * unit + half : (shard + 1) * unit]
+            parts.append(jnp.where(core == 0, low, high))
+        out_ref[:, index * (inner // 2) : (index + 1) * (inner // 2)] = jnp.concatenate(parts, 1)
+
+
+def pick_columns(w_gate, w_up):
+    return pl.pallas_call(
+        pick_kernel,
+        in_specs=[VMEM, VMEM],
+        out_specs=VMEM,
+        out_shape=jax.ShapeDtypeStruct(w_gate.shape, BF16),
+    )(w_gate, w_up)
+
+
+def spread_kernel(low_ref, high_ref, gate_ref, up_ref):
+    inner = gate_ref.shape[1]
+    shards = lax.axis_size("shard")
+    half = inner // shards // 2
+    for index, ref in enumerate((gate_ref, up_ref)):
+        parts = []
+        for shard in range(shards):
+            start = index * (inner // 2) + shard * half
+            parts += [low_ref[:, start : start + half], high_ref[:, start : start + half]]
+        ref[...] = jnp.concatenate(parts, 1).astype(F32)
+
+
+def spread_columns(low, high):
+    shape = jax.ShapeDtypeStruct(low.shape, F32)
+    return pl.pallas_call(
+        spread_kernel,
+        in_specs=[VMEM, VMEM],
+        out_specs=[VMEM, VMEM],
+        out_shape=[shape, shape],
+    )(low, high)
+
+
+def gate_up_call(own, other, pieces, places):
+    rows, width = own.shape
+    count = len(pieces)
+    inner = places[0][1]
+    half = inner // 2
+    tile = 256
+
+    def kernel(own_ref, other_ref, *rest):
+        piece_refs = rest[:count]
+        slope_ref, act_ref, hidden_ref, keep_ref, both, weights, sems = rest[count:]
+        rank, chip = axis_ranks()
+        copies = [(own_ref, both.at[:rows]), (other_ref, both.at[rows:])]
+        for ref, place in zip(piece_refs, places[1:]):
+            row, column = place(rank, chip)
+            copies.append(
+                (ref, weights.at[pl.ds(row, ref.shape[0]), pl.ds(column, ref.shape[1])])
+            )
+        for copy in run_copies(copies, sems):
+            copy.wait()
+        keep = pltpu.make_async_copy(weights, keep_ref, sems.at[count + 2])
+        keep.start()
+
+        def step(index, carry):
+            start = pl.multiple_of(index * tile, tile)
+            gate = jnp.dot(both[...], weights[:, pl.ds(start, tile)], preferred_element_type=F32)
+            up = jnp.dot(
+                both[...],
+                weights[:, pl.ds(pl.multiple_of(half + start, tile), tile)],
+                preferred_element_type=F32,
+            )
+            act, slope = gelu_parts(gate)
+            act_ref[:, pl.ds(start, tile)] = act.astype(BF16)
+            slope_ref[:, pl.ds(start, tile)] = (up * slope).astype(BF16)
+            hidden_ref[:, pl.ds(start, tile)] = (act * up).astype(BF16)
+            return carry
+
+        lax.fori_loop(0, half // tile, step, 0)
+        keep.wait()
+
+    shape = jax.ShapeDtypeStruct((2 * rows, half), BF16)
+    return pl.pallas_call(
+        kernel,
+        in_specs=[ANY] * (2 + count),
+        out_specs=[VMEM, VMEM, VMEM, ANY],
+        out_shape=[shape, shape, shape, jax.ShapeDtypeStruct((width, inner), BF16)],
+        scratch_shapes=[
+            pltpu.VMEM((2 * rows, width), BF16),
+            pltpu.VMEM((width, inner), BF16),
+            pltpu.SemaphoreType.DMA((count + 3,)),
+        ],
+        cost_estimate=pl.CostEstimate(
+            flops=4 * rows * width * inner,
+            bytes_accessed=4 * width * inner + 6 * rows * inner,
+            transcendentals=rows * inner,
+        ),
+    )(own, other, *pieces)
+
+
+def col_tiles(width):
+    return [(start, min(512, width - start)) for start in range(0, width, 512)]
+
+
+def down_call(hidden, pieces, places):
+    double, half = hidden.shape
+    rows = double // 2
+    count = len(pieces)
+    width = pieces[0].shape[1]
+
+    def kernel(hidden_ref, *rest):
+        piece_refs = rest[:count]
+        own_ref, other_ref, keep_ref, weights, sems = rest[count:]
+        rank, chip = axis_ranks()
+        copies = []
+        for ref, place in zip(piece_refs, places):
+            copies.append((ref, weights.at[pl.ds(place(rank, chip), ref.shape[0])]))
+        for copy in run_copies(copies, sems):
+            copy.wait()
+        keep = pltpu.make_async_copy(weights, keep_ref, sems.at[count])
+        keep.start()
+        for start, size in col_tiles(width):
+            columns = slice(start, start + size)
+            own_ref[:, columns] = jnp.dot(
+                hidden_ref[:rows], weights[:, columns], preferred_element_type=F32
+            )
+            other_ref[:, columns] = jnp.dot(
+                hidden_ref[rows:], weights[:, columns], preferred_element_type=F32
+            ).astype(BF16)
+        keep.wait()
+
+    return pl.pallas_call(
+        kernel,
+        in_specs=[VMEM] + [ANY] * count,
+        out_specs=[VMEM, VMEM, ANY],
+        out_shape=[
+            jax.ShapeDtypeStruct((rows, width), F32),
+            jax.ShapeDtypeStruct((rows, width), BF16),
+            jax.ShapeDtypeStruct((half, width), BF16),
+        ],
+        scratch_shapes=[pltpu.VMEM((half, width), BF16), pltpu.SemaphoreType.DMA((count + 1,))],
+        cost_estimate=pl.CostEstimate(
+            flops=4 * rows * width * half, bytes_accessed=4 * width * half, transcendentals=0
+        ),
+    )(hidden, *pieces)
+
+
+def hidden_grad_call(own, other, down, slope, act):
+    rows, width = own.shape
+    half = down.shape[0]
+    tile = 256
+
+    def kernel(own_ref, other_ref, down_ref, slope_ref, act_ref, out_ref, both, sems):
+        for copy in run_copies(
+            [(own_ref, both.at[:rows]), (other_ref, both.at[rows:])], sems
+        ):
+            copy.wait()
+
+        def step(index, carry):
+            start = pl.multiple_of(index * tile, tile)
+            upstream = lax.dot_general(
+                both[...],
+                down_ref[pl.ds(start, tile)],
+                (((1,), (1,)), ((), ())),
+                preferred_element_type=F32,
+            )
+            gate = upstream * slope_ref[:, pl.ds(start, tile)].astype(F32)
+            up = upstream * act_ref[:, pl.ds(start, tile)].astype(F32)
+            out_ref[:, pl.ds(start, tile)] = gate.astype(BF16)
+            out_ref[:, pl.ds(pl.multiple_of(half + start, tile), tile)] = up.astype(BF16)
+            return carry
+
+        lax.fori_loop(0, half // tile, step, 0)
+
+    return pl.pallas_call(
+        kernel,
+        in_specs=[ANY, ANY, VMEM, VMEM, VMEM],
+        out_specs=VMEM,
+        out_shape=jax.ShapeDtypeStruct((2 * rows, 2 * half), BF16),
+        scratch_shapes=[pltpu.VMEM((2 * rows, width), BF16), pltpu.SemaphoreType.DMA((2,))],
+        cost_estimate=pl.CostEstimate(
+            flops=4 * rows * width * half,
+            bytes_accessed=2 * width * half + 16 * rows * half,
+            transcendentals=0,
+        ),
+    )(own, other, down, slope, act)
+
+
+def weight_grad_call(left, right, outputs):
+    left_own, left_other = left
+    right_own, right_other = right
+    rows = left_own.shape[0]
+    depth, width = left_own.shape[1], right_own.shape[1]
+    count = len(outputs)
+    copies_out = sum(len(moves) for _, moves in outputs)
+    split = left_other is not None
+    total = 2 * rows if split else rows
+    right_split = right_other is not None
+    inputs = [left_own] + ([left_other] if split else []) + [right_own]
+    inputs += [right_other] if right_split else []
+
+    def kernel(*refs):
+        in_refs = list(refs[: len(inputs)])
+        out_refs = refs[len(inputs) : len(inputs) + count]
+        lefts, rights, result, sems = refs[len(inputs) + count :]
+        copies = []
+        for target, parted in ((lefts, split), (rights, right_split)):
+            first = in_refs.pop(0)
+            size = first.shape[0]
+            copies.append((first, target.at[:size]))
+            if parted:
+                copies.append((in_refs.pop(0), target.at[size:]))
+        for copy in run_copies(copies, sems):
+            copy.wait()
+        tile = 512 if width % 512 == 0 else width
+        for begin in range(0, depth, 256):
+            size = min(256, depth - begin)
+            turned = lefts[:, begin : begin + size].T
+            if tile == width:
+                for start, span in col_tiles(width):
+                    result[begin : begin + size, start : start + span] = jnp.dot(
+                        turned, rights[:, start : start + span], preferred_element_type=F32
+                    ).astype(BF16)
+            else:
+
+                def step(index, carry):
+                    start = pl.multiple_of(index * tile, tile)
+                    result[begin : begin + size, pl.ds(start, tile)] = jnp.dot(
+                        turned, rights[:, pl.ds(start, tile)], preferred_element_type=F32
+                    ).astype(BF16)
+                    return carry
+
+                lax.fori_loop(0, width // tile, step, 0)
+        rank, chip = axis_ranks()
+        moves_out = []
+        for ref, (shape, moves) in zip(out_refs, outputs):
+            for index, place in moves:
+                row, column = place(rank, chip)
+                moves_out.append(
+                    (result.at[pl.ds(row, shape[1]), pl.ds(column, shape[2])], ref.at[index])
+                )
+        for copy in run_copies(moves_out, sems):
+            copy.wait()
+
+    return pl.pallas_call(
+        kernel,
+        in_specs=[ANY] * len(inputs),
+        out_specs=[ANY] * count,
+        out_shape=[jax.ShapeDtypeStruct(shape, BF16) for shape, _ in outputs],
+        scratch_shapes=[
+            pltpu.VMEM((total, depth), BF16),
+            pltpu.VMEM((total, width), BF16),
+            pltpu.VMEM((depth, width), BF16),
+            pltpu.SemaphoreType.DMA((max(4, copies_out),)),
+        ],
+        cost_estimate=pl.CostEstimate(
+            flops=2 * total * depth * width,
+            bytes_accessed=2 * (depth * width + total * (depth + width)),
+            transcendentals=0,
+        ),
+    )(*inputs)
 
 
 def on_device(
@@ -124,7 +417,7 @@
     down_block = w_down.shape[0]
     down_half = down_block // 2
     down_piece = down_half // chips
-    half_shards = shards // 2
+    aligned = block % 16 == 0 and down_piece % 16 == 0 and col_piece % 128 == 0
 
     def swap(value, mask):
         return lax.ppermute(value, "rep", [(i, i ^ mask) for i in range(reps)])
@@ -158,36 +451,41 @@
             bit *= 2
         return found
 
-    def plane_reduce(take):
-        def reduce_level(get, level):
-            if level == 1:
-                return get(0)
-            if level == 2:
-                return (get(0).astype(F32) + swap(get(1), 2).astype(F32)).astype(BF16)
-            if level == 4:
-                diagonal = get(3)
-                middle = cut(diagonal.shape[0])
-                top = swap(diagonal[:middle], 2)
-                low = swap(diagonal[middle:], 4)
-                far, near = get(2), get(1)
-                far = jnp.concatenate(
-                    [(far[:middle].astype(F32) + top.astype(F32)).astype(BF16), far[middle:]]
+    def add(*values):
+        return sum(value.astype(F32) for value in values).astype(BF16)
+
+    def plane_reduce(parts, axis):
+        def level_two(get):
+            if chips == 1:
+                return get("own")
+            if chips == 2:
+                return add(get("own"), swap(get("near"), 2))
+            top, low = swap(get("top"), 2), swap(get("low"), 4)
+            far, near = get("far"), get("near")
+            middle = top.shape[axis]
+
+            def pair(value):
+                return (
+                    lax.slice_in_dim(value, 0, middle, axis=axis),
+                    lax.slice_in_dim(value, middle, value.shape[axis], axis=axis),
                 )
-                near = jnp.concatenate(
-                    [near[:middle], (near[middle:].astype(F32) + low.astype(F32)).astype(BF16)]
-                )
-                return (
-                    get(0).astype(F32) + swap(far, 4).astype(F32) + swap(near, 2).astype(F32)
-                ).astype(BF16)
-            bit = level // 2
-            return reduce_level(
-                lambda mask: (
-                    get(mask).astype(F32) + swap(get(mask ^ bit), 2 * bit).astype(F32)
-                ).astype(BF16),
-                bit,
-            )
-
-        return reduce_level(take, chips)
+
+            (far_top, far_low), (near_top, near_low) = pair(far), pair(near)
+            far = jnp.concatenate([add(far_top, top), far_low], axis)
+            near = jnp.concatenate([near_top, add(near_low, low)], axis)
+            return add(get("own"), swap(far, 4), swap(near, 2))
+
+        def level(base, bit):
+            if bit < 4:
+                return lambda name: parts[base][name]
+            lower, upper = level(base, bit // 2), level(base ^ bit, bit // 2)
+            return lambda name: add(lower(name), swap(upper(name), 2 * bit))
+
+        return level_two(level(0, chips // 2))
+
+    names = {"own": 0, "near": 1, "far": 2, "top": 3, "low": 3}
+    bases = [base for base in range(chips) if base & 3 == 0]
+    used = ["own", "near", "far", "top", "low"] if chips >= 4 else ["own", "near"][:chips]
 
     def ring_reduce(block_of):
         total = block_of(1)
@@ -246,39 +544,52 @@
     value_full = attn_full[2].reshape(width, proj)
     out_full = attn_full[3].reshape(proj, width)
 
-    column = core * half_inner
-    gate_up_own = jnp.concatenate(
-        [
-            lax.dynamic_slice_in_dim(w_gate, column, half_inner, 1),
-            lax.dynamic_slice_in_dim(w_up, column, half_inner, 1),
-        ],
-        axis=1,
-    )
-    gate_up = jnp.zeros((width, inner), BF16)
-    gate_up = lax.dynamic_update_slice(gate_up, gate_up_own, (rank * block, 0))
+    gate_up_own = pick_columns(w_gate, w_up)
+    gate_up_parts = [(0, 0, 0, gate_up_own)]
     moving = lax.dynamic_slice_in_dim(gate_up_own, chip * col_piece, col_piece, 1)
     for step in range(1, shards):
         moving = shift(moving)
-        for mask, start, part in [(0, 0, moving)] + plane_gather(moving):
-            gate_up = lax.dynamic_update_slice(
-                gate_up, part, (source(step) * block + start, (chip ^ mask) * col_piece)
-            )
+        gate_up_parts += [
+            (step, mask, start, part) for mask, start, part in [(0, 0, moving)] + plane_gather(moving)
+        ]
+
+    def gate_up_place(step, mask, start):
+        def place(at, chip_at):
+            column = 0 if step == 0 else (chip_at ^ mask) * col_piece
+            return (at - step) % shards * block + start, column
+
+        return place
 
     down_own = lax.dynamic_slice_in_dim(w_down, core * down_half, down_half, 0)
-    carried = jnp.zeros((shards, down_half, width), BF16)
-    carried = lax.dynamic_update_slice(carried, down_own[None], (rank, 0, 0))
+    down_parts = [(0, 0, 0, down_own)]
     moving = lax.dynamic_slice_in_dim(down_own, chip * down_piece, down_piece, 0)
     for step in range(1, shards):
         moving = shift(moving)
-        for mask, start, part in [(0, 0, moving)] + plane_gather(moving):
-            carried = lax.dynamic_update_slice(
-                carried, part[None], (source(step), (chip ^ mask) * down_piece + start, 0)
-            )
-    kept = lax.dynamic_slice_in_dim(carried, core * half_shards, half_shards, 0)
-    given = swap(lax.dynamic_slice_in_dim(carried, (1 - core) * half_shards, half_shards, 0), 1)
-    down = jnp.stack(
-        [jnp.where(core == 0, kept, given), jnp.where(core == 0, given, kept)], axis=1
-    ).reshape(half_inner, width)
+        down_parts += [
+            (step, mask, start, part) for mask, start, part in [(0, 0, moving)] + plane_gather(moving)
+        ]
+
+    def down_place(step, mask, start):
+        def place(at, chip_at):
+            row = start if step == 0 else (chip_at ^ mask) * down_piece + start
+            return (at - step) % shards * down_half + row
+
+        return place
+
+    if aligned:
+        gate_up_pieces = [part for _, _, _, part in gate_up_parts]
+        gate_up_places = [tile_hint(gate_up_place(*where), 16, 128) for *where, _ in gate_up_parts]
+        down_pieces = [part for _, _, _, part in down_parts]
+        down_places = [row_hint(down_place(*where), 16) for *where, _ in down_parts]
+    else:
+        whole = jnp.zeros((width, inner), BF16)
+        for *where, part in gate_up_parts:
+            whole = lax.dynamic_update_slice(whole, part, gate_up_place(*where)(rank, chip))
+        gate_up_pieces, gate_up_places = [whole], [lambda at, chip_at: (0, 0)]
+        whole = jnp.zeros((half_inner, width), BF16)
+        for *where, part in down_parts:
+            whole = lax.dynamic_update_slice(whole, part, (down_place(*where)(rank, chip), 0))
+        down_pieces, down_places = [whole], [lambda at, chip_at: 0]
 
     slots = slot_of[:, 0]
     own_slots = lax.dynamic_slice_in_dim(slots, rank * local_rows, local_rows, 1)
@@ -327,12 +638,12 @@
 
     scale_two = rms_scale(hidden_mid)
     normed_two = (hidden_mid * scale_two * ffn_gain).astype(BF16)
-    normed_pair = jnp.concatenate([normed_two, swap(normed_two, 1)])
-    both = dot(normed_pair, gate_up)
-    gate_pre, up_pre = both[:, :half_inner], both[:, half_inner:]
-    inner_act = (gelu_tanh(gate_pre) * up_pre).astype(BF16)
-    partial = dot(inner_act, down)
-    hidden_out = hidden_mid + partial[:rows] + swap(partial[rows:].astype(BF16), 1).astype(F32)
+    normed_two_other = swap(normed_two, 1)
+    gate_slope_act, gate_act, inner_act, gate_up = gate_up_call(
+        normed_two, normed_two_other, gate_up_pieces, [("inner", inner)] + gate_up_places
+    )
+    down_part, down_given, down = down_call(inner_act, down_pieces, down_places)
+    hidden_out = hidden_mid + down_part + swap(down_given, 1).astype(F32)
     scale_three = rms_scale(hidden_out)
     delete_norm = hidden_out * scale_three * delete_gain
     sigmoid_val = jax.nn.sigmoid(jnp.sum(delete_norm * delete_vec, axis=-1))
@@ -347,49 +658,97 @@
         hidden_out, scale_three, delete_gain, delete_up
     )
     down_up = grad_out.astype(BF16)
-    down_up_pair = jnp.concatenate([down_up, swap(down_up, 1)])
-
-    grad_down = jnp.einsum("tf,td->fd", inner_act, down_up_pair, preferred_element_type=F32)
-    grad_down = grad_down.astype(BF16).reshape(half_shards, 2, down_half, width)
-    kept = lax.dynamic_index_in_dim(grad_down, core, 1, keepdims=False)
-    given = swap(lax.dynamic_index_in_dim(grad_down, 1 - core, 1, keepdims=False), 1)
-    carried = jnp.concatenate(
-        [jnp.where(core == 0, kept, given), jnp.where(core == 0, given, kept)]
-    )
-
-    def down_block_of(step):
-        return plane_reduce(
-            lambda mask: lax.dynamic_slice(
-                carried,
-                (source(step), (chip ^ mask) * down_piece, 0),
-                (1, down_piece, width),
-            )[0]
+    down_up_other = swap(down_up, 1)
+
+    def reduce_plan(piece_rows, piece_columns, place):
+        middle = cut(piece_rows)
+        spans = {"own": (0, piece_rows), "near": (0, piece_rows), "far": (0, piece_rows)}
+        spans["top"], spans["low"] = (0, middle), (middle, piece_rows - middle)
+        first = shards // 2
+        plan = []
+        for steps in (range(1, first + 1), range(first + 1, shards + 1)):
+            for base in bases:
+                for name in used:
+                    start, size = spans[name]
+                    moves = [
+                        (index, place(step % shards, base ^ names[name], start))
+                        for index, step in enumerate(steps)
+                    ]
+                    plan.append(((len(moves), size, piece_columns), moves))
+        return plan
+
+    def reduce_run(plan, left, right):
+        if aligned:
+            buffers = weight_grad_call(left, right, plan)
+        else:
+            shape = (left[0].shape[1], right[0].shape[1])
+            whole = weight_grad_call(
+                left, right, [((1,) + shape, [(0, lambda at, chip_at: (0, 0))])]
+            )[0][0]
+            buffers = []
+            for (_, size, columns), moves in plan:
+                buffers.append(
+                    jnp.stack(
+                        [
+                            lax.dynamic_slice(whole, place(rank, chip), (size, columns))
+                            for _, place in moves
+                        ]
+                    )
+                )
+        return buffers
+
+    def reduce_groups(buffers):
+        each = len(buffers) // 2
+        sums = []
+        for group_index in range(2):
+            chosen = buffers[group_index * each : (group_index + 1) * each]
+            parts = {
+                base: dict(zip(used, chosen[i * len(used) : (i + 1) * len(used)]))
+                for i, base in enumerate(bases)
+            }
+            sums.append(plane_reduce(parts, 1))
+        return sums
+
+    def ring_of(sums):
+        first = sums[0].shape[0]
+
+        def block_of(step):
+            step = step if step else shards
+            return sums[0][step - 1] if step <= first else sums[1][step - 1 - first]
+
+        return ring_reduce(block_of)
+
+    def down_grad_place(step, mask, start):
+        return tile_hint(
+            lambda at, chip_at: (
+                (at - step) % shards * down_half + (chip_at ^ mask) * down_piece + start,
+                0,
+            ),
+            16,
+            128,
+        ) if aligned else lambda at, chip_at: (
+            (at - step) % shards * down_half + (chip_at ^ mask) * down_piece + start,
+            0,
         )
 
-    down_sum = ring_reduce(down_block_of)
-
-    inner_grad = jnp.einsum("td,fd->tf", down_up_pair, down, preferred_element_type=F32)
-    activated, gelu_pull = jax.vjp(gelu_tanh, gate_pre)
-    both_grad = jnp.concatenate(
-        [
-            gelu_pull(inner_grad * up_pre)[0].astype(BF16),
-            (inner_grad * activated).astype(BF16),
-        ],
-        axis=1,
-    )
-    grad_gate_up = jnp.einsum("td,tf->df", normed_pair, both_grad, preferred_element_type=F32)
-    grad_gate_up = grad_gate_up.astype(BF16)
-
-    def gate_up_block_of(step):
-        return plane_reduce(
-            lambda mask: lax.dynamic_slice(
-                grad_gate_up,
-                (source(step) * block, (chip ^ mask) * col_piece),
-                (block, col_piece),
-            )
+    def gate_up_grad_place(step, mask, start):
+        plain = lambda at, chip_at: (
+            (at - step) % shards * block + start,
+            (chip_at ^ mask) * col_piece,
         )
-
-    gate_up_sum = ring_reduce(gate_up_block_of)
+        return tile_hint(plain, 16, 128) if aligned else plain
+
+    down_buffers = reduce_run(
+        reduce_plan(down_piece, width, down_grad_place), (inner_act, None), (down_up, down_up_other)
+    )
+    both_grad = hidden_grad_call(down_up, down_up_other, down, gate_slope_act, gate_act)
+    gate_up_buffers = reduce_run(
+        reduce_plan(block, col_piece, gate_up_grad_place),
+        (normed_two, normed_two_other),
+        (both_grad, None),
+    )
+    down_sum = ring_of(reduce_groups(down_buffers))
+    gate_up_sum = ring_of(reduce_groups(gate_up_buffers))
 
     partial = jnp.einsum("tf,df->td", both_grad, gate_up, preferred_element_type=F32)
     normed_two_grad = partial[:rows] + swap(partial[rows:].astype(BF16), 1).astype(F32)
@@ -442,9 +801,17 @@
     kept = lax.dynamic_index_in_dim(attn_grads, core, 2, keepdims=False)
     given = swap(lax.dynamic_index_in_dim(attn_grads, 1 - core, 2, keepdims=False), 1)
     attn_grads = (kept.astype(F32) + given.astype(F32)).astype(BF16)
-    attn_sum = plane_reduce(
-        lambda mask: lax.dynamic_index_in_dim(attn_grads, chip ^ mask, 1, keepdims=False)
-    )
+    middle = cut(shards)
+    attn_parts = {}
+    for base in bases:
+        attn_parts[base] = {}
+        for name in used:
+            part = lax.dynamic_index_in_dim(
+                attn_grads, chip ^ base ^ names[name], 1, keepdims=False
+            )
+            part = part[:middle] if name == "top" else part[middle:] if name == "low" else part
+            attn_parts[base][name] = part
+    attn_sum = plane_reduce(attn_parts, 0)
     attn_sum = ring_reduce(lambda step: attn_sum[step])
 
     gate_up_half = jnp.zeros((block, inner), BF16)
@@ -453,10 +820,10 @@
             gate_up_half, part, (start, (chip ^ mask) * col_piece)
         )
     gate_up_other = swap(gate_up_half, 1)
-    low = jnp.where(core == 0, gate_up_half, gate_up_other).astype(F32)
-    high = jnp.where(core == 0, gate_up_other, gate_up_half).astype(F32)
-    grad_gate = jnp.concatenate([low[:, :half_inner], high[:, :half_inner]], axis=1)
-    grad_up = jnp.concatenate([low[:, half_inner:], high[:, half_inner:]], axis=1)
+    grad_gate, grad_up = spread_columns(
+        jnp.where(core == 0, gate_up_half, gate_up_other),
+        jnp.where(core == 0, gate_up_other, gate_up_half),
+    )
 
     down_half_sum = jnp.zeros((down_half, width), BF16)
     for mask, start, part in [(0, 0, down_sum)] + plane_gather(down_sum):
@@ -520,6 +887,18 @@
     return plane_gather(stacked)
 
 
+def tile_hint(place, row_unit, column_unit):
+    def hinted(at, chip_at):
+        row, column = place(at, chip_at)
+        return pl.multiple_of(row, row_unit), pl.multiple_of(column, column_unit)
+
+    return hinted
+
+
+def row_hint(place, unit):
+    return lambda at, chip_at: pl.multiple_of(place(at, chip_at), unit)
+
+
 def solution(mesh):
     rows = P(None, ("rep", "shard"), None)
     flat = P(None, ("rep", "shard"))

time: 846 us -> 782 us (0.924)
  local copies, waits for them, and re-layouts: 279 us -> 167 us
  Pallas kernels: 12.3 us -> 103 us
  waiting for transfers between devices: 194 us -> 263 us
  matrix products: 100 us -> 52.1 us
  starting transfers between devices: 123 us -> 93.7 us
  other arithmetic: 118 us -> 89.2 us
    dynamic_update_slice x31 -> x0, local copies, waits for them, and re-layouts: 102 us -> none  [the longest x15 87.6 us: on_device(): lax.dynamic_update_slice(gate_up, part, (source(step) * block + start, (c...]
    pallas_call x0 -> x7, Pallas kernels: none -> 91.2 us  [the longest x2 33.1 us: weight_grad_call(): pl.pallas_call(kernel, in_specs=[ANY] * len(inputs), out_specs=[ANY] * co...]
    ppermute x30, waiting for transfers between devices: 58.3 us -> 108 us  [shift(): lax.ppermute(value, 'shard', [(i, (i + 1) % shards) for i in range(shards)])]
    dot_general x3 -> x0, matrix products: 32.7 us -> none  [the longest x1 12.9 us: on_device(): jnp.einsum('td,fd->tf', down_up_pair, down, preferred_element_type=F32)]
    ppermute x94 -> x76, waiting for transfers between devices: 135 us -> 155 us  [swap(): return lax.ppermute(value, 'rep', [(i, i ^ mask) for i in range(reps)])]
    dot_general x6 -> x4, matrix products: 23.3 us -> 4.92 us  [dot(): return jnp.dot(left, right, preferred_element_type=F32).astype(kind)]
    ppermute x94 -> x76, starting transfers between devices: 88 us -> 71.4 us  [swap(): return lax.ppermute(value, 'rep', [(i, i ^ mask) for i in range(reps)])]
    concatenate x23 -> x10, other arithmetic: 20.7 us -> 5.08 us  [the longest x5 2.54 us: level_two(): far = jnp.concatenate([add(far_top, top), far_low], axis)]
  transfers between devices with their start and end apart: 124 -> 106, of which waited for: 46 -> 37; matrix products, arithmetic and copies ran while one was open for 50% -> 35% of each run, Pallas kernels for 1% -> 10%
where the time goes in v2:
time: 782 us; the launch traced here: 772 us
  waiting for transfers between devices  263 us (34%)
  local copies, waits for them, and re-layouts  167 us (21%)
  Pallas kernels  103 us (13%)
  starting transfers between devices  93.7 us (12%)
  other arithmetic  89.2 us (11%)
  matrix products  52.1 us (7%)
    ppermute x76, waiting for transfers between devices, swap(): return lax.ppermute(value, 'rep', [(i, i ^ mask) for i in range(reps)])  155 us
    ppermute x30, waiting for transfers between devices, shift(): lax.ppermute(value, 'shard', [(i, (i + 1) % shards) for i in range(shards)])  108 us
    ppermute x76, starting transfers between devices, swap(): return lax.ppermute(value, 'rep', [(i, i ^ mask) for i in range(reps)])  71.4 us
    pallas_call x2, Pallas kernels, weight_grad_call(): pl.pallas_call(kernel, in_specs=[ANY] * len(inputs), out_specs=[ANY] * co...  33.1 us
    unnamed x227, local copies, waits for them, and re-layouts  28.2 us
    ppermute x30, starting transfers between devices, shift(): lax.ppermute(value, 'shard', [(i, (i + 1) % shards) for i in range(shards)])  22.4 us
    pallas_call x1, Pallas kernels, gate_up_call(): pl.pallas_call(kernel, in_specs=[ANY] * (2 + count), out_specs=[VMEM, VME...  20.3 us
    dynamic_update_slice x24, local copies, waits for them, and re-layouts, on_device(): lax.dynamic_update_slice(attn_full, part[index][None, None, None], (owner...  17.1 us
  transfers between devices with their start and end apart: 106, of which 37 were waited for; matrix products, arithmetic and copies ran while one was open for 35% of the time, Pallas kernels for 10%

profile of v2, /device:TPU:0, one launch (start us, length us, event | category | flops | bytes accessed | tf_op | source)
XLA Modules:
  0.0 771.7 jit_solution(9175963092602509940)
XLA Ops:
  9.1 5.3 shard_map.290.rest_0_
  28.5 13.5 %collective-permute-done.1 = bf16[1,1520]{1,0:T(2,128)(2,1)S(1)} collective-permute-done((bf16[1,1520]{1,0:T(2,128)(2,1)S(1)}, bf16[1,1520]{1,0:T(2,128)(2,1)S(1)}, u32[]{:S(2)}, u32[]{:S(2)}) %collective-permute-start.1) | collective-permute-done | bytes 3072 | tf_op jit(solution)/shard_map/ppermute | solution.py:426
  42.3 5.1 collective-permute-done.2
  56.9 5.3 collective-permute-done.5
  67.6 6.9 collective-permute-done.7
  92.4 4.2 fusion.134
  99.9 15.7 %collective-permute-done.15 = bf16[384,768]{0,1:T(8,128)(2,1)} collective-permute-done((bf16[384,768]{0,1:T(8,128)(2,1)S(1)}, bf16[384,768]{0,1:T(8,128)(2,1)}, u32[]{:S(2)}, u32[]{:S(2)}) %collective-permute-start.15) | collective-permute-done | bytes 589856 | tf_op jit(solution)/shard_map/ppermute | solution.py:426
  121.3 10.8 %collective-permute-done.16 = bf16[384,768]{0,1:T(8,128)(2,1)} collective-permute-done((bf16[384,768]{0,1:T(8,128)(2,1)}, bf16[384,768]{0,1:T(8,128)(2,1)}, u32[]{:S(2)}, u32[]{:S(2)}) %collective-permute-start.16) | collective-permute-done | bytes 589856 | tf_op jit(solution)/shard_map/ppermute | solution.py:426
  134.8 5.8 shard_map.289
  147.2 3.5 reshape_squeeze.28
  166.1 4.3 copy.185
  173.7 6.8 fusion.138
  190.6 4.3 collective-permute-start.44
  198.8 11.8 %collective-permute-done.41.rest_8_ = bf16[112,1472]{1,0:T(8,128)(2,1)S(1)} collective-permute-done((bf16[112,1472]{1,0:T(8,128)(2,1)}, bf16[112,1472]{1,0:T(8,128)(2,1)S(1)}, u32[]{:S(2)}, u32[]{:S(2)}) %collective-permute-start.41) | collective-permute-done | bytes 329760 | tf_op jit(solution)/shard_map/ppermute | solution.py:423
  215.4 6.3 collective-permute-done.45.rest_12_
  232.6 9.9 %collective-permute-done.25.rest_7_ = bf16[368,896]{1,0:T(8,128)(2,1)S(1)} collective-permute-done((bf16[368,896]{1,0:T(8,128)(2,1)}, bf16[368,896]{1,0:T(8,128)(2,1)S(1)}, u32[]{:S(2)}, u32[]{:S(2)}) %collective-permute-start.25) | collective-permute-done | bytes 659488 | tf_op jit(solution)/shard_map/ppermute | solution.py:423
  245.1 11.2 %collective-permute-done.30.rest_12_ = bf16[368,896]{1,0:T(8,128)(2,1)S(1)} collective-permute-done((bf16[368,896]{1,0:T(8,128)(2,1)}, bf16[368,896]{1,0:T(8,128)(2,1)S(1)}, u32[]{:S(2)}, u32[]{:S(2)}) %collective-permute-start.30) | collective-permute-done | bytes 659488 | tf_op jit(solution)/shard_map/ppermute | solution.py:423
  279.7 20.3 %shard_map.291 = (bf16[768,1792]{1,0:T(8,128)(2,1)}, bf16[768,1792]{1,0:T(8,128)(2,1)}, bf16[768,1792]{1,0:T(8,128)(2,1)}, bf16[1472,3584]{1,0:T(8,128)(2,1)}) custom-call(bf16[384,1472]{1,0:T(8,128)(2,1)} %multiply_convert_fusion.1.own_ref.refs_0_, bf16[384,1472]{1,0:T(8,128)(2,1)} %copy.195.other_ref.refs_1_, bf16[368,3584]{1,0:T(8,128)(2,1)} %shard_map.290.rest_0_, ...), custom_call_target="tpu_custom_call" | custom-call | flops 8103395328 | bytes 29360128 | tf_op jit(solution)/shard_map/pallas_call | solution.py:197
  301.0 10.7 %shard_map.292 = (f32[384,1472]{1,0:T(8,128)}, bf16[384,1472]{1,0:T(8,128)(2,1)}, bf16[1792,1472]{1,0:T(8,128)(2,1)}) custom-call(bf16[768,1792]{1,0:T(8,128)(2,1)} %get-tuple-element.44.hidden_ref.refs_0_, bf16[448,1472]{1,0:T(8,128)(2,1)} %copy.243.rest_0_, bf16[112,1472]{1,0:T(8,128)(2,1)} %collective-permute-done.34.rest_1_, ...), custom_call_target="tpu_custom_call" | custom-call | flops 4051697664 | bytes 10551296 | tf_op jit(solution)/shard_map/pallas_call | solution.py:246
  337.9 9.5 %shard_map.297 = (bf16[2,112,1472]{2,1,0:T(8,128)(2,1)}, bf16[2,112,1472]{2,1,0:T(8,128)(2,1)}, bf16[2,112,1472]{2,1,0:T(8,128)(2,1)}, bf16[2,48,1472]{2,1,0:T(8...) custom-call(bf16[768,1792]{1,0:T(8,128)(2,1)} %get-tuple-element.44., ...), custom_call_target="tpu_custom_call" | custom-call | flops 4051697664 | bytes 10289152 | tf_op jit(solution)/shard_map/pallas_call | solution.py:359
  348.7 14.1 %shard_map.293.refs_2_ = bf16[768,3584]{1,0:T(8,128)(2,1)} custom-call(bf16[384,1472]{1,0:T(8,128)(2,1)} %get-tuple-element.150.own_ref.refs_1_, bf16[384,1472]{1,0:T(8,128)(2,1)} %copy.202.other_ref.refs_2_, bf16[1792,1472]{1,0:T(8,128)(2,1)} %get-tuple-element.47.down_ref, bf16[768,1792]{1,0:T(8,128)(2,1)} %get-tuple-element.48.slope_ref, ...), custom_call_target="tpu_custom_call" | custom-call | flops 4051697664 | bytes 16285696 | tf_op jit(solution)/shard_map/pallas_call | solution.py:289
  362.8 14.1 %fusion.141 = f32[768,1472]{0,1:T(8,128)} fusion(bf16[768,3584]{1,0:T(8,128)(2,1)} %shard_map.293.refs_2_, bf16[1472,3584]{1,0:T(8,128)(2,1)} %get-tuple-element.50), kind=kOutput, calls=%fused_computation.318 | convolution fusion | flops 8103395328 | bytes 20578304 | tf_op jit(solution)/shard_map/tf,df->td/dot_general | solution.py:753
  376.9 23.6 %shard_map.295 = (bf16[2,368,896]{2,1,0:T(8,128)(2,1)}, bf16[2,368,896]{2,1,0:T(8,128)(2,1)}, bf16[2,368,896]{2,1,0:T(8,128)(2,1)}, bf16[2,176,896]{2,1,0:T(8,12...) custom-call(bf16[384,1472]{1,0:T(8,128)(2,1)} %multiply_convert_fusi, ...), custom_call_target="tpu_custom_call" | custom-call | flops 8103395328 | bytes 18317312 | tf_op jit(solution)/shard_map/pallas_call | solution.py:359
  413.7 17.9 %collective-permute-done.90 = bf16[2,48,1472]{2,1,0:T(8,128)(2,1)S(1)} collective-permute-done((bf16[2,48,1472]{2,1,0:T(8,128)(2,1)S(1)}, bf16[2,48,1472]{2,1,0:T(8,128)(2,1)S(1)}, u32[]{:S(2)}, u32[]{:S(2)}) %collective-permute-start.90) | collective-permute-done | bytes 282656 | tf_op jit(solution)/shard_map/ppermute | solution.py:423
  433.6 13.6 %collective-permute-done.98 = bf16[2,64,1472]{2,1,0:T(8,128)(2,1)S(1)} collective-permute-done((bf16[2,64,1472]{2,1,0:T(8,128)(2,1)S(1)}, bf16[2,64,1472]{2,1,0:T(8,128)(2,1)S(1)}, u32[]{:S(2)}, u32[]{:S(2)}) %collective-permute-start.98) | collective-permute-done | bytes 376864 | tf_op jit(solution)/shard_map/ppermute | solution.py:423
  447.5 10.3 %collective-permute-done.92 = bf16[2,64,1472]{2,1,0:T(8,128)(2,1)S(1)} collective-permute-done((bf16[2,64,1472]{2,1,0:T(8,128)(2,1)S(1)}, bf16[2,64,1472]{2,1,0:T(8,128)(2,1)S(1)}, u32[]{:S(2)}, u32[]{:S(2)}) %collective-permute-start.92) | collective-permute-done | bytes 376864 | tf_op jit(solution)/shard_map/ppermute | solution.py:423
  460.5 12.2 %collective-permute-done.74 = bf16[2,176,896]{2,1,0:T(8,128)(2,1)S(1)} collective-permute-done((bf16[2,176,896]{2,1,0:T(8,128)(2,1)S(1)}, bf16[2,176,896]{2,1,0:T(8,128)(2,1)S(1)}, u32[]{:S(2)}, u32[]{:S(2)}) %collective-permute-start.74) | collective-permute-done | bytes 630816 | tf_op jit(solution)/shard_map/ppermute | solution.py:423
  480.3 9.2 %collective-permute-done.91 = bf16[2,112,1472]{2,1,0:T(8,128)(2,1)S(1)} collective-permute-done((bf16[2,112,1472]{2,1,0:T(8,128)(2,1)S(1)}, bf16[2,112,1472]{2,1,0:T(8,128)(2,1)S(1)}, u32[]{:S(2)}, u32[]{:S(2)}) %collective-permute-start.91) | collective-permute-done | bytes 659488 | tf_op jit(solution)/shard_map/ppermute | solution.py:423
  489.8 4.1 collective-permute-done.93
  497.5 11.1 %collective-permute-done.99 = bf16[2,112,1472]{2,1,0:T(8,128)(2,1)S(1)} collective-permute-done((bf16[2,112,1472]{2,1,0:T(8,128)(2,1)S(1)}, bf16[2,112,1472]{2,1,0:T(8,128)(2,1)S(1)}, u32[]{:S(2)}, u32[]{:S(2)}) %collective-permute-start.99) | collective-permute-done | bytes 659488 | tf_op jit(solution)/shard_map/ppermute | solution.py:423
  508.7 4.0 collective-permute-start.94
  532.7 12.8 %multiply_convert_fusion = bf16[6,3,128,512]{3,2,1,0:T(8,128)(2,1)S(1)} fusion(f32[6,3,128,512]{3,2,1,0:T(8,128)S(1)} %fusion.60, f32[6,3,128,512]{3,2,1,0:T(8,128)S(1)} %bitcast.364, f32[6,3,128]{2,1,0:T(4,128)S(1)} %copy-done.74), kind=kOutput, calls=%fused_computation.6 | output fusion | flops 7080703 | bytes 11805696 | tf_op jit(solution)/shard_map/sub | solution.py:763
  562.4 6.5 shard_map.294
  576.7 4.7 collective-permute-done.52
  586.5 7.6 collective-permute-done.100
  596.9 9.9 %collective-permute-done.53 = bf16[384,768]{1,0:T(8,128)(2,1)S(1)} collective-permute-done((bf16[384,768]{1,0:T(8,128)(2,1)S(1)}, bf16[384,768]{1,0:T(8,128)(2,1)S(1)}, u32[]{:S(2)}, u32[]{:S(2)}) %collective-permute-start.53) | collective-permute-done | bytes 589856 | tf_op jit(solution)/shard_map/ppermute | solution.py:426
  618.7 6.0 collective-permute-done.54
  630.3 4.8 fusion.26
  641.2 5.7 gather_fusion.2
  666.4 13.6 %collective-permute-done.58 = f32[1,1520]{1,0:T(1,128)S(1)} collective-permute-done((f32[1,1520]{1,0:T(1,128)S(1)}, f32[1,1520]{1,0:T(1,128)S(1)}, u32[]{:S(2)}, u32[]{:S(2)}) %collective-permute-start.58) | collective-permute-done | bytes 6112 | tf_op jit(solution)/shard_map/ppermute | solution.py:426
  684.7 5.4 collective-permute-done.62
  699.1 7.8 %collective-permute-done.65 = bf16[4,184,384]{2,1,0:T(8,128)(2,1)S(1)} collective-permute-done((bf16[4,184,384]{2,1,0:T(8,128)(2,1)S(1)}, bf16[4,184,384]{2,1,0:T(8,128)(2,1)S(1)}, u32[]{:S(2)}, u32[]{:S(2)}) %collective-permute-start.65) | collective-permute-done | bytes 565280 | tf_op jit(solution)/shard_map/ppermute | solution.py:423
  707.8 6.6 collective-permute-done.66
  726.7 3.4 collective-permute-done.68
  734.3 3.3 collective-permute-done.70
  749.4 6.0 copy.232
  759.1 4.4 broadcast_select_fusion.1
  763.5 7.7 shard_map.296
  (660 shorter events, 346.9 us)
Async XLA Ops:
  4.3 44.0 %collective-permute-start.3 = (bf16[184,384]{1,0:T(8,128)(2,1)}, bf16[184,384]{1,0:T(8,128)(2,1)}, u32[]{:S(2)}, u32[]{:S(2)}) collective-permute-start(bf16[184,384]{1,0:T(8,128)(2,1)} %dynamic-slice_bitcast_fusion.7), channel_id=1, source_target_pairs={{0,1},{1,2},{2,3},{3,0},{4,5},{5,6},{6,7},{7,4},{8,9},{9,10},{10,1... | collective-permute-start | bytes 423944 | tf_op jit(solution)/shard_map/ppermute | solution.py:426
  16.4 127.8 %collective-permute-start.19 = (bf16[368,896]{1,0:T(8,128)(2,1)}, bf16[368,896]{1,0:T(8,128)(2,1)}, u32[]{:S(2)}, u32[]{:S(2)}) collective-permute-start(bf16[368,896]{1,0:T(8,128)(2,1)} %constant_dynamic-slice_fusion.2), channel_id=1, source_target_pairs={{0,1},{1,2},{2,3},{3,0},{4,5},{5,6},{6,7},{7,4},{8,9},{9,10},{10,1... | collective-permute-start | bytes 1978376 | tf_op jit(solution)/shard_map/ppermute | solution.py:426
  19.1 100.3 %collective-permute-start.34 = (bf16[112,1472]{1,0:T(8,128)(2,1)}, bf16[112,1472]{1,0:T(8,128)(2,1)}, u32[]{:S(2)}, u32[]{:S(2)}) collective-permute-start(bf16[112,1472]{1,0:T(8,128)(2,1)} %copy.244), channel_id=1, source_target_pairs={{0,1},{1,2},{2,3},{3,0},{4,5},{5,6},{6,7},{7,4},{8,9},{9,10},{10,1... | collective-permute-start | bytes 989192 | tf_op jit(solution)/shard_map/ppermute | solution.py:426
  119.4 23.1 %collective-permute-start.36 = (bf16[112,1472]{1,0:T(8,128)(2,1)}, bf16[112,1472]{1,0:T(8,128)(2,1)}, u32[]{:S(2)}, u32[]{:S(2)}) collective-permute-start(bf16[112,1472]{1,0:T(8,128)(2,1)} %collective-permute-done.34.rest_1_), channel_id=1, source_target_pairs={{0,16},{4,20},{8,24},{12,28},{16,0},{20,4},{24,8},{28,12},{1,17},{... | collective-permute-start | bytes 989192 | tf_op jit(solution)/shard_map/ppermute | solution.py:423
  132.1 26.2 %collective-permute-start.17 = (bf16[384,768]{0,1:T(8,128)(2,1)}, bf16[384,768]{0,1:T(8,128)(2,1)}, u32[]{:S(2)}, u32[]{:S(2)}) collective-permute-start(bf16[384,768]{0,1:T(8,128)(2,1)} %collective-permute-done.16), channel_id=1, source_target_pairs={{0,1},{1,2},{2,3},{3,0},{4,5},{5,6},{6,7},{7,4},{8,9},{9,10},{10,1... | collective-permute-start | bytes 1769480 | tf_op jit(solution)/shard_map/ppermute | solution.py:426
  133.1 24.6 %collective-permute-start.39 = (bf16[112,1472]{1,0:T(8,128)(2,1)}, bf16[112,1472]{1,0:T(8,128)(2,1)}, u32[]{:S(2)}, u32[]{:S(2)}) collective-permute-start(bf16[112,1472]{1,0:T(8,128)(2,1)} %collective-permute-done.34.rest_1_), channel_id=1, source_target_pairs={{0,1},{1,2},{2,3},{3,0},{4,5},{5,6},{6,7},{7,4},{8,9},{9,10},{10,1... | collective-permute-start | bytes 989192 | tf_op jit(solution)/shard_map/ppermute | solution.py:426
  140.6 47.5 %collective-permute-start.35 = (bf16[112,1472]{1,0:T(8,128)(2,1)}, bf16[112,1472]{1,0:T(8,128)(2,1)}, u32[]{:S(2)}, u32[]{:S(2)}) collective-permute-start(bf16[112,1472]{1,0:T(8,128)(2,1)} %collective-permute-done.34.rest_1_), channel_id=1, source_target_pairs={{0,8},{4,12},{8,0},{12,4},{16,24},{20,28},{24,16},{28,20},{1,9},{5... | collective-permute-start | bytes 989192 | tf_op jit(solution)/shard_map/ppermute | solution.py:423
  144.1 46.4 %collective-permute-start.37 = (bf16[48,1472]{1,0:T(8,128)(2,1)}, bf16[48,1472]{1,0:T(8,128)(2,1)}, u32[]{:S(2)}, u32[]{:S(2)}) collective-permute-start(bf16[48,1472]{1,0:T(8,128)(2,1)} %slice.514), channel_id=1, source_target_pairs={{0,8},{4,12},{8,0},{12,4},{16,24},{20,28},{24,16},{28,20},{1,9},{5... | collective-permute-start | bytes 423944 | tf_op jit(solution)/shard_map/ppermute | solution.py:423
  144.2 70.9 %collective-permute-start.20 = (bf16[368,896]{1,0:T(8,128)(2,1)}, bf16[368,896]{1,0:T(8,128)(2,1)}, u32[]{:S(2)}, u32[]{:S(2)}) collective-permute-start(bf16[368,896]{1,0:T(8,128)(2,1)} %collective-permute-done.19.rest_1_), channel_id=1, source_target_pairs={{0,8},{4,12},{8,0},{12,4},{16,24},{20,28},{24,16},{28,20},{1,9},{5... | collective-permute-start | bytes 1978376 | tf_op jit(solution)/shard_map/ppermute | solution.py:423
  157.7 37.2 %collective-permute-start.24 = (bf16[368,896]{1,0:T(8,128)(2,1)}, bf16[368,896]{1,0:T(8,128)(2,1)}, u32[]{:S(2)}, u32[]{:S(2)}) collective-permute-start(bf16[368,896]{1,0:T(8,128)(2,1)} %collective-permute-done.19.rest_1_), channel_id=1, source_target_pairs={{0,1},{1,2},{2,3},{3,0},{4,5},{5,6},{6,7},{7,4},{8,9},{9,10},{10,1... | collective-permute-start | bytes 1978376 | tf_op jit(solution)/shard_map/ppermute | solution.py:426
  158.3 32.3 %collective-permute-start.40 = (bf16[112,1472]{1,0:T(8,128)(2,1)}, bf16[112,1472]{1,0:T(8,128)(2,1)}, u32[]{:S(2)}, u32[]{:S(2)}) collective-permute-start(bf16[112,1472]{1,0:T(8,128)(2,1)} %collective-permute-done.39.rest_6_), channel_id=1, source_target_pairs={{0,8},{4,12},{8,0},{12,4},{16,24},{20,28},{24,16},{28,20},{1,9},{5... | collective-permute-start | bytes 989192 | tf_op jit(solution)/shard_map/ppermute | solution.py:423
  188.1 24.2 %collective-permute-start.21 = (bf16[368,896]{1,0:T(8,128)(2,1)}, bf16[368,896]{1,0:T(8,128)(2,1)}, u32[]{:S(2)}, u32[]{:S(2)}) collective-permute-start(bf16[368,896]{1,0:T(8,128)(2,1)} %collective-permute-done.19.rest_1_), channel_id=1, source_target_pairs={{0,16},{4,20},{8,24},{12,28},{16,0},{20,4},{24,8},{28,12},{1,17},{... | collective-permute-start | bytes 1978376 | tf_op jit(solution)/shard_map/ppermute | solution.py:423
  190.5 20.0 %collective-permute-start.41 = (bf16[112,1472]{1,0:T(8,128)(2,1)}, bf16[112,1472]{1,0:T(8,128)(2,1)S(1)}, u32[]{:S(2)}, u32[]{:S(2)}) collective-permute-start(bf16[112,1472]{1,0:T(8,128)(2,1)} %collective-permute-done.39.rest_6_), channel_id=1, source_target_pairs={{0,16},{4,20},{8,24},{12,28},{16,0},{20,4},{24,8},{28,12},{1,17},{... | collective-permute-start | bytes 989192 | tf_op jit(solution)/shard_map/ppermute | solution.py:423
  190.6 19.9 %collective-permute-start.44 = (bf16[112,1472]{1,0:T(8,128)(2,1)}, bf16[112,1472]{1,0:T(8,128)(2,1)}, u32[]{:S(2)}, u32[]{:S(2)}) collective-permute-start(bf16[112,1472]{1,0:T(8,128)(2,1)} %collective-permute-done.39.rest_6_), channel_id=1, source_target_pairs={{0,1},{1,2},{2,3},{3,0},{4,5},{5,6},{6,7},{7,4},{8,9},{9,10},{10,1... | collective-permute-start | bytes 989192 | tf_op jit(solution)/shard_map/ppermute | solution.py:426
  194.9 28.6 %collective-permute-start.29 = (bf16[368,896]{1,0:T(8,128)(2,1)}, bf16[368,896]{1,0:T(8,128)(2,1)}, u32[]{:S(2)}, u32[]{:S(2)}) collective-permute-start(bf16[368,896]{1,0:T(8,128)(2,1)} %collective-permute-done.24.rest_6_), channel_id=1, source_target_pairs={{0,1},{1,2},{2,3},{3,0},{4,5},{5,6},{6,7},{7,4},{8,9},{9,10},{10,1... | collective-permute-start | bytes 1978376 | tf_op jit(solution)/shard_map/ppermute | solution.py:426
  210.5 51.2 %collective-permute-start.18 = (bf16[384,1472]{0,1:T(8,128)(2,1)}, bf16[384,1472]{0,1:T(8,128)(2,1)}, u32[]{:S(2)}, u32[]{:S(2)}) collective-permute-start(bf16[384,1472]{0,1:T(8,128)(2,1)} %copy.194), channel_id=1, source_target_pairs={{0,4},{4,0},{8,12},{12,8},{16,20},{20,16},{24,28},{28,24},{1,5},{5... | collective-permute-start | bytes 3391496 | tf_op jit(solution)/shard_map/ppermute | solution.py:423
  221.8 20.8 %collective-permute-start.25 = (bf16[368,896]{1,0:T(8,128)(2,1)}, bf16[368,896]{1,0:T(8,128)(2,1)S(1)}, u32[]{:S(2)}, u32[]{:S(2)}) collective-permute-start(bf16[368,896]{1,0:T(8,128)(2,1)} %collective-permute-done.24.rest_6_), channel_id=1, source_target_pairs={{0,8},{4,12},{8,0},{12,4},{16,24},{20,28},{24,16},{28,20},{1,9},{5... | collective-permute-start | bytes 1978376 | tf_op jit(solution)/shard_map/ppermute | solution.py:423
  223.5 32.7 %collective-permute-start.30 = (bf16[368,896]{1,0:T(8,128)(2,1)}, bf16[368,896]{1,0:T(8,128)(2,1)S(1)}, u32[]{:S(2)}, u32[]{:S(2)}) collective-permute-start(bf16[368,896]{1,0:T(8,128)(2,1)} %collective-permute-done.29.rest_11_), channel_id=1, source_target_pairs={{0,8},{4,12},{8,0},{12,4},{16,24},{20,28},{24,16},{28,20},{1,9},{5... | collective-permute-start | bytes 1978376 | tf_op jit(solution)/shard_map/ppermute | solution.py:423
  223.8 34.2 %collective-permute-start.26 = (bf16[368,896]{1,0:T(8,128)(2,1)}, bf16[368,896]{1,0:T(8,128)(2,1)S(1)}, u32[]{:S(2)}, u32[]{:S(2)}) collective-permute-start(bf16[368,896]{1,0:T(8,128)(2,1)} %collective-permute-done.24.rest_6_), channel_id=1, source_target_pairs={{0,16},{4,20},{8,24},{12,28},{16,0},{20,4},{24,8},{28,12},{1,17},{... | collective-permute-start | bytes 1978376 | tf_op jit(solution)/shard_map/ppermute | solution.py:423
  229.1 30.0 %collective-permute-start.31 = (bf16[368,896]{1,0:T(8,128)(2,1)}, bf16[368,896]{1,0:T(8,128)(2,1)S(1)}, u32[]{:S(2)}, u32[]{:S(2)}) collective-permute-start(bf16[368,896]{1,0:T(8,128)(2,1)} %collective-permute-done.29.rest_11_), channel_id=1, source_target_pairs={{0,16},{4,20},{8,24},{12,28},{16,0},{20,4},{24,8},{28,12},{1,17},{... | collective-permute-start | bytes 1978376 | tf_op jit(solution)/shard_map/ppermute | solution.py:423
  242.6 31.4 %collective-permute-start.23 = (bf16[192,896]{1,0:T(8,128)(2,1)}, bf16[192,896]{1,0:T(8,128)(2,1)}, u32[]{:S(2)}, u32[]{:S(2)}) collective-permute-start(bf16[192,896]{1,0:T(8,128)(2,1)} %slice.509), channel_id=1, source_target_pairs={{0,16},{4,20},{8,24},{12,28},{16,0},{20,4},{24,8},{28,12},{1,17},{... | collective-permute-start | bytes 1032200 | tf_op jit(solution)/shard_map/ppermute | solution.py:423
  256.2 20.7 %collective-permute-start.28 = (bf16[192,896]{1,0:T(8,128)(2,1)}, bf16[192,896]{1,0:T(8,128)(2,1)}, u32[]{:S(2)}, u32[]{:S(2)}) collective-permute-start(bf16[192,896]{1,0:T(8,128)(2,1)} %slice.511), channel_id=1, source_target_pairs={{0,16},{4,20},{8,24},{12,28},{16,0},{20,4},{24,8},{28,12},{1,17},{... | collective-permute-start | bytes 1032200 | tf_op jit(solution)/shard_map/ppermute | solution.py:423
  258.0 20.0 %collective-permute-start.33 = (bf16[192,896]{1,0:T(8,128)(2,1)S(1)}, bf16[192,896]{1,0:T(8,128)(2,1)}, u32[]{:S(2)}, u32[]{:S(2)}) collective-permute-start(bf16[192,896]{1,0:T(8,128)(2,1)S(1)} %slice.513), channel_id=1, source_target_pairs={{0,16},{4,20},{8,24},{12,28},{16,0},{20,4},{24,8},{28,12},{1,17},{... | collective-permute-start | bytes 1032200 | tf_op jit(solution)/shard_map/ppermute | solution.py:423
  273.9 26.2 %collective-permute-start.38 = (bf16[64,1472]{1,0:T(8,128)(2,1)S(1)}, bf16[64,1472]{1,0:T(8,128)(2,1)S(1)}, u32[]{:S(2)}, u32[]{:S(2)}) collective-permute-start(bf16[64,1472]{1,0:T(8,128)(2,1)S(1)} %slice.515), channel_id=1, source_target_pairs={{0,16},{4,20},{8,24},{12,28},{16,0},{20,4},{24,8},{28,12},{1,17},{... | collective-permute-start | bytes 565256 | tf_op jit(solution)/shard_map/ppermute | solution.py:423
  275.7 24.4 %collective-permute-start.42 = (bf16[48,1472]{1,0:T(8,128)(2,1)S(1)}, bf16[48,1472]{1,0:T(8,128)(2,1)S(1)}, u32[]{:S(2)}, u32[]{:S(2)}) collective-permute-start(bf16[48,1472]{1,0:T(8,128)(2,1)S(1)} %slice.516), channel_id=1, source_target_pairs={{0,8},{4,12},{8,0},{12,4},{16,24},{20,28},{24,16},{28,20},{1,9},{5... | collective-permute-start | bytes 423944 | tf_op jit(solution)/shard_map/ppermute | solution.py:423
  276.9 23.2 %collective-permute-start.43 = (bf16[64,1472]{1,0:T(8,128)(2,1)S(1)}, bf16[64,1472]{1,0:T(8,128)(2,1)S(1)}, u32[]{:S(2)}, u32[]{:S(2)}) collective-permute-start(bf16[64,1472]{1,0:T(8,128)(2,1)S(1)} %slice.517), channel_id=1, source_target_pairs={{0,16},{4,20},{8,24},{12,28},{16,0},{20,4},{24,8},{28,12},{1,17},{... | collective-permute-start | bytes 565256 | tf_op jit(solution)/shard_map/ppermute | solution.py:423
  277.2 22.9 %collective-permute-start.47 = (bf16[48,1472]{1,0:T(8,128)(2,1)S(1)}, bf16[48,1472]{1,0:T(8,128)(2,1)S(1)}, u32[]{:S(2)}, u32[]{:S(2)}) collective-permute-start(bf16[48,1472]{1,0:T(8,128)(2,1)S(1)} %slice.518), channel_id=1, source_target_pairs={{0,8},{4,12},{8,0},{12,4},{16,24},{20,28},{24,16},{28,20},{1,9},{5... | collective-permute-start | bytes 423944 | tf_op jit(solution)/shard_map/ppermute | solution.py:423
  278.0 22.2 %collective-permute-start.48 = (bf16[64,1472]{1,0:T(8,128)(2,1)S(1)}, bf16[64,1472]{1,0:T(8,128)(2,1)S(1)}, u32[]{:S(2)}, u32[]{:S(2)}) collective-permute-start(bf16[64,1472]{1,0:T(8,128)(2,1)S(1)} %slice.519), channel_id=1, source_target_pairs={{0,16},{4,20},{8,24},{12,28},{16,0},{20,4},{24,8},{28,12},{1,17},{... | collective-permute-start | bytes 565256 | tf_op jit(solution)/shard_map/ppermute | solution.py:423
  347.4 64.3 %collective-permute-start.96 = (bf16[2,48,1472]{2,1,0:T(8,128)(2,1)}, bf16[2,48,1472]{2,1,0:T(8,128)(2,1)S(1)}, u32[]{:S(2)}, u32[]{:S(2)}) collective-permute-start(bf16[2,48,1472]{2,1,0:T(8,128)(2,1)} %get-tuple-element.70), channel_id=1, source_target_pairs={{0,8},{4,12},{8,0},{12,4},{16,24},{20,28},{24,16},{28,20},{1,9},{5... | collective-permute-start | bytes 847880 | tf_op jit(solution)/shard_map/ppermute | solution.py:423
  405.9 107.9 %collective-permute-start.51 = (bf16[384,1472]{0,1:T(8,128)(2,1)}, bf16[384,1472]{0,1:T(8,128)(2,1)}, u32[]{:S(2)}, u32[]{:S(2)}) collective-permute-start(bf16[384,1472]{0,1:T(8,128)(2,1)} %slice.683), channel_id=1, source_target_pairs={{0,4},{4,0},{8,12},{12,8},{16,20},{20,16},{24,28},{28,24},{1,5},{5... | collective-permute-start | bytes 3391496 | tf_op jit(solution)/shard_map/ppermute | solution.py:423
  405.9 69.6 %collective-permute-start.82 = (bf16[2,192,896]{2,1,0:T(8,128)(2,1)}, bf16[2,192,896]{2,1,0:T(8,128)(2,1)S(1)}, u32[]{:S(2)}, u32[]{:S(2)}) collective-permute-start(bf16[2,192,896]{2,1,0:T(8,128)(2,1)} %get-tuple-element.60), channel_id=1, source_target_pairs={{0,16},{4,20},{8,24},{12,28},{16,0},{20,4},{24,8},{28,12},{1,17},{... | collective-permute-start | bytes 2064392 | tf_op jit(solution)/shard_map/ppermute | solution.py:423
  408.9 50.0 %collective-permute-start.80 = (bf16[2,176,896]{2,1,0:T(8,128)(2,1)}, bf16[2,176,896]{2,1,0:T(8,128)(2,1)S(1)}, u32[]{:S(2)}, u32[]{:S(2)}) collective-permute-start(bf16[2,176,896]{2,1,0:T(8,128)(2,1)} %get-tuple-element.58), channel_id=1, source_target_pairs={{0,8},{4,12},{8,0},{12,4},{16,24},{20,28},{24,16},{28,20},{1,9},{5... | collective-permute-start | bytes 1892360 | tf_op jit(solution)/shard_map/ppermute | solution.py:423
  409.7 68.0 %collective-permute-start.76 = (bf16[2,192,896]{2,1,0:T(8,128)(2,1)}, bf16[2,192,896]{2,1,0:T(8,128)(2,1)S(1)}, u32[]{:S(2)}, u32[]{:S(2)}) collective-permute-start(bf16[2,192,896]{2,1,0:T(8,128)(2,1)} %get-tuple-element.55), channel_id=1, source_target_pairs={{0,16},{4,20},{8,24},{12,28},{16,0},{20,4},{24,8},{28,12},{1,17},{... | collective-permute-start | bytes 2064392 | tf_op jit(solution)/shard_map/ppermute | solution.py:423
  458.9 37.9 %collective-permute-start.97 = (bf16[2,112,1472]{2,1,0:T(8,128)(2,1)S(1)}, bf16[2,112,1472]{2,1,0:T(8,128)(2,1)S(1)}, u32[]{:S(2)}, u32[]{:S(2)}) collective-permute-start(bf16[2,112,1472]{2,1,0:T(8,128)(2,1)S(1)} %pad_maximum_fusion.9), channel_id=1, source_target_pairs={{0,16},{4,20},{8,24},{12,28},{16,0},{20,4},{24,8},{28,12},{1,17},{... | collective-permute-start | bytes 1978376 | tf_op jit(solution)/shard_map/ppermute | solution.py:423
  477.8 30.9 %collective-permute-start.99 = (bf16[2,112,1472]{2,1,0:T(8,128)(2,1)S(1)}, bf16[2,112,1472]{2,1,0:T(8,128)(2,1)S(1)}, u32[]{:S(2)}, u32[]{:S(2)}) collective-permute-start(bf16[2,112,1472]{2,1,0:T(8,128)(2,1)S(1)} %pad_maximum_fusion.10), channel_id=1, source_target_pairs={{0,8},{4,12},{8,0},{12,4},{16,24},{20,28},{24,16},{28,20},{1,9},{5... | collective-permute-start | bytes 1978376 | tf_op jit(solution)/shard_map/ppermute | solution.py:423
  489.5 119.2 %collective-permute-start.81 = (bf16[2,368,896]{2,1,0:T(8,128)(2,1)}, bf16[2,368,896]{2,1,0:T(8,128)(2,1)}, u32[]{:S(2)}, u32[]{:S(2)}) collective-permute-start(bf16[2,368,896]{2,1,0:T(8,128)(2,1)} %pad_maximum_fusion.4), channel_id=1, source_target_pairs={{0,16},{4,20},{8,24},{12,28},{16,0},{20,4},{24,8},{28,12},{1,17},{... | collective-permute-start | bytes 3956744 | tf_op jit(solution)/shard_map/ppermute | solution.py:423
  493.9 88.6 %collective-permute-start.75 = (bf16[2,368,896]{2,1,0:T(8,128)(2,1)}, bf16[2,368,896]{2,1,0:T(8,128)(2,1)}, u32[]{:S(2)}, u32[]{:S(2)}) collective-permute-start(bf16[2,368,896]{2,1,0:T(8,128)(2,1)} %pad_maximum_fusion.2), channel_id=1, source_target_pairs={{0,16},{4,20},{8,24},{12,28},{16,0},{20,4},{24,8},{28,12},{1,17},{... | collective-permute-start | bytes 3956744 | tf_op jit(solution)/shard_map/ppermute | solution.py:423
  496.7 85.9 %collective-permute-start.77 = (bf16[2,368,896]{2,1,0:T(8,128)(2,1)}, bf16[2,368,896]{2,1,0:T(8,128)(2,1)}, u32[]{:S(2)}, u32[]{:S(2)}) collective-permute-start(bf16[2,368,896]{2,1,0:T(8,128)(2,1)} %pad_maximum_fusion.3), channel_id=1, source_target_pairs={{0,8},{4,12},{8,0},{12,4},{16,24},{20,28},{24,16},{28,20},{1,9},{5... | collective-permute-start | bytes 3956744 | tf_op jit(solution)/shard_map/ppermute | solution.py:423
  508.7 49.8 %collective-permute-start.94 = (bf16[112,1472]{1,0:T(8,128)(2,1)}, bf16[112,1472]{1,0:T(8,128)(2,1)}, u32[]{:S(2)}, u32[]{:S(2)}) collective-permute-start(bf16[112,1472]{1,0:T(8,128)(2,1)} %slice_bitcast_fusion.8), channel_id=1, source_target_pairs={{0,1},{1,2},{2,3},{3,0},{4,5},{5,6},{6,7},{7,4},{8,9},{9,10},{10,1... | collective-permute-start | bytes 989192 | tf_op jit(solution)/shard_map/ppermute | solution.py:426
  574.8 34.0 %collective-permute-start.83 = (bf16[2,368,896]{2,1,0:T(8,128)(2,1)}, bf16[2,368,896]{2,1,0:T(8,128)(2,1)S(1)}, u32[]{:S(2)}, u32[]{:S(2)}) collective-permute-start(bf16[2,368,896]{2,1,0:T(8,128)(2,1)} %pad_maximum_fusion.5), channel_id=1, source_target_pairs={{0,8},{4,12},{8,0},{12,4},{16,24},{20,28},{24,16},{28,20},{1,9},{5... | collective-permute-start | bytes 3956744 | tf_op jit(solution)/shard_map/ppermute | solution.py:423
  582.6 24.2 %collective-permute-start.53 = (bf16[384,768]{1,0:T(8,128)(2,1)S(1)}, bf16[384,768]{1,0:T(8,128)(2,1)S(1)}, u32[]{:S(2)}, u32[]{:S(2)}) collective-permute-start(bf16[384,768]{1,0:T(8,128)(2,1)S(1)} %fusion.59), channel_id=1, source_target_pairs={{0,1},{1,2},{2,3},{3,0},{4,5},{5,6},{6,7},{7,4},{8,9},{9,10},{10,1... | collective-permute-start | bytes 1769480 | tf_op jit(solution)/shard_map/ppermute | solution.py:426
  585.9 75.2 %collective-permute-start.78 = (bf16[368,896]{1,0:T(8,128)(2,1)}, bf16[368,896]{1,0:T(8,128)(2,1)}, u32[]{:S(2)}, u32[]{:S(2)}) collective-permute-start(bf16[368,896]{1,0:T(8,128)(2,1)} %slice_bitcast_fusion.4), channel_id=1, source_target_pairs={{0,1},{1,2},{2,3},{3,0},{4,5},{5,6},{6,7},{7,4},{8,9},{9,10},{10,1... | collective-permute-start | bytes 1978376 | tf_op jit(solution)/shard_map/ppermute | solution.py:426
  614.8 41.5 %collective-permute-start.103 = (bf16[48,1472]{1,0:T(8,128)(2,1)}, bf16[48,1472]{1,0:T(8,128)(2,1)}, u32[]{:S(2)}, u32[]{:S(2)}) collective-permute-start(bf16[48,1472]{1,0:T(8,128)(2,1)} %slice.561), channel_id=1, source_target_pairs={{0,8},{4,12},{8,0},{12,4},{16,24},{20,28},{24,16},{28,20},{1,9},{5... | collective-permute-start | bytes 423944 | tf_op jit(solution)/shard_map/ppermute | solution.py:423
  616.2 47.1 %collective-permute-start.104 = (bf16[64,1472]{1,0:T(8,128)(2,1)}, bf16[64,1472]{1,0:T(8,128)(2,1)S(1)}, u32[]{:S(2)}, u32[]{:S(2)}) collective-permute-start(bf16[64,1472]{1,0:T(8,128)(2,1)} %slice.562), channel_id=1, source_target_pairs={{0,16},{4,20},{8,24},{12,28},{16,0},{20,4},{24,8},{28,12},{1,17},{... | collective-permute-start | bytes 565256 | tf_op jit(solution)/shard_map/ppermute | solution.py:423
  651.4 29.0 %collective-permute-start.61 = (bf16[4,4,184,384]{3,2,1,0:T(8,128)(2,1)}, bf16[4,4,184,384]{3,2,1,0:T(8,128)(2,1)}, u32[]{:S(2)}, u32[]{:S(2)}) collective-permute-start(bf16[4,4,184,384]{3,2,1,0:T(8,128)(2,1)} %dynamic-slice_bitcast_fusion), channel_id=1, source_target_pairs={{0,4},{4,0},{8,12},{12,8},{16,20},{20,16},{24,28},{28,24},{1,5},{5... | collective-permute-start | bytes 6782984 | tf_op jit(solution)/shard_map/ppermute | solution.py:423
  664.1 80.3 %collective-permute-start.105 = (bf16[448,1472]{1,0:T(8,128)(2,1)}, bf16[448,1472]{1,0:T(8,128)(2,1)}, u32[]{:S(2)}, u32[]{:S(2)}) collective-permute-start(bf16[448,1472]{1,0:T(8,128)(2,1)} %constant_dynamic-update-slice_fusion), channel_id=1, source_target_pairs={{0,4},{4,0},{8,12},{12,8},{16,20},{20,16},{24,28},{28,24},{1,5},{5... | collective-permute-start | bytes 3956744 | tf_op jit(solution)/shard_map/ppermute | solution.py:423
  698.3 22.9 %collective-permute-start.85 = (bf16[368,896]{1,0:T(8,128)(2,1)}, bf16[368,896]{1,0:T(8,128)(2,1)}, u32[]{:S(2)}, u32[]{:S(2)}) collective-permute-start(bf16[368,896]{1,0:T(8,128)(2,1)} %get-tuple-element.147), channel_id=1, source_target_pairs={{0,8},{4,12},{8,0},{12,4},{16,24},{20,28},{24,16},{28,20},{1,9},{5... | collective-permute-start | bytes 1978376 | tf_op jit(solution)/shard_map/ppermute | solution.py:423
  734.2 24.9 %collective-permute-start.89 = (bf16[368,3584]{1,0:T(8,128)(2,1)S(1)}, bf16[368,3584]{1,0:T(8,128)(2,1)}, u32[]{:S(2)}, u32[]{:S(2)}) collective-permute-start(bf16[368,3584]{1,0:T(8,128)(2,1)S(1)} %constant_dynamic-update-slice_fusion.9), channel_id=1, source_target_pairs={{0,4},{4,0},{8,12},{12,8},{16,20},{20,16},{24,28},{28,24},{1,5},{5... | collective-permute-start | bytes 7913480 | tf_op jit(solution)/shard_map/ppermute | solution.py:423
  (169 other events, 1418.4 us)

commit v3 on v2

v3 whole, which is shorter than its diff:
```python
import functools

import math

import jax
import jax.numpy as jnp
from jax import lax
from jax.experimental import pallas as pl
from jax.experimental.pallas import tpu as pltpu
from jax.sharding import PartitionSpec as P

EPSILON = 1e-06
HIGHEST = lax.Precision.HIGHEST
MASKED = -1000000000.0
BF16 = jnp.bfloat16
F32 = jnp.float32


def gelu_tanh(value):
    return jax.nn.gelu(value, approximate=True)


def rms_scale(hidden):
    return lax.rsqrt(jnp.mean(hidden * hidden, axis=-1, keepdims=True) + EPSILON)


def rms_back(hidden, scale_row, gain, upstream):
    scaled = upstream * gain
    return scale_row * scaled - hidden * (scale_row * scale_row * scale_row) * jnp.mean(
        hidden * scaled, axis=-1, keepdims=True
    )


def dot(left, right, kind=F32):
    return jnp.dot(left, right, preferred_element_type=F32).astype(kind)


def bias_kernel(rows_ref, slots_ref, out_ref):
    group = out_ref.shape[2]
    row = jnp.broadcast_to(rows_ref[0], (group, rows_ref.shape[2]))
    grid = pltpu.roll(row, group + 1, 1, stride=1, stride_axis=0)[:, :group].astype(BF16)
    tokens = slots_ref.shape[0]
    pick = (slots_ref[...] == lax.broadcasted_iota(jnp.int32, (tokens, group), 1)).astype(BF16)
    out_ref[0] = jnp.dot(pick, grid, preferred_element_type=F32).astype(BF16)


def bias_of_queries(bias_rows, slots, group):
    heads, width = bias_rows.shape
    tokens = slots.shape[0]
    return pl.pallas_call(
        bias_kernel,
        grid=(heads,),
        in_specs=[
            pl.BlockSpec((1, 1, width), lambda h: (h, 0, 0)),
            pl.BlockSpec((tokens, 1), lambda h: (0, 0)),
        ],
        out_specs=pl.BlockSpec((1, tokens, group), lambda h: (h, 0, 0)),
        out_shape=jax.ShapeDtypeStruct((heads, tokens, group), BF16),
    )(bias_rows.reshape(heads, 1, width), slots.reshape(tokens, 1))


def bias_fold(score_grads, slots):
    heads, local, group = score_grads[0].shape
    count = len(score_grads)

    def kernel(*refs):
        grad_refs, slots_ref, out_ref = refs[:count], refs[count], refs[count + 1]
        square = None
        for index, ref in enumerate(grad_refs):
            mine = slots_ref[:, index * local : (index + 1) * local]
            row = lax.broadcasted_iota(jnp.int32, (group, local), 0)
            place = (row == (group - 1) - mine).astype(BF16)
            part = jnp.dot(place, ref[0], preferred_element_type=F32)
            square = part if square is None else square + part
        wide = jnp.concatenate([square, jnp.zeros_like(square)], axis=1)
        rolled = pltpu.roll(wide, 0, 1, stride=1, stride_axis=0)
        out_ref[0] = jnp.sum(rolled, axis=0, keepdims=True)

    return pl.pallas_call(
        kernel,
        grid=(heads,),
        in_specs=[pl.BlockSpec((1, local, group), lambda h: (h, 0, 0))] * count
        + [pl.BlockSpec((1, count * local), lambda h: (0, 0))],
        out_specs=pl.BlockSpec((1, 1, 2 * group), lambda h: (h, 0, 0)),
        out_shape=jax.ShapeDtypeStruct((heads, 1, 2 * group), F32),
    )(*score_grads, slots.reshape(1, count * local)).reshape(heads, 2 * group)


def by_head(value, head, head_size):
    per_block = 128 // head_size
    start = head // per_block * 128
    lanes = lax.broadcasted_iota(jnp.int32, (1, 128), 1) // head_size
    block = value[:, start : start + 128]
    return jnp.where(lanes == head % per_block, block, jnp.zeros_like(block)), start


def dot_last(left, right):
    return lax.dot_general(left, right, (((1,), (1,)), ((), ())), preferred_element_type=F32)


def attention_call(micro, lengths, queries, pairs, own_slots, key_slots, bias):
    heads, rows, group = bias.shape
    double = pairs[0].shape[1]
    count = len(pairs)
    local = group // count
    proj = double // 2
    head_size = proj // heads

    def kernel(lengths_ref, query_ref, *rest):
        pair_refs = rest[:count]
        own_ref, key_ref, bias_ref, context_ref, prob_ref, packed_ref, arrived = rest[count:]
        for index, ref in enumerate(pair_refs):
            arrived[index * local : (index + 1) * local] = ref[...]
        place = (
            lax.broadcasted_iota(jnp.int32, (group, group), 0) == key_ref[...]
        ).astype(BF16)
        packed_ref[...] = jnp.dot(place, arrived[...], preferred_element_type=F32).astype(BF16)
        first = lengths_ref[0]
        key_seg = lax.broadcasted_iota(jnp.int32, (local, group), 1) >= first
        same = key_seg == (own_ref[...] >= first)
        per_block = 128 // head_size
        total = None
        for head in range(heads):
            query, start = by_head(query_ref[...], head, head_size)
            scores = dot_last(query, packed_ref[:, start : start + 128])
            scores = jnp.where(same, scores + bias_ref[head].astype(F32), MASKED)
            weights = jnp.exp(scores - jnp.max(scores, axis=1, keepdims=True))
            weights = (weights / jnp.sum(weights, axis=1, keepdims=True)).astype(BF16)
            prob_ref[head] = weights
            value, _ = by_head(packed_ref[:, proj:], head, head_size)
            part = jnp.dot(weights, value, preferred_element_type=F32)
            total = part if head % per_block == 0 else total + part
            if head % per_block == per_block - 1:
                context_ref[:, start : start + 128] = total.astype(BF16)

    return pl.pallas_call(
        kernel,
        grid=(1,),
        in_specs=[
            pl.BlockSpec(memory_space=pltpu.SMEM),
            pl.BlockSpec((local, proj), lambda i: (micro, 0)),
        ]
        + [pl.BlockSpec((local, double), lambda i: (micro, 0))] * count
        + [
            pl.BlockSpec((local, 1), lambda i: (micro, 0)),
            pl.BlockSpec((1, group), lambda i: (0, 0)),
            pl.BlockSpec((heads, local, group), lambda i: (0, micro, 0)),
        ],
        out_specs=[
            pl.BlockSpec((local, proj), lambda i: (0, 0)),
            pl.BlockSpec((heads, local, group), lambda i: (0, 0, 0)),
            pl.BlockSpec((group, double), lambda i: (0, 0)),
        ],
        out_shape=[
            jax.ShapeDtypeStruct((local, proj), BF16),
            jax.ShapeDtypeStruct((heads, local, group), BF16),
            jax.ShapeDtypeStruct((group, double), BF16),
        ],
        scratch_shapes=[pltpu.VMEM((group, double), BF16)],
        cost_estimate=pl.CostEstimate(
            flops=2 * group * group * double + 8 * local * group * proj,
            bytes_accessed=4 * group * double + 4 * heads * local * group,
            transcendentals=heads * local * group,
        ),
    )(lengths, queries, *pairs, own_slots, key_slots, bias)


def attention_back_call(micro, queries, context_grad, probs, packed, key_slots, shards):
    heads, local, group = probs.shape
    double = packed.shape[1]
    proj = double // 2
    head_size = proj // heads

    def kernel(query_ref, context_ref, prob_ref, packed_ref, key_ref, score_ref, dq_ref, *rest):
        part_refs, sums = rest[:shards], rest[shards]
        per_block = 128 // head_size
        for head in range(heads):
            context, start = by_head(context_ref[...], head, head_size)
            query, _ = by_head(query_ref[...], head, head_size)
            key, _ = by_head(packed_ref[:, :proj], head, head_size)
            weights = prob_ref[head]
            wide = weights.astype(F32)
            upstream = dot_last(context, packed_ref[:, proj + start : proj + start + 128])
            inner = jnp.sum(wide * upstream, axis=1, keepdims=True)
            grad = (wide * (upstream - inner)).astype(BF16)
            score_ref[head] = grad
            query_part = jnp.dot(grad, key, preferred_element_type=F32)
            key_part = jnp.dot(grad.T, query, preferred_element_type=F32)
            value_part = jnp.dot(weights.T, context, preferred_element_type=F32)
            if head % per_block == 0:
                totals = [query_part, key_part, value_part]
            else:
                totals = [
                    total + part
                    for total, part in zip(totals, (query_part, key_part, value_part))
                ]
            if head % per_block == per_block - 1:
                dq_ref[:, start : start + 128] = totals[0].astype(BF16)
                sums[:, start : start + 128] = totals[1].astype(BF16)
                sums[:, proj + start : proj + start + 128] = totals[2].astype(BF16)
        for index, ref in enumerate(part_refs):
            slots = key_ref[index * local : (index + 1) * local]
            pick = (lax.broadcasted_iota(jnp.int32, (local, group), 1) == slots).astype(BF16)
            ref[...] = jnp.dot(pick, sums[...], preferred_element_type=F32).astype(BF16)

    return pl.pallas_call(
        kernel,
        grid=(1,),
        in_specs=[
            pl.BlockSpec((local, proj), lambda i: (micro, 0)),
            pl.BlockSpec((local, proj), lambda i: (micro, 0)),
            pl.BlockSpec((heads, local, group), lambda i: (0, 0, 0)),
            pl.BlockSpec((group, double), lambda i: (0, 0)),
            pl.BlockSpec((group, 1), lambda i: (0, 0)),
        ],
        out_specs=[
            pl.BlockSpec((heads, local, group), lambda i: (0, 0, 0)),
            pl.BlockSpec((local, proj), lambda i: (0, 0)),
        ]
        + [pl.BlockSpec((local, double), lambda i: (0, 0))] * shards,
        out_shape=[
            jax.ShapeDtypeStruct((heads, local, group), BF16),
            jax.ShapeDtypeStruct((local, proj), BF16),
        ]
        + [jax.ShapeDtypeStruct((local, double), BF16)] * shards,
        scratch_shapes=[pltpu.VMEM((group, double), BF16)],
        cost_estimate=pl.CostEstimate(
            flops=2 * group * group * double + 16 * local * group * proj,
            bytes_accessed=4 * group * double + 4 * heads * local * group,
            transcendentals=0,
        ),
    )(queries, context_grad, probs, packed, key_slots)


def axis_ranks():
    return lax.axis_index("shard"), lax.axis_index("rep") // 2


def gelu_parts(value):
    inner = math.sqrt(2.0 / math.pi)
    square = value * value
    bend = jnp.tanh(inner * value * (1.0 + 0.044715 * square))
    outside = 0.5 * (1.0 + bend)
    slope = outside + 0.5 * value * (1.0 - bend * bend) * (inner * (1.0 + 0.134145 * square))
    return value * outside, slope


def run_copies(copies, sems):
    started = [pltpu.make_async_copy(src, dst, sems.at[i]) for i, (src, dst) in enumerate(copies)]
    for copy in started:
        copy.start()
    return started


ANY = pl.BlockSpec(memory_space=pl.ANY)
VMEM = pl.BlockSpec(memory_space=pltpu.VMEM)


def pick_kernel(gate_ref, up_ref, out_ref):
    core = lax.axis_index("rep") % 2
    inner = gate_ref.shape[1]
    shards = lax.axis_size("shard")
    unit = inner // shards
    half = unit // 2
    for index, ref in enumerate((gate_ref, up_ref)):
        parts = []
        for shard in range(shards):
            low = ref[:, shard * unit : shard * unit + half]
            high = ref[:, shard * unit + half : (shard + 1) * unit]
            parts.append(jnp.where(core == 0, low, high))
        out_ref[:, index * (inner // 2) : (index + 1) * (inner // 2)] = jnp.concatenate(parts, 1)


def pick_columns(w_gate, w_up):
    return pl.pallas_call(
        pick_kernel,
        in_specs=[VMEM, VMEM],
        out_specs=VMEM,
        out_shape=jax.ShapeDtypeStruct(w_gate.shape, BF16),
    )(w_gate, w_up)


def spread_kernel(low_ref, high_ref, gate_ref, up_ref):
    inner = gate_ref.shape[1]
    shards = lax.axis_size("shard")
    half = inner // shards // 2
    for index, ref in enumerate((gate_ref, up_ref)):
        parts = []
        for shard in range(shards):
            start = index * (inner // 2) + shard * half
            parts += [low_ref[:, start : start + half], high_ref[:, start : start + half]]
        ref[...] = jnp.concatenate(parts, 1).astype(F32)


def spread_columns(low, high):
    shape = jax.ShapeDtypeStruct(low.shape, F32)
    return pl.pallas_call(
        spread_kernel,
        in_specs=[VMEM, VMEM],
        out_specs=[VMEM, VMEM],
        out_shape=[shape, shape],
    )(low, high)


def project_call(tokens, gain, pieces, places, block, proj):
    rows, width = tokens.shape
    count = len(pieces)
    moves = 2 * sum(len(place) for place in places)

    def kernel(token_ref, gain_ref, *rest):
        piece_refs = rest[:count]
        normed_ref, query_ref, pair_ref, keep_ref, weights, sems = rest[count:]
        rank, rep = lax.axis_index("shard"), lax.axis_index("rep")
        copies = []
        for ref, place in zip(piece_refs, places):
            for index, where in place:
                source = ref if index is None else ref.at[index]
                for start, size, matrix, row in where(rank, rep):
                    copies.append(
                        (source.at[pl.ds(start, size)], weights.at[matrix, pl.ds(row, size)])
                    )
        copies = run_copies(copies, sems)
        hidden = token_ref[...].astype(F32)
        scale = lax.rsqrt(jnp.mean(hidden * hidden, axis=1, keepdims=True) + EPSILON)
        normed = (hidden * scale * gain_ref[...]).astype(BF16)
        normed_ref[...] = normed
        for copy in copies:
            copy.wait()
        keep = pltpu.make_async_copy(weights, keep_ref, sems.at[moves])
        keep.start()
        query_ref[...] = jnp.dot(normed, weights[0], preferred_element_type=F32).astype(BF16)
        pair_ref[:, :proj] = jnp.dot(normed, weights[1], preferred_element_type=F32).astype(BF16)
        pair_ref[:, proj:] = jnp.dot(normed, weights[2], preferred_element_type=F32).astype(BF16)
        keep.wait()

    return pl.pallas_call(
        kernel,
        in_specs=[VMEM, VMEM] + [ANY] * count,
        out_specs=[VMEM, VMEM, VMEM, ANY],
        out_shape=[
            jax.ShapeDtypeStruct((rows, width), BF16),
            jax.ShapeDtypeStruct((rows, proj), BF16),
            jax.ShapeDtypeStruct((rows, 2 * proj), BF16),
            jax.ShapeDtypeStruct((4, width, proj), BF16),
        ],
        scratch_shapes=[
            pltpu.VMEM((4, width, proj), BF16),
            pltpu.SemaphoreType.DMA((moves + 1,)),
        ],
        cost_estimate=pl.CostEstimate(
            flops=6 * rows * width * proj, bytes_accessed=16 * width * proj, transcendentals=0
        ),
    )(tokens, gain, *pieces)


def project_grad_call(normed, query_grad, pair_grad, out_grads, small, outputs):
    rows, width = normed.shape
    proj = query_grad.shape[1]
    count = len(outputs)
    moves = sum(len(items) for _, items in outputs)

    small_rows = small.shape[1]

    def kernel(normed_ref, query_ref, pair_ref, out_grad_ref, small_ref, *rest):
        out_refs, result, sems = rest[:count], rest[count], rest[count + 1]
        fourth = pltpu.make_async_copy(out_grad_ref, result.at[3], sems.at[2 * moves])
        fourth.start()
        for begin in range(0, width, 256):
            size = min(256, width - begin)
            turned = normed_ref[:, begin : begin + size].T
            for index in range(3):
                right = query_ref[...] if index == 0 else pair_ref[:, (index - 1) * proj : index * proj]
                result[index, begin : begin + size] = jnp.dot(
                    turned, right, preferred_element_type=F32
                ).astype(BF16)
        fourth.wait()
        rank, rep = lax.axis_index("shard"), lax.axis_index("rep")
        copies = []
        for ref, (shape, items) in zip(out_refs, outputs):
            for index, where, step in items:
                matrix, row = where(rank, rep)
                size = shape[-2] - (small_rows if step is not None else 0)
                copies.append((result.at[matrix, pl.ds(row, size)], ref.at[index + (pl.ds(0, size),)]))
                if step is not None:
                    copies.append(
                        (
                            small_ref.at[(rank - step) % lax.axis_size("shard")],
                            ref.at[index + (pl.ds(size, small_rows),)],
                        )
                    )
        for copy in run_copies(copies, sems):
            copy.wait()

    return pl.pallas_call(
        kernel,
        in_specs=[VMEM, VMEM, VMEM, ANY, VMEM],
        out_specs=[ANY] * count,
        out_shape=[jax.ShapeDtypeStruct(shape, BF16) for shape, _ in outputs],
        scratch_shapes=[
            pltpu.VMEM((4, width, proj), BF16),
            pltpu.SemaphoreType.DMA((2 * moves + 1,)),
        ],
        cost_estimate=pl.CostEstimate(
            flops=6 * rows * width * proj, bytes_accessed=16 * width * proj, transcendentals=0
        ),
    )(normed, query_grad, pair_grad, out_grads, small)


def part_of(ref, row, count, columns):
    if (row, count, columns) == (0,) + ref.shape:
        return ref
    return ref.at[pl.ds(row, count), pl.ds(0, columns)]


def gate_up_call(own, other, inner, pieces, moves):
    rows, width = own.shape
    count, steps = len(pieces), len(moves)
    half = inner // 2
    tile = 256

    def kernel(own_ref, other_ref, *rest):
        piece_refs = rest[:count]
        slope_ref, act_ref, hidden_ref, keep_ref, both, weights, sems = rest[count:]
        rank, chip = axis_ranks()
        copies = [(own_ref, both.at[:rows]), (other_ref, both.at[rows:])]
        for piece, row, size, columns, place in moves:
            to_row, to_column = place(rank, chip)
            copies.append(
                (
                    part_of(piece_refs[piece], row, size, columns),
                    weights.at[pl.ds(to_row, size), pl.ds(to_column, columns)],
                )
            )
        for copy in run_copies(copies, sems):
            copy.wait()
        keep = pltpu.make_async_copy(weights, keep_ref, sems.at[steps + 2])
        keep.start()

        def step(index, carry):
            start = pl.multiple_of(index * tile, tile)
            gate = jnp.dot(both[...], weights[:, pl.ds(start, tile)], preferred_element_type=F32)
            up = jnp.dot(
                both[...],
                weights[:, pl.ds(pl.multiple_of(half + start, tile), tile)],
                preferred_element_type=F32,
            )
            act, slope = gelu_parts(gate)
            act_ref[:, pl.ds(start, tile)] = act.astype(BF16)
            slope_ref[:, pl.ds(start, tile)] = (up * slope).astype(BF16)
            hidden_ref[:, pl.ds(start, tile)] = (act * up).astype(BF16)
            return carry

        lax.fori_loop(0, half // tile, step, 0)
        keep.wait()

    shape = jax.ShapeDtypeStruct((2 * rows, half), BF16)
    return pl.pallas_call(
        kernel,
        in_specs=[ANY] * (2 + count),
        out_specs=[VMEM, VMEM, VMEM, ANY],
        out_shape=[shape, shape, shape, jax.ShapeDtypeStruct((width, inner), BF16)],
        scratch_shapes=[
            pltpu.VMEM((2 * rows, width), BF16),
            pltpu.VMEM((width, inner), BF16),
            pltpu.SemaphoreType.DMA((steps + 3,)),
        ],
        cost_estimate=pl.CostEstimate(
            flops=4 * rows * width * inner,
            bytes_accessed=4 * width * inner + 6 * rows * inner,
            transcendentals=rows * inner,
        ),
    )(own, other, *pieces)


def col_tiles(width):
    return [(start, min(512, width - start)) for start in range(0, width, 512)]


def down_call(hidden, width, padded, pieces, moves):
    double, half = hidden.shape
    rows = double // 2
    count, steps = len(pieces), len(moves)

    def kernel(hidden_ref, *rest):
        piece_refs = rest[:count]
        own_ref, other_ref, keep_ref, weights, sems = rest[count:]
        rank, chip = axis_ranks()
        copies = []
        for piece, row, size, columns, place in moves:
            to_row, to_column = place(rank, chip)
            copies.append(
                (
                    part_of(piece_refs[piece], row, size, columns),
                    weights.at[pl.ds(to_row, size), pl.ds(to_column, columns)],
                )
            )
        for copy in run_copies(copies, sems):
            copy.wait()
        keep = pltpu.make_async_copy(weights, keep_ref, sems.at[steps])
        keep.start()
        for start, size in col_tiles(width):
            columns = slice(start, start + size)
            own_ref[:, columns] = jnp.dot(
                hidden_ref[:rows], weights[:, columns], preferred_element_type=F32
            )
            other_ref[:, columns] = jnp.dot(
                hidden_ref[rows:], weights[:, columns], preferred_element_type=F32
            ).astype(BF16)
        keep.wait()

    return pl.pallas_call(
        kernel,
        in_specs=[VMEM] + [ANY] * count,
        out_specs=[VMEM, VMEM, ANY],
        out_shape=[
            jax.ShapeDtypeStruct((rows, width), F32),
            jax.ShapeDtypeStruct((rows, width), BF16),
            jax.ShapeDtypeStruct((half, padded), BF16),
        ],
        scratch_shapes=[pltpu.VMEM((half, padded), BF16), pltpu.SemaphoreType.DMA((steps + 1,))],
        cost_estimate=pl.CostEstimate(
            flops=4 * rows * width * half, bytes_accessed=4 * width * half, transcendentals=0
        ),
    )(hidden, *pieces)


def finish_call(pieces, gate_up_moves, down_moves, block, inner, down_rows, width, padded):
    count = len(pieces)
    steps = len(gate_up_moves) + len(down_moves)

    def kernel(*refs):
        piece_refs = refs[:count]
        gate_ref, up_ref, down_ref, columns_of, rows_of, sems = refs[count:]
        chip, core = axis_ranks()[1], lax.axis_index("rep") % 2
        shards = lax.axis_size("shard")
        copies = []
        for piece, row, size, columns, place in gate_up_moves:
            to_core, to_row, to_column = place(core, chip)
            copies.append(
                (
                    part_of(piece_refs[piece], row, size, columns),
                    columns_of.at[to_core, pl.ds(to_row, size), pl.ds(to_column, columns)],
                )
            )
        for piece, row, size, columns, place in down_moves:
            to_row, to_column = place(core, chip)
            copies.append(
                (
                    part_of(piece_refs[piece], row, size, columns),
                    rows_of.at[pl.ds(to_row, size), pl.ds(to_column, columns)],
                )
            )
        for copy in run_copies(copies, sems):
            copy.wait()
        half = inner // shards // 2
        for index, ref in enumerate((gate_ref, up_ref)):
            for shard in range(shards):
                start = index * (inner // 2) + shard * half
                both = [columns_of[at, :, start : start + half] for at in range(2)]
                ref[:, 2 * half * shard : 2 * half * (shard + 1)] = jnp.concatenate(
                    both, 1
                ).astype(F32)
        down_ref[...] = rows_of[:, :width].astype(F32)

    return pl.pallas_call(
        kernel,
        in_specs=[ANY] * count,
        out_specs=[VMEM] * 3,
        out_shape=[
            jax.ShapeDtypeStruct((block, inner), F32),
            jax.ShapeDtypeStruct((block, inner), F32),
            jax.ShapeDtypeStruct((down_rows, width), F32),
        ],
        scratch_shapes=[
            pltpu.VMEM((2, block, inner), BF16),
            pltpu.VMEM((down_rows, padded), BF16),
            pltpu.SemaphoreType.DMA((steps,)),
        ],
    )(*pieces)


def attn_finish_call(pieces, moves, block, proj):
    count = len(pieces)

    def kernel(*refs):
        piece_refs = refs[:count]
        out_refs, whole, sems = refs[count : count + 4], refs[count + 4], refs[count + 5]
        rep = lax.axis_index("rep")
        copies = []
        for piece, index, place in moves:
            for start, size, matrix, row in place(rep):
                copies.append(
                    (
                        piece_refs[piece].at[index, pl.ds(start, size)],
                        whole.at[matrix, pl.ds(row, size)],
                    )
                )
        for copy in run_copies(copies, sems):
            copy.wait()
        for index, ref in enumerate(out_refs):
            ref[...] = whole[index].astype(F32)

    return pl.pallas_call(
        kernel,
        in_specs=[ANY] * count,
        out_specs=[VMEM] * 4,
        out_shape=[jax.ShapeDtypeStruct((block, proj), F32)] * 4,
        scratch_shapes=[
            pltpu.VMEM((4, block, proj), BF16),
            pltpu.SemaphoreType.DMA((2 * len(moves),)),
        ],
    )(*pieces)


def hidden_grad_call(own, other, down, slope, act):
    rows, width = own.shape
    half = down.shape[0]
    tile = 256

    def kernel(own_ref, other_ref, down_ref, slope_ref, act_ref, out_ref, both, sems):
        for copy in run_copies(
            [(own_ref, both.at[:rows]), (other_ref, both.at[rows:])], sems
        ):
            copy.wait()

        def step(index, carry):
            start = pl.multiple_of(index * tile, tile)
            upstream = lax.dot_general(
                both[...],
                down_ref[pl.ds(start, tile), :width],
                (((1,), (1,)), ((), ())),
                preferred_element_type=F32,
            )
            gate = upstream * slope_ref[:, pl.ds(start, tile)].astype(F32)
            up = upstream * act_ref[:, pl.ds(start, tile)].astype(F32)
            out_ref[:, pl.ds(start, tile)] = gate.astype(BF16)
            out_ref[:, pl.ds(pl.multiple_of(half + start, tile), tile)] = up.astype(BF16)
            return carry

        lax.fori_loop(0, half // tile, step, 0)

    return pl.pallas_call(
        kernel,
        in_specs=[ANY, ANY, VMEM, VMEM, VMEM],
        out_specs=VMEM,
        out_shape=jax.ShapeDtypeStruct((2 * rows, 2 * half), BF16),
        scratch_shapes=[pltpu.VMEM((2 * rows, width), BF16), pltpu.SemaphoreType.DMA((2,))],
        cost_estimate=pl.CostEstimate(
            flops=4 * rows * width * half,
            bytes_accessed=2 * width * half + 16 * rows * half,
            transcendentals=0,
        ),
    )(own, other, down, slope, act)


def weight_grad_call(left, right, outputs):
    left_own, left_other = left
    right_own, right_other = right
    rows = left_own.shape[0]
    depth, width = left_own.shape[1], right_own.shape[1]
    count = len(outputs)
    copies_out = sum(len(moves) for _, moves in outputs)
    split = left_other is not None
    total = 2 * rows if split else rows
    right_split = right_other is not None
    inputs = [left_own] + ([left_other] if split else []) + [right_own]
    inputs += [right_other] if right_split else []

    def kernel(*refs):
        in_refs = list(refs[: len(inputs)])
        out_refs = refs[len(inputs) : len(inputs) + count]
        lefts, rights, result, sems = refs[len(inputs) + count :]
        copies = []
        for target, parted in ((lefts, split), (rights, right_split)):
            first = in_refs.pop(0)
            size = first.shape[0]
            copies.append((first, target.at[:size]))
            if parted:
                copies.append((in_refs.pop(0), target.at[size:]))
        for copy in run_copies(copies, sems):
            copy.wait()
        tile = 512 if width % 512 == 0 else width
        for begin in range(0, depth, 256):
            size = min(256, depth - begin)
            turned = lefts[:, begin : begin + size].T
            if tile == width:
                for start, span in col_tiles(width):
                    result[begin : begin + size, start : start + span] = jnp.dot(
                        turned, rights[:, start : start + span], preferred_element_type=F32
                    ).astype(BF16)
            else:

                def step(index, carry):
                    start = pl.multiple_of(index * tile, tile)
                    result[begin : begin + size, pl.ds(start, tile)] = jnp.dot(
                        turned, rights[:, pl.ds(start, tile)], preferred_element_type=F32
                    ).astype(BF16)
                    return carry

                lax.fori_loop(0, width // tile, step, 0)
        rank, chip = axis_ranks()
        moves_out = []
        for ref, (shape, moves) in zip(out_refs, outputs):
            for index, place in moves:
                row, column = place(rank, chip)
                moves_out.append(
                    (result.at[pl.ds(row, shape[1]), pl.ds(column, shape[2])], ref.at[index])
                )
        for copy in run_copies(moves_out, sems):
            copy.wait()

    return pl.pallas_call(
        kernel,
        in_specs=[ANY] * len(inputs),
        out_specs=[ANY] * count,
        out_shape=[jax.ShapeDtypeStruct(shape, BF16) for shape, _ in outputs],
        scratch_shapes=[
            pltpu.VMEM((total, depth), BF16),
            pltpu.VMEM((total, width), BF16),
            pltpu.VMEM((depth, width), BF16),
            pltpu.SemaphoreType.DMA((max(4, copies_out),)),
        ],
        cost_estimate=pl.CostEstimate(
            flops=2 * total * depth * width,
            bytes_accessed=2 * (depth * width + total * (depth + width)),
            transcendentals=0,
        ),
    )(*inputs)


def on_device(
    tokens,
    cotangent,
    gate_cotangent,
    slot_of,
    seq_lengths,
    buckets,
    gain_attn,
    w_query,
    w_key,
    w_value,
    w_out,
    rel_bias,
    gain_ffn,
    w_gate,
    w_up,
    w_down,
    gain_delete,
    w_delete,
):
    shards = lax.axis_size("shard")
    reps = lax.axis_size("rep")
    chips = reps // 2
    rank = lax.axis_index("shard")
    rep_rank = lax.axis_index("rep")
    core = rep_rank % 2
    chip = rep_rank // 2
    micro_count, local_rows, width = tokens.shape
    group = local_rows * shards
    rows = micro_count * local_rows
    heads = rel_bias.shape[1]
    bucket_rows = rel_bias.shape[0]
    bucket_count = bucket_rows * shards
    proj = w_query.shape[1]
    head_size = proj // heads
    block = gain_attn.shape[0]
    inner = w_gate.shape[1]
    half_inner = inner // 2
    col_piece = inner // chips
    down_block = w_down.shape[0]
    down_half = down_block // 2
    down_piece = down_half // chips
    down_parts_count = -(-width // col_piece)
    padded = -(-width // 128) * 128
    aligned = reps == 8 and block % 16 == 0 and down_piece % 16 == 0 and col_piece % 128 == 0

    def swap(value, mask):
        return lax.ppermute(value, "rep", [(i, i ^ mask) for i in range(reps)])

    def shift(value, by=1):
        return lax.ppermute(value, "shard", [(i, (i + by) % shards) for i in range(shards)])

    def tie(value, moved):
        return lax.optimization_barrier((value, moved))

    def cut(count):
        half = count // 2
        return half // 16 * 16 if half >= 16 else half

    def gather_near(piece):
        if chips == 1:
            return []
        return [swap(piece, 2)] + ([swap(piece, 4)] if chips >= 4 else [])

    def gather_rest(near):
        if chips < 4:
            return []
        middle = cut(near[0].shape[0])
        return [swap(near[1][:middle], 2), swap(near[0][middle:], 4)]

    def gather_list(piece, near, rest):
        middle = cut(piece.shape[0])
        found = [(0, 0, piece)] + [(1 + i, 0, part) for i, part in enumerate(near)]
        found += [(3, i * middle, part) for i, part in enumerate(rest)]
        bit = 4
        while bit < chips:
            found += [
                (mask ^ bit, start, swap(part, 2 * bit)) for mask, start, part in found
            ]
            bit *= 2
        return found

    def plane_gather(piece):
        near = gather_near(piece)
        return gather_list(piece, near, gather_rest(near))

    def add(*values):
        return sum(value.astype(F32) for value in values).astype(BF16)

    def plane_reduce(parts, axis):
        state = reduce_begin(parts, axis)
        return reduce_end(reduce_middle(state, axis))

    def reduce_begin(parts, axis):
        def level(base, bit):
            if bit < 4:
                return lambda name: parts[base][name]
            lower, upper = level(base, bit // 2), level(base ^ bit, bit // 2)
            return lambda name: add(lower(name), swap(upper(name), 2 * bit))

        get = level(0, chips // 2)
        if chips < 4:
            return [get("own")] + ([swap(get("near"), 2)] if chips == 2 else [])
        return [get("own"), get("far"), get("near"), swap(get("top"), 2), swap(get("low"), 4)]

    def reduce_middle(state, axis):
        if chips < 4:
            return state
        own, far, near, top, low = state
        middle = top.shape[axis]

        def pair(value):
            return (
                lax.slice_in_dim(value, 0, middle, axis=axis),
                lax.slice_in_dim(value, middle, value.shape[axis], axis=axis),
            )

        (far_top, far_low), (near_top, near_low) = pair(far), pair(near)
        far = jnp.concatenate([add(far_top, top), far_low], axis)
        near = jnp.concatenate([near_top, add(near_low, low)], axis)
        return [own, swap(far, 4), swap(near, 2)]

    def reduce_end(state):
        return add(*state) if len(state) > 1 else state[0]

    names = {"own": 0, "near": 1, "far": 2, "top": 3, "low": 3}
    bases = [base for base in range(chips) if base & 3 == 0]
    used = ["own", "near", "far", "top", "low"] if chips >= 4 else ["own", "near"][:chips]

    def source(step):
        return (rank - step) % shards

    order = (rank - jnp.arange(shards, dtype=jnp.int32)) % shards
    per_matrix = reps // 4
    attn_rows = block // per_matrix
    if aligned:
        attn_rows = -(-attn_rows // 16) * 16
    last_row = block - attn_rows

    def part_row(part):
        return jnp.minimum(part * attn_rows, last_row)

    attn_own = jnp.stack([w_query, w_key, w_value, w_out.reshape(block, proj)])
    attn_piece = lax.dynamic_slice(
        attn_own,
        (rep_rank // per_matrix, part_row(rep_rank % per_matrix), 0),
        (1, attn_rows, proj),
    )[0]
    vector_pack = jnp.concatenate(
        [gain_attn, gain_ffn, gain_delete, w_delete, rel_bias.reshape(-1)]
    )
    pack_rows = -(-vector_pack.shape[0] // (16 * proj)) * 16
    vector_pack = jnp.pad(vector_pack, (0, pack_rows * proj - vector_pack.shape[0]))
    vector_pack = vector_pack.reshape(pack_rows, proj)
    attn_sent = jnp.concatenate([attn_piece, vector_pack])
    attn_arrived = [shift(attn_sent, step) for step in range(1, shards)]
    vectors = jnp.stack([vector_pack] + [part[attn_rows:] for part in attn_arrived])
    vectors = jnp.take(vectors, order, axis=0).reshape(shards, pack_rows * proj)
    attn_gain = vectors[:, :block].reshape(width).astype(F32)
    ffn_gain = vectors[:, block : 2 * block].reshape(width).astype(F32)
    delete_gain = vectors[:, 2 * block : 3 * block].reshape(width).astype(F32)
    delete_vec = vectors[:, 3 * block : 4 * block].reshape(width).astype(F32)
    bias_table = vectors[:, 4 * block : 4 * block + bucket_rows * heads]
    bias_table = bias_table.reshape(bucket_count, heads)
    stacked = jnp.stack([part[:attn_rows] for part in attn_arrived])

    def pack(gate_up_part, down_part):
        wide = jnp.pad(down_part, ((0, 0), (0, down_parts_count * col_piece - width)))
        cuts = [wide[:, i * col_piece : (i + 1) * col_piece] for i in range(down_parts_count)]
        return jnp.concatenate([gate_up_part] + cuts)

    def overlaps(start, count):
        bounds = [(None, 0, block)] + [
            (i, block + i * down_piece, block + (i + 1) * down_piece)
            for i in range(down_parts_count)
        ]
        found = []
        for part, low, high in bounds:
            first, last = max(low, start), min(high, start + count)
            if first < last:
                found.append((part, first - start, first - low, last - first))
        return found

    def part_columns(part):
        return min(col_piece, padded - part * col_piece)

    gate_up_own = pick_columns(w_gate, w_up)
    down_own = lax.dynamic_slice_in_dim(w_down, core * down_half, down_half, 0)
    packed_own = pack(
        lax.dynamic_slice_in_dim(gate_up_own, chip * col_piece, col_piece, 1),
        lax.dynamic_slice_in_dim(down_own, chip * down_piece, down_piece, 0),
    )
    packed_own, stacked = tie(packed_own, stacked)
    ring = [shift(packed_own)]
    for step in range(2, shards):
        ring.append(shift(ring[-1]))
    attn_plane = [stacked] + [swap(stacked, 2 * mask) for mask in range(1, chips)]
    attn_plane = jnp.stack(attn_plane)
    attn_other = swap(attn_plane, 1)

    def attn_place(mask, flip, step):
        def place(at, rep):
            owner = rep ^ (2 * mask + flip)
            row = (at - step) % shards * block + part_row(owner % per_matrix)
            return owner // per_matrix, pl.multiple_of(row, 16) if aligned else row

        return place

    shared = per_matrix * attn_rows - block

    def split_place(place, flip):
        def places_of(*at):
            matrix, row = place(*at)
            part = (at[-1] ^ flip) % per_matrix
            first = row - last_row * part
            moves = [
                (
                    pl.multiple_of(shared * part, 16),
                    attn_rows - shared,
                    matrix,
                    pl.multiple_of(first + attn_rows * part, 16),
                )
            ]
            if shared and flip == 0:
                moves.append(
                    (
                        pl.multiple_of(last_row * (1 - part), 16),
                        shared,
                        matrix,
                        pl.multiple_of(first + last_row, 16),
                    )
                )
            return moves

        return places_of

    attn_pieces = [w_query, w_key, w_value, attn_own[3]]
    attn_places = [
        [(None, lambda at, rep, matrix=matrix: [(0, block, matrix, pl.multiple_of(at * block, 16))])]
        for matrix in range(4)
    ]
    for flip, found in enumerate((attn_plane, attn_other)):
        attn_pieces.append(found)
        attn_places.append(
            [
                ((mask, step - 1), attn_place(mask, flip, step), flip)
                for mask in range(chips)
                for step in range(1, shards)
            ]
        )
    if not aligned:
        whole = jnp.zeros((4, width, proj), BF16)
        whole = lax.dynamic_update_slice(whole, attn_own, (0, rank * block, 0))
        for piece, place in zip(attn_pieces[4:], attn_places[4:]):
            for index, where, _ in place:
                matrix, row = where(rank, rep_rank)
                whole = lax.dynamic_update_slice(whole, piece[index][None], (matrix, row, 0))
        attn_pieces = [whole[matrix] for matrix in range(4)]
        attn_places = [
            [(None, lambda at, rep, matrix=matrix: [(0, width, matrix, 0)])] for matrix in range(4)
        ]
    else:
        attn_places[4:] = [
            [(index, split_place(where, flip)) for index, where, flip in place]
            for place in attn_places[4:]
        ]

    slots = slot_of[:, 0]
    own_slots = lax.dynamic_slice_in_dim(slots, rank * local_rows, local_rows, 1)
    key_slots = jnp.take(slots.reshape(micro_count, shards, local_rows), order, axis=1)
    key_slots = key_slots.reshape(micro_count, group)
    onehot = (buckets[:, None] == jnp.arange(bucket_count, dtype=jnp.int32)[None, :]).astype(F32)
    onehot = jnp.pad(onehot, ((0, 1), (0, 0)))
    bias_rows = jnp.dot(onehot, bias_table.astype(F32), precision=HIGHEST).T
    bias = bias_of_queries(bias_rows, own_slots.reshape(rows), group)
    first_len = seq_lengths[:, 0, 0]

    hidden_in = tokens.reshape(rows, width).astype(F32)
    scale_one = rms_scale(hidden_in)
    normed_one, queries, own_pairs, attn_full = project_call(
        tokens.reshape(rows, width), attn_gain[None], attn_pieces, attn_places, block, proj
    )
    query_full, key_full, value_full = attn_full[0], attn_full[1], attn_full[2]
    out_full = attn_full[3].reshape(proj, width)

    nears, rests = [], []
    ring[0], attn_plane = tie(ring[0], attn_plane)
    for step in range(1, shards):
        nears.append(gather_near(ring[step - 1]))
        rests.append(gather_rest(nears[-1]))
        if step < shards - 1:
            ring[step], rests = tie(ring[step], rests)
    own_pairs, (ring, nears[0]) = tie(own_pairs, (ring, nears[0]))
    pairs = [own_pairs]
    for step in range(1, shards):
        pairs.append(shift(pairs[-1]))
    pairs, (nears, rests[:-1]) = tie(pairs, (nears, rests[:-1]))
    contexts, probs, packed = [], [], []
    for micro in range(micro_count):
        context, prob, pair = attention_call(
            micro,
            first_len[micro : micro + 1],
            queries,
            pairs,
            own_slots.reshape(rows, 1),
            key_slots[micro : micro + 1],
            bias,
        )
        contexts.append(context)
        probs.append(prob)
        packed.append(pair)
    context = jnp.concatenate(contexts)
    hidden_mid = hidden_in + dot(context, out_full)

    scale_two = rms_scale(hidden_mid)
    normed_two = (hidden_mid * scale_two * ffn_gain).astype(BF16)
    normed_two_other = swap(normed_two, 1)
    pieces = [gate_up_own, jnp.pad(down_own, ((0, 0), (0, padded - width)))]
    gate_up_moves = [(0, 0, block, inner, lambda at, chip_at: (pl.multiple_of(at * block, 16), 0))]
    down_moves = [
        (1, 0, down_half, padded, lambda at, chip_at: (pl.multiple_of(at * down_half, 16), 0))
    ]

    def gate_up_place(step, mask, row):
        return lambda at, chip_at: (
            pl.multiple_of((at - step) % shards * block + row, 16),
            pl.multiple_of((chip_at ^ mask) * col_piece, 128),
        )

    def down_place(step, mask, row, part):
        return lambda at, chip_at: (
            pl.multiple_of((at - step) % shards * down_half + (chip_at ^ mask) * down_piece + row, 16),
            part * col_piece,
        )

    for step in range(1, shards):
        for mask, start, array in gather_list(ring[step - 1], nears[step - 1], rests[step - 1]):
            for part, here, there, size in overlaps(start, array.shape[0]):
                if part is None:
                    gate_up_moves.append(
                        (len(pieces), here, size, col_piece, gate_up_place(step, mask, there))
                    )
                else:
                    down_moves.append(
                        (
                            len(pieces),
                            here,
                            size,
                            part_columns(part),
                            down_place(step, mask, there, part),
                        )
                    )
            pieces.append(array)
    if not aligned:

        def put_together(moves, shape):
            whole = jnp.zeros(shape, BF16)
            for piece, row, size, columns, place in moves:
                value = pieces[piece][row : row + size, :columns]
                whole = lax.dynamic_update_slice(whole, value, place(rank, chip))
            return whole

        pieces = [
            put_together(gate_up_moves, (width, inner)),
            put_together(down_moves, (half_inner, padded)),
        ]
        gate_up_moves = [(0, 0, width, inner, lambda at, chip_at: (0, 0))]
        down_moves = [(1, 0, half_inner, padded, lambda at, chip_at: (0, 0))]
    gate_slope_act, gate_act, inner_act, gate_up = gate_up_call(
        normed_two, normed_two_other, inner, pieces, gate_up_moves
    )
    down_part, down_given, down = down_call(inner_act, width, padded, pieces, down_moves)
    hidden_out = hidden_mid + down_part + swap(down_given, 1).astype(F32)
    scale_three = rms_scale(hidden_out)
    delete_norm = hidden_out * scale_three * delete_gain
    sigmoid_val = jax.nn.sigmoid(jnp.sum(delete_norm * delete_vec, axis=-1))
    deleted = -30.0 * sigmoid_val

    gate_upstream = gate_cotangent.reshape(rows).astype(F32)
    gate_slope = gate_upstream * -30.0 * sigmoid_val * (1.0 - sigmoid_val)
    grad_delete_vec = jnp.sum(gate_slope[:, None] * delete_norm, axis=0)
    delete_up = gate_slope[:, None] * delete_vec
    grad_delete_gain = jnp.sum(delete_up * hidden_out * scale_three, axis=0)
    grad_out = cotangent.reshape(rows, width).astype(F32) + rms_back(
        hidden_out, scale_three, delete_gain, delete_up
    )
    down_up = grad_out.astype(BF16)
    down_up_other = swap(down_up, 1)

    def reduce_plan(piece_rows, piece_columns, place, groups):
        middle = cut(piece_rows)
        spans = {"own": (0, piece_rows), "near": (0, piece_rows), "far": (0, piece_rows)}
        spans["top"], spans["low"] = (0, middle), (middle, piece_rows - middle)
        plan = []
        for steps in groups:
            for base in bases:
                for name in used:
                    start, size = spans[name]
                    moves = [
                        (index, place(step % shards, base ^ names[name], start))
                        for index, step in enumerate(steps)
                    ]
                    plan.append(((len(moves), size, piece_columns), moves))
        return plan

    def reduce_run(plan, left, right):
        if aligned:
            buffers = weight_grad_call(left, right, plan)
        else:
            shape = (left[0].shape[1], right[0].shape[1])
            whole = weight_grad_call(
                left, right, [((1,) + shape, [(0, lambda at, chip_at: (0, 0))])]
            )[0][0]
            buffers = []
            for (_, size, columns), moves in plan:
                buffers.append(
                    jnp.stack(
                        [
                            lax.dynamic_slice(whole, place(rank, chip), (size, columns))
                            for _, place in moves
                        ]
                    )
                )
        return buffers

    def group_parts(buffers, group_index, group_count):
        each = len(buffers) // group_count
        chosen = buffers[group_index * each : (group_index + 1) * each]
        return {
            base: dict(zip(used, chosen[i * len(used) : (i + 1) * len(used)]))
            for i, base in enumerate(bases)
        }

    all_steps = [range(1, shards + 1)]
    two_steps = [range(1, shards // 2 + 1), range(shards // 2 + 1, shards + 1)]

    def send_blocks(state, steps):
        sent = []
        for index, step in enumerate(steps):
            total = reduce_end([value[index] for value in state])
            sent.append(shift(total, -step) if step < shards else total)
        return sent

    def down_grad_place(step, mask, start):
        return tile_hint(
            lambda at, chip_at: (
                (at - step) % shards * down_half + (chip_at ^ mask) * down_piece + start,
                0,
            ),
            16,
            128,
        ) if aligned else lambda at, chip_at: (
            (at - step) % shards * down_half + (chip_at ^ mask) * down_piece + start,
            0,
        )

    def gate_up_grad_place(step, mask, start):
        plain = lambda at, chip_at: (
            (at - step) % shards * block + start,
            (chip_at ^ mask) * col_piece,
        )
        return tile_hint(plain, 16, 128) if aligned else plain

    down_buffers = reduce_run(
        reduce_plan(down_piece, width, down_grad_place, all_steps),
        (inner_act, None),
        (down_up, down_up_other),
    )
    down_state = reduce_begin(group_parts(down_buffers, 0, 1), 1)
    both_grad = hidden_grad_call(down_up, down_up_other, down, gate_slope_act, gate_act)
    both_grad, down_state = tie(both_grad, down_state)
    gate_up_buffers = reduce_run(
        reduce_plan(block, col_piece, gate_up_grad_place, two_steps),
        (normed_two, normed_two_other),
        (both_grad, None),
    )
    down_state = reduce_middle(down_state, 1)
    partial = jnp.einsum("tf,df->td", both_grad, gate_up, preferred_element_type=F32)
    gate_up_state = reduce_begin(group_parts(gate_up_buffers, 0, 2), 1)
    partial_given = swap(partial[rows:].astype(BF16), 1)
    partial_given, down_state = tie(partial_given, down_state)
    normed_two_grad = partial[:rows] + partial_given.astype(F32)
    grad_ffn_gain = jnp.sum(normed_two_grad * hidden_mid * scale_two, axis=0)
    grad_mid = grad_out + rms_back(hidden_mid, scale_two, ffn_gain, normed_two_grad)
    out_grad = grad_mid.astype(BF16)
    grad_w_out = jnp.einsum("th,td->hd", context, out_grad, preferred_element_type=F32)
    context_grad = jnp.einsum("td,hd->th", out_grad, out_full, preferred_element_type=F32)
    context_grad = context_grad.astype(BF16)
    down_sent = send_blocks(down_state, all_steps[0])
    context_grad, gate_up_state = tie(context_grad, gate_up_state)
    gate_up_state = reduce_middle(gate_up_state, 1)
    score_grads, query_grads, pair_parts = [], [], []
    for micro in range(micro_count):
        score_grad, query_grad, *parts = attention_back_call(
            micro,
            queries,
            context_grad,
            probs[micro],
            packed[micro],
            key_slots[micro].reshape(group, 1),
            shards,
        )
        score_grads.append(score_grad)
        query_grads.append(query_grad)
        pair_parts.append(parts)
    pair_parts = [jnp.concatenate(parts) for parts in zip(*pair_parts)]
    pair_parts, down_sent = tie(pair_parts, down_sent)
    pair_sent = [shift(pair_parts[step], -step) for step in range(1, shards)]
    pair_sent, gate_up_state = tie(pair_sent, gate_up_state)
    gate_up_later = reduce_begin(group_parts(gate_up_buffers, 1, 2), 1)
    gate_up_sent = send_blocks(gate_up_state, two_steps[0])
    pair_sum = add(pair_parts[0], *pair_sent)
    down_sum = add(*down_sent)
    query_grad = jnp.concatenate(query_grads)
    grad_bias_rows = bias_fold(score_grads, own_slots.reshape(rows))
    grad_bias = jnp.einsum("ob,ho->bh", onehot, grad_bias_rows, precision=HIGHEST)

    normed_one_grad = (
        jnp.einsum("th,dh->td", query_grad, query_full, preferred_element_type=F32)
        + jnp.einsum("th,dh->td", pair_sum[:, :proj], key_full, preferred_element_type=F32)
        + jnp.einsum("th,dh->td", pair_sum[:, proj:], value_full, preferred_element_type=F32)
    )
    grad_attn_gain = jnp.sum(normed_one_grad * hidden_in * scale_one, axis=0)
    grad_in = grad_mid + rms_back(hidden_in, scale_one, attn_gain, normed_one_grad)

    small = jnp.concatenate(
        [
            grad_attn_gain.reshape(shards, block),
            grad_ffn_gain.reshape(shards, block),
            grad_delete_gain.reshape(shards, block),
            grad_delete_vec.reshape(shards, block),
            grad_bias.reshape(shards, bucket_rows * heads),
        ],
        axis=1,
    ).astype(BF16)
    small = jnp.pad(small, ((0, 0), (0, pack_rows * proj - small.shape[1])))
    small = small.reshape(shards, pack_rows, proj)

    out_grads = grad_w_out.astype(BF16).reshape(width, proj)
    attn_plan = [
        (
            (chips, shards, attn_rows + pack_rows, proj),
            [
                ((mask, step), attn_place(mask, flip, step), step)
                for mask in range(chips)
                for step in range(shards)
            ],
        )
        for flip in range(2)
    ]
    if aligned:
        kept, given = project_grad_call(
            normed_one, query_grad, pair_sum, out_grads, small, attn_plan
        )
    else:
        whole_plan = [
            (
                (4, width, proj),
                [((matrix,), lambda at, rep, matrix=matrix: (matrix, 0), None) for matrix in range(4)],
            )
        ]
        whole = project_grad_call(
            normed_one, query_grad, pair_sum, out_grads, small, whole_plan
        )[0]
        kept, given = [
            jnp.stack(
                [
                    jnp.concatenate(
                        [
                            lax.dynamic_slice(
                                whole, where(rank, rep_rank) + (0,), (1, attn_rows, proj)
                            )[0],
                            lax.dynamic_index_in_dim(small, source(step), 0, keepdims=False),
                        ]
                    )
                    for _, where, step in items
                ]
            ).reshape(shape)
            for shape, items in attn_plan
        ]
    given = swap(given, 1)
    given, gate_up_later = tie(given, gate_up_later)
    gate_up_later = reduce_middle(gate_up_later, 1)
    attn_own_sum = add(kept[0], given[0])
    attn_send = [add(kept[mask], given[mask]) for mask in range(1, chips)]
    attn_send, (gate_up_later, gate_up_sent) = tie(attn_send, (gate_up_later, gate_up_sent))
    attn_found = [swap(part, 2 * mask + 2) for mask, part in enumerate(attn_send)]
    gate_up_sent = gate_up_sent + send_blocks(gate_up_later, two_steps[1])
    attn_sum = add(attn_own_sum, *attn_found)
    attn_sum = add(attn_sum[0], *[shift(attn_sum[step], -step) for step in range(1, shards)])
    gate_up_sum = add(*gate_up_sent)
    total = attn_sum[attn_rows:].astype(F32).reshape(-1)
    attn_sum = attn_sum[:attn_rows]

    packed_sum = pack(gate_up_sum, down_sum)
    found = plane_gather(packed_sum)
    pieces, gate_up_moves, down_moves = [], [], []

    def gate_up_to(flip, mask, row):
        return lambda core_at, chip_at: (
            core_at ^ flip,
            row,
            pl.multiple_of((chip_at ^ mask) * col_piece, 128),
        )

    def down_to(flip, mask, row, part):
        return lambda core_at, chip_at: (
            pl.multiple_of((core_at ^ flip) * down_half + (chip_at ^ mask) * down_piece + row, 16),
            part * col_piece,
        )

    for flip in range(2):
        for mask, start, array in found:
            array = swap(array, 1) if flip else array
            for part, here, there, size in overlaps(start, array.shape[0]):
                if part is None:
                    gate_up_moves.append(
                        (len(pieces), here, size, col_piece, gate_up_to(flip, mask, there))
                    )
                else:
                    down_moves.append(
                        (
                            len(pieces),
                            here,
                            size,
                            part_columns(part),
                            down_to(flip, mask, there, part),
                        )
                    )
            pieces.append(array)
    if aligned:
        grad_gate, grad_up, grad_down_out = finish_call(
            pieces, gate_up_moves, down_moves, block, inner, down_block, width, padded
        )
    else:
        halves = jnp.zeros((2, block, inner), BF16)
        for piece, row, size, columns, place in gate_up_moves:
            value = pieces[piece][None, row : row + size, :columns]
            halves = lax.dynamic_update_slice(halves, value, place(core, chip))
        whole = jnp.zeros((down_block, padded), BF16)
        for piece, row, size, columns, place in down_moves:
            value = pieces[piece][row : row + size, :columns]
            whole = lax.dynamic_update_slice(whole, value, place(core, chip))
        grad_gate, grad_up = spread_columns(halves[0], halves[1])
        grad_down_out = whole[:, :width].astype(F32)

    attn_half = jnp.stack([attn_sum] + [swap(attn_sum, 2 * mask) for mask in range(1, chips)])
    attn_found = [attn_half, swap(attn_half, 1)]

    def attn_to(mask, flip):
        def place(rep):
            owner = rep ^ (2 * mask + flip)
            row = part_row(owner % per_matrix)
            return owner // per_matrix, pl.multiple_of(row, 16) if aligned else row

        return place

    attn_moves = [(flip, mask, attn_to(mask, flip)) for flip in range(2) for mask in range(chips)]
    if aligned:
        attn_moves = [
            (flip, mask, split_place(place, flip)) for flip, mask, place in attn_moves
        ]
        attn_shard = attn_finish_call(attn_found, attn_moves, block, proj)
    else:
        attn_shard = jnp.zeros((4, block, proj), BF16)
        for piece, index, place in attn_moves:
            attn_shard = lax.dynamic_update_slice(
                attn_shard, attn_found[piece][index][None], place(rep_rank) + (0,)
            )
        attn_shard = attn_shard.astype(F32)

    return (
        hidden_out.reshape(micro_count, local_rows, width),
        deleted.reshape(micro_count, local_rows),
        grad_in.astype(BF16).reshape(micro_count, local_rows, width),
        total[:block],
        attn_shard[0],
        attn_shard[1],
        attn_shard[2],
        attn_shard[3].reshape(proj // shards, width),
        total[4 * block : 4 * block + bucket_rows * heads].reshape(bucket_rows, heads),
        total[block : 2 * block],
        grad_gate,
        grad_up,
        grad_down_out,
        total[2 * block : 3 * block],
        total[3 * block : 4 * block],
    )


def tile_hint(place, row_unit, column_unit):
    def hinted(at, chip_at):
        row, column = place(at, chip_at)
        return pl.multiple_of(row, row_unit), pl.multiple_of(column, column_unit)

    return hinted


def solution(mesh):
    rows = P(None, ("rep", "shard"), None)
    flat = P(None, ("rep", "shard"))
    by_rep = P(None, "rep", None)
    vector = P("shard")
    matrix = P("shard", None)
    in_specs = (
        (rows, rows, flat, by_rep, by_rep, P(), vector)
        + (matrix,) * 5
        + (vector,)
        + (matrix,) * 3
        + (vector, vector)
    )
    out_specs = (
        (rows, flat, rows, vector) + (matrix,) * 5 + (vector,) + (matrix,) * 3 + (vector, vector)
    )
    return jax.shard_map(
        on_device, mesh=mesh, in_specs=in_specs, out_specs=out_specs, check_vma=False
    )
```

time: 782 us -> 677 us (0.87)
  local copies, waits for them, and re-layouts: 167 us -> 105 us
  Pallas kernels: 103 us -> 154 us
  other arithmetic: 89.2 us -> 49 us
  starting transfers between devices: 93.7 us -> 65.1 us
  matrix products: 52.1 us -> 26.5 us
    pallas_call x2 -> x11, Pallas kernels: 14.2 us -> 64.1 us  [the longest x3 16.2 us: attention_call(): pl.pallas_call(kernel, grid=(1,), in_specs=[pl.BlockSpec(memory_space=plt...]
    ppermute x76 -> x49, starting transfers between devices: 71.4 us -> 41.6 us  [swap(): return lax.ppermute(value, 'rep', [(i, i ^ mask) for i in range(reps)])]
    dynamic_update_slice x40 -> x0, local copies, waits for them, and re-layouts: 26.1 us -> none  [the longest x24 17.1 us: on_device(): lax.dynamic_update_slice(attn_full, part[index][None, None, None], (owner...]
    ppermute x30 -> x21, waiting for transfers between devices: 108 us -> 129 us  [shift(): lax.ppermute(value, 'shard', [(i, (i + by) % shards) for i in range(shard...]
    convert_element_type x15 -> x1, other arithmetic: 22.4 us -> 3.33 us  [on_device(): grad_in.astype(BF16).reshape(micro_count, local_rows, width)]
    ppermute x76 -> x49, waiting for transfers between devices: 155 us -> 138 us  [swap(): return lax.ppermute(value, 'rep', [(i, i ^ mask) for i in range(reps)])]
    dot_general x8 -> x0, matrix products: 16.1 us -> none  [the longest x1 2.95 us: on_device(): jnp.einsum('msj,mjc->msc', to_slots, pairs, preferred_element_type=F32)]
    sub x1 -> x0, other arithmetic: 12.8 us -> none  [on_device(): score_grad = (probabilities * (prob_grad - inner_sum)).astype(BF16)]
  transfers between devices with their start and end apart: 106 -> 70, of which waited for: 37 -> 26; matrix products, arithmetic and copies ran while one was open for 35% -> 17% of each run, Pallas kernels for 10% -> 12%
where the time goes in v3:
time: 677 us; the launch traced here: 669 us
  waiting for transfers between devices  267 us (39%)
  Pallas kernels  154 us (23%)
  local copies, waits for them, and re-layouts  105 us (16%)
  starting transfers between devices  65.1 us (10%)
  other arithmetic  49 us (7%)
  matrix products  26.5 us (4%)
    ppermute x49, waiting for transfers between devices, swap(): return lax.ppermute(value, 'rep', [(i, i ^ mask) for i in range(reps)])  138 us
    ppermute x21, waiting for transfers between devices, shift(): lax.ppermute(value, 'shard', [(i, (i + by) % shards) for i in range(shard...  129 us
    ppermute x49, starting transfers between devices, swap(): return lax.ppermute(value, 'rep', [(i, i ^ mask) for i in range(reps)])  41.6 us
    pallas_call x2, Pallas kernels, weight_grad_call(): pl.pallas_call(kernel, in_specs=[ANY] * len(inputs), out_specs=[ANY] * co...  33.2 us
    unnamed x131, local copies, waits for them, and re-layouts  28.2 us
    ppermute x21, starting transfers between devices, shift(): lax.ppermute(value, 'shard', [(i, (i + by) % shards) for i in range(shard...  23.5 us
    pallas_call x1, Pallas kernels, gate_up_call(): pl.pallas_call(kernel, in_specs=[ANY] * (2 + count), out_specs=[VMEM, VME...  20.7 us
    pallas_call x3, Pallas kernels, attention_call(): pl.pallas_call(kernel, grid=(1,), in_specs=[pl.BlockSpec(memory_space=plt...  16.2 us
  transfers between devices with their start and end apart: 70, of which 26 were waited for; matrix products, arithmetic and copies ran while one was open for 17% of the time, Pallas kernels for 12%

profile of v3, /device:TPU:0, one launch (start us, length us, event | category | flops | bytes accessed | tf_op | source)
XLA Modules:
  0.0 668.6 jit_solution(9903001351149235668)
XLA Ops:
  7.7 5.0 collective-permute-start.2
  14.2 5.3 shard_map.289.rest_0_
  20.8 5.8 collective-permute-done.1
  32.2 9.6 %collective-permute-done.3 = bf16[3,192,384]{2,1,0:T(8,128)(2,1)S(1)} collective-permute-done((bf16[3,192,384]{2,1,0:T(8,128)(2,1)S(1)}, bf16[3,192,384]{2,1,0:T(8,128)(2,1)S(1)}, u32[]{:S(2)}, u32[]{:S(2)}) %collective-permute-start.3) | collective-permute-done | bytes 442400 | tf_op jit(solution)/shard_map/ppermute | solution.py:778
  41.8 9.2 %collective-permute-done.4 = bf16[3,192,384]{2,1,0:T(8,128)(2,1)S(1)} collective-permute-done((bf16[3,192,384]{2,1,0:T(8,128)(2,1)S(1)}, bf16[3,192,384]{2,1,0:T(8,128)(2,1)S(1)}, u32[]{:S(2)}, u32[]{:S(2)}) %collective-permute-start.4) | collective-permute-done | bytes 442400 | tf_op jit(solution)/shard_map/ppermute | solution.py:778
  57.5 22.0 %collective-permute-done.11.rest_3_ = bf16[592,896]{1,0:T(8,128)(2,1)S(1)} collective-permute-done((bf16[592,896]{1,0:T(8,128)(2,1)}, bf16[592,896]{1,0:T(8,128)(2,1)S(1)}, u32[]{:S(2)}, u32[]{:S(2)}) %collective-permute-start.11) | collective-permute-done | bytes 1060896 | tf_op jit(solution)/shard_map/ppermute | solution.py:778
  85.3 11.3 %collective-permute-done.10.rest_5_ = bf16[288,896]{1,0:T(8,128)(2,1)} collective-permute-done((bf16[288,896]{1,0:T(8,128)(2,1)}, bf16[288,896]{1,0:T(8,128)(2,1)}, u32[]{:S(2)}, u32[]{:S(2)}) %collective-permute-start.10) | collective-permute-done | bytes 516128 | tf_op jit(solution)/shard_map/ppermute | solution.py:778
  105.1 13.9 %collective-permute-done.16.rest_8_ = bf16[592,896]{1,0:T(8,128)(2,1)} collective-permute-done((bf16[592,896]{1,0:T(8,128)(2,1)}, bf16[592,896]{1,0:T(8,128)(2,1)}, u32[]{:S(2)}, u32[]{:S(2)}) %collective-permute-start.16) | collective-permute-done | bytes 1060896 | tf_op jit(solution)/shard_map/ppermute | solution.py:778
  126.2 7.6 %shard_map.290 = (bf16[384,1472]{1,0:T(8,128)(2,1)}, bf16[384,384]{1,0:T(8,128)(2,1)}, bf16[384,768]{1,0:T(8,128)(2,1)}, bf16[4,1472,384]{2,1,0:T(8,128)(2,1)}) custom-call(bf16[384,1472]{1,0:T(8,128)(2,1)} %bitcast.139, f32[1,1472]{1,0:T(1,128)} %reshape.391.gain_ref, bf16[368,384]{1,0:T(8,128)(2,1)} %rest_0_.1, bf16[368,384]{1,0:T(8,128)(2,1)} %rest_1_.1, ...), custom_call_target="tpu_custom_call" | custom-call | flops 1302331392 | bytes 9043968 | tf_op jit(solution)/shard_map/pallas_call | solution.py:336
  134.6 16.2 %collective-permute-done.18.rest_1_ = bf16[384,768]{1,0:T(8,128)(2,1)S(1)} collective-permute-done((bf16[384,768]{1,0:T(8,128)(2,1)}, bf16[384,768]{1,0:T(8,128)(2,1)S(1)}, u32[]{:S(2)}, u32[]{:S(2)}) %collective-permute-start.18) | collective-permute-done | bytes 589856 | tf_op jit(solution)/shard_map/ppermute | solution.py:781
  154.2 11.8 %collective-permute-done.19.rest_2_ = bf16[384,768]{1,0:T(8,128)(2,1)} collective-permute-done((bf16[384,768]{1,0:T(8,128)(2,1)S(1)}, bf16[384,768]{1,0:T(8,128)(2,1)}, u32[]{:S(2)}, u32[]{:S(2)}) %collective-permute-start.19) | collective-permute-done | bytes 589856 | tf_op jit(solution)/shard_map/ppermute | solution.py:781
  169.6 5.3 shard_map.291.rest_6_
  177.3 3.5 reshape_squeeze.16
  180.8 5.4 shard_map.292
  187.1 5.4 shard_map.294
  192.5 5.4 shard_map.293
  219.5 5.5 collective-permute-done.24.rest_15_
  225.8 20.7 %shard_map.295 = (bf16[768,1792]{1,0:T(8,128)(2,1)}, bf16[768,1792]{1,0:T(8,128)(2,1)}, bf16[768,1792]{1,0:T(8,128)(2,1)}, bf16[1472,3584]{1,0:T(8,128)(2,1)}) custom-call(bf16[384,1472]{1,0:T(8,128)(2,1)} %multiply_convert_fusion.own_ref.refs_0_, bf16[384,1472]{1,0:T(8,128)(2,1)} %copy.102.other_ref.refs_1_, bf16[368,3584]{1,0:T(8,128)(2,1)} %shard_map.289.rest_0_, ...), custom_call_target="tpu_custom_call" | custom-call | flops 8103395328 | bytes 29360128 | tf_op jit(solution)/shard_map/pallas_call | solution.py:457
  246.6 10.7 %shard_map.296 = (f32[384,1472]{1,0:T(8,128)}, bf16[384,1472]{1,0:T(8,128)(2,1)}, bf16[1792,1536]{1,0:T(8,128)(2,1)}) custom-call(bf16[768,1792]{1,0:T(8,128)(2,1)} %get-tuple-element.189.hidden_ref.refs_0_, bf16[368,3584]{1,0:T(8,128)(2,1)} %shard_map.289.rest_0_, bf16[448,1536]{1,0:T(8,128)(2,1)} %pad.30.rest_1_, ...), custom_call_target="tpu_custom_call" | custom-call | flops 4051697664 | bytes 10551296 | tf_op jit(solution)/shard_map/pallas_call | solution.py:511
  264.7 3.2 multiply_reduce_fusion.4
  280.7 9.5 %shard_map.298 = (bf16[4,112,1472]{2,1,0:T(8,128)(2,1)}, bf16[4,112,1472]{2,1,0:T(8,128)(2,1)}, bf16[4,112,1472]{2,1,0:T(8,128)(2,1)}, bf16[4,48,1472]{2,1,0:T(8,128)(2,1)}, bf16[4,64,1472]{2,1,0:T(8,128)(2,1)}) custom-call(bf16[768,1792]{1,0:T(8,128)(2,1)} %get-tuple-element.189.hidden_ref.refs_0_, bf16[384,1472]{1,0:T(8,128)(2,1)} %get-tuple-element.356.own_ref.refs_1_, ...), custom_call_target="tpu_custom_call" | custom-call | flops 4051697664 | bytes 10289152 | tf_op jit(solution)/shard_map/pallas_call | solution.py:712
  294.8 14.2 %shard_map.297.refs_2_ = bf16[768,3584]{1,0:T(8,128)(2,1)} custom-call(bf16[384,1472]{1,0:T(8,128)(2,1)} %get-tuple-element.356.own_ref.refs_1_, bf16[384,1472]{1,0:T(8,128)(2,1)} %copy.107.other_ref.refs_2_, bf16[1792,1536]{1,0:T(8,128)(2,1)} %get-tuple-element.192.down_ref, bf16[768,1792]{1,0:T(8,128)(2,1)} %get-tuple-element.193.slope_ref, ...), custom_call_target="tpu_custom_call" | custom-call | flops 4051697664 | bytes 16285696 | tf_op jit(solution)/shard_map/pallas_call | solution.py:642
  318.1 11.2 %fusion.67 = f32[768,1472]{0,1:T(8,128)S(1)} fusion(bf16[768,3584]{1,0:T(8,128)(2,1)S(1)} %bitcast.142, bf16[1472,3584]{1,0:T(8,128)(2,1)} %get-tuple-element.201), kind=kOutput, calls=%fused_computation.196 | convolution fusion | flops 8103395328 | bytes 20578304 | tf_op jit(solution)/shard_map/tf,df->td/dot_general | solution.py:1208
  332.0 3.2 slice.427
  335.2 23.7 %shard_map.299 = (bf16[2,368,896]{2,1,0:T(8,128)(2,1)}, bf16[2,368,896]{2,1,0:T(8,128)(2,1)}, bf16[2,368,896]{2,1,0:T(8,128)(2,1)}, bf16[2,176,896]{2,1,0:T(8,12...) custom-call(bf16[384,1472]{1,0:T(8,128)(2,1)} %multiply_convert_fusi, ...), custom_call_target="tpu_custom_call" | custom-call | flops 8103395328 | bytes 18317312 | tf_op jit(solution)/shard_map/pallas_call | solution.py:712
  366.5 3.6 multiply_reduce_fusion.1
  386.3 3.8 collective-permute-start.35
  390.7 4.6 shard_map.300
  395.3 4.6 shard_map.301
  399.9 4.6 shard_map.302
  404.5 6.9 %shard_map.303 = f32[6,1,1024]{2,1,0:T(1,128)} custom-call(bf16[6,128,512]{2,1,0:T(8,128)(2,1)} %get-tuple-element.251.refs_0_, bf16[6,128,512]{2,1,0:T(8,128)(2,1)} %get-tuple-element.252.refs_1_, bf16[6,128,512]{2,1,0:T(8,128)(2,1)} %get-tuple-element.253.refs_2_, s32[1,384]{1,0:T(1,128)} %get-tuple-element.392.refs_3_), custom_call_target="tpu_custom_call" | custom-call | tf_op jit(solution)/shard_map/pallas_call | solution.py:79
  417.2 3.3 collective-permute-start.38
  427.4 3.6 reshape.379.out_grad_ref
  434.7 36.9 %collective-permute-done.39 = bf16[384,768]{1,0:T(8,128)(2,1)} collective-permute-done((bf16[384,768]{1,0:T(8,128)(2,1)}, bf16[384,768]{1,0:T(8,128)(2,1)}, u32[]{:S(2)}, u32[]{:S(2)}) %collective-permute-start.39) | collective-permute-done | bytes 589856 | tf_op jit(solution)/shard_map/ppermute | solution.py:781
  477.8 3.7 fusion.13
  482.4 6.7 %shard_map.304 = (bf16[4,4,208,384]{3,2,1,0:T(8,128)(2,1)}, bf16[4,4,208,384]{3,2,1,0:T(8,128)(2,1)}) custom-call(bf16[384,1472]{1,0:T(8,128)(2,1)} %get-tuple-element.250.normed_ref, bf16[384,384]{1,0:T(8,128)(2,1)} %copy-done.37, bf16[384,768]{1,0:T(8,128)(2,1)} %copy-done.19, bf16[1472,384]{1,0:T(8,128)(2,1)} %reshape.379.out_grad_ref, ...), custom_call_target="tpu_custom_call" | custom-call | flops 1302331392 | bytes 9043968 | tf_op jit(solution)/shard_map/pallas_call | solution.py:394
  491.3 15.5 %collective-permute-done.44 = bf16[2,176,896]{2,1,0:T(8,128)(2,1)S(1)} collective-permute-done((bf16[2,176,896]{2,1,0:T(8,128)(2,1)}, bf16[2,176,896]{2,1,0:T(8,128)(2,1)S(1)}, u32[]{:S(2)}, u32[]{:S(2)}) %collective-permute-start.44) | collective-permute-done | bytes 630816 | tf_op jit(solution)/shard_map/ppermute | solution.py:778
  516.2 15.7 %collective-permute-done.48 = bf16[368,896]{1,0:T(8,128)(2,1)S(1)} collective-permute-done((bf16[368,896]{1,0:T(8,128)(2,1)S(1)}, bf16[368,896]{1,0:T(8,128)(2,1)S(1)}, u32[]{:S(2)}, u32[]{:S(2)}) %collective-permute-start.48) | collective-permute-done | bytes 659488 | tf_op jit(solution)/shard_map/ppermute | solution.py:781
  531.9 26.6 %collective-permute-done.49 = bf16[368,896]{1,0:T(8,128)(2,1)S(1)} collective-permute-done((bf16[368,896]{1,0:T(8,128)(2,1)S(1)}, bf16[368,896]{1,0:T(8,128)(2,1)S(1)}, u32[]{:S(2)}, u32[]{:S(2)}) %collective-permute-start.49) | collective-permute-done | bytes 659488 | tf_op jit(solution)/shard_map/ppermute | solution.py:781
  563.8 12.4 %collective-permute-done.50 = bf16[4,208,384]{2,1,0:T(8,128)(2,1)S(1)} collective-permute-done((bf16[4,208,384]{2,1,0:T(8,128)(2,1)S(1)}, bf16[4,208,384]{2,1,0:T(8,128)(2,1)S(1)}, u32[]{:S(2)}, u32[]{:S(2)}) %collective-permute-start.50) | collective-permute-done | bytes 639008 | tf_op jit(solution)/shard_map/ppermute | solution.py:778
  576.2 13.2 %collective-permute-done.51 = bf16[4,208,384]{2,1,0:T(8,128)(2,1)S(1)} collective-permute-done((bf16[4,208,384]{2,1,0:T(8,128)(2,1)S(1)}, bf16[4,208,384]{2,1,0:T(8,128)(2,1)S(1)}, u32[]{:S(2)}, u32[]{:S(2)}) %collective-permute-start.51) | collective-permute-done | bytes 639008 | tf_op jit(solution)/shard_map/ppermute | solution.py:778
  592.7 3.5 collective-permute-start.53
  600.5 8.5 %collective-permute-done.54 = bf16[208,384]{1,0:T(8,128)(2,1)S(1)} collective-permute-done((bf16[208,384]{1,0:T(8,128)(2,1)S(1)}, bf16[208,384]{1,0:T(8,128)(2,1)S(1)}, u32[]{:S(2)}, u32[]{:S(2)}) %collective-permute-start.54) | collective-permute-done | bytes 159776 | tf_op jit(solution)/shard_map/ppermute | solution.py:781
  612.7 6.5 collective-permute-done.56
  628.3 10.7 %collective-permute-done.63.refs_3_ = bf16[288,896]{1,0:T(8,128)(2,1)} collective-permute-done((bf16[288,896]{1,0:T(8,128)(2,1)}, bf16[288,896]{1,0:T(8,128)(2,1)}, u32[]{:S(2)}, u32[]{:S(2)}) %collective-permute-start.63) | collective-permute-done | bytes 516128 | tf_op jit(solution)/shard_map/ppermute | solution.py:778
  639.6 3.3 fusion.10
  651.9 10.1 %shard_map.306 = (f32[368,3584]{1,0:T(8,128)}, f32[368,3584]{1,0:T(8,128)}, f32[896,1472]{1,0:T(8,128)}) custom-call(bf16[592,896]{1,0:T(8,128)(2,1)} %copy-done.13, bf16[592,896]{1,0:T(8,128)(2,1)} %copy-done.17, bf16[592,896]{1,0:T(8,128)(2,1)} %copy-done.21, bf16[288,896]{1,0:T(8,128)(2,1)} %collective-permute-done.63.refs_3_, ...), custom_call_target="tpu_custom_call" | custom-call | tf_op jit(solution)/shard_map/pallas_call | solution.py:565
  662.0 6.2 copy.122
  (389 shorter events, 207.2 us)
Async XLA Ops:
  28.6 26.8 %collective-permute-start.7 = (bf16[592,896]{1,0:T(8,128)(2,1)S(1)}, bf16[592,896]{1,0:T(8,128)(2,1)}, u32[]{:S(2)}, u32[]{:S(2)}) collective-permute-start(bf16[592,896]{1,0:T(8,128)(2,1)S(1)} %pad_maximum_fusion.7), channel_id=1, source_target_pairs={{0,1},{1,2},{2,3},{3,0},{4,5},{5,6},{6,7},{7,4},{8,9},{9,10},{10,1... | collective-permute-start | bytes 3182600 | tf_op jit(solution)/shard_map/ppermute | solution.py:781
  30.2 20.8 %collective-permute-start.4 = (bf16[3,192,384]{2,1,0:T(8,128)(2,1)S(1)}, bf16[3,192,384]{2,1,0:T(8,128)(2,1)S(1)}, u32[]{:S(2)}, u32[]{:S(2)}) collective-permute-start(bf16[3,192,384]{2,1,0:T(8,128)(2,1)S(1)} %pad_maximum_fusion.14), channel_id=1, source_target_pairs={{0,16},{4,20},{8,24},{12,28},{16,0},{20,4},{24,8},{28,12},{1,17},{... | collective-permute-start | bytes 1327112 | tf_op jit(solution)/shard_map/ppermute | solution.py:778
  30.8 20.2 %collective-permute-start.5 = (bf16[3,192,384]{2,1,0:T(8,128)(2,1)S(1)}, bf16[3,192,384]{2,1,0:T(8,128)(2,1)S(1)}, u32[]{:S(2)}, u32[]{:S(2)}) collective-permute-start(bf16[3,192,384]{2,1,0:T(8,128)(2,1)S(1)} %pad_maximum_fusion.14), channel_id=1, source_target_pairs={{0,24},{4,28},{8,16},{12,20},{16,8},{20,12},{24,0},{28,4},{1,25},{... | collective-permute-start | bytes 1327112 | tf_op jit(solution)/shard_map/ppermute | solution.py:778
  55.4 24.1 %collective-permute-start.11 = (bf16[592,896]{1,0:T(8,128)(2,1)}, bf16[592,896]{1,0:T(8,128)(2,1)S(1)}, u32[]{:S(2)}, u32[]{:S(2)}) collective-permute-start(bf16[592,896]{1,0:T(8,128)(2,1)} %collective-permute-done.7.rest_2_), channel_id=1, source_target_pairs={{0,8},{4,12},{8,0},{12,4},{16,24},{20,28},{24,16},{28,20},{1,9},{5... | collective-permute-start | bytes 3182600 | tf_op jit(solution)/shard_map/ppermute | solution.py:778
  56.9 26.0 %collective-permute-start.9 = (bf16[592,896]{1,0:T(8,128)(2,1)}, bf16[592,896]{1,0:T(8,128)(2,1)S(1)}, u32[]{:S(2)}, u32[]{:S(2)}) collective-permute-start(bf16[592,896]{1,0:T(8,128)(2,1)} %collective-permute-done.7.rest_2_), channel_id=1, source_target_pairs={{0,16},{4,20},{8,24},{12,28},{16,0},{20,4},{24,8},{28,12},{1,17},{... | collective-permute-start | bytes 3182600 | tf_op jit(solution)/shard_map/ppermute | solution.py:778
  57.5 27.8 %collective-permute-start.8 = (bf16[592,896]{1,0:T(8,128)(2,1)}, bf16[592,896]{1,0:T(8,128)(2,1)}, u32[]{:S(2)}, u32[]{:S(2)}) collective-permute-start(bf16[592,896]{1,0:T(8,128)(2,1)} %collective-permute-done.7.rest_2_), channel_id=1, source_target_pairs={{0,1},{1,2},{2,3},{3,0},{4,5},{5,6},{6,7},{7,4},{8,9},{9,10},{10,1... | collective-permute-start | bytes 3182600 | tf_op jit(solution)/shard_map/ppermute | solution.py:781
  81.4 15.3 %collective-permute-start.12 = (bf16[304,896]{1,0:T(8,128)(2,1)}, bf16[304,896]{1,0:T(8,128)(2,1)S(1)}, u32[]{:S(2)}, u32[]{:S(2)}) collective-permute-start(bf16[304,896]{1,0:T(8,128)(2,1)} %slice.415), channel_id=1, source_target_pairs={{0,16},{4,20},{8,24},{12,28},{16,0},{20,4},{24,8},{28,12},{1,17},{... | collective-permute-start | bytes 1634312 | tf_op jit(solution)/shard_map/ppermute | solution.py:778
  96.6 22.3 %collective-permute-start.16 = (bf16[592,896]{1,0:T(8,128)(2,1)}, bf16[592,896]{1,0:T(8,128)(2,1)}, u32[]{:S(2)}, u32[]{:S(2)}) collective-permute-start(bf16[592,896]{1,0:T(8,128)(2,1)} %collective-permute-done.8.rest_7_), channel_id=1, source_target_pairs={{0,8},{4,12},{8,0},{12,4},{16,24},{20,28},{24,16},{28,20},{1,9},{5... | collective-permute-start | bytes 3182600 | tf_op jit(solution)/shard_map/ppermute | solution.py:778
  97.2 24.1 %collective-permute-start.14 = (bf16[592,896]{1,0:T(8,128)(2,1)}, bf16[592,896]{1,0:T(8,128)(2,1)}, u32[]{:S(2)}, u32[]{:S(2)}) collective-permute-start(bf16[592,896]{1,0:T(8,128)(2,1)} %collective-permute-done.8.rest_7_), channel_id=1, source_target_pairs={{0,16},{4,20},{8,24},{12,28},{16,0},{20,4},{24,8},{28,12},{1,17},{... | collective-permute-start | bytes 3182600 | tf_op jit(solution)/shard_map/ppermute | solution.py:778
  103.7 22.5 %collective-permute-start.6 = (bf16[4,3,192,384]{3,2,1,0:T(8,128)(2,1)}, bf16[4,3,192,384]{3,2,1,0:T(8,128)(2,1)}, u32[]{:S(2)}, u32[]{:S(2)}) collective-permute-start(bf16[4,3,192,384]{3,2,1,0:T(8,128)(2,1)} %pad_maximum_fusion.rest_4_), channel_id=1, source_target_pairs={{0,4},{4,0},{8,12},{12,8},{16,20},{20,16},{24,28},{28,24},{1,5},{5... | collective-permute-start | bytes 5308424 | tf_op jit(solution)/shard_map/ppermute | solution.py:778
  105.0 28.7 %collective-permute-start.13 = (bf16[592,896]{1,0:T(8,128)(2,1)}, bf16[592,896]{1,0:T(8,128)(2,1)}, u32[]{:S(2)}, u32[]{:S(2)}) collective-permute-start(bf16[592,896]{1,0:T(8,128)(2,1)} %collective-permute-done.8.rest_7_), channel_id=1, source_target_pairs={{0,1},{1,2},{2,3},{3,0},{4,5},{5,6},{6,7},{7,4},{8,9},{9,10},{10,1... | collective-permute-start | bytes 3182600 | tf_op jit(solution)/shard_map/ppermute | solution.py:781
  134.6 16.2 %collective-permute-start.18 = (bf16[384,768]{1,0:T(8,128)(2,1)}, bf16[384,768]{1,0:T(8,128)(2,1)S(1)}, u32[]{:S(2)}, u32[]{:S(2)}) collective-permute-start(bf16[384,768]{1,0:T(8,128)(2,1)} %get-tuple-element.168.rest_0_), channel_id=1, source_target_pairs={{0,1},{1,2},{2,3},{3,0},{4,5},{5,6},{6,7},{7,4},{8,9},{9,10},{10,1... | collective-permute-start | bytes 1769480 | tf_op jit(solution)/shard_map/ppermute | solution.py:781
  150.8 15.2 %collective-permute-start.19 = (bf16[384,768]{1,0:T(8,128)(2,1)S(1)}, bf16[384,768]{1,0:T(8,128)(2,1)}, u32[]{:S(2)}, u32[]{:S(2)}) collective-permute-start(bf16[384,768]{1,0:T(8,128)(2,1)S(1)} %collective-permute-done.18.rest_1_), channel_id=1, source_target_pairs={{0,1},{1,2},{2,3},{3,0},{4,5},{5,6},{6,7},{7,4},{8,9},{9,10},{10,1... | collective-permute-start | bytes 1769480 | tf_op jit(solution)/shard_map/ppermute | solution.py:781
  151.4 29.4 %collective-permute-start.21 = (bf16[592,896]{1,0:T(8,128)(2,1)}, bf16[592,896]{1,0:T(8,128)(2,1)}, u32[]{:S(2)}, u32[]{:S(2)}) collective-permute-start(bf16[592,896]{1,0:T(8,128)(2,1)} %collective-permute-done.13.rest_12_), channel_id=1, source_target_pairs={{0,8},{4,12},{8,0},{12,4},{16,24},{20,28},{24,16},{28,20},{1,9},{5... | collective-permute-start | bytes 3182600 | tf_op jit(solution)/shard_map/ppermute | solution.py:778
  152.0 28.8 %collective-permute-start.22 = (bf16[592,896]{1,0:T(8,128)(2,1)}, bf16[592,896]{1,0:T(8,128)(2,1)}, u32[]{:S(2)}, u32[]{:S(2)}) collective-permute-start(bf16[592,896]{1,0:T(8,128)(2,1)} %collective-permute-done.13.rest_12_), channel_id=1, source_target_pairs={{0,16},{4,20},{8,24},{12,28},{16,0},{20,4},{24,8},{28,12},{1,17},{... | collective-permute-start | bytes 3182600 | tf_op jit(solution)/shard_map/ppermute | solution.py:778
  208.3 16.7 %collective-permute-start.25 = (bf16[304,896]{1,0:T(8,128)(2,1)}, bf16[304,896]{1,0:T(8,128)(2,1)S(1)}, u32[]{:S(2)}, u32[]{:S(2)}) collective-permute-start(bf16[304,896]{1,0:T(8,128)(2,1)} %slice.424), channel_id=1, source_target_pairs={{0,16},{4,20},{8,24},{12,28},{16,0},{20,4},{24,8},{28,12},{1,17},{... | collective-permute-start | bytes 1634312 | tf_op jit(solution)/shard_map/ppermute | solution.py:778
  290.3 20.2 %collective-permute-start.29 = (bf16[4,64,1472]{2,1,0:T(8,128)(2,1)}, bf16[4,64,1472]{2,1,0:T(8,128)(2,1)}, u32[]{:S(2)}, u32[]{:S(2)}) collective-permute-start(bf16[4,64,1472]{2,1,0:T(8,128)(2,1)} %get-tuple-element.199), channel_id=1, source_target_pairs={{0,16},{4,20},{8,24},{12,28},{16,0},{20,4},{24,8},{28,12},{1,17},{... | collective-permute-start | bytes 2261000 | tf_op jit(solution)/shard_map/ppermute | solution.py:778
  291.7 17.3 %collective-permute-start.28 = (bf16[4,48,1472]{2,1,0:T(8,128)(2,1)}, bf16[4,48,1472]{2,1,0:T(8,128)(2,1)S(1)}, u32[]{:S(2)}, u32[]{:S(2)}) collective-permute-start(bf16[4,48,1472]{2,1,0:T(8,128)(2,1)} %get-tuple-element.198), channel_id=1, source_target_pairs={{0,8},{4,12},{8,0},{12,4},{16,24},{20,28},{24,16},{28,20},{1,9},{5... | collective-permute-start | bytes 1695752 | tf_op jit(solution)/shard_map/ppermute | solution.py:778
  314.7 49.4 %collective-permute-start.32 = (bf16[4,112,1472]{2,1,0:T(8,128)(2,1)}, bf16[4,112,1472]{2,1,0:T(8,128)(2,1)}, u32[]{:S(2)}, u32[]{:S(2)}) collective-permute-start(bf16[4,112,1472]{2,1,0:T(8,128)(2,1)} %pad_maximum_fusion.2), channel_id=1, source_target_pairs={{0,8},{4,12},{8,0},{12,4},{16,24},{20,28},{24,16},{28,20},{1,9},{5... | collective-permute-start | bytes 3956744 | tf_op jit(solution)/shard_map/ppermute | solution.py:778
  317.5 46.6 %collective-permute-start.31 = (bf16[4,112,1472]{2,1,0:T(8,128)(2,1)}, bf16[4,112,1472]{2,1,0:T(8,128)(2,1)}, u32[]{:S(2)}, u32[]{:S(2)}) collective-permute-start(bf16[4,112,1472]{2,1,0:T(8,128)(2,1)} %pad_maximum_fusion.1), channel_id=1, source_target_pairs={{0,16},{4,20},{8,24},{12,28},{16,0},{20,4},{24,8},{28,12},{1,17},{... | collective-permute-start | bytes 3956744 | tf_op jit(solution)/shard_map/ppermute | solution.py:778
  330.4 33.6 %collective-permute-start.30 = (bf16[384,1472]{0,1:T(8,128)(2,1)}, bf16[384,1472]{0,1:T(8,128)(2,1)}, u32[]{:S(2)}, u32[]{:S(2)}) collective-permute-start(bf16[384,1472]{0,1:T(8,128)(2,1)} %slice.526), channel_id=1, source_target_pairs={{0,4},{4,0},{8,12},{12,8},{16,20},{20,16},{24,28},{28,24},{1,5},{5... | collective-permute-start | bytes 3391496 | tf_op jit(solution)/shard_map/ppermute | solution.py:778
  358.8 17.2 %collective-permute-start.34 = (bf16[2,192,896]{2,1,0:T(8,128)(2,1)}, bf16[2,192,896]{2,1,0:T(8,128)(2,1)}, u32[]{:S(2)}, u32[]{:S(2)}) collective-permute-start(bf16[2,192,896]{2,1,0:T(8,128)(2,1)} %get-tuple-element.212), channel_id=1, source_target_pairs={{0,16},{4,20},{8,24},{12,28},{16,0},{20,4},{24,8},{28,12},{1,17},{... | collective-permute-start | bytes 2064392 | tf_op jit(solution)/shard_map/ppermute | solution.py:778
  360.4 15.6 %collective-permute-start.33 = (bf16[2,176,896]{2,1,0:T(8,128)(2,1)}, bf16[2,176,896]{2,1,0:T(8,128)(2,1)}, u32[]{:S(2)}, u32[]{:S(2)}) collective-permute-start(bf16[2,176,896]{2,1,0:T(8,128)(2,1)} %get-tuple-element.211), channel_id=1, source_target_pairs={{0,8},{4,12},{8,0},{12,4},{16,24},{20,28},{24,16},{28,20},{1,9},{5... | collective-permute-start | bytes 1892360 | tf_op jit(solution)/shard_map/ppermute | solution.py:778
  378.5 93.1 %collective-permute-start.42 = (bf16[2,368,896]{2,1,0:T(8,128)(2,1)}, bf16[2,368,896]{2,1,0:T(8,128)(2,1)}, u32[]{:S(2)}, u32[]{:S(2)}) collective-permute-start(bf16[2,368,896]{2,1,0:T(8,128)(2,1)} %pad_maximum_fusion.4), channel_id=1, source_target_pairs={{0,8},{4,12},{8,0},{12,4},{16,24},{20,28},{24,16},{28,20},{1,9},{5... | collective-permute-start | bytes 3956744 | tf_op jit(solution)/shard_map/ppermute | solution.py:778
  382.5 89.1 %collective-permute-start.41 = (bf16[2,368,896]{2,1,0:T(8,128)(2,1)}, bf16[2,368,896]{2,1,0:T(8,128)(2,1)}, u32[]{:S(2)}, u32[]{:S(2)}) collective-permute-start(bf16[2,368,896]{2,1,0:T(8,128)(2,1)} %pad_maximum_fusion.3), channel_id=1, source_target_pairs={{0,16},{4,20},{8,24},{12,28},{16,0},{20,4},{24,8},{28,12},{1,17},{... | collective-permute-start | bytes 3956744 | tf_op jit(solution)/shard_map/ppermute | solution.py:778
  386.3 30.9 %collective-permute-start.35 = (bf16[112,1472]{1,0:T(8,128)(2,1)}, bf16[112,1472]{1,0:T(8,128)(2,1)}, u32[]{:S(2)}, u32[]{:S(2)}) collective-permute-start(bf16[112,1472]{1,0:T(8,128)(2,1)} %get-tuple-element.366), channel_id=1, source_target_pairs={{0,3},{1,0},{2,1},{3,2},{4,7},{5,4},{6,5},{7,6},{8,11},{9,8},{10,9... | collective-permute-start | bytes 989192 | tf_op jit(solution)/shard_map/ppermute | solution.py:781
  390.1 27.1 %collective-permute-start.36 = (bf16[112,1472]{1,0:T(8,128)(2,1)}, bf16[112,1472]{1,0:T(8,128)(2,1)}, u32[]{:S(2)}, u32[]{:S(2)}) collective-permute-start(bf16[112,1472]{1,0:T(8,128)(2,1)} %get-tuple-element.365), channel_id=1, source_target_pairs={{0,2},{1,3},{2,0},{3,1},{4,6},{5,7},{6,4},{7,5},{8,10},{9,11},{10,... | collective-permute-start | bytes 989192 | tf_op jit(solution)/shard_map/ppermute | solution.py:781
  390.1 27.1 %collective-permute-start.37 = (bf16[112,1472]{1,0:T(8,128)(2,1)}, bf16[112,1472]{1,0:T(8,128)(2,1)}, u32[]{:S(2)}, u32[]{:S(2)}) collective-permute-start(bf16[112,1472]{1,0:T(8,128)(2,1)} %get-tuple-element.364), channel_id=1, source_target_pairs={{0,1},{1,2},{2,3},{3,0},{4,5},{5,6},{6,7},{7,4},{8,9},{9,10},{10,1... | collective-permute-start | bytes 989192 | tf_op jit(solution)/shard_map/ppermute | solution.py:781
  417.2 17.5 %collective-permute-start.38 = (bf16[384,768]{1,0:T(8,128)(2,1)}, bf16[384,768]{1,0:T(8,128)(2,1)}, u32[]{:S(2)}, u32[]{:S(2)}) collective-permute-start(bf16[384,768]{1,0:T(8,128)(2,1)} %get-tuple-element.239), channel_id=1, source_target_pairs={{0,3},{1,0},{2,1},{3,2},{4,7},{5,4},{6,5},{7,6},{8,11},{9,8},{10,9... | collective-permute-start | bytes 1769480 | tf_op jit(solution)/shard_map/ppermute | solution.py:781
  420.5 51.1 %collective-permute-start.39 = (bf16[384,768]{1,0:T(8,128)(2,1)}, bf16[384,768]{1,0:T(8,128)(2,1)}, u32[]{:S(2)}, u32[]{:S(2)}) collective-permute-start(bf16[384,768]{1,0:T(8,128)(2,1)} %get-tuple-element.240), channel_id=1, source_target_pairs={{0,2},{1,3},{2,0},{3,1},{4,6},{5,7},{6,4},{7,5},{8,10},{9,11},{10,... | collective-permute-start | bytes 1769480 | tf_op jit(solution)/shard_map/ppermute | solution.py:781
  421.6 50.0 %collective-permute-start.40 = (bf16[384,768]{1,0:T(8,128)(2,1)}, bf16[384,768]{1,0:T(8,128)(2,1)}, u32[]{:S(2)}, u32[]{:S(2)}) collective-permute-start(bf16[384,768]{1,0:T(8,128)(2,1)} %get-tuple-element.241), channel_id=1, source_target_pairs={{0,1},{1,2},{2,3},{3,0},{4,5},{5,6},{6,7},{7,4},{8,9},{9,10},{10,1... | collective-permute-start | bytes 1769480 | tf_op jit(solution)/shard_map/ppermute | solution.py:781
  489.1 17.9 %collective-permute-start.43 = (bf16[4,4,208,384]{3,2,1,0:T(8,128)(2,1)}, bf16[4,4,208,384]{3,2,1,0:T(8,128)(2,1)S(1)}, u32[]{:S(2)}, u32[]{:S(2)}) collective-permute-start(bf16[4,4,208,384]{3,2,1,0:T(8,128)(2,1)} %get-tuple-element.255), channel_id=1, source_target_pairs={{0,4},{4,0},{8,12},{12,8},{16,20},{20,16},{24,28},{28,24},{1,5},{5... | collective-permute-start | bytes 7667720 | tf_op jit(solution)/shard_map/ppermute | solution.py:778
  489.2 17.8 %collective-permute-start.45 = (bf16[2,192,896]{2,1,0:T(8,128)(2,1)S(1)}, bf16[2,192,896]{2,1,0:T(8,128)(2,1)S(1)}, u32[]{:S(2)}, u32[]{:S(2)}) collective-permute-start(bf16[2,192,896]{2,1,0:T(8,128)(2,1)S(1)} %copy-done.56), channel_id=1, source_target_pairs={{0,16},{4,20},{8,24},{12,28},{16,0},{20,4},{24,8},{28,12},{1,17},{... | collective-permute-start | bytes 2064392 | tf_op jit(solution)/shard_map/ppermute | solution.py:778
  490.4 16.5 %collective-permute-start.44 = (bf16[2,176,896]{2,1,0:T(8,128)(2,1)}, bf16[2,176,896]{2,1,0:T(8,128)(2,1)S(1)}, u32[]{:S(2)}, u32[]{:S(2)}) collective-permute-start(bf16[2,176,896]{2,1,0:T(8,128)(2,1)} %get-tuple-element.259), channel_id=1, source_target_pairs={{0,8},{4,12},{8,0},{12,4},{16,24},{20,28},{24,16},{28,20},{1,9},{5... | collective-permute-start | bytes 1892360 | tf_op jit(solution)/shard_map/ppermute | solution.py:778
  509.6 48.9 %collective-permute-start.47 = (bf16[2,368,896]{2,1,0:T(8,128)(2,1)S(1)}, bf16[2,368,896]{2,1,0:T(8,128)(2,1)S(1)}, u32[]{:S(2)}, u32[]{:S(2)}) collective-permute-start(bf16[2,368,896]{2,1,0:T(8,128)(2,1)S(1)} %pad_maximum_fusion.6), channel_id=1, source_target_pairs={{0,8},{4,12},{8,0},{12,4},{16,24},{20,28},{24,16},{28,20},{1,9},{5... | collective-permute-start | bytes 3956744 | tf_op jit(solution)/shard_map/ppermute | solution.py:778
  511.1 47.4 %collective-permute-start.46 = (bf16[2,368,896]{2,1,0:T(8,128)(2,1)S(1)}, bf16[2,368,896]{2,1,0:T(8,128)(2,1)S(1)}, u32[]{:S(2)}, u32[]{:S(2)}) collective-permute-start(bf16[2,368,896]{2,1,0:T(8,128)(2,1)S(1)} %pad_maximum_fusion.5), channel_id=1, source_target_pairs={{0,16},{4,20},{8,24},{12,28},{16,0},{20,4},{24,8},{28,12},{1,17},{... | collective-permute-start | bytes 3956744 | tf_op jit(solution)/shard_map/ppermute | solution.py:778
  514.6 17.3 %collective-permute-start.48 = (bf16[368,896]{1,0:T(8,128)(2,1)S(1)}, bf16[368,896]{1,0:T(8,128)(2,1)S(1)}, u32[]{:S(2)}, u32[]{:S(2)}) collective-permute-start(bf16[368,896]{1,0:T(8,128)(2,1)S(1)} %get-tuple-element.368), channel_id=1, source_target_pairs={{0,3},{1,0},{2,1},{3,2},{4,7},{5,4},{6,5},{7,6},{8,11},{9,8},{10,9... | collective-permute-start | bytes 1978376 | tf_op jit(solution)/shard_map/ppermute | solution.py:781
  514.6 43.9 %collective-permute-start.49 = (bf16[368,896]{1,0:T(8,128)(2,1)S(1)}, bf16[368,896]{1,0:T(8,128)(2,1)S(1)}, u32[]{:S(2)}, u32[]{:S(2)}) collective-permute-start(bf16[368,896]{1,0:T(8,128)(2,1)S(1)} %get-tuple-element.367), channel_id=1, source_target_pairs={{0,2},{1,3},{2,0},{3,1},{4,6},{5,7},{6,4},{7,5},{8,10},{9,11},{10,... | collective-permute-start | bytes 1978376 | tf_op jit(solution)/shard_map/ppermute | solution.py:781
  558.8 31.1 %collective-permute-start.60 = (bf16[368,896]{1,0:T(8,128)(2,1)S(1)}, bf16[368,896]{1,0:T(8,128)(2,1)S(1)}, u32[]{:S(2)}, u32[]{:S(2)}) collective-permute-start(bf16[368,896]{1,0:T(8,128)(2,1)S(1)} %fusion.27), channel_id=1, source_target_pairs={{0,1},{1,2},{2,3},{3,0},{4,5},{5,6},{6,7},{7,4},{8,9},{9,10},{10,1... | collective-permute-start | bytes 1978376 | tf_op jit(solution)/shard_map/ppermute | solution.py:781
  558.9 17.4 %collective-permute-start.50 = (bf16[4,208,384]{2,1,0:T(8,128)(2,1)S(1)}, bf16[4,208,384]{2,1,0:T(8,128)(2,1)S(1)}, u32[]{:S(2)}, u32[]{:S(2)}) collective-permute-start(bf16[4,208,384]{2,1,0:T(8,128)(2,1)S(1)} %get-tuple-element.270), channel_id=1, source_target_pairs={{0,8},{4,12},{8,0},{12,4},{16,24},{20,28},{24,16},{28,20},{1,9},{5... | collective-permute-start | bytes 1916936 | tf_op jit(solution)/shard_map/ppermute | solution.py:778
  560.0 29.4 %collective-permute-start.51 = (bf16[4,208,384]{2,1,0:T(8,128)(2,1)S(1)}, bf16[4,208,384]{2,1,0:T(8,128)(2,1)S(1)}, u32[]{:S(2)}, u32[]{:S(2)}) collective-permute-start(bf16[4,208,384]{2,1,0:T(8,128)(2,1)S(1)} %get-tuple-element.271), channel_id=1, source_target_pairs={{0,16},{4,20},{8,24},{12,28},{16,0},{20,4},{24,8},{28,12},{1,17},{... | collective-permute-start | bytes 1916936 | tf_op jit(solution)/shard_map/ppermute | solution.py:778
  561.0 28.4 %collective-permute-start.52 = (bf16[4,208,384]{2,1,0:T(8,128)(2,1)S(1)}, bf16[4,208,384]{2,1,0:T(8,128)(2,1)S(1)}, u32[]{:S(2)}, u32[]{:S(2)}) collective-permute-start(bf16[4,208,384]{2,1,0:T(8,128)(2,1)S(1)} %get-tuple-element.272), channel_id=1, source_target_pairs={{0,24},{4,28},{8,16},{12,20},{16,8},{20,12},{24,0},{28,4},{1,25},{... | collective-permute-start | bytes 1916936 | tf_op jit(solution)/shard_map/ppermute | solution.py:778
  590.5 31.1 %collective-permute-start.61 = (bf16[592,896]{1,0:T(8,128)(2,1)S(1)}, bf16[592,896]{1,0:T(8,128)(2,1)S(1)}, u32[]{:S(2)}, u32[]{:S(2)}) collective-permute-start(bf16[592,896]{1,0:T(8,128)(2,1)S(1)} %pad_maximum_fusion.8.refs_0_), channel_id=1, source_target_pairs={{0,8},{4,12},{8,0},{12,4},{16,24},{20,28},{24,16},{28,20},{1,9},{5... | collective-permute-start | bytes 3182600 | tf_op jit(solution)/shard_map/ppermute | solution.py:778
  591.5 32.3 %collective-permute-start.62 = (bf16[592,896]{1,0:T(8,128)(2,1)S(1)}, bf16[592,896]{1,0:T(8,128)(2,1)S(1)}, u32[]{:S(2)}, u32[]{:S(2)}) collective-permute-start(bf16[592,896]{1,0:T(8,128)(2,1)S(1)} %pad_maximum_fusion.8.refs_0_), channel_id=1, source_target_pairs={{0,16},{4,20},{8,24},{12,28},{16,0},{20,4},{24,8},{28,12},{1,17},{... | collective-permute-start | bytes 3182600 | tf_op jit(solution)/shard_map/ppermute | solution.py:778
  622.7 16.4 %collective-permute-start.64 = (bf16[304,896]{1,0:T(8,128)(2,1)}, bf16[304,896]{1,0:T(8,128)(2,1)}, u32[]{:S(2)}, u32[]{:S(2)}) collective-permute-start(bf16[304,896]{1,0:T(8,128)(2,1)} %slice.442), channel_id=1, source_target_pairs={{0,16},{4,20},{8,24},{12,28},{16,0},{20,4},{24,8},{28,12},{1,17},{... | collective-permute-start | bytes 1634312 | tf_op jit(solution)/shard_map/ppermute | solution.py:778
  627.8 23.1 %collective-permute-start.65 = (bf16[592,896]{1,0:T(8,128)(2,1)}, bf16[592,896]{1,0:T(8,128)(2,1)S(1)}, u32[]{:S(2)}, u32[]{:S(2)}) collective-permute-start(bf16[592,896]{1,0:T(8,128)(2,1)} %copy-done.13), channel_id=1, source_target_pairs={{0,4},{4,0},{8,12},{12,8},{16,20},{20,16},{24,28},{28,24},{1,5},{5... | collective-permute-start | bytes 3182600 | tf_op jit(solution)/shard_map/ppermute | solution.py:778
  627.8 23.1 %collective-permute-start.66 = (bf16[592,896]{1,0:T(8,128)(2,1)}, bf16[592,896]{1,0:T(8,128)(2,1)}, u32[]{:S(2)}, u32[]{:S(2)}) collective-permute-start(bf16[592,896]{1,0:T(8,128)(2,1)} %copy-done.17), channel_id=1, source_target_pairs={{0,4},{4,0},{8,12},{12,8},{16,20},{20,16},{24,28},{28,24},{1,5},{5... | collective-permute-start | bytes 3182600 | tf_op jit(solution)/shard_map/ppermute | solution.py:778
  628.3 22.6 %collective-permute-start.67 = (bf16[592,896]{1,0:T(8,128)(2,1)}, bf16[592,896]{1,0:T(8,128)(2,1)}, u32[]{:S(2)}, u32[]{:S(2)}) collective-permute-start(bf16[592,896]{1,0:T(8,128)(2,1)} %copy-done.21), channel_id=1, source_target_pairs={{0,4},{4,0},{8,12},{12,8},{16,20},{20,16},{24,28},{28,24},{1,5},{5... | collective-permute-start | bytes 3182600 | tf_op jit(solution)/shard_map/ppermute | solution.py:778
  (81 other events, 849.8 us)

commit v4 on v3

--- a/solution.py
+++ b/solution.py
@@ -13,11 +13,12 @@
 HIGHEST = lax.Precision.HIGHEST
 MASKED = -1000000000.0
 BF16 = jnp.bfloat16
+LIGHT = pl.CostEstimate(flops=1000, bytes_accessed=1000, transcendentals=0)
 F32 = jnp.float32
 
 
-def gelu_tanh(value):
-    return jax.nn.gelu(value, approximate=True)
+ANY = pl.BlockSpec(memory_space=pl.ANY)
+VMEM = pl.BlockSpec(memory_space=pltpu.VMEM)
 
 
 def rms_scale(hidden):
@@ -29,10 +30,6 @@
     return scale_row * scaled - hidden * (scale_row * scale_row * scale_row) * jnp.mean(
         hidden * scaled, axis=-1, keepdims=True
     )
-
-
-def dot(left, right, kind=F32):
-    return jnp.dot(left, right, preferred_element_type=F32).astype(kind)
 
 
 def bias_kernel(rows_ref, slots_ref, out_ref):
@@ -98,7 +95,7 @@
     return lax.dot_general(left, right, (((1,), (1,)), ((), ())), preferred_element_type=F32)
 
 
-def attention_call(micro, lengths, queries, pairs, own_slots, key_slots, bias):
+def attention_call(micro, lengths, queries, pairs, own_slots, key_slots, bias, context):
     heads, rows, group = bias.shape
     double = pairs[0].shape[1]
     count = len(pairs)
@@ -108,7 +105,8 @@
 
     def kernel(lengths_ref, query_ref, *rest):
         pair_refs = rest[:count]
-        own_ref, key_ref, bias_ref, context_ref, prob_ref, packed_ref, arrived = rest[count:]
+        own_ref, key_ref, bias_ref = rest[count : count + 3]
+        context_ref, prob_ref, packed_ref, arrived = rest[-4:]
         for index, ref in enumerate(pair_refs):
             arrived[index * local : (index + 1) * local] = ref[...]
         place = (
@@ -145,34 +143,32 @@
             pl.BlockSpec((local, 1), lambda i: (micro, 0)),
             pl.BlockSpec((1, group), lambda i: (0, 0)),
             pl.BlockSpec((heads, local, group), lambda i: (0, micro, 0)),
-        ],
+        ]
+        + [ANY] * len(context),
         out_specs=[
-            pl.BlockSpec((local, proj), lambda i: (0, 0)),
+            pl.BlockSpec((local, proj), lambda i: (micro, 0)),
             pl.BlockSpec((heads, local, group), lambda i: (0, 0, 0)),
             pl.BlockSpec((group, double), lambda i: (0, 0)),
         ],
         out_shape=[
-            jax.ShapeDtypeStruct((local, proj), BF16),
+            jax.ShapeDtypeStruct(queries.shape, BF16),
             jax.ShapeDtypeStruct((heads, local, group), BF16),
             jax.ShapeDtypeStruct((group, double), BF16),
         ],
+        input_output_aliases={count + 5: 0} if context else {},
         scratch_shapes=[pltpu.VMEM((group, double), BF16)],
-        cost_estimate=pl.CostEstimate(
-            flops=2 * group * group * double + 8 * local * group * proj,
-            bytes_accessed=4 * group * double + 4 * heads * local * group,
-            transcendentals=heads * local * group,
-        ),
-    )(lengths, queries, *pairs, own_slots, key_slots, bias)
-
-
-def attention_back_call(micro, queries, context_grad, probs, packed, key_slots, shards):
+        cost_estimate=LIGHT,
+    )(lengths, queries, *pairs, own_slots, key_slots, bias, *context)
+
+
+def attention_back_call(micro, queries, context_grad, probs, packed, key_slots, shards, sums):
     heads, local, group = probs.shape
     double = packed.shape[1]
     proj = double // 2
     head_size = proj // heads
 
-    def kernel(query_ref, context_ref, prob_ref, packed_ref, key_ref, score_ref, dq_ref, *rest):
-        part_refs, sums = rest[:shards], rest[shards]
+    def kernel(query_ref, context_ref, prob_ref, packed_ref, key_ref, *rest):
+        score_ref, dq_ref, part_ref, sums = rest[-4:]
         per_block = 128 // head_size
         for head in range(heads):
             context, start = by_head(context_ref[...], head, head_size)
@@ -198,10 +194,10 @@
                 dq_ref[:, start : start + 128] = totals[0].astype(BF16)
                 sums[:, start : start + 128] = totals[1].astype(BF16)
                 sums[:, proj + start : proj + start + 128] = totals[2].astype(BF16)
-        for index, ref in enumerate(part_refs):
+        for index in range(shards):
             slots = key_ref[index * local : (index + 1) * local]
             pick = (lax.broadcasted_iota(jnp.int32, (local, group), 1) == slots).astype(BF16)
-            ref[...] = jnp.dot(pick, sums[...], preferred_element_type=F32).astype(BF16)
+            part_ref[index] = jnp.dot(pick, sums[...], preferred_element_type=F32).astype(BF16)
 
     return pl.pallas_call(
         kernel,
@@ -212,24 +208,22 @@
             pl.BlockSpec((heads, local, group), lambda i: (0, 0, 0)),
             pl.BlockSpec((group, double), lambda i: (0, 0)),
             pl.BlockSpec((group, 1), lambda i: (0, 0)),
-        ],
+        ]
+        + [ANY] * len(sums),
         out_specs=[
             pl.BlockSpec((heads, local, group), lambda i: (0, 0, 0)),
-            pl.BlockSpec((local, proj), lambda i: (0, 0)),
-        ]
-        + [pl.BlockSpec((local, double), lambda i: (0, 0))] * shards,
+            pl.BlockSpec((local, proj), lambda i: (micro, 0)),
+            pl.BlockSpec((shards, local, double), lambda i: (0, micro, 0)),
+        ],
         out_shape=[
             jax.ShapeDtypeStruct((heads, local, group), BF16),
-            jax.ShapeDtypeStruct((local, proj), BF16),
-        ]
-        + [jax.ShapeDtypeStruct((local, double), BF16)] * shards,
+            jax.ShapeDtypeStruct(queries.shape, BF16),
+            jax.ShapeDtypeStruct((shards, queries.shape[0], double), BF16),
+        ],
+        input_output_aliases={5 + i: 1 + i for i in range(len(sums))},
         scratch_shapes=[pltpu.VMEM((group, double), BF16)],
-        cost_estimate=pl.CostEstimate(
-            flops=2 * group * group * double + 16 * local * group * proj,
-            bytes_accessed=4 * group * double + 4 * heads * local * group,
-            transcendentals=0,
-        ),
-    )(queries, context_grad, probs, packed, key_slots)
+        cost_estimate=LIGHT,
+    )(queries, context_grad, probs, packed, key_slots, *sums)
 
 
 def axis_ranks():
@@ -250,10 +244,6 @@
     for copy in started:
         copy.start()
     return started
-
-
-ANY = pl.BlockSpec(memory_space=pl.ANY)
-VMEM = pl.BlockSpec(memory_space=pltpu.VMEM)
 
 
 def pick_kernel(gate_ref, up_ref, out_ref):
@@ -347,9 +337,7 @@
             pltpu.VMEM((4, width, proj), BF16),
             pltpu.SemaphoreType.DMA((moves + 1,)),
         ],
-        cost_estimate=pl.CostEstimate(
-            flops=6 * rows * width * proj, bytes_accessed=16 * width * proj, transcendentals=0
-        ),
+        cost_estimate=LIGHT,
     )(tokens, gain, *pieces)
 
 
@@ -384,7 +372,7 @@
                 if step is not None:
                     copies.append(
                         (
-                            small_ref.at[(rank - step) % lax.axis_size("shard")],
+                            small_ref.at[step],
                             ref.at[index + (pl.ds(size, small_rows),)],
                         )
                     )
@@ -400,9 +388,7 @@
             pltpu.VMEM((4, width, proj), BF16),
             pltpu.SemaphoreType.DMA((2 * moves + 1,)),
         ],
-        cost_estimate=pl.CostEstimate(
-            flops=6 * rows * width * proj, bytes_accessed=16 * width * proj, transcendentals=0
-        ),
+        cost_estimate=LIGHT,
     )(normed, query_grad, pair_grad, out_grads, small)
 
 
@@ -412,8 +398,8 @@
     return ref.at[pl.ds(row, count), pl.ds(0, columns)]
 
 
-def gate_up_call(own, other, inner, pieces, moves):
-    rows, width = own.shape
+def gate_up_call(own, other, width, inner, pieces, moves):
+    rows, wide = own.shape
     count, steps = len(pieces), len(moves)
     half = inner // 2
     tile = 256
@@ -438,9 +424,10 @@
 
         def step(index, carry):
             start = pl.multiple_of(index * tile, tile)
-            gate = jnp.dot(both[...], weights[:, pl.ds(start, tile)], preferred_element_type=F32)
+            left = both[:, :width]
+            gate = jnp.dot(left, weights[:, pl.ds(start, tile)], preferred_element_type=F32)
             up = jnp.dot(
-                both[...],
+                left,
                 weights[:, pl.ds(pl.multiple_of(half + start, tile), tile)],
                 preferred_element_type=F32,
             )
@@ -460,15 +447,11 @@
         out_specs=[VMEM, VMEM, VMEM, ANY],
         out_shape=[shape, shape, shape, jax.ShapeDtypeStruct((width, inner), BF16)],
         scratch_shapes=[
-            pltpu.VMEM((2 * rows, width), BF16),
+            pltpu.VMEM((2 * rows, wide), BF16),
             pltpu.VMEM((width, inner), BF16),
             pltpu.SemaphoreType.DMA((steps + 3,)),
         ],
-        cost_estimate=pl.CostEstimate(
-            flops=4 * rows * width * inner,
-            bytes_accessed=4 * width * inner + 6 * rows * inner,
-            transcendentals=rows * inner,
-        ),
+        cost_estimate=LIGHT,
     )(own, other, *pieces)
 
 
@@ -506,6 +489,8 @@
             other_ref[:, columns] = jnp.dot(
                 hidden_ref[rows:], weights[:, columns], preferred_element_type=F32
             ).astype(BF16)
+        if padded > width:
+            other_ref[:, width:] = jnp.zeros((rows, padded - width), BF16)
         keep.wait()
 
     return pl.pallas_call(
@@ -514,13 +499,11 @@
         out_specs=[VMEM, VMEM, ANY],
         out_shape=[
             jax.ShapeDtypeStruct((rows, width), F32),
-            jax.ShapeDtypeStruct((rows, width), BF16),
+            jax.ShapeDtypeStruct((rows, padded), BF16),
             jax.ShapeDtypeStruct((half, padded), BF16),
         ],
         scratch_shapes=[pltpu.VMEM((half, padded), BF16), pltpu.SemaphoreType.DMA((steps + 1,))],
-        cost_estimate=pl.CostEstimate(
-            flops=4 * rows * width * half, bytes_accessed=4 * width * half, transcendentals=0
-        ),
+        cost_estimate=LIGHT,
     )(hidden, *pieces)
 
 
@@ -560,7 +543,7 @@
                 ref[:, 2 * half * shard : 2 * half * (shard + 1)] = jnp.concatenate(
                     both, 1
                 ).astype(F32)
-        down_ref[...] = rows_of[:, :width].astype(F32)
+        down_ref[...] = rows_of[...].T[:width].astype(F32)
 
     return pl.pallas_call(
         kernel,
@@ -569,7 +552,7 @@
         out_shape=[
             jax.ShapeDtypeStruct((block, inner), F32),
             jax.ShapeDtypeStruct((block, inner), F32),
-            jax.ShapeDtypeStruct((down_rows, width), F32),
+            jax.ShapeDtypeStruct((width, down_rows), F32),
         ],
         scratch_shapes=[
             pltpu.VMEM((2, block, inner), BF16),
@@ -617,51 +600,268 @@
     half = down.shape[0]
     tile = 256
 
-    def kernel(own_ref, other_ref, down_ref, slope_ref, act_ref, out_ref, both, sems):
-        for copy in run_copies(
-            [(own_ref, both.at[:rows]), (other_ref, both.at[rows:])], sems
-        ):
-            copy.wait()
-
-        def step(index, carry):
-            start = pl.multiple_of(index * tile, tile)
-            upstream = lax.dot_general(
-                both[...],
-                down_ref[pl.ds(start, tile), :width],
-                (((1,), (1,)), ((), ())),
-                preferred_element_type=F32,
-            )
-            gate = upstream * slope_ref[:, pl.ds(start, tile)].astype(F32)
-            up = upstream * act_ref[:, pl.ds(start, tile)].astype(F32)
-            out_ref[:, pl.ds(start, tile)] = gate.astype(BF16)
-            out_ref[:, pl.ds(pl.multiple_of(half + start, tile), tile)] = up.astype(BF16)
-            return carry
-
-        lax.fori_loop(0, half // tile, step, 0)
-
+    def kernel(own_ref, other_ref, down_ref, slope_ref, act_ref, gate_ref, up_ref):
+        for index, ref in enumerate((own_ref, other_ref)):
+            part = slice(index * rows, (index + 1) * rows)
+            upstream = dot_last(ref[...], down_ref[...])
+            gate_ref[part] = (upstream * slope_ref[part].astype(F32)).astype(BF16)
+            up_ref[part] = (upstream * act_ref[part].astype(F32)).astype(BF16)
+
+    whole = pl.BlockSpec((rows, width), lambda i: (0, 0))
+    columns = pl.BlockSpec((2 * rows, tile), lambda i: (0, i))
+    shape = jax.ShapeDtypeStruct((2 * rows, half), BF16)
     return pl.pallas_call(
         kernel,
-        in_specs=[ANY, ANY, VMEM, VMEM, VMEM],
-        out_specs=VMEM,
-        out_shape=jax.ShapeDtypeStruct((2 * rows, 2 * half), BF16),
-        scratch_shapes=[pltpu.VMEM((2 * rows, width), BF16), pltpu.SemaphoreType.DMA((2,))],
-        cost_estimate=pl.CostEstimate(
-            flops=4 * rows * width * half,
-            bytes_accessed=2 * width * half + 16 * rows * half,
-            transcendentals=0,
-        ),
+        grid=(half // tile,),
+        in_specs=[
+            whole,
+            whole,
+            pl.BlockSpec((tile, down.shape[1]), lambda i: (i, 0)),
+            columns,
+            columns,
+        ],
+        out_specs=[columns, columns],
+        out_shape=[shape, shape],
+        cost_estimate=LIGHT,
     )(own, other, down, slope, act)
 
 
-def weight_grad_call(left, right, outputs):
+def normed_grad_call(gate, up, weights):
+    double, half = gate.shape
+    rows = double // 2
+    width = weights.shape[0]
+    tile = 256
+
+    def kernel(gate_ref, up_ref, low_ref, high_ref, own_ref, other_ref):
+        for index, ref in enumerate((own_ref, other_ref)):
+            part = slice(index * rows, (index + 1) * rows)
+            total = dot_last(gate_ref[part], low_ref[...]) + dot_last(up_ref[part], high_ref[...])
+            ref[...] = total.astype(ref.dtype)
+
+    whole = pl.BlockSpec((double, half), lambda i: (0, 0))
+    return pl.pallas_call(
+        kernel,
+        grid=(pl.cdiv(width, tile),),
+        in_specs=[
+            whole,
+            whole,
+            pl.BlockSpec((tile, half), lambda i: (i, 0)),
+            pl.BlockSpec((tile, half), lambda i: (i, 1)),
+        ],
+        out_specs=[pl.BlockSpec((rows, tile), lambda i: (0, i))] * 2,
+        out_shape=[
+            jax.ShapeDtypeStruct((rows, width), F32),
+            jax.ShapeDtypeStruct((rows, lane_tiles(width)), BF16),
+        ],
+        cost_estimate=LIGHT,
+    )(gate, up, weights, weights)
+
+
+def row_specs(micro_count, local, width):
+    return pl.BlockSpec((local, width), lambda i: (i, 0)), pl.BlockSpec((1, width), lambda i: (0, 0))
+
+
+def sum_rows(ref, value):
+    total = jnp.sum(value, axis=0, keepdims=True)
+
+    @pl.when(pl.program_id(0) == 0)
+    def _():
+        ref[...] = total
+
+    @pl.when(pl.program_id(0) > 0)
+    def _():
+        ref[...] += total
+
+
+def put_padded(ref, value):
+    width = value.shape[1]
+    ref[:, :width] = value.astype(BF16)
+    if ref.shape[1] > width:
+        ref[:, width:] = jnp.zeros((value.shape[0], ref.shape[1] - width), BF16)
+
+
+def lane_tiles(width):
+    return -(-width // 128) * 128
+
+
+def mid_call(tokens, context, w_out, gain, micro_count):
+    rows, width = tokens.shape
+    local = rows // micro_count
+    by_row, vector = row_specs(micro_count, local, width)
+
+    def kernel(token_ref, context_ref, out_ref, gain_ref, hidden_ref, normed_ref):
+        hidden = token_ref[...].astype(F32) + jnp.dot(
+            context_ref[...], out_ref[...], preferred_element_type=F32
+        )
+        hidden_ref[...] = hidden
+        put_padded(normed_ref, hidden * rms_scale(hidden) * gain_ref[...])
+
+    return pl.pallas_call(
+        kernel,
+        grid=(micro_count,),
+        in_specs=[
+            by_row,
+            pl.BlockSpec((local, context.shape[1]), lambda i: (i, 0)),
+            pl.BlockSpec(w_out.shape, lambda i: (0, 0)),
+            vector,
+        ],
+        out_specs=[by_row, pl.BlockSpec((local, lane_tiles(width)), lambda i: (i, 0))],
+        out_shape=[
+            jax.ShapeDtypeStruct((rows, width), F32),
+            jax.ShapeDtypeStruct((rows, lane_tiles(width)), BF16),
+        ],
+        cost_estimate=LIGHT,
+    )(tokens, context, w_out, gain)
+
+
+def out_call(hidden, part, given, cotangent, gate_cotangent, gain, vector_in, micro_count):
+    rows, width = hidden.shape
+    local = rows // micro_count
+    by_row, vector = row_specs(micro_count, local, width)
+    one = pl.BlockSpec((local, 1), lambda i: (i, 0))
+    turned = pl.BlockSpec((1, width, local), lambda i: (i, 0, 0))
+    padded = pl.BlockSpec((local, lane_tiles(width)), lambda i: (i, 0))
+
+    def kernel(
+        hidden_ref, part_ref, given_ref, up_ref, gate_ref, gain_ref, vector_ref,
+        state_ref, deleted_ref, grad_ref, low_ref, gain_grad_ref, vector_grad_ref,
+    ):
+        state = hidden_ref[...] + part_ref[...] + given_ref[:, :width].astype(F32)
+        state_ref[0] = state.T
+        scale = rms_scale(state)
+        normed = state * scale * gain_ref[...]
+        logit = jnp.sum(normed * vector_ref[...], axis=1, keepdims=True)
+        sigmoid = lax.logistic(logit)
+        deleted_ref[...] = -30.0 * sigmoid
+        slope = gate_ref[...] * -30.0 * sigmoid * (1.0 - sigmoid)
+        upstream = slope * vector_ref[...]
+        sum_rows(vector_grad_ref, slope * normed)
+        sum_rows(gain_grad_ref, upstream * state * scale)
+        grad = up_ref[...].astype(F32) + rms_back(state, scale, gain_ref[...], upstream)
+        grad_ref[...] = grad
+        put_padded(low_ref, grad)
+
+    return pl.pallas_call(
+        kernel,
+        grid=(micro_count,),
+        in_specs=[by_row, by_row, padded, by_row, one, vector, vector],
+        out_specs=[turned, one, by_row, padded, vector, vector],
+        out_shape=[
+            jax.ShapeDtypeStruct((micro_count, width, local), F32),
+            jax.ShapeDtypeStruct((rows, 1), F32),
+            jax.ShapeDtypeStruct((rows, width), F32),
+            jax.ShapeDtypeStruct((rows, lane_tiles(width)), BF16),
+            jax.ShapeDtypeStruct((1, width), F32),
+            jax.ShapeDtypeStruct((1, width), F32),
+        ],
+        cost_estimate=LIGHT,
+    )(hidden, part, given, cotangent, gate_cotangent, gain, vector_in)
+
+
+def back_call(part, given, grad_out, hidden, gain, context, w_out, micro_count):
+    rows, width = hidden.shape
+    local = rows // micro_count
+    proj = context.shape[1]
+    by_row, vector = row_specs(micro_count, local, width)
+    by_proj = pl.BlockSpec((local, proj), lambda i: (i, 0))
+    padded = pl.BlockSpec((local, lane_tiles(width)), lambda i: (i, 0))
+    whole = pl.BlockSpec((proj, width), lambda i: (0, 0))
+
+    def kernel(
+        part_ref, given_ref, grad_ref, hidden_ref, gain_ref, context_ref, out_ref,
+        mid_ref, context_grad_ref, out_grad_ref, gain_grad_ref, total,
+    ):
+        normed_grad = part_ref[...] + given_ref[:, :width].astype(F32)
+        hidden = hidden_ref[...]
+        scale = rms_scale(hidden)
+        sum_rows(gain_grad_ref, normed_grad * hidden * scale)
+        mid = grad_ref[...] + rms_back(hidden, scale, gain_ref[...], normed_grad)
+        mid_ref[...] = mid
+        low = mid.astype(BF16)
+        context_grad_ref[...] = dot_last(low, out_ref[...]).astype(BF16)
+        product = jnp.dot(context_ref[...].T, low, preferred_element_type=F32)
+        step = pl.program_id(0)
+
+        @pl.when(step == 0)
+        def _():
+            total[...] = product
+
+        @pl.when(step > 0)
+        def _():
+            total[...] += product
+
+        @pl.when(step == micro_count - 1)
+        def _():
+            out_grad_ref[...] = total[...].astype(BF16)
+
+    return pl.pallas_call(
+        kernel,
+        grid=(micro_count,),
+        in_specs=[by_row, padded, by_row, by_row, vector, by_proj, whole],
+        out_specs=[by_row, by_proj, whole, vector],
+        out_shape=[
+            jax.ShapeDtypeStruct((rows, width), F32),
+            jax.ShapeDtypeStruct((rows, proj), BF16),
+            jax.ShapeDtypeStruct((proj, width), BF16),
+            jax.ShapeDtypeStruct((1, width), F32),
+        ],
+        scratch_shapes=[pltpu.VMEM((proj, width), F32)],
+        cost_estimate=LIGHT,
+    )(part, given, grad_out, hidden, gain, context, w_out)
+
+
+def in_call(query_grad, pair_parts, weights, grad_mid, tokens, gain, micro_count):
+    rows, width = tokens.shape
+    local = rows // micro_count
+    proj = query_grad.shape[1]
+    count = pair_parts.shape[0]
+    by_row, vector = row_specs(micro_count, local, width)
+    by_proj = pl.BlockSpec((local, proj), lambda i: (i, 0))
+    by_pair = pl.BlockSpec((local, 2 * proj), lambda i: (i, 0))
+
+    def kernel(
+        query_ref, part_ref, wq_ref, wk_ref, wv_ref, mid_ref, token_ref, gain_ref,
+        pair_ref, grad_ref, gain_grad_ref,
+    ):
+        pair = sum(part_ref[index].astype(F32) for index in range(count)).astype(BF16)
+        pair_ref[...] = pair
+        normed_grad = (
+            dot_last(query_ref[...], wq_ref[0])
+            + dot_last(pair[:, :proj], wk_ref[0])
+            + dot_last(pair[:, proj:], wv_ref[0])
+        )
+        hidden = token_ref[...].astype(F32)
+        scale = rms_scale(hidden)
+        sum_rows(gain_grad_ref, normed_grad * hidden * scale)
+        grad = mid_ref[...] + rms_back(hidden, scale, gain_ref[...], normed_grad)
+        grad_ref[0] = grad.astype(BF16).T
+
+    return pl.pallas_call(
+        kernel,
+        grid=(micro_count,),
+        in_specs=[by_proj, pl.BlockSpec((count, local, 2 * proj), lambda i: (0, i, 0))]
+        + [pl.BlockSpec((1, width, proj), lambda i, m=m: (m, 0, 0)) for m in range(3)]
+        + [by_row, by_row, vector],
+        out_specs=[by_pair, pl.BlockSpec((1, width, local), lambda i: (i, 0, 0)), vector],
+        out_shape=[
+            jax.ShapeDtypeStruct((rows, 2 * proj), BF16),
+            jax.ShapeDtypeStruct((micro_count, width, local), BF16),
+            jax.ShapeDtypeStruct((1, width), F32),
+        ],
+        cost_estimate=LIGHT,
+    )(query_grad, pair_parts, weights, weights, weights, grad_mid, tokens, gain)
+
+
+def weight_grad_call(left, right, depth, width, outputs):
     left_own, left_other = left
     right_own, right_other = right
     rows = left_own.shape[0]
-    depth, width = left_own.shape[1], right_own.shape[1]
+    total = 2 * rows if left_other is not None else rows
+    beside = right_other is not None and right_own.shape[0] == total
+    right_width = right_own.shape[1] * (2 if beside else 1)
     count = len(outputs)
     copies_out = sum(len(moves) for _, moves in outputs)
     split = left_other is not None
-    total = 2 * rows if split else rows
     right_split = right_other is not None
     inputs = [left_own] + ([left_other] if split else []) + [right_own]
     inputs += [right_other] if right_split else []
@@ -671,11 +871,16 @@
         out_refs = refs[len(inputs) : len(inputs) + count]
         lefts, rights, result, sems = refs[len(inputs) + count :]
         copies = []
-        for target, parted in ((lefts, split), (rights, right_split)):
+        for target, parted, aside in ((lefts, split, False), (rights, right_split, beside)):
             first = in_refs.pop(0)
-            size = first.shape[0]
-            copies.append((first, target.at[:size]))
-            if parted:
+            size = first.shape[1] if aside else first.shape[0]
+            if not parted:
+                copies.append((first, target))
+            elif aside:
+                copies.append((first, target.at[:, :size]))
+                copies.append((in_refs.pop(0), target.at[:, size:]))
+            else:
+                copies.append((first, target.at[:size]))
                 copies.append((in_refs.pop(0), target.at[size:]))
         for copy in run_copies(copies, sems):
             copy.wait()
@@ -715,16 +920,12 @@
         out_specs=[ANY] * count,
         out_shape=[jax.ShapeDtypeStruct(shape, BF16) for shape, _ in outputs],
         scratch_shapes=[
-            pltpu.VMEM((total, depth), BF16),
-            pltpu.VMEM((total, width), BF16),
+            pltpu.VMEM((total, left_own.shape[1]), BF16),
+            pltpu.VMEM((total, right_width), BF16),
             pltpu.VMEM((depth, width), BF16),
             pltpu.SemaphoreType.DMA((max(4, copies_out),)),
         ],
-        cost_estimate=pl.CostEstimate(
-            flops=2 * total * depth * width,
-            bytes_accessed=2 * (depth * width + total * (depth + width)),
-            transcendentals=0,
-        ),
+        cost_estimate=LIGHT,
     )(*inputs)
 
 
@@ -921,11 +1122,12 @@
         lax.dynamic_slice_in_dim(down_own, chip * down_piece, down_piece, 0),
     )
     packed_own, stacked = tie(packed_own, stacked)
-    ring = [shift(packed_own)]
-    for step in range(2, shards):
-        ring.append(shift(ring[-1]))
     attn_plane = [stacked] + [swap(stacked, 2 * mask) for mask in range(1, chips)]
     attn_plane = jnp.stack(attn_plane)
+    ring = [packed_own, shift(packed_own)]
+    attn_plane, ring = tie(attn_plane, ring)
+    nears, rests = [None] * shards, [None] * shards
+    nears[1] = gather_near(ring[1])
     attn_other = swap(attn_plane, 1)
 
     def attn_place(mask, flip, step):
@@ -1005,29 +1207,41 @@
     bias = bias_of_queries(bias_rows, own_slots.reshape(rows), group)
     first_len = seq_lengths[:, 0, 0]
 
-    hidden_in = tokens.reshape(rows, width).astype(F32)
-    scale_one = rms_scale(hidden_in)
+    token_rows = tokens.reshape(rows, width)
     normed_one, queries, own_pairs, attn_full = project_call(
-        tokens.reshape(rows, width), attn_gain[None], attn_pieces, attn_places, block, proj
+        token_rows, attn_gain[None], attn_pieces, attn_places, block, proj
     )
-    query_full, key_full, value_full = attn_full[0], attn_full[1], attn_full[2]
     out_full = attn_full[3].reshape(proj, width)
 
-    nears, rests = [], []
-    ring[0], attn_plane = tie(ring[0], attn_plane)
-    for step in range(1, shards):
-        nears.append(gather_near(ring[step - 1]))
-        rests.append(gather_rest(nears[-1]))
-        if step < shards - 1:
-            ring[step], rests = tie(ring[step], rests)
-    own_pairs, (ring, nears[0]) = tie(own_pairs, (ring, nears[0]))
+    for step in range(2, shards - 1):
+        ring.append(shift(ring[-1]))
+    own_pairs, ring = tie(own_pairs, ring)
+    early = (
+        out_full,
+        jnp.pad(down_own, ((0, 0), (0, padded - width))),
+        cotangent.reshape(rows, width),
+        gate_cotangent.reshape(rows, 1).astype(F32),
+        [value[None] for value in (ffn_gain, delete_gain, delete_vec)],
+        [slots[micro].reshape(group, 1) for micro in range(micro_count)],
+    )
     pairs = [own_pairs]
     for step in range(1, shards):
         pairs.append(shift(pairs[-1]))
-    pairs, (nears, rests[:-1]) = tie(pairs, (nears, rests[:-1]))
-    contexts, probs, packed = [], [], []
+        if step == 1:
+            pairs[-1], (nears[1], bias) = tie(pairs[-1], (nears[1], bias))
+            rests[1] = gather_rest(nears[1])
+        if step == 2:
+            pairs[-1], (rests[1], early) = tie(pairs[-1], (rests[1], early))
+            ring[2], rests[1] = tie(ring[2], rests[1])
+            nears[2] = gather_near(ring[2])
+    ring[-1], pairs[-1] = tie(ring[-1], pairs[-1])
+    last = shift(ring[-1][:block])
+    context, probs, packed = [], [], []
     for micro in range(micro_count):
-        context, prob, pair = attention_call(
+        if micro == micro_count - 1:
+            context, nears[2] = tie(context, nears[2])
+            rests[2] = gather_rest(nears[2])
+        *context, prob, pair = attention_call(
             micro,
             first_len[micro : micro + 1],
             queries,
@@ -1035,17 +1249,28 @@
             own_slots.reshape(rows, 1),
             key_slots[micro : micro + 1],
             bias,
+            context,
         )
-        contexts.append(context)
         probs.append(prob)
         packed.append(pair)
-    context = jnp.concatenate(contexts)
-    hidden_mid = hidden_in + dot(context, out_full)
-
-    scale_two = rms_scale(hidden_mid)
-    normed_two = (hidden_mid * scale_two * ffn_gain).astype(BF16)
+    for step in range(3, shards - 1):
+        ring[step], rests[step - 1] = tie(ring[step], rests[step - 1])
+        nears[step] = gather_near(ring[step])
+        rests[step] = gather_rest(nears[step])
+    context, (last, rests[shards - 2]) = tie(context, (last, rests[shards - 2]))
+    last_near = gather_near(last)
+    last_down = shift(ring[-1][block:])
+    (context,) = context
+    out_full, down_wide, cotangent_rows, gate_rows, gains, key_columns = early
+    ffn_gain, delete_gain, delete_vec = gains
+
+    hidden_mid, normed_two = mid_call(token_rows, context, out_full, ffn_gain, micro_count)
+    normed_two, (last_near, last_down) = tie(normed_two, (last_near, last_down))
+    last_rest = gather_rest(last_near)
     normed_two_other = swap(normed_two, 1)
-    pieces = [gate_up_own, jnp.pad(down_own, ((0, 0), (0, padded - width)))]
+    normed_two_other, (last_rest, last_down) = tie(normed_two_other, (last_rest, last_down))
+    last_down_found = [(mask, 0, swap(last_down, 2 * mask)) for mask in range(1, chips)]
+    pieces = [gate_up_own, down_wide]
     gate_up_moves = [(0, 0, block, inner, lambda at, chip_at: (pl.multiple_of(at * block, 16), 0))]
     down_moves = [
         (1, 0, down_half, padded, lambda at, chip_at: (pl.multiple_of(at * down_half, 16), 0))
@@ -1063,9 +1288,14 @@
             part * col_piece,
         )
 
-    for step in range(1, shards):
-        for mask, start, array in gather_list(ring[step - 1], nears[step - 1], rests[step - 1]):
-            for part, here, there, size in overlaps(start, array.shape[0]):
+    arrived = [
+        (step, 0, gather_list(ring[step], nears[step], rests[step])) for step in range(1, shards - 1)
+    ]
+    arrived.append((shards - 1, 0, gather_list(last, last_near, last_rest)))
+    arrived.append((shards - 1, block, [(0, 0, last_down)] + last_down_found))
+    for step, below, found in arrived:
+        for mask, start, array in found:
+            for part, here, there, size in overlaps(below + start, array.shape[0]):
                 if part is None:
                     gate_up_moves.append(
                         (len(pieces), here, size, col_piece, gate_up_place(step, mask, there))
@@ -1096,50 +1326,48 @@
         ]
         gate_up_moves = [(0, 0, width, inner, lambda at, chip_at: (0, 0))]
         down_moves = [(1, 0, half_inner, padded, lambda at, chip_at: (0, 0))]
+    gate_up_pieces, gate_up_moves = used_by(pieces, gate_up_moves)
+    down_pieces, down_moves = used_by(pieces, down_moves)
     gate_slope_act, gate_act, inner_act, gate_up = gate_up_call(
-        normed_two, normed_two_other, inner, pieces, gate_up_moves
+        normed_two, normed_two_other, width, inner, gate_up_pieces, gate_up_moves
     )
-    down_part, down_given, down = down_call(inner_act, width, padded, pieces, down_moves)
-    hidden_out = hidden_mid + down_part + swap(down_given, 1).astype(F32)
-    scale_three = rms_scale(hidden_out)
-    delete_norm = hidden_out * scale_three * delete_gain
-    sigmoid_val = jax.nn.sigmoid(jnp.sum(delete_norm * delete_vec, axis=-1))
-    deleted = -30.0 * sigmoid_val
-
-    gate_upstream = gate_cotangent.reshape(rows).astype(F32)
-    gate_slope = gate_upstream * -30.0 * sigmoid_val * (1.0 - sigmoid_val)
-    grad_delete_vec = jnp.sum(gate_slope[:, None] * delete_norm, axis=0)
-    delete_up = gate_slope[:, None] * delete_vec
-    grad_delete_gain = jnp.sum(delete_up * hidden_out * scale_three, axis=0)
-    grad_out = cotangent.reshape(rows, width).astype(F32) + rms_back(
-        hidden_out, scale_three, delete_gain, delete_up
+    down_part, down_given, down = down_call(inner_act, width, padded, down_pieces, down_moves)
+    hidden_out, deleted, grad_out, down_up, grad_delete_gain, grad_delete_vec = out_call(
+        hidden_mid,
+        down_part,
+        swap(down_given, 1),
+        cotangent_rows,
+        gate_rows,
+        delete_gain,
+        delete_vec,
+        micro_count,
     )
-    down_up = grad_out.astype(BF16)
+
     down_up_other = swap(down_up, 1)
 
-    def reduce_plan(piece_rows, piece_columns, place, groups):
-        middle = cut(piece_rows)
-        spans = {"own": (0, piece_rows), "near": (0, piece_rows), "far": (0, piece_rows)}
-        spans["top"], spans["low"] = (0, middle), (middle, piece_rows - middle)
+    def reduce_plan(groups, piece_columns, place):
         plan = []
-        for steps in groups:
+        for first, size in groups:
+            middle = cut(size)
+            spans = {"own": (0, size), "near": (0, size), "far": (0, size)}
+            spans["top"], spans["low"] = (0, middle), (middle, size - middle)
             for base in bases:
                 for name in used:
-                    start, size = spans[name]
+                    start, count = spans[name]
                     moves = [
-                        (index, place(step % shards, base ^ names[name], start))
-                        for index, step in enumerate(steps)
+                        (index, place(index, base ^ names[name], first + start))
+                        for index in range(shards)
                     ]
-                    plan.append(((len(moves), size, piece_columns), moves))
+                    plan.append(((shards, count, piece_columns), moves))
         return plan
 
-    def reduce_run(plan, left, right):
+    def reduce_run(plan, left, right, left_width, right_width):
         if aligned:
-            buffers = weight_grad_call(left, right, plan)
+            buffers = weight_grad_call(left, right, left_width, right_width, plan)
         else:
-            shape = (left[0].shape[1], right[0].shape[1])
+            shape = (left_width, right_width)
             whole = weight_grad_call(
-                left, right, [((1,) + shape, [(0, lambda at, chip_at: (0, 0))])]
+                left, right, left_width, right_width, [((1,) + shape, [(0, lambda at, chip_at: (0, 0))])]
             )[0][0]
             buffers = []
             for (_, size, columns), moves in plan:
@@ -1161,97 +1389,94 @@
             for i, base in enumerate(bases)
         }
 
-    all_steps = [range(1, shards + 1)]
-    two_steps = [range(1, shards // 2 + 1), range(shards // 2 + 1, shards + 1)]
-
-    def send_blocks(state, steps):
-        sent = []
-        for index, step in enumerate(steps):
-            total = reduce_end([value[index] for value in state])
-            sent.append(shift(total, -step) if step < shards else total)
-        return sent
-
-    def down_grad_place(step, mask, start):
-        return tile_hint(
-            lambda at, chip_at: (
-                (at - step) % shards * down_half + (chip_at ^ mask) * down_piece + start,
-                0,
-            ),
-            16,
-            128,
-        ) if aligned else lambda at, chip_at: (
-            (at - step) % shards * down_half + (chip_at ^ mask) * down_piece + start,
+    def exchange(value):
+        return lax.all_to_all(value, "shard", split_axis=0, concat_axis=0, tiled=True)
+
+    def total_of(arrived):
+        return jnp.sum(arrived.astype(F32), axis=0).astype(BF16)
+
+    def down_grad_place(index, mask, start):
+        plain = lambda at, chip_at: (
+            index * down_half + (chip_at ^ mask) * down_piece + start,
             0,
         )
-
-    def gate_up_grad_place(step, mask, start):
-        plain = lambda at, chip_at: (
-            (at - step) % shards * block + start,
-            (chip_at ^ mask) * col_piece,
-        )
         return tile_hint(plain, 16, 128) if aligned else plain
 
+    def gate_up_grad_place(index, mask, start):
+        plain = lambda at, chip_at: (index * block + start, (chip_at ^ mask) * col_piece)
+        return tile_hint(plain, 16, 128) if aligned else plain
+
     down_buffers = reduce_run(
-        reduce_plan(down_piece, width, down_grad_place, all_steps),
+        reduce_plan([(0, down_piece)], width, down_grad_place),
         (inner_act, None),
         (down_up, down_up_other),
+        half_inner,
+        width,
     )
     down_state = reduce_begin(group_parts(down_buffers, 0, 1), 1)
-    both_grad = hidden_grad_call(down_up, down_up_other, down, gate_slope_act, gate_act)
-    both_grad, down_state = tie(both_grad, down_state)
+    gate_grad, up_grad = hidden_grad_call(down_up, down_up_other, down, gate_slope_act, gate_act)
+    gate_grad, down_state = tie(gate_grad, down_state)
     gate_up_buffers = reduce_run(
-        reduce_plan(block, col_piece, gate_up_grad_place, two_steps),
+        reduce_plan([(0, cut(block)), (cut(block), block - cut(block))], col_piece, gate_up_grad_place),
         (normed_two, normed_two_other),
-        (both_grad, None),
+        (gate_grad, up_grad),
+        width,
+        inner,
     )
     down_state = reduce_middle(down_state, 1)
-    partial = jnp.einsum("tf,df->td", both_grad, gate_up, preferred_element_type=F32)
+    gate_grad, (gate_up_buffers, down_state) = tie(gate_grad, (gate_up_buffers, down_state))
     gate_up_state = reduce_begin(group_parts(gate_up_buffers, 0, 2), 1)
-    partial_given = swap(partial[rows:].astype(BF16), 1)
-    partial_given, down_state = tie(partial_given, down_state)
-    normed_two_grad = partial[:rows] + partial_given.astype(F32)
-    grad_ffn_gain = jnp.sum(normed_two_grad * hidden_mid * scale_two, axis=0)
-    grad_mid = grad_out + rms_back(hidden_mid, scale_two, ffn_gain, normed_two_grad)
-    out_grad = grad_mid.astype(BF16)
-    grad_w_out = jnp.einsum("th,td->hd", context, out_grad, preferred_element_type=F32)
-    context_grad = jnp.einsum("td,hd->th", out_grad, out_full, preferred_element_type=F32)
-    context_grad = context_grad.astype(BF16)
-    down_sent = send_blocks(down_state, all_steps[0])
-    context_grad, gate_up_state = tie(context_grad, gate_up_state)
+    normed_part, normed_given = normed_grad_call(gate_grad, up_grad, gate_up)
+    normed_given, gate_up_state = tie(normed_given, gate_up_state)
     gate_up_state = reduce_middle(gate_up_state, 1)
-    score_grads, query_grads, pair_parts = [], [], []
+    normed_given = swap(normed_given, 1)
+    down_arrived = exchange(reduce_end(down_state))
+    grad_mid, context_grad, grad_w_out, grad_ffn_gain = back_call(
+        normed_part,
+        normed_given,
+        grad_out,
+        hidden_mid,
+        ffn_gain,
+        context,
+        out_full,
+        micro_count,
+    )
+    score_grads, sums = [], []
     for micro in range(micro_count):
-        score_grad, query_grad, *parts = attention_back_call(
+        score_grad, *sums = attention_back_call(
             micro,
             queries,
             context_grad,
             probs[micro],
             packed[micro],
-            key_slots[micro].reshape(group, 1),
+            key_columns[micro],
             shards,
+            sums,
         )
         score_grads.append(score_grad)
-        query_grads.append(query_grad)
-        pair_parts.append(parts)
-    pair_parts = [jnp.concatenate(parts) for parts in zip(*pair_parts)]
-    pair_parts, down_sent = tie(pair_parts, down_sent)
-    pair_sent = [shift(pair_parts[step], -step) for step in range(1, shards)]
-    pair_sent, gate_up_state = tie(pair_sent, gate_up_state)
-    gate_up_later = reduce_begin(group_parts(gate_up_buffers, 1, 2), 1)
-    gate_up_sent = send_blocks(gate_up_state, two_steps[0])
-    pair_sum = add(pair_parts[0], *pair_sent)
-    down_sum = add(*down_sent)
-    query_grad = jnp.concatenate(query_grads)
+    query_grad, pair_parts = sums
+    gate_up_parts = group_parts(gate_up_buffers, 1, 2)
+    pair_parts, gate_up_state = tie(pair_parts, gate_up_state)
+    pair_arrived = exchange(pair_parts)
+    gate_up_parts, gate_up_state = tie(gate_up_parts, gate_up_state)
+    gate_up_later = reduce_begin(gate_up_parts, 1)
     grad_bias_rows = bias_fold(score_grads, own_slots.reshape(rows))
     grad_bias = jnp.einsum("ob,ho->bh", onehot, grad_bias_rows, precision=HIGHEST)
-
-    normed_one_grad = (
-        jnp.einsum("th,dh->td", query_grad, query_full, preferred_element_type=F32)
-        + jnp.einsum("th,dh->td", pair_sum[:, :proj], key_full, preferred_element_type=F32)
-        + jnp.einsum("th,dh->td", pair_sum[:, proj:], value_full, preferred_element_type=F32)
+    out_grads = grad_w_out.reshape(width, proj)
+    gate_up_later, (grad_bias, out_grads) = tie(gate_up_later, (grad_bias, out_grads))
+    gate_up_later = reduce_middle(gate_up_later, 1)
+    pair_arrived, (gate_up_later, down_arrived) = tie(pair_arrived, (gate_up_later, down_arrived))
+    gate_up_arrived = exchange(reduce_end(gate_up_state))
+    down_sum = total_of(down_arrived)
+    pair_sum, grad_in, grad_attn_gain = in_call(
+        query_grad,
+        pair_arrived,
+        attn_full,
+        grad_mid,
+        token_rows,
+        attn_gain[None],
+        micro_count,
     )
-    grad_attn_gain = jnp.sum(normed_one_grad * hidden_in * scale_one, axis=0)
-    grad_in = grad_mid + rms_back(hidden_in, scale_one, attn_gain, normed_one_grad)
 
     small = jnp.concatenate(
         [
@@ -1266,14 +1491,21 @@
     small = jnp.pad(small, ((0, 0), (0, pack_rows * proj - small.shape[1])))
     small = small.reshape(shards, pack_rows, proj)
 
-    out_grads = grad_w_out.astype(BF16).reshape(width, proj)
+    def attn_grad_place(mask, flip, index):
+        def place(at, rep):
+            owner = rep ^ (2 * mask + flip)
+            row = index * block + part_row(owner % per_matrix)
+            return owner // per_matrix, pl.multiple_of(row, 16) if aligned else row
+
+        return place
+
     attn_plan = [
         (
             (chips, shards, attn_rows + pack_rows, proj),
             [
-                ((mask, step), attn_place(mask, flip, step), step)
+                ((mask, index), attn_grad_place(mask, flip, index), index)
                 for mask in range(chips)
-                for step in range(shards)
+                for index in range(shards)
             ],
         )
         for flip in range(2)
@@ -1300,30 +1532,29 @@
                             lax.dynamic_slice(
                                 whole, where(rank, rep_rank) + (0,), (1, attn_rows, proj)
                             )[0],
-                            lax.dynamic_index_in_dim(small, source(step), 0, keepdims=False),
+                            small[index],
                         ]
                     )
-                    for _, where, step in items
+                    for _, where, index in items
                 ]
             ).reshape(shape)
             for shape, items in attn_plan
         ]
     given = swap(given, 1)
-    given, gate_up_later = tie(given, gate_up_later)
-    gate_up_later = reduce_middle(gate_up_later, 1)
     attn_own_sum = add(kept[0], given[0])
     attn_send = [add(kept[mask], given[mask]) for mask in range(1, chips)]
-    attn_send, (gate_up_later, gate_up_sent) = tie(attn_send, (gate_up_later, gate_up_sent))
     attn_found = [swap(part, 2 * mask + 2) for mask, part in enumerate(attn_send)]
-    gate_up_sent = gate_up_sent + send_blocks(gate_up_later, two_steps[1])
+    gate_up_rest = exchange(reduce_end(gate_up_later))
     attn_sum = add(attn_own_sum, *attn_found)
-    attn_sum = add(attn_sum[0], *[shift(attn_sum[step], -step) for step in range(1, shards)])
-    gate_up_sum = add(*gate_up_sent)
+    attn_sum = total_of(exchange(attn_sum))
+    gate_up_sum = jnp.concatenate([total_of(gate_up_arrived), total_of(gate_up_rest)])
     total = attn_sum[attn_rows:].astype(F32).reshape(-1)
     attn_sum = attn_sum[:attn_rows]
 
     packed_sum = pack(gate_up_sum, down_sum)
-    found = plane_gather(packed_sum)
+    near = gather_near(packed_sum)
+    attn_sum, near = tie(attn_sum, near)
+    found = gather_list(packed_sum, near, gather_rest(near))
     pieces, gate_up_moves, down_moves = [], [], []
 
     def gate_up_to(flip, mask, row):
@@ -1362,6 +1593,7 @@
         grad_gate, grad_up, grad_down_out = finish_call(
             pieces, gate_up_moves, down_moves, block, inner, down_block, width, padded
         )
+        grad_down_out = grad_down_out.T
     else:
         halves = jnp.zeros((2, block, inner), BF16)
         for piece, row, size, columns, place in gate_up_moves:
@@ -1400,9 +1632,9 @@
         attn_shard = attn_shard.astype(F32)
 
     return (
-        hidden_out.reshape(micro_count, local_rows, width),
+        jnp.swapaxes(hidden_out, 1, 2),
         deleted.reshape(micro_count, local_rows),
-        grad_in.astype(BF16).reshape(micro_count, local_rows, width),
+        jnp.swapaxes(grad_in, 1, 2),
         total[:block],
         attn_shard[0],
         attn_shard[1],
@@ -1416,6 +1648,11 @@
         total[2 * block : 3 * block],
         total[3 * block : 4 * block],
     )
+
+
+def used_by(pieces, moves):
+    wanted = sorted({move[0] for move in moves})
+    return [pieces[i] for i in wanted], [(wanted.index(move[0]),) + move[1:] for move in moves]
 
 
 def tile_hint(place, row_unit, column_unit):

time: 677 us -> 594 us (0.88)
  waiting for transfers between devices: 267 us -> 181 us
  Pallas kernels: 154 us -> 204 us
  local copies, waits for them, and re-layouts: 105 us -> 67 us
  matrix products: 26.5 us -> 1.32 us
  blocking collectives: 0 us -> 18.9 us
  other arithmetic: 49 us -> 37.3 us
    ppermute x21 -> x10, waiting for transfers between devices: 129 us -> 47.5 us  [shift(): lax.ppermute(value, 'shard', [(i, (i + by) % shards) for i in range(shard...]
    ppermute x49 -> x52, waiting for transfers between devices: 138 us -> 75.5 us  [swap(): return lax.ppermute(value, 'rep', [(i, i ^ mask) for i in range(reps)])]
    all_to_all x0 -> x4, waiting for transfers between devices: none -> 57.9 us  [exchange(): lax.all_to_all(value, 'shard', split_axis=0, concat_axis=0, tiled=True)]
    pallas_call x1 -> x6, Pallas kernels: 14.2 us -> 55.1 us  [the longest x1 13.9 us: normed_grad_call(): pl.pallas_call(kernel, grid=(pl.cdiv(width, tile),), in_specs=[whole, who...]
    dot_general x7 -> x0, matrix products: 25.3 us -> none  [the longest x1 11.2 us: on_device(): jnp.einsum('tf,df->td', both_grad, gate_up, preferred_element_type=F32)]
    all_to_all x0 -> x1, blocking collectives: none -> 18.9 us  [exchange(): lax.all_to_all(value, 'shard', split_axis=0, concat_axis=0, tiled=True)]
    all_to_all x0 -> x4, starting transfers between devices: none -> 17.6 us  [exchange(): lax.all_to_all(value, 'shard', split_axis=0, concat_axis=0, tiled=True)]
    ppermute x21 -> x10, starting transfers between devices: 23.5 us -> 8.44 us  [shift(): lax.ppermute(value, 'shard', [(i, (i + by) % shards) for i in range(shard...]
  transfers between devices with their start and end apart: 70 -> 66, of which waited for: 26 -> 26; matrix products, arithmetic and copies ran while one was open for 17% -> 15% of each run, Pallas kernels for 12% -> 28%
where the time goes in v4:
time: 594 us; the launch traced here: 583 us
  Pallas kernels  204 us (34%)
  waiting for transfers between devices  181 us (30%)
  starting transfers between devices  71.3 us (12%)
  local copies, waits for them, and re-layouts  67 us (11%)
  other arithmetic  37.3 us (6%)
  blocking collectives  18.9 us (3%)
    ppermute x52, waiting for transfers between devices, swap(): return lax.ppermute(value, 'rep', [(i, i ^ mask) for i in range(reps)])  75.5 us
    all_to_all x4, waiting for transfers between devices, exchange(): lax.all_to_all(value, 'shard', split_axis=0, concat_axis=0, tiled=True)  57.9 us
    ppermute x10, waiting for transfers between devices, shift(): lax.ppermute(value, 'shard', [(i, (i + by) % shards) for i in range(shard...  47.5 us
    ppermute x52, starting transfers between devices, swap(): return lax.ppermute(value, 'rep', [(i, i ^ mask) for i in range(reps)])  45.2 us
    pallas_call x2, Pallas kernels, weight_grad_call(): pl.pallas_call(kernel, in_specs=[ANY] * len(inputs), out_specs=[ANY] * co...  41.7 us
    pallas_call x1, Pallas kernels, gate_up_call(): pl.pallas_call(kernel, in_specs=[ANY] * (2 + count), out_specs=[VMEM, VME...  20.3 us
    convert_element_type x11, other arithmetic, add(): return sum((value.astype(F32) for value in values)).astype(BF16)  19.9 us
    all_to_all x1, blocking collectives, exchange(): lax.all_to_all(value, 'shard', split_axis=0, concat_axis=0, tiled=True)  18.9 us
  transfers between devices with their start and end apart: 66, of which 26 were waited for; matrix products, arithmetic and copies ran while one was open for 15% of the time, Pallas kernels for 28%

profile of v4, /device:TPU:0, one launch (start us, length us, event | category | flops | bytes accessed | tf_op | source)
XLA Modules:
  0.0 582.8 jit_solution(8129295173873848624)
XLA Ops:
  7.7 5.0 collective-permute-start.2
  14.2 5.3 shard_map.289.rest_0_
  22.7 4.0 collective-permute-done.1
  36.9 9.1 %collective-permute-done.5 = bf16[3,192,384]{2,1,0:T(8,128)(2,1)S(1)} collective-permute-done((bf16[3,192,384]{2,1,0:T(8,128)(2,1)S(1)}, bf16[3,192,384]{2,1,0:T(8,128)(2,1)S(1)}, u32[]{:S(2)}, u32[]{:S(2)}) %collective-permute-start.5) | collective-permute-done | bytes 442400 | tf_op jit(solution)/shard_map/ppermute | solution.py:979
  46.1 7.9 %collective-permute-done.4 = bf16[3,192,384]{2,1,0:T(8,128)(2,1)S(1)} collective-permute-done((bf16[3,192,384]{2,1,0:T(8,128)(2,1)S(1)}, bf16[3,192,384]{2,1,0:T(8,128)(2,1)S(1)}, u32[]{:S(2)}, u32[]{:S(2)}) %collective-permute-start.4) | collective-permute-done | bytes 442400 | tf_op jit(solution)/shard_map/ppermute | solution.py:979
  60.9 7.5 %shard_map.290 = (bf16[384,1472]{1,0:T(8,128)(2,1)}, bf16[384,384]{1,0:T(8,128)(2,1)}, bf16[384,768]{1,0:T(8,128)(2,1)}, bf16[4,1472,384]{2,1,0:T(8,128)(2,1)}) custom-call(bf16[384,1472]{1,0:T(8,128)(2,1)} %bitcast.83, f32[1,1472]{1,0:T(1,128)} %reshape.272.gain_ref, bf16[368,384]{1,0:T(8,128)(2,1)} %rest_0_.1, bf16[368,384]{1,0:T(8,128)(2,1)} %rest_1_.1, ...), custom_call_target="tpu_custom_call" | custom-call | flops 1000 | bytes 1000 | tf_op jit(solution)/shard_map/pallas_call | solution.py:326
  68.4 15.8 %collective-permute-done.8.rest_6_.rest_5_ = bf16[592,896]{1,0:T(8,128)(2,1)} collective-permute-done((bf16[592,896]{1,0:T(8,128)(2,1)}, bf16[592,896]{1,0:T(8,128)(2,1)}, u32[]{:S(2)}, u32[]{:S(2)}) %collective-permute-start.8) | collective-permute-done | bytes 1060896 | tf_op jit(solution)/shard_map/ppermute | solution.py:982
  86.8 5.4 shard_map.291.rest_6_
  92.2 8.9 %collective-permute-done.9.rest_1_ = bf16[384,768]{1,0:T(8,128)(2,1)S(1)} collective-permute-done((bf16[384,768]{1,0:T(8,128)(2,1)}, bf16[384,768]{1,0:T(8,128)(2,1)S(1)}, u32[]{:S(2)}, u32[]{:S(2)}) %collective-permute-start.9) | collective-permute-done | bytes 589856 | tf_op jit(solution)/shard_map/ppermute | solution.py:982
  122.9 14.3 %collective-permute-done.15.rest_3_ = bf16[384,768]{1,0:T(8,128)(2,1)S(1)} collective-permute-done((bf16[384,768]{1,0:T(8,128)(2,1)}, bf16[384,768]{1,0:T(8,128)(2,1)S(1)}, u32[]{:S(2)}, u32[]{:S(2)}) %collective-permute-start.15) | collective-permute-done | bytes 589856 | tf_op jit(solution)/shard_map/ppermute | solution.py:982
  140.8 5.4 shard_map.292
  146.2 5.4 shard_map.293
  154.4 5.4 shard_map.294
  159.8 5.3 collective-permute-done.19.rest_9_
  168.8 4.8 shard_map.295
  173.6 4.6 collective-permute-done.23.rest_9_
  182.6 8.2 %collective-permute-done.25.rest_14_ = bf16[176,896]{1,0:T(8,128)(2,1)S(1)} collective-permute-done((bf16[176,896]{1,0:T(8,128)(2,1)S(1)}, bf16[176,896]{1,0:T(8,128)(2,1)S(1)}, u32[]{:S(2)}, u32[]{:S(2)}) %collective-permute-start.25) | collective-permute-done | bytes 315424 | tf_op jit(solution)/shard_map/ppermute | solution.py:979
  195.1 20.3 %shard_map.296 = (bf16[768,1792]{1,0:T(8,128)(2,1)}, bf16[768,1792]{1,0:T(8,128)(2,1)}, bf16[768,1792]{1,0:T(8,128)(2,1)}, bf16[1472,3584]{1,0:T(8,128)(2,1)}) custom-call(bf16[384,1536]{1,0:T(8,128)(2,1)} %get-tuple-element.215.own_ref.refs_0_, bf16[384,1536]{1,0:T(8,128)(2,1)} %copy-done.10, bf16[368,3584]{1,0:T(8,128)(2,1)} %shard_map.289.rest_0_, ...), custom_call_target="tpu_custom_call" | custom-call | flops 1000 | bytes 1000 | tf_op jit(solution)/shard_map/pallas_call | solution.py:444
  216.4 10.8 %shard_map.297 = (f32[384,1472]{1,0:T(8,128)}, bf16[384,1536]{1,0:T(8,128)(2,1)}, bf16[1792,1536]{1,0:T(8,128)(2,1)}) custom-call(bf16[768,1792]{1,0:T(8,128)(2,1)} %get-tuple-element.227.hidden_ref.refs_0_, bf16[448,1536]{1,0:T(8,128)(2,1)} %pad.30.rest_0_, bf16[592,896]{1,0:T(8,128)(2,1)} %collective-permute-done.6.rest_1_, ...), custom_call_target="tpu_custom_call" | custom-call | flops 1000 | bytes 1000 | tf_op jit(solution)/shard_map/pallas_call | solution.py:496
  231.3 7.7 %shard_map.298 = (f32[3,1472,128]{2,1,0:T(8,128)}, f32[384,1]{1,0:T(8,128)}, f32[384,1472]{1,0:T(8,128)}, bf16[384,1536]{1,0:T(8,128)(2,1)}, f32[1,1472]{1,0:T(1,128)}, /*index=5*/f32[1,1472]{1,0:T(1,128)}) custom-call(f32[384,1472]{1,0:T(8,128)} %get-tuple-element.212.hidden_ref, f32[384,1472]{1,0:T(8,128)} %get-tuple-element.230.part_ref, ...), custom_call_target="tpu_custom_call" | custom-call | flops 1000 | bytes 1000 | tf_op jit(solution)/shard_map/pallas_call | solution.py:744
  243.2 9.5 %shard_map.300 = (bf16[4,112,1472]{2,1,0:T(8,128)(2,1)}, bf16[4,112,1472]{2,1,0:T(8,128)(2,1)}, bf16[4,112,1472]{2,1,0:T(8,128)(2,1)}, bf16[4,48,1472]{2,1,0:T(8,128)(2,1)}, bf16[4,64,1472]{2,1,0:T(8,128)(2,1)}) custom-call(bf16[768,1792]{1,0:T(8,128)(2,1)} %get-tuple-element.227.hidden_ref.refs_0_, bf16[384,1536]{1,0:T(8,128)(2,1)} %get-tuple-element.238.own_ref.refs_1_, ...), custom_call_target="tpu_custom_call" | custom-call | flops 1000 | bytes 1000 | tf_op jit(solution)/shard_map/pallas_call | solution.py:917
  255.2 11.7 %shard_map.299 = (bf16[768,1792]{1,0:T(8,128)(2,1)}, bf16[768,1792]{1,0:T(8,128)(2,1)}) custom-call(bf16[384,1536]{1,0:T(8,128)(2,1)} %get-tuple-element.238.own_ref.refs_1_, bf16[384,1536]{1,0:T(8,128)(2,1)} %copy-done.9, bf16[1792,1536]{1,0:T(8,128)(2,1)} %get-tuple-element.239.down_ref, bf16[768,1792]{1,0:T(8,128)(2,1)} %get-tuple-element.240.slope_ref, ...), custom_call_target="tpu_custom_call" | custom-call | flops 1000 | bytes 1000 | tf_op jit(solution)/shard_map/pallas_call | solution.py:613
  279.9 32.3 %shard_map.301 = (bf16[4,176,896]{2,1,0:T(8,128)(2,1)}, bf16[4,176,896]{2,1,0:T(8,128)(2,1)}, bf16[4,176,896]{2,1,0:T(8,128)(2,1)}, bf16[4,80,896]{2,1,0:T(8,128...) custom-call(bf16[384,1536]{1,0:T(8,128)(2,1)} %get-tuple-element.215, ...), custom_call_target="tpu_custom_call" | custom-call | flops 1000 | bytes 1000 | tf_op jit(solution)/shard_map/pallas_call | solution.py:917
  314.3 3.4 add_convert_fusion.1
  317.6 4.0 all-to-all-start.1
  321.6 13.9 %shard_map.302 = (f32[384,1472]{1,0:T(8,128)}, bf16[384,1536]{1,0:T(8,128)(2,1)}) custom-call(bf16[768,1792]{1,0:T(8,128)(2,1)} %get-tuple-element.265.refs_2_.gate_ref, bf16[768,1792]{1,0:T(8,128)(2,1)} %get-tuple-element.249.refs_3_.up_ref, bf16[1472,3584]{1,0:T(8,128)(2,1)} %get-tuple-element.266.low_ref.high_ref, ...), custom_call_target="tpu_custom_call" | custom-call | flops 1000 | bytes 1000 | tf_op jit(solution)/shard_map/pallas_call | solution.py:642
  346.5 8.7 %shard_map.303 = (f32[384,1472]{1,0:T(8,128)}, bf16[384,384]{1,0:T(8,128)(2,1)}, bf16[384,1472]{1,0:T(8,128)(2,1)}, f32[1,1472]{1,0:T(1,128)}) custom-call(f32[384,1472]{1,0:T(8,128)} %get-tuple-element.267.part_ref, bf16[384,1536]{1,0:T(8,128)(2,1)} %collective-permute-done.38.given_ref, f32[384,1472]{1,0:T(8,128)} %get-tuple-element.275.grad_ref, ...), custom_call_target="tpu_custom_call" | custom-call | flops 1000 | bytes 1000 | tf_op jit(solution)/shard_map/pallas_call | solution.py:797
  355.2 4.8 shard_map.304
  360.0 4.8 shard_map.305
  364.8 4.8 shard_map.306
  371.4 5.0 all-to-all-start
  378.5 3.6 reshape.261.out_grad_ref
  382.1 6.8 %shard_map.307 = f32[6,1,1024]{2,1,0:T(1,128)} custom-call(bf16[6,128,512]{2,1,0:T(8,128)(2,1)} %get-tuple-element.311.refs_0_, bf16[6,128,512]{2,1,0:T(8,128)(2,1)} %get-tuple-element.312.refs_1_, bf16[6,128,512]{2,1,0:T(8,128)(2,1)} %get-tuple-element.313.refs_2_, s32[1,384]{1,0:T(1,128)} %get-tuple-element.371.refs_3_), custom_call_target="tpu_custom_call" | custom-call | tf_op jit(solution)/shard_map/pallas_call | solution.py:76
  390.0 3.9 collective-permute-done.41
  405.9 24.6 %all-to-all-done.part_ref = bf16[4,384,768]{2,1,0:T(8,128)(2,1)S(1)} async-done(((bf16[4,384,768]{2,1,0:T(8,128)(2,1)}), bf16[4,384,768]{2,1,0:T(8,128)(2,1)S(1)}, u32[]{:S(2)}, u32[]{:S(2)}) %all-to-all-start) | async-done | bytes 2359328 | tf_op jit(solution)/shard_map/all_to_all | solution.py:1393
  430.4 4.3 all-to-all-start.3
  435.3 8.2 %shard_map.308 = (bf16[384,768]{1,0:T(8,128)(2,1)}, bf16[3,1472,128]{2,1,0:T(8,128)(2,1)}, f32[1,1472]{1,0:T(1,128)}) custom-call(bf16[384,384]{1,0:T(8,128)(2,1)} %get-tuple-element.290.query_ref, bf16[4,384,768]{2,1,0:T(8,128)(2,1)} %copy-done.2, bf16[4,1472,384]{2,1,0:T(8,128)(2,1)} %get-tuple-element.194.wq_ref.wk_ref.wv_ref, ...), custom_call_target="tpu_custom_call" | custom-call | flops 1000 | bytes 1000 | tf_op jit(solution)/shard_map/pallas_call | solution.py:839
  445.1 6.7 %shard_map.309 = (bf16[4,4,208,384]{3,2,1,0:T(8,128)(2,1)}, bf16[4,4,208,384]{3,2,1,0:T(8,128)(2,1)}) custom-call(bf16[384,1472]{1,0:T(8,128)(2,1)} %get-tuple-element.326.normed_ref, bf16[384,384]{1,0:T(8,128)(2,1)} %get-tuple-element.290.query_ref, bf16[384,768]{1,0:T(8,128)(2,1)} %get-tuple-element.327.pair_ref, bf16[1472,384]{1,0:T(8,128)(2,1)} %reshape.261.out_grad_ref, ...), custom_call_target="tpu_custom_call" | custom-call | flops 1000 | bytes 1000 | tf_op jit(solution)/shard_map/pallas_call | solution.py:382
  452.0 3.3 add_convert_fusion
  455.3 9.3 %all-to-all-done.3 = bf16[4,176,896]{2,1,0:T(8,128)(2,1)} async-done(((bf16[4,176,896]{2,1,0:T(8,128)(2,1)}), bf16[4,176,896]{2,1,0:T(8,128)(2,1)}, u32[]{:S(2)}, u32[]{:S(2)}) %all-to-all-start.3) | async-done | bytes 1261600 | tf_op jit(solution)/shard_map/all_to_all | solution.py:1393
  464.6 4.3 all-to-all-start.4
  469.0 3.0 fusion.4
  477.3 24.0 %all-to-all-done.4 = bf16[4,192,896]{2,1,0:T(8,128)(2,1)} async-done(((bf16[4,192,896]{2,1,0:T(8,128)(2,1)}), bf16[4,192,896]{2,1,0:T(8,128)(2,1)}, u32[]{:S(2)}, u32[]{:S(2)}) %all-to-all-start.4) | async-done | bytes 1376288 | tf_op jit(solution)/shard_map/all_to_all | solution.py:1393
  507.3 18.9 %all_to_all.25 = bf16[4,208,384]{2,1,0:T(8,128)(2,1)S(1)} all-to-all(bf16[4,208,384]{2,1,0:T(8,128)(2,1)S(1)} %fusion.2), channel_id=1, replica_groups=mesh['rep'=8,'shard'=4] {'shard'}, dimensions={0} | all-to-all | bytes 1277952 | tf_op jit(solution)/shard_map/all_to_all | solution.py:1393
  534.0 12.3 %collective-permute-done.53 = bf16[192,384]{1,0:T(8,128)(2,1)S(1)} collective-permute-done((bf16[192,384]{1,0:T(8,128)(2,1)S(1)}, bf16[192,384]{1,0:T(8,128)(2,1)S(1)}, u32[]{:S(2)}, u32[]{:S(2)}) %collective-permute-start.53) | collective-permute-done | bytes 147488 | tf_op jit(solution)/shard_map/ppermute | solution.py:979
  550.5 13.0 %collective-permute-done.56.refs_4_ = bf16[304,896]{1,0:T(8,128)(2,1)S(1)} collective-permute-done((bf16[304,896]{1,0:T(8,128)(2,1)S(1)}, bf16[304,896]{1,0:T(8,128)(2,1)S(1)}, u32[]{:S(2)}, u32[]{:S(2)}) %collective-permute-start.56) | collective-permute-done | bytes 544800 | tf_op jit(solution)/shard_map/ppermute | solution.py:979
  566.1 2.9 shard_map.310
  571.4 10.9 %shard_map.311 = (f32[368,3584]{1,0:T(8,128)}, f32[368,3584]{1,0:T(8,128)}, f32[1472,896]{1,0:T(8,128)}) custom-call(bf16[592,896]{1,0:T(8,128)(2,1)} %copy-done.11, bf16[592,896]{1,0:T(8,128)(2,1)} %collective-permute-done.49.refs_1_, bf16[592,896]{1,0:T(8,128)(2,1)} %collective-permute-done.50.refs_2_, bf16[288,896]{1,0:T(8,128)(2,1)} %collective-permute-done.55.refs_3_, ...), custom_call_target="tpu_custom_call" | custom-call | tf_op jit(solution)/shard_map/pallas_call | solution.py:548
  (330 shorter events, 156.7 us)
Async XLA Ops:
  12.8 14.8 %collective-permute-start = (bf16[208,384]{1,0:T(8,128)(2,1)}, bf16[208,384]{1,0:T(8,128)(2,1)S(1)}, u32[]{:S(2)}, u32[]{:S(2)}) collective-permute-start(bf16[208,384]{1,0:T(8,128)(2,1)} %pad_maximum_fusion.11), channel_id=1, source_target_pairs={{0,1},{1,2},{2,3},{3,0},{4,5},{5,6},{6,7},{7,4},{8,9},{9,10},{10,1... | collective-permute-start | bytes 479240 | tf_op jit(solution)/shard_map/ppermute | solution.py:982
  27.7 27.9 %collective-permute-start.6 = (bf16[592,896]{1,0:T(8,128)(2,1)}, bf16[592,896]{1,0:T(8,128)(2,1)}, u32[]{:S(2)}, u32[]{:S(2)}) collective-permute-start(bf16[592,896]{1,0:T(8,128)(2,1)} %pad_maximum_fusion.7), channel_id=1, source_target_pairs={{0,1},{1,2},{2,3},{3,0},{4,5},{5,6},{6,7},{7,4},{8,9},{9,10},{10,1... | collective-permute-start | bytes 3182600 | tf_op jit(solution)/shard_map/ppermute | solution.py:982
  33.6 20.4 %collective-permute-start.4 = (bf16[3,192,384]{2,1,0:T(8,128)(2,1)S(1)}, bf16[3,192,384]{2,1,0:T(8,128)(2,1)S(1)}, u32[]{:S(2)}, u32[]{:S(2)}) collective-permute-start(bf16[3,192,384]{2,1,0:T(8,128)(2,1)S(1)} %pad_maximum_fusion.10), channel_id=1, source_target_pairs={{0,16},{4,20},{8,24},{12,28},{16,0},{20,4},{24,8},{28,12},{1,17},{... | collective-permute-start | bytes 1327112 | tf_op jit(solution)/shard_map/ppermute | solution.py:979
  35.0 19.1 %collective-permute-start.3 = (bf16[3,192,384]{2,1,0:T(8,128)(2,1)S(1)}, bf16[3,192,384]{2,1,0:T(8,128)(2,1)S(1)}, u32[]{:S(2)}, u32[]{:S(2)}) collective-permute-start(bf16[3,192,384]{2,1,0:T(8,128)(2,1)S(1)} %pad_maximum_fusion.10), channel_id=1, source_target_pairs={{0,8},{4,12},{8,0},{12,4},{16,24},{20,28},{24,16},{28,20},{1,9},{5... | collective-permute-start | bytes 1327112 | tf_op jit(solution)/shard_map/ppermute | solution.py:979
  56.2 28.0 %collective-permute-start.8 = (bf16[592,896]{1,0:T(8,128)(2,1)}, bf16[592,896]{1,0:T(8,128)(2,1)}, u32[]{:S(2)}, u32[]{:S(2)}) collective-permute-start(bf16[592,896]{1,0:T(8,128)(2,1)} %collective-permute-done.6.rest_1_), channel_id=1, source_target_pairs={{0,1},{1,2},{2,3},{3,0},{4,5},{5,6},{6,7},{7,4},{8,9},{9,10},{10,1... | collective-permute-start | bytes 3182600 | tf_op jit(solution)/shard_map/ppermute | solution.py:982
  58.0 34.2 %collective-permute-start.10 = (bf16[592,896]{1,0:T(8,128)(2,1)}, bf16[592,896]{1,0:T(8,128)(2,1)}, u32[]{:S(2)}, u32[]{:S(2)}) collective-permute-start(bf16[592,896]{1,0:T(8,128)(2,1)} %collective-permute-done.6.rest_1_), channel_id=1, source_target_pairs={{0,8},{4,12},{8,0},{12,4},{16,24},{20,28},{24,16},{28,20},{1,9},{5... | collective-permute-start | bytes 3182600 | tf_op jit(solution)/shard_map/ppermute | solution.py:979
  59.4 32.8 %collective-permute-start.11 = (bf16[592,896]{1,0:T(8,128)(2,1)}, bf16[592,896]{1,0:T(8,128)(2,1)}, u32[]{:S(2)}, u32[]{:S(2)}) collective-permute-start(bf16[592,896]{1,0:T(8,128)(2,1)} %collective-permute-done.6.rest_1_), channel_id=1, source_target_pairs={{0,16},{4,20},{8,24},{12,28},{16,0},{20,4},{24,8},{28,12},{1,17},{... | collective-permute-start | bytes 3182600 | tf_op jit(solution)/shard_map/ppermute | solution.py:979
  84.2 16.9 %collective-permute-start.9 = (bf16[384,768]{1,0:T(8,128)(2,1)}, bf16[384,768]{1,0:T(8,128)(2,1)S(1)}, u32[]{:S(2)}, u32[]{:S(2)}) collective-permute-start(bf16[384,768]{1,0:T(8,128)(2,1)} %get-tuple-element.190.rest_0_), channel_id=1, source_target_pairs={{0,1},{1,2},{2,3},{3,0},{4,5},{5,6},{6,7},{7,4},{8,9},{9,10},{10,1... | collective-permute-start | bytes 1769480 | tf_op jit(solution)/shard_map/ppermute | solution.py:982
  101.1 18.9 %collective-permute-start.12 = (bf16[384,768]{1,0:T(8,128)(2,1)S(1)}, bf16[384,768]{1,0:T(8,128)(2,1)}, u32[]{:S(2)}, u32[]{:S(2)}) collective-permute-start(bf16[384,768]{1,0:T(8,128)(2,1)S(1)} %collective-permute-done.9.rest_1_), channel_id=1, source_target_pairs={{0,1},{1,2},{2,3},{3,0},{4,5},{5,6},{6,7},{7,4},{8,9},{9,10},{10,1... | collective-permute-start | bytes 1769480 | tf_op jit(solution)/shard_map/ppermute | solution.py:982
  103.2 16.8 %collective-permute-start.13 = (bf16[288,896]{1,0:T(8,128)(2,1)}, bf16[288,896]{1,0:T(8,128)(2,1)}, u32[]{:S(2)}, u32[]{:S(2)}) collective-permute-start(bf16[288,896]{1,0:T(8,128)(2,1)} %slice.225), channel_id=1, source_target_pairs={{0,8},{4,12},{8,0},{12,4},{16,24},{20,28},{24,16},{28,20},{1,9},{5... | collective-permute-start | bytes 1548296 | tf_op jit(solution)/shard_map/ppermute | solution.py:979
  120.0 31.5 %collective-permute-start.16 = (bf16[592,896]{1,0:T(8,128)(2,1)}, bf16[592,896]{1,0:T(8,128)(2,1)S(1)}, u32[]{:S(2)}, u32[]{:S(2)}) collective-permute-start(bf16[592,896]{1,0:T(8,128)(2,1)} %collective-permute-done.8.rest_6_.rest_5_), channel_id=1, source_target_pairs={{0,8},{4,12},{8,0},{12,4},{16,24},{20,28},{24,16},{28,20},{1,9},{5... | collective-permute-start | bytes 3182600 | tf_op jit(solution)/shard_map/ppermute | solution.py:979
  121.5 30.1 %collective-permute-start.17 = (bf16[592,896]{1,0:T(8,128)(2,1)}, bf16[592,896]{1,0:T(8,128)(2,1)S(1)}, u32[]{:S(2)}, u32[]{:S(2)}) collective-permute-start(bf16[592,896]{1,0:T(8,128)(2,1)} %collective-permute-done.8.rest_6_.rest_5_), channel_id=1, source_target_pairs={{0,16},{4,20},{8,24},{12,28},{16,0},{20,4},{24,8},{28,12},{1,17},{... | collective-permute-start | bytes 3182600 | tf_op jit(solution)/shard_map/ppermute | solution.py:979
  122.2 14.9 %collective-permute-start.15 = (bf16[384,768]{1,0:T(8,128)(2,1)}, bf16[384,768]{1,0:T(8,128)(2,1)S(1)}, u32[]{:S(2)}, u32[]{:S(2)}) collective-permute-start(bf16[384,768]{1,0:T(8,128)(2,1)} %collective-permute-done.12.rest_2_), channel_id=1, source_target_pairs={{0,1},{1,2},{2,3},{3,0},{4,5},{5,6},{6,7},{7,4},{8,9},{9,10},{10,1... | collective-permute-start | bytes 1769480 | tf_op jit(solution)/shard_map/ppermute | solution.py:982
  139.4 20.4 %collective-permute-start.18 = (bf16[368,896]{1,0:T(8,128)(2,1)}, bf16[368,896]{1,0:T(8,128)(2,1)}, u32[]{:S(2)}, u32[]{:S(2)}) collective-permute-start(bf16[368,896]{1,0:T(8,128)(2,1)} %slice.244), channel_id=1, source_target_pairs={{0,1},{1,2},{2,3},{3,0},{4,5},{5,6},{6,7},{7,4},{8,9},{9,10},{10,1... | collective-permute-start | bytes 1978376 | tf_op jit(solution)/shard_map/ppermute | solution.py:982
  191.6 23.8 %collective-permute-start.27 = (bf16[224,896]{1,0:T(8,128)(2,1)}, bf16[224,896]{1,0:T(8,128)(2,1)S(1)}, u32[]{:S(2)}, u32[]{:S(2)}) collective-permute-start(bf16[224,896]{1,0:T(8,128)(2,1)} %copy-done.36), channel_id=1, source_target_pairs={{0,8},{4,12},{8,0},{12,4},{16,24},{20,28},{24,16},{28,20},{1,9},{5... | collective-permute-start | bytes 1204232 | tf_op jit(solution)/shard_map/ppermute | solution.py:979
  193.0 22.5 %collective-permute-start.28 = (bf16[224,896]{1,0:T(8,128)(2,1)}, bf16[224,896]{1,0:T(8,128)(2,1)S(1)}, u32[]{:S(2)}, u32[]{:S(2)}) collective-permute-start(bf16[224,896]{1,0:T(8,128)(2,1)} %copy-done.36), channel_id=1, source_target_pairs={{0,16},{4,20},{8,24},{12,28},{16,0},{20,4},{24,8},{28,12},{1,17},{... | collective-permute-start | bytes 1204232 | tf_op jit(solution)/shard_map/ppermute | solution.py:979
  194.1 21.4 %collective-permute-start.29 = (bf16[224,896]{1,0:T(8,128)(2,1)}, bf16[224,896]{1,0:T(8,128)(2,1)}, u32[]{:S(2)}, u32[]{:S(2)}) collective-permute-start(bf16[224,896]{1,0:T(8,128)(2,1)} %copy-done.36), channel_id=1, source_target_pairs={{0,24},{4,28},{8,16},{12,20},{16,8},{20,12},{24,0},{28,4},{1,25},{... | collective-permute-start | bytes 1204232 | tf_op jit(solution)/shard_map/ppermute | solution.py:979
  252.7 19.9 %collective-permute-start.33 = (bf16[4,64,1472]{2,1,0:T(8,128)(2,1)}, bf16[4,64,1472]{2,1,0:T(8,128)(2,1)S(1)}, u32[]{:S(2)}, u32[]{:S(2)}) collective-permute-start(bf16[4,64,1472]{2,1,0:T(8,128)(2,1)} %get-tuple-element.247), channel_id=1, source_target_pairs={{0,16},{4,20},{8,24},{12,28},{16,0},{20,4},{24,8},{28,12},{1,17},{... | collective-permute-start | bytes 2261000 | tf_op jit(solution)/shard_map/ppermute | solution.py:979
  254.5 15.3 %collective-permute-start.32 = (bf16[4,48,1472]{2,1,0:T(8,128)(2,1)}, bf16[4,48,1472]{2,1,0:T(8,128)(2,1)S(1)}, u32[]{:S(2)}, u32[]{:S(2)}) collective-permute-start(bf16[4,48,1472]{2,1,0:T(8,128)(2,1)} %get-tuple-element.246), channel_id=1, source_target_pairs={{0,8},{4,12},{8,0},{12,4},{16,24},{20,28},{24,16},{28,20},{1,9},{5... | collective-permute-start | bytes 1695752 | tf_op jit(solution)/shard_map/ppermute | solution.py:979
  275.9 36.2 %collective-permute-start.34 = (bf16[4,112,1472]{2,1,0:T(8,128)(2,1)}, bf16[4,112,1472]{2,1,0:T(8,128)(2,1)}, u32[]{:S(2)}, u32[]{:S(2)}) collective-permute-start(bf16[4,112,1472]{2,1,0:T(8,128)(2,1)} %pad_maximum_fusion.1), channel_id=1, source_target_pairs={{0,16},{4,20},{8,24},{12,28},{16,0},{20,4},{24,8},{28,12},{1,17},{... | collective-permute-start | bytes 3956744 | tf_op jit(solution)/shard_map/ppermute | solution.py:979
  279.1 33.0 %collective-permute-start.35 = (bf16[4,112,1472]{2,1,0:T(8,128)(2,1)}, bf16[4,112,1472]{2,1,0:T(8,128)(2,1)}, u32[]{:S(2)}, u32[]{:S(2)}) collective-permute-start(bf16[4,112,1472]{2,1,0:T(8,128)(2,1)} %pad_maximum_fusion.2), channel_id=1, source_target_pairs={{0,8},{4,12},{8,0},{12,4},{16,24},{20,28},{24,16},{28,20},{1,9},{5... | collective-permute-start | bytes 3956744 | tf_op jit(solution)/shard_map/ppermute | solution.py:979
  312.2 23.3 %collective-permute-start.37 = (bf16[4,96,896]{2,1,0:T(8,128)(2,1)}, bf16[4,96,896]{2,1,0:T(8,128)(2,1)S(1)}, u32[]{:S(2)}, u32[]{:S(2)}) collective-permute-start(bf16[4,96,896]{2,1,0:T(8,128)(2,1)} %get-tuple-element.273), channel_id=1, source_target_pairs={{0,16},{4,20},{8,24},{12,28},{16,0},{20,4},{24,8},{28,12},{1,17},{... | collective-permute-start | bytes 2064392 | tf_op jit(solution)/shard_map/ppermute | solution.py:979
  313.1 22.4 %collective-permute-start.36 = (bf16[4,80,896]{2,1,0:T(8,128)(2,1)}, bf16[4,80,896]{2,1,0:T(8,128)(2,1)S(1)}, u32[]{:S(2)}, u32[]{:S(2)}) collective-permute-start(bf16[4,80,896]{2,1,0:T(8,128)(2,1)} %get-tuple-element.272), channel_id=1, source_target_pairs={{0,8},{4,12},{8,0},{12,4},{16,24},{20,28},{24,16},{28,20},{1,9},{5... | collective-permute-start | bytes 1720328 | tf_op jit(solution)/shard_map/ppermute | solution.py:979
  317.6 52.3 %all-to-all-start.1 = ((bf16[4,112,1472]{2,1,0:T(8,128)(2,1)}), bf16[4,112,1472]{2,1,0:T(8,128)(2,1)S(1)}, u32[]{:S(2)}, u32[]{:S(2)}) async-start(bf16[4,112,1472]{2,1,0:T(8,128)(2,1)} %add_convert_fusion.1), calls=%async_computation.1 | async-start | bytes 2752512 | tf_op jit(solution)/shard_map/all_to_all | solution.py:1393
  339.9 29.6 %collective-permute-start.39 = (bf16[4,176,896]{2,1,0:T(8,128)(2,1)}, bf16[4,176,896]{2,1,0:T(8,128)(2,1)}, u32[]{:S(2)}, u32[]{:S(2)}) collective-permute-start(bf16[4,176,896]{2,1,0:T(8,128)(2,1)} %pad_maximum_fusion.5), channel_id=1, source_target_pairs={{0,16},{4,20},{8,24},{12,28},{16,0},{20,4},{24,8},{28,12},{1,17},{... | collective-permute-start | bytes 3784712 | tf_op jit(solution)/shard_map/ppermute | solution.py:979
  342.4 27.5 %collective-permute-start.40 = (bf16[4,176,896]{2,1,0:T(8,128)(2,1)}, bf16[4,176,896]{2,1,0:T(8,128)(2,1)S(1)}, u32[]{:S(2)}, u32[]{:S(2)}) collective-permute-start(bf16[4,176,896]{2,1,0:T(8,128)(2,1)} %pad_maximum_fusion.6), channel_id=1, source_target_pairs={{0,8},{4,12},{8,0},{12,4},{16,24},{20,28},{24,16},{28,20},{1,9},{5... | collective-permute-start | bytes 3784712 | tf_op jit(solution)/shard_map/ppermute | solution.py:979
  371.4 59.0 %all-to-all-start = ((bf16[4,384,768]{2,1,0:T(8,128)(2,1)}), bf16[4,384,768]{2,1,0:T(8,128)(2,1)S(1)}, u32[]{:S(2)}, u32[]{:S(2)}) async-start(bf16[4,384,768]{2,1,0:T(8,128)(2,1)} %get-tuple-element.297), calls=%async_computation | async-start | bytes 4718592 | tf_op jit(solution)/shard_map/all_to_all | solution.py:1393
  376.4 17.5 %collective-permute-start.41 = (bf16[4,96,896]{2,1,0:T(8,128)(2,1)}, bf16[4,96,896]{2,1,0:T(8,128)(2,1)}, u32[]{:S(2)}, u32[]{:S(2)}) collective-permute-start(bf16[4,96,896]{2,1,0:T(8,128)(2,1)} %get-tuple-element.309), channel_id=1, source_target_pairs={{0,8},{4,12},{8,0},{12,4},{16,24},{20,28},{24,16},{28,20},{1,9},{5... | collective-permute-start | bytes 2064392 | tf_op jit(solution)/shard_map/ppermute | solution.py:979
  377.5 17.2 %collective-permute-start.42 = (bf16[4,96,896]{2,1,0:T(8,128)(2,1)}, bf16[4,96,896]{2,1,0:T(8,128)(2,1)}, u32[]{:S(2)}, u32[]{:S(2)}) collective-permute-start(bf16[4,96,896]{2,1,0:T(8,128)(2,1)} %get-tuple-element.310), channel_id=1, source_target_pairs={{0,16},{4,20},{8,24},{12,28},{16,0},{20,4},{24,8},{28,12},{1,17},{... | collective-permute-start | bytes 2064392 | tf_op jit(solution)/shard_map/ppermute | solution.py:979
  398.3 37.0 %collective-permute-start.43 = (bf16[4,192,896]{2,1,0:T(8,128)(2,1)}, bf16[4,192,896]{2,1,0:T(8,128)(2,1)}, u32[]{:S(2)}, u32[]{:S(2)}) collective-permute-start(bf16[4,192,896]{2,1,0:T(8,128)(2,1)} %pad_maximum_fusion.3), channel_id=1, source_target_pairs={{0,16},{4,20},{8,24},{12,28},{16,0},{20,4},{24,8},{28,12},{1,17},{... | collective-permute-start | bytes 4128776 | tf_op jit(solution)/shard_map/ppermute | solution.py:979
  402.0 33.3 %collective-permute-start.44 = (bf16[4,192,896]{2,1,0:T(8,128)(2,1)}, bf16[4,192,896]{2,1,0:T(8,128)(2,1)}, u32[]{:S(2)}, u32[]{:S(2)}) collective-permute-start(bf16[4,192,896]{2,1,0:T(8,128)(2,1)} %pad_maximum_fusion.4), channel_id=1, source_target_pairs={{0,8},{4,12},{8,0},{12,4},{16,24},{20,28},{24,16},{28,20},{1,9},{5... | collective-permute-start | bytes 4128776 | tf_op jit(solution)/shard_map/ppermute | solution.py:979
  430.4 34.2 %all-to-all-start.3 = ((bf16[4,176,896]{2,1,0:T(8,128)(2,1)}), bf16[4,176,896]{2,1,0:T(8,128)(2,1)}, u32[]{:S(2)}, u32[]{:S(2)}) async-start(bf16[4,176,896]{2,1,0:T(8,128)(2,1)} %add_convert_fusion.2), calls=%async_computation.3 | async-start | bytes 2523136 | tf_op jit(solution)/shard_map/all_to_all | solution.py:1393
  451.9 17.1 %collective-permute-start.45 = (bf16[4,4,208,384]{3,2,1,0:T(8,128)(2,1)}, bf16[4,4,208,384]{3,2,1,0:T(8,128)(2,1)}, u32[]{:S(2)}, u32[]{:S(2)}) collective-permute-start(bf16[4,4,208,384]{3,2,1,0:T(8,128)(2,1)} %get-tuple-element.335), channel_id=1, source_target_pairs={{0,4},{4,0},{8,12},{12,8},{16,20},{20,16},{24,28},{28,24},{1,5},{5... | collective-permute-start | bytes 7667720 | tf_op jit(solution)/shard_map/ppermute | solution.py:979
  464.6 36.6 %all-to-all-start.4 = ((bf16[4,192,896]{2,1,0:T(8,128)(2,1)}), bf16[4,192,896]{2,1,0:T(8,128)(2,1)}, u32[]{:S(2)}, u32[]{:S(2)}) async-start(bf16[4,192,896]{2,1,0:T(8,128)(2,1)} %add_convert_fusion), calls=%async_computation.4 | async-start | bytes 2752512 | tf_op jit(solution)/shard_map/all_to_all | solution.py:1393
  472.0 33.2 %collective-permute-start.48 = (bf16[4,208,384]{2,1,0:T(8,128)(2,1)}, bf16[4,208,384]{2,1,0:T(8,128)(2,1)S(1)}, u32[]{:S(2)}, u32[]{:S(2)}) collective-permute-start(bf16[4,208,384]{2,1,0:T(8,128)(2,1)} %get-tuple-element.354), channel_id=1, source_target_pairs={{0,24},{4,28},{8,16},{12,20},{16,8},{20,12},{24,0},{28,4},{1,25},{... | collective-permute-start | bytes 1916936 | tf_op jit(solution)/shard_map/ppermute | solution.py:979
  473.5 31.7 %collective-permute-start.47 = (bf16[4,208,384]{2,1,0:T(8,128)(2,1)}, bf16[4,208,384]{2,1,0:T(8,128)(2,1)}, u32[]{:S(2)}, u32[]{:S(2)}) collective-permute-start(bf16[4,208,384]{2,1,0:T(8,128)(2,1)} %get-tuple-element.355), channel_id=1, source_target_pairs={{0,16},{4,20},{8,24},{12,28},{16,0},{20,4},{24,8},{28,12},{1,17},{... | collective-permute-start | bytes 1916936 | tf_op jit(solution)/shard_map/ppermute | solution.py:979
  474.5 30.7 %collective-permute-start.46 = (bf16[4,208,384]{2,1,0:T(8,128)(2,1)}, bf16[4,208,384]{2,1,0:T(8,128)(2,1)}, u32[]{:S(2)}, u32[]{:S(2)}) collective-permute-start(bf16[4,208,384]{2,1,0:T(8,128)(2,1)} %get-tuple-element.353), channel_id=1, source_target_pairs={{0,8},{4,12},{8,0},{12,4},{16,24},{20,28},{24,16},{28,20},{1,9},{5... | collective-permute-start | bytes 1916936 | tf_op jit(solution)/shard_map/ppermute | solution.py:979
  503.0 24.5 %collective-permute-start.49 = (bf16[592,896]{1,0:T(8,128)(2,1)S(1)}, bf16[592,896]{1,0:T(8,128)(2,1)}, u32[]{:S(2)}, u32[]{:S(2)}) collective-permute-start(bf16[592,896]{1,0:T(8,128)(2,1)S(1)} %pad_maximum_fusion.8.refs_0_), channel_id=1, source_target_pairs={{0,8},{4,12},{8,0},{12,4},{16,24},{20,28},{24,16},{28,20},{1,9},{5... | collective-permute-start | bytes 3182600 | tf_op jit(solution)/shard_map/ppermute | solution.py:979
  504.2 24.2 %collective-permute-start.50 = (bf16[592,896]{1,0:T(8,128)(2,1)S(1)}, bf16[592,896]{1,0:T(8,128)(2,1)}, u32[]{:S(2)}, u32[]{:S(2)}) collective-permute-start(bf16[592,896]{1,0:T(8,128)(2,1)S(1)} %pad_maximum_fusion.8.refs_0_), channel_id=1, source_target_pairs={{0,16},{4,20},{8,24},{12,28},{16,0},{20,4},{24,8},{28,12},{1,17},{... | collective-permute-start | bytes 3182600 | tf_op jit(solution)/shard_map/ppermute | solution.py:979
  529.5 20.9 %collective-permute-start.55 = (bf16[288,896]{1,0:T(8,128)(2,1)S(1)}, bf16[288,896]{1,0:T(8,128)(2,1)}, u32[]{:S(2)}, u32[]{:S(2)}) collective-permute-start(bf16[288,896]{1,0:T(8,128)(2,1)S(1)} %slice.277), channel_id=1, source_target_pairs={{0,8},{4,12},{8,0},{12,4},{16,24},{20,28},{24,16},{28,20},{1,9},{5... | collective-permute-start | bytes 1548296 | tf_op jit(solution)/shard_map/ppermute | solution.py:979
  530.5 15.8 %collective-permute-start.53 = (bf16[192,384]{1,0:T(8,128)(2,1)S(1)}, bf16[192,384]{1,0:T(8,128)(2,1)S(1)}, u32[]{:S(2)}, u32[]{:S(2)}) collective-permute-start(bf16[192,384]{1,0:T(8,128)(2,1)S(1)} %slice.306), channel_id=1, source_target_pairs={{0,24},{4,28},{8,16},{12,20},{16,8},{20,12},{24,0},{28,4},{1,25},{... | collective-permute-start | bytes 442376 | tf_op jit(solution)/shard_map/ppermute | solution.py:979
  532.0 14.2 %collective-permute-start.52 = (bf16[192,384]{1,0:T(8,128)(2,1)S(1)}, bf16[192,384]{1,0:T(8,128)(2,1)S(1)}, u32[]{:S(2)}, u32[]{:S(2)}) collective-permute-start(bf16[192,384]{1,0:T(8,128)(2,1)S(1)} %slice.306), channel_id=1, source_target_pairs={{0,16},{4,20},{8,24},{12,28},{16,0},{20,4},{24,8},{28,12},{1,17},{... | collective-permute-start | bytes 442376 | tf_op jit(solution)/shard_map/ppermute | solution.py:979
  533.0 14.3 %collective-permute-start.51 = (bf16[192,384]{1,0:T(8,128)(2,1)S(1)}, bf16[192,384]{1,0:T(8,128)(2,1)S(1)}, u32[]{:S(2)}, u32[]{:S(2)}) collective-permute-start(bf16[192,384]{1,0:T(8,128)(2,1)S(1)} %slice.306), channel_id=1, source_target_pairs={{0,8},{4,12},{8,0},{12,4},{16,24},{20,28},{24,16},{28,20},{1,9},{5... | collective-permute-start | bytes 442376 | tf_op jit(solution)/shard_map/ppermute | solution.py:979
  547.4 16.0 %collective-permute-start.54 = (bf16[4,192,384]{2,1,0:T(8,128)(2,1)S(1)}, bf16[4,192,384]{2,1,0:T(8,128)(2,1)S(1)}, u32[]{:S(2)}, u32[]{:S(2)}) collective-permute-start(bf16[4,192,384]{2,1,0:T(8,128)(2,1)S(1)} %pad_maximum_fusion.9.refs_0_), channel_id=1, source_target_pairs={{0,4},{4,0},{8,12},{12,8},{16,20},{20,16},{24,28},{28,24},{1,5},{5... | collective-permute-start | bytes 1769480 | tf_op jit(solution)/shard_map/ppermute | solution.py:979
  548.8 14.7 %collective-permute-start.56 = (bf16[304,896]{1,0:T(8,128)(2,1)S(1)}, bf16[304,896]{1,0:T(8,128)(2,1)S(1)}, u32[]{:S(2)}, u32[]{:S(2)}) collective-permute-start(bf16[304,896]{1,0:T(8,128)(2,1)S(1)} %slice.278), channel_id=1, source_target_pairs={{0,16},{4,20},{8,24},{12,28},{16,0},{20,4},{24,8},{28,12},{1,17},{... | collective-permute-start | bytes 1634312 | tf_op jit(solution)/shard_map/ppermute | solution.py:979
  549.9 21.4 %collective-permute-start.57 = (bf16[592,896]{1,0:T(8,128)(2,1)S(1)}, bf16[592,896]{1,0:T(8,128)(2,1)}, u32[]{:S(2)}, u32[]{:S(2)}) collective-permute-start(bf16[592,896]{1,0:T(8,128)(2,1)S(1)} %pad_maximum_fusion.8.refs_0_), channel_id=1, source_target_pairs={{0,4},{4,0},{8,12},{12,8},{16,20},{20,16},{24,28},{28,24},{1,5},{5... | collective-permute-start | bytes 3182600 | tf_op jit(solution)/shard_map/ppermute | solution.py:979
  550.0 21.4 %collective-permute-start.58 = (bf16[592,896]{1,0:T(8,128)(2,1)}, bf16[592,896]{1,0:T(8,128)(2,1)}, u32[]{:S(2)}, u32[]{:S(2)}) collective-permute-start(bf16[592,896]{1,0:T(8,128)(2,1)} %collective-permute-done.49.refs_1_), channel_id=1, source_target_pairs={{0,4},{4,0},{8,12},{12,8},{16,20},{20,16},{24,28},{28,24},{1,5},{5... | collective-permute-start | bytes 3182600 | tf_op jit(solution)/shard_map/ppermute | solution.py:979
  550.4 20.9 %collective-permute-start.59 = (bf16[592,896]{1,0:T(8,128)(2,1)}, bf16[592,896]{1,0:T(8,128)(2,1)}, u32[]{:S(2)}, u32[]{:S(2)}) collective-permute-start(bf16[592,896]{1,0:T(8,128)(2,1)} %collective-permute-done.50.refs_2_), channel_id=1, source_target_pairs={{0,4},{4,0},{8,12},{12,8},{16,20},{20,16},{24,28},{28,24},{1,5},{5... | collective-permute-start | bytes 3182600 | tf_op jit(solution)/shard_map/ppermute | solution.py:979
  (68 other events, 657.7 us)

commit v5 on v4

--- a/solution.py
+++ b/solution.py
@@ -406,7 +406,9 @@
 
     def kernel(own_ref, other_ref, *rest):
         piece_refs = rest[:count]
-        slope_ref, act_ref, hidden_ref, keep_ref, both, weights, sems = rest[count:]
+        out_refs, keep_ref = rest[count : count + 3], rest[count + 3]
+        both, weights, slopes, acts, hiddens, sems = rest[count + 4 :]
+        results = (slopes, acts, hiddens)
         rank, chip = axis_ranks()
         copies = [(own_ref, both.at[:rows]), (other_ref, both.at[rows:])]
         for piece, row, size, columns, place in moves:
@@ -432,24 +434,36 @@
                 preferred_element_type=F32,
             )
             act, slope = gelu_parts(gate)
-            act_ref[:, pl.ds(start, tile)] = act.astype(BF16)
-            slope_ref[:, pl.ds(start, tile)] = (up * slope).astype(BF16)
-            hidden_ref[:, pl.ds(start, tile)] = (act * up).astype(BF16)
+            columns = pl.ds(start, tile)
+            for number, value in enumerate((up * slope, act, act * up)):
+                results[number][:, columns] = value.astype(BF16)
+                pltpu.make_async_copy(
+                    results[number].at[:, columns],
+                    out_refs[number].at[:, columns],
+                    sems.at[steps + 3 + number],
+                ).start()
             return carry
 
         lax.fori_loop(0, half // tile, step, 0)
         keep.wait()
+        for number in range(3):
+            pltpu.make_async_copy(
+                results[number], out_refs[number], sems.at[steps + 3 + number]
+            ).wait()
 
     shape = jax.ShapeDtypeStruct((2 * rows, half), BF16)
     return pl.pallas_call(
         kernel,
         in_specs=[ANY] * (2 + count),
-        out_specs=[VMEM, VMEM, VMEM, ANY],
+        out_specs=[ANY] * 4,
         out_shape=[shape, shape, shape, jax.ShapeDtypeStruct((width, inner), BF16)],
         scratch_shapes=[
             pltpu.VMEM((2 * rows, wide), BF16),
             pltpu.VMEM((width, inner), BF16),
-            pltpu.SemaphoreType.DMA((steps + 3,)),
+        ]
+        + [pltpu.VMEM((2 * rows, half), BF16)] * 3
+        + [
+            pltpu.SemaphoreType.DMA((steps + 6,)),
         ],
         cost_estimate=LIGHT,
     )(own, other, *pieces)
@@ -513,7 +527,8 @@
 
     def kernel(*refs):
         piece_refs = refs[:count]
-        gate_ref, up_ref, down_ref, columns_of, rows_of, sems = refs[count:]
+        out_refs = refs[count : count + 3]
+        columns_of, rows_of, gate_ref, up_ref, down_ref, sems = refs[count + 3 :]
         chip, core = axis_ranks()[1], lax.axis_index("rep") % 2
         shards = lax.axis_size("shard")
         copies = []
@@ -533,9 +548,14 @@
                     rows_of.at[pl.ds(to_row, size), pl.ds(to_column, columns)],
                 )
             )
-        for copy in run_copies(copies, sems):
+        copies = run_copies(copies, sems)
+        for copy in copies[: len(gate_up_moves)]:
             copy.wait()
         half = inner // shards // 2
+        outs = [
+            pltpu.make_async_copy(ref, out, sems.at[steps + number])
+            for number, (ref, out) in enumerate(zip((gate_ref, up_ref, down_ref), out_refs))
+        ]
         for index, ref in enumerate((gate_ref, up_ref)):
             for shard in range(shards):
                 start = index * (inner // 2) + shard * half
@@ -543,12 +563,18 @@
                 ref[:, 2 * half * shard : 2 * half * (shard + 1)] = jnp.concatenate(
                     both, 1
                 ).astype(F32)
+            outs[index].start()
+        for copy in copies[len(gate_up_moves) :]:
+            copy.wait()
         down_ref[...] = rows_of[...].T[:width].astype(F32)
+        outs[2].start()
+        for copy in outs:
+            copy.wait()
 
     return pl.pallas_call(
         kernel,
         in_specs=[ANY] * count,
-        out_specs=[VMEM] * 3,
+        out_specs=[ANY] * 3,
         out_shape=[
             jax.ShapeDtypeStruct((block, inner), F32),
             jax.ShapeDtypeStruct((block, inner), F32),
@@ -557,7 +583,10 @@
         scratch_shapes=[
             pltpu.VMEM((2, block, inner), BF16),
             pltpu.VMEM((down_rows, padded), BF16),
-            pltpu.SemaphoreType.DMA((steps,)),
+            pltpu.VMEM((block, inner), F32),
+            pltpu.VMEM((block, inner), F32),
+            pltpu.VMEM((width, down_rows), F32),
+            pltpu.SemaphoreType.DMA((steps + 3,)),
         ],
     )(*pieces)
 
@@ -852,7 +881,7 @@
     )(query_grad, pair_parts, weights, weights, weights, grad_mid, tokens, gain)
 
 
-def weight_grad_call(left, right, depth, width, outputs):
+def weight_grad_call(left, right, picks, width, outputs, in_halves):
     left_own, left_other = left
     right_own, right_other = right
     rows = left_own.shape[0]
@@ -860,7 +889,9 @@
     beside = right_other is not None and right_own.shape[0] == total
     right_width = right_own.shape[1] * (2 if beside else 1)
     count = len(outputs)
-    copies_out = sum(len(moves) for _, moves in outputs)
+    copies_out = sum(len(moves) for _, moves, _ in outputs)
+    depth = sum(size for _, size in picks)
+    tile = 256
     split = left_other is not None
     right_split = right_other is not None
     inputs = [left_own] + ([left_other] if split else []) + [right_own]
@@ -869,7 +900,7 @@
     def kernel(*refs):
         in_refs = list(refs[: len(inputs)])
         out_refs = refs[len(inputs) : len(inputs) + count]
-        lefts, rights, result, sems = refs[len(inputs) + count :]
+        lefts, turned, rights, result, sems = refs[len(inputs) + count :]
         copies = []
         for target, parted, aside in ((lefts, split, False), (rights, right_split, beside)):
             first = in_refs.pop(0)
@@ -884,43 +915,54 @@
                 copies.append((in_refs.pop(0), target.at[size:]))
         for copy in run_copies(copies, sems):
             copy.wait()
-        tile = 512 if width % 512 == 0 else width
-        for begin in range(0, depth, 256):
-            size = min(256, depth - begin)
-            turned = lefts[:, begin : begin + size].T
-            if tile == width:
-                for start, span in col_tiles(width):
-                    result[begin : begin + size, start : start + span] = jnp.dot(
-                        turned, rights[:, start : start + span], preferred_element_type=F32
-                    ).astype(BF16)
-            else:
-
-                def step(index, carry):
-                    start = pl.multiple_of(index * tile, tile)
-                    result[begin : begin + size, pl.ds(start, tile)] = jnp.dot(
-                        turned, rights[:, pl.ds(start, tile)], preferred_element_type=F32
-                    ).astype(BF16)
-                    return carry
-
-                lax.fori_loop(0, width // tile, step, 0)
+        to_row = 0
+        for first, size in picks:
+            for begin in range(0, size, tile):
+                span = min(tile, size - begin)
+                turned[to_row : to_row + span] = lefts[:, first + begin : first + begin + span].T
+                to_row += span
+
+        def product(start, size):
+            result[:, pl.ds(start, size)] = jnp.dot(
+                turned[...], rights[:, pl.ds(start, size)], preferred_element_type=F32
+            ).astype(BF16)
+
         rank, chip = axis_ranks()
-        moves_out = []
-        for ref, (shape, moves) in zip(out_refs, outputs):
-            for index, place in moves:
-                row, column = place(rank, chip)
-                moves_out.append(
-                    (result.at[pl.ds(row, shape[1]), pl.ds(column, shape[2])], ref.at[index])
-                )
-        for copy in run_copies(moves_out, sems):
+        started = []
+        for half in range(2 if in_halves else 1):
+            first = (chip // 2 ^ (1 - half)) * (width // 2) if in_halves else 0
+            tiles = (width // 2 if in_halves else width) // tile
+
+            def step(index, carry, first=first):
+                product(pl.multiple_of(first + index * tile, tile), tile)
+                return carry
+
+            lax.fori_loop(0, tiles, step, 0)
+            if not in_halves and width % tile:
+                product(tiles * tile, width % tile)
+            for ref, (shape, moves, mask) in zip(out_refs, outputs):
+                if in_halves and mask & 2 == 2 * half:
+                    continue
+                for index, place in moves:
+                    row, column = place(rank, chip)
+                    copy = pltpu.make_async_copy(
+                        result.at[pl.ds(row, shape[1]), pl.ds(column, shape[2])],
+                        ref.at[index],
+                        sems.at[len(started)],
+                    )
+                    copy.start()
+                    started.append(copy)
+        for copy in started:
             copy.wait()
 
     return pl.pallas_call(
         kernel,
         in_specs=[ANY] * len(inputs),
         out_specs=[ANY] * count,
-        out_shape=[jax.ShapeDtypeStruct(shape, BF16) for shape, _ in outputs],
+        out_shape=[jax.ShapeDtypeStruct(shape, BF16) for shape, _, _ in outputs],
         scratch_shapes=[
             pltpu.VMEM((total, left_own.shape[1]), BF16),
+            pltpu.VMEM((depth, total), BF16),
             pltpu.VMEM((total, right_width), BF16),
             pltpu.VMEM((depth, width), BF16),
             pltpu.SemaphoreType.DMA((max(4, copies_out),)),
@@ -1345,32 +1387,31 @@
 
     down_up_other = swap(down_up, 1)
 
-    def reduce_plan(groups, piece_columns, place):
+    def reduce_plan(size, piece_columns, place):
+        middle = cut(size)
+        spans = {"own": (0, size), "near": (0, size), "far": (0, size)}
+        spans["top"], spans["low"] = (0, middle), (middle, size - middle)
         plan = []
-        for first, size in groups:
-            middle = cut(size)
-            spans = {"own": (0, size), "near": (0, size), "far": (0, size)}
-            spans["top"], spans["low"] = (0, middle), (middle, size - middle)
-            for base in bases:
-                for name in used:
-                    start, count = spans[name]
-                    moves = [
-                        (index, place(index, base ^ names[name], first + start))
-                        for index in range(shards)
-                    ]
-                    plan.append(((shards, count, piece_columns), moves))
+        for base in bases:
+            for name in used:
+                start, count = spans[name]
+                moves = [
+                    (index, place(index, base ^ names[name], start)) for index in range(shards)
+                ]
+                plan.append(((shards, count, piece_columns), moves, base ^ names[name]))
         return plan
 
-    def reduce_run(plan, left, right, left_width, right_width):
+    def reduce_run(plan, left, right, picks, right_width, in_halves):
         if aligned:
-            buffers = weight_grad_call(left, right, left_width, right_width, plan)
+            buffers = weight_grad_call(left, right, picks, right_width, plan, in_halves)
         else:
-            shape = (left_width, right_width)
+            shape = (sum(size for _, size in picks), right_width)
             whole = weight_grad_call(
-                left, right, left_width, right_width, [((1,) + shape, [(0, lambda at, chip_at: (0, 0))])]
+                left, right, picks, right_width,
+                [((1,) + shape, [(0, lambda at, chip_at: (0, 0))], 0)], False,
             )[0][0]
             buffers = []
-            for (_, size, columns), moves in plan:
+            for (_, size, columns), moves, _ in plan:
                 buffers.append(
                     jnp.stack(
                         [
@@ -1379,13 +1420,8 @@
                         ]
                     )
                 )
-        return buffers
-
-    def group_parts(buffers, group_index, group_count):
-        each = len(buffers) // group_count
-        chosen = buffers[group_index * each : (group_index + 1) * each]
         return {
-            base: dict(zip(used, chosen[i * len(used) : (i + 1) * len(used)]))
+            base: dict(zip(used, buffers[i * len(used) : (i + 1) * len(used)]))
             for i, base in enumerate(bases)
         }
 
@@ -1402,35 +1438,40 @@
         )
         return tile_hint(plain, 16, 128) if aligned else plain
 
-    def gate_up_grad_place(index, mask, start):
-        plain = lambda at, chip_at: (index * block + start, (chip_at ^ mask) * col_piece)
-        return tile_hint(plain, 16, 128) if aligned else plain
+    def gate_up_grads(first, size, left, right):
+        def place(index, mask, start):
+            plain = lambda at, chip_at: (index * size + start, (chip_at ^ mask) * col_piece)
+            return tile_hint(plain, 16, 128) if aligned else plain
+
+        return reduce_run(
+            reduce_plan(size, col_piece, place),
+            left,
+            right,
+            [(index * block + first, size) for index in range(shards)],
+            inner,
+            chips == 4 and half_inner % 256 == 0,
+        )
 
     down_buffers = reduce_run(
-        reduce_plan([(0, down_piece)], width, down_grad_place),
+        reduce_plan(down_piece, width, down_grad_place),
         (inner_act, None),
         (down_up, down_up_other),
-        half_inner,
+        [(0, half_inner)],
         width,
+        False,
     )
-    down_state = reduce_begin(group_parts(down_buffers, 0, 1), 1)
+    down_state = reduce_begin(down_buffers, 1)
     gate_grad, up_grad = hidden_grad_call(down_up, down_up_other, down, gate_slope_act, gate_act)
     gate_grad, down_state = tie(gate_grad, down_state)
-    gate_up_buffers = reduce_run(
-        reduce_plan([(0, cut(block)), (cut(block), block - cut(block))], col_piece, gate_up_grad_place),
-        (normed_two, normed_two_other),
-        (gate_grad, up_grad),
-        width,
-        inner,
-    )
     down_state = reduce_middle(down_state, 1)
-    gate_grad, (gate_up_buffers, down_state) = tie(gate_grad, (gate_up_buffers, down_state))
-    gate_up_state = reduce_begin(group_parts(gate_up_buffers, 0, 2), 1)
+    normed_both = (normed_two, normed_two_other)
+    gate_up_buffers = gate_up_grads(0, cut(block), normed_both, (gate_grad, up_grad))
+    gate_grad, gate_up_buffers = tie(gate_grad, gate_up_buffers)
     normed_part, normed_given = normed_grad_call(gate_grad, up_grad, gate_up)
-    normed_given, gate_up_state = tie(normed_given, gate_up_state)
-    gate_up_state = reduce_middle(gate_up_state, 1)
+    normed_given, (down_state, gate_up_buffers) = tie(normed_given, (down_state, gate_up_buffers))
+    gate_up_state = reduce_begin(gate_up_buffers, 1)
+    down_arrived = exchange(reduce_end(down_state))
     normed_given = swap(normed_given, 1)
-    down_arrived = exchange(reduce_end(down_state))
     grad_mid, context_grad, grad_w_out, grad_ffn_gain = back_call(
         normed_part,
         normed_given,
@@ -1441,6 +1482,8 @@
         out_full,
         micro_count,
     )
+    context_grad, gate_up_state = tie(context_grad, gate_up_state)
+    gate_up_state = reduce_middle(gate_up_state, 1)
     score_grads, sums = [], []
     for micro in range(micro_count):
         score_grad, *sums = attention_back_call(
@@ -1455,17 +1498,19 @@
         )
         score_grads.append(score_grad)
     query_grad, pair_parts = sums
-    gate_up_parts = group_parts(gate_up_buffers, 1, 2)
-    pair_parts, gate_up_state = tie(pair_parts, gate_up_state)
+    gate_grad, pair_parts = tie(gate_grad, pair_parts)
     pair_arrived = exchange(pair_parts)
-    gate_up_parts, gate_up_state = tie(gate_up_parts, gate_up_state)
-    gate_up_later = reduce_begin(gate_up_parts, 1)
+    gate_up_buffers = gate_up_grads(
+        cut(block), block - cut(block), normed_both, (gate_grad, up_grad)
+    )
+    gate_up_buffers, gate_up_state = tie(gate_up_buffers, gate_up_state)
+    gate_up_later = reduce_begin(gate_up_buffers, 1)
     grad_bias_rows = bias_fold(score_grads, own_slots.reshape(rows))
     grad_bias = jnp.einsum("ob,ho->bh", onehot, grad_bias_rows, precision=HIGHEST)
     out_grads = grad_w_out.reshape(width, proj)
     gate_up_later, (grad_bias, out_grads) = tie(gate_up_later, (grad_bias, out_grads))
     gate_up_later = reduce_middle(gate_up_later, 1)
-    pair_arrived, (gate_up_later, down_arrived) = tie(pair_arrived, (gate_up_later, down_arrived))
+    pair_arrived, down_arrived = tie(pair_arrived, down_arrived)
     gate_up_arrived = exchange(reduce_end(gate_up_state))
     down_sum = total_of(down_arrived)
     pair_sum, grad_in, grad_attn_gain = in_call(
@@ -1477,6 +1522,7 @@
         attn_gain[None],
         micro_count,
     )
+    pair_sum, gate_up_later = tie(pair_sum, gate_up_later)
 
     small = jnp.concatenate(
         [
@@ -1545,6 +1591,7 @@
     attn_send = [add(kept[mask], given[mask]) for mask in range(1, chips)]
     attn_found = [swap(part, 2 * mask + 2) for mask, part in enumerate(attn_send)]
     gate_up_rest = exchange(reduce_end(gate_up_later))
+    attn_found, gate_up_rest = tie(attn_found, gate_up_rest)
     attn_sum = add(attn_own_sum, *attn_found)
     attn_sum = total_of(exchange(attn_sum))
     gate_up_sum = jnp.concatenate([total_of(gate_up_arrived), total_of(gate_up_rest)])
@@ -1554,7 +1601,13 @@
     packed_sum = pack(gate_up_sum, down_sum)
     near = gather_near(packed_sum)
     attn_sum, near = tie(attn_sum, near)
-    found = gather_list(packed_sum, near, gather_rest(near))
+    rest = gather_rest(near)
+    attn_half = [attn_sum] + [swap(attn_sum, 2 * mask) for mask in range(1, chips)]
+    bounds = [0, block, 2 * block, 3 * block, 4 * block, 4 * block + bucket_rows * heads]
+    totals = [total[low:high] for low, high in zip(bounds, bounds[1:])]
+    totals[4] = totals[4].reshape(bucket_rows, heads)
+    attn_half, (rest, totals) = tie(attn_half, (rest, totals))
+    found = gather_list(packed_sum, near, rest)
     pieces, gate_up_moves, down_moves = [], [], []
 
     def gate_up_to(flip, mask, row):
@@ -1606,7 +1659,7 @@
         grad_gate, grad_up = spread_columns(halves[0], halves[1])
         grad_down_out = whole[:, :width].astype(F32)
 
-    attn_half = jnp.stack([attn_sum] + [swap(attn_sum, 2 * mask) for mask in range(1, chips)])
+    attn_half = jnp.stack(attn_half)
     attn_found = [attn_half, swap(attn_half, 1)]
 
     def attn_to(mask, flip):
@@ -1635,18 +1688,18 @@
         jnp.swapaxes(hidden_out, 1, 2),
         deleted.reshape(micro_count, local_rows),
         jnp.swapaxes(grad_in, 1, 2),
-        total[:block],
+        totals[0],
         attn_shard[0],
         attn_shard[1],
         attn_shard[2],
         attn_shard[3].reshape(proj // shards, width),
-        total[4 * block : 4 * block + bucket_rows * heads].reshape(bucket_rows, heads),
-        total[block : 2 * block],
+        totals[4],
+        totals[1],
         grad_gate,
         grad_up,
         grad_down_out,
-        total[2 * block : 3 * block],
-        total[3 * block : 4 * block],
+        totals[2],
+        totals[3],
     )
 
 

time: 594 us -> 564 us (0.949)
  blocking collectives: 18.9 us -> 0 us
  Pallas kernels: 204 us -> 195 us
  waiting for transfers between devices: 181 us -> 175 us
    all_to_all x1 -> x0, blocking collectives: 18.9 us -> none  [exchange(): lax.all_to_all(value, 'shard', split_axis=0, concat_axis=0, tiled=True)]
    ppermute x52, waiting for transfers between devices: 75.5 us -> 68.1 us  [swap(): return lax.ppermute(value, 'rep', [(i, i ^ mask) for i in range(reps)])]
    pallas_call x2 -> x3, Pallas kernels: 41.7 us -> 35.9 us  [weight_grad_call(): pl.pallas_call(kernel, in_specs=[ANY] * len(inputs), out_specs=[ANY] * co...]
    all_to_all x4 -> x5, starting transfers between devices: 17.6 us -> 22.4 us  [exchange(): lax.all_to_all(value, 'shard', split_axis=0, concat_axis=0, tiled=True)]
    all_to_all x4 -> x5, waiting for transfers between devices: 57.9 us -> 59.2 us  [exchange(): lax.all_to_all(value, 'shard', split_axis=0, concat_axis=0, tiled=True)]
    unnamed x107 -> x97, local copies, waits for them, and re-layouts: 15.9 us -> 15 us
  transfers between devices with their start and end apart: 66 -> 67, of which waited for: 26 -> 31; matrix products, arithmetic and copies ran while one was open for 15% -> 15% of each run, Pallas kernels for 28% -> 29%
where the time goes in v5:
time: 564 us; the launch traced here: 553 us
  Pallas kernels  195 us (35%)
  waiting for transfers between devices  175 us (31%)
  starting transfers between devices  74.9 us (13%)
  local copies, waits for them, and re-layouts  65.7 us (12%)
  other arithmetic  39.5 us (7%)
    ppermute x52, waiting for transfers between devices, swap(): return lax.ppermute(value, 'rep', [(i, i ^ mask) for i in range(reps)])  68.1 us
    all_to_all x5, waiting for transfers between devices, exchange(): lax.all_to_all(value, 'shard', split_axis=0, concat_axis=0, tiled=True)  59.2 us
    ppermute x10, waiting for transfers between devices, shift(): lax.ppermute(value, 'shard', [(i, (i + by) % shards) for i in range(shard...  47.6 us
    ppermute x52, starting transfers between devices, swap(): return lax.ppermute(value, 'rep', [(i, i ^ mask) for i in range(reps)])  43.9 us
    pallas_call x3, Pallas kernels, weight_grad_call(): pl.pallas_call(kernel, in_specs=[ANY] * len(inputs), out_specs=[ANY] * co...  35.9 us
    all_to_all x5, starting transfers between devices, exchange(): lax.all_to_all(value, 'shard', split_axis=0, concat_axis=0, tiled=True)  22.4 us
    convert_element_type x11, other arithmetic, add(): return sum((value.astype(F32) for value in values)).astype(BF16)  22.2 us
    pallas_call x1, Pallas kernels, gate_up_call(): pl.pallas_call(kernel, in_specs=[ANY] * (2 + count), out_specs=[ANY] * 4,...  18.1 us
  transfers between devices with their start and end apart: 67, of which 31 were waited for; matrix products, arithmetic and copies ran while one was open for 15% of the time, Pallas kernels for 29%

profile of v5, /device:TPU:0, one launch (start us, length us, event | category | flops | bytes accessed | tf_op | source)
XLA Modules:
  0.0 552.9 jit_solution(4842193042324558)
XLA Ops:
  7.7 5.0 collective-permute-start.2
  14.2 5.3 shard_map.289.rest_0_
  22.7 4.0 collective-permute-done.1
  37.0 9.1 %collective-permute-done.5 = bf16[3,192,384]{2,1,0:T(8,128)(2,1)S(1)} collective-permute-done((bf16[3,192,384]{2,1,0:T(8,128)(2,1)S(1)}, bf16[3,192,384]{2,1,0:T(8,128)(2,1)S(1)}, u32[]{:S(2)}, u32[]{:S(2)}) %collective-permute-start.5) | collective-permute-done | bytes 442400 | tf_op jit(solution)/shard_map/ppermute | solution.py:1021
  46.1 7.9 %collective-permute-done.4 = bf16[3,192,384]{2,1,0:T(8,128)(2,1)S(1)} collective-permute-done((bf16[3,192,384]{2,1,0:T(8,128)(2,1)S(1)}, bf16[3,192,384]{2,1,0:T(8,128)(2,1)S(1)}, u32[]{:S(2)}, u32[]{:S(2)}) %collective-permute-start.4) | collective-permute-done | bytes 442400 | tf_op jit(solution)/shard_map/ppermute | solution.py:1021
  60.9 7.5 %shard_map.290 = (bf16[384,1472]{1,0:T(8,128)(2,1)}, bf16[384,384]{1,0:T(8,128)(2,1)}, bf16[384,768]{1,0:T(8,128)(2,1)}, bf16[4,1472,384]{2,1,0:T(8,128)(2,1)}) custom-call(bf16[384,1472]{1,0:T(8,128)(2,1)} %bitcast.83, f32[1,1472]{1,0:T(1,128)} %reshape.272.gain_ref, bf16[368,384]{1,0:T(8,128)(2,1)} %rest_0_.1, bf16[368,384]{1,0:T(8,128)(2,1)} %rest_1_.1, ...), custom_call_target="tpu_custom_call" | custom-call | flops 1000 | bytes 1000 | tf_op jit(solution)/shard_map/pallas_call | solution.py:326
  68.5 15.8 %collective-permute-done.8.rest_6_.rest_5_ = bf16[592,896]{1,0:T(8,128)(2,1)} collective-permute-done((bf16[592,896]{1,0:T(8,128)(2,1)}, bf16[592,896]{1,0:T(8,128)(2,1)}, u32[]{:S(2)}, u32[]{:S(2)}) %collective-permute-start.8) | collective-permute-done | bytes 1060896 | tf_op jit(solution)/shard_map/ppermute | solution.py:1024
  86.9 5.3 shard_map.291.rest_6_
  92.2 8.9 %collective-permute-done.9.rest_1_ = bf16[384,768]{1,0:T(8,128)(2,1)S(1)} collective-permute-done((bf16[384,768]{1,0:T(8,128)(2,1)}, bf16[384,768]{1,0:T(8,128)(2,1)S(1)}, u32[]{:S(2)}, u32[]{:S(2)}) %collective-permute-start.9) | collective-permute-done | bytes 589856 | tf_op jit(solution)/shard_map/ppermute | solution.py:1024
  123.0 14.3 %collective-permute-done.15.rest_3_ = bf16[384,768]{1,0:T(8,128)(2,1)S(1)} collective-permute-done((bf16[384,768]{1,0:T(8,128)(2,1)}, bf16[384,768]{1,0:T(8,128)(2,1)S(1)}, u32[]{:S(2)}, u32[]{:S(2)}) %collective-permute-start.15) | collective-permute-done | bytes 589856 | tf_op jit(solution)/shard_map/ppermute | solution.py:1024
  141.0 5.4 shard_map.292
  146.4 5.4 shard_map.293
  154.6 5.4 shard_map.294
  160.0 5.3 collective-permute-done.19.rest_9_
  169.1 4.8 shard_map.295
  173.9 4.6 collective-permute-done.23.rest_9_
  181.0 8.2 %collective-permute-done.25.rest_14_ = bf16[176,896]{1,0:T(8,128)(2,1)S(1)} collective-permute-done((bf16[176,896]{1,0:T(8,128)(2,1)S(1)}, bf16[176,896]{1,0:T(8,128)(2,1)S(1)}, u32[]{:S(2)}, u32[]{:S(2)}) %collective-permute-start.25) | collective-permute-done | bytes 315424 | tf_op jit(solution)/shard_map/ppermute | solution.py:1021
  194.0 18.1 %shard_map.296 = (bf16[768,1792]{1,0:T(8,128)(2,1)}, bf16[768,1792]{1,0:T(8,128)(2,1)}, bf16[768,1792]{1,0:T(8,128)(2,1)}, bf16[1472,3584]{1,0:T(8,128)(2,1)}) custom-call(bf16[384,1536]{1,0:T(8,128)(2,1)} %get-tuple-element.230.own_ref.refs_0_, bf16[384,1536]{1,0:T(8,128)(2,1)} %copy-done.2, bf16[368,3584]{1,0:T(8,128)(2,1)} %shard_map.289.rest_0_, ...), custom_call_target="tpu_custom_call" | custom-call | flops 1000 | bytes 1000 | tf_op jit(solution)/shard_map/pallas_call | solution.py:455
  212.9 10.8 %shard_map.297 = (f32[384,1472]{1,0:T(8,128)}, bf16[384,1536]{1,0:T(8,128)(2,1)}, bf16[1792,1536]{1,0:T(8,128)(2,1)}) custom-call(bf16[768,1792]{1,0:T(8,128)(2,1)} %get-tuple-element.242.hidden_ref.refs_0_, bf16[448,1536]{1,0:T(8,128)(2,1)} %pad.30.rest_0_, bf16[592,896]{1,0:T(8,128)(2,1)} %collective-permute-done.6.rest_1_, ...), custom_call_target="tpu_custom_call" | custom-call | flops 1000 | bytes 1000 | tf_op jit(solution)/shard_map/pallas_call | solution.py:510
  227.9 7.8 %shard_map.298 = (f32[3,1472,128]{2,1,0:T(8,128)}, f32[384,1]{1,0:T(8,128)}, f32[384,1472]{1,0:T(8,128)}, bf16[384,1536]{1,0:T(8,128)(2,1)}, f32[1,1472]{1,0:T(1,128)}, /*index=5*/f32[1,1472]{1,0:T(1,128)}) custom-call(f32[384,1472]{1,0:T(8,128)} %get-tuple-element.227.hidden_ref, f32[384,1472]{1,0:T(8,128)} %get-tuple-element.245.part_ref, ...), custom_call_target="tpu_custom_call" | custom-call | flops 1000 | bytes 1000 | tf_op jit(solution)/shard_map/pallas_call | solution.py:773
  239.8 11.1 %shard_map.300 = (bf16[4,112,1472]{2,1,0:T(8,128)(2,1)}, bf16[4,112,1472]{2,1,0:T(8,128)(2,1)}, bf16[4,112,1472]{2,1,0:T(8,128)(2,1)}, bf16[4,48,1472]{2,1,0:T(8,128)(2,1)}, bf16[4,64,1472]{2,1,0:T(8,128)(2,1)}) custom-call(bf16[768,1792]{1,0:T(8,128)(2,1)} %get-tuple-element.242.hidden_ref.refs_0_, bf16[384,1536]{1,0:T(8,128)(2,1)} %get-tuple-element.253.own_ref.refs_1_, ...), custom_call_target="tpu_custom_call" | custom-call | flops 1000 | bytes 1000 | tf_op jit(solution)/shard_map/pallas_call | solution.py:958
  253.0 11.7 %shard_map.299 = (bf16[768,1792]{1,0:T(8,128)(2,1)}, bf16[768,1792]{1,0:T(8,128)(2,1)}) custom-call(bf16[384,1536]{1,0:T(8,128)(2,1)} %get-tuple-element.253.own_ref.refs_1_, bf16[384,1536]{1,0:T(8,128)(2,1)} %copy-done.10, bf16[1792,1536]{1,0:T(8,128)(2,1)} %get-tuple-element.254.down_ref, bf16[768,1792]{1,0:T(8,128)(2,1)} %get-tuple-element.255.slope_ref, ...), custom_call_target="tpu_custom_call" | custom-call | flops 1000 | bytes 1000 | tf_op jit(solution)/shard_map/pallas_call | solution.py:642
  267.5 3.2 collective-permute-done.33
  277.7 12.3 %shard_map.301 = (bf16[4,176,896]{2,1,0:T(8,128)(2,1)}, bf16[4,176,896]{2,1,0:T(8,128)(2,1)}, bf16[4,176,896]{2,1,0:T(8,128)(2,1)}, bf16[4,80,896]{2,1,0:T(8,128)(2,1)}, bf16[4,96,896]{2,1,0:T(8,128)(2,1)}) custom-call(bf16[384,1536]{1,0:T(8,128)(2,1)} %get-tuple-element.230.own_ref.refs_0_, bf16[384,1536]{1,0:T(8,128)(2,1)} %copy-done.2, ...), custom_call_target="tpu_custom_call" | custom-call | flops 1000 | bytes 1000 | tf_op jit(solution)/shard_map/pallas_call | solution.py:958
  290.0 14.1 %shard_map.302 = (f32[384,1472]{1,0:T(8,128)}, bf16[384,1536]{1,0:T(8,128)(2,1)}) custom-call(bf16[768,1792]{1,0:T(8,128)(2,1)} %get-tuple-element.317.refs_2_.gate_ref, bf16[768,1792]{1,0:T(8,128)(2,1)} %get-tuple-element.264.refs_3_.up_ref, bf16[1472,3584]{1,0:T(8,128)(2,1)} %get-tuple-element.271.low_ref.high_ref, ...), custom_call_target="tpu_custom_call" | custom-call | flops 1000 | bytes 1000 | tf_op jit(solution)/shard_map/pallas_call | solution.py:671
  308.3 3.4 add_convert_fusion.1
  311.7 3.8 all-to-all-start.1
  318.6 8.7 %shard_map.303 = (f32[384,1472]{1,0:T(8,128)}, bf16[384,384]{1,0:T(8,128)(2,1)}, bf16[384,1472]{1,0:T(8,128)(2,1)}, f32[1,1472]{1,0:T(1,128)}) custom-call(f32[384,1472]{1,0:T(8,128)} %get-tuple-element.272.part_ref, bf16[384,1536]{1,0:T(8,128)(2,1)} %copy-done.25, f32[384,1472]{1,0:T(8,128)} %get-tuple-element.285.grad_ref, ...), custom_call_target="tpu_custom_call" | custom-call | flops 1000 | bytes 1000 | tf_op jit(solution)/shard_map/pallas_call | solution.py:826
  327.3 4.4 collective-permute-done.37
  344.0 4.8 shard_map.304
  348.8 4.8 shard_map.305
  353.5 4.8 shard_map.306
  359.4 5.0 all-to-all-start
  364.5 12.5 %shard_map.308 = (bf16[4,192,896]{2,1,0:T(8,128)(2,1)}, bf16[4,192,896]{2,1,0:T(8,128)(2,1)}, bf16[4,192,896]{2,1,0:T(8,128)(2,1)}, bf16[4,96,896]{2,1,0:T(8,128)(2,1)}, bf16[4,96,896]{2,1,0:T(8,128)(2,1)}) custom-call(bf16[384,1536]{1,0:T(8,128)(2,1)} %get-tuple-element.230.own_ref.refs_0_, bf16[384,1536]{1,0:T(8,128)(2,1)} %copy-done.2, ...), custom_call_target="tpu_custom_call" | custom-call | flops 1000 | bytes 1000 | tf_op jit(solution)/shard_map/pallas_call | solution.py:958
  379.1 3.6 reshape.261.out_grad_ref
  382.7 6.8 %shard_map.309 = f32[6,1,1024]{2,1,0:T(1,128)} custom-call(bf16[6,128,512]{2,1,0:T(8,128)(2,1)} %get-tuple-element.333.refs_0_, bf16[6,128,512]{2,1,0:T(8,128)(2,1)} %get-tuple-element.334.refs_1_, bf16[6,128,512]{2,1,0:T(8,128)(2,1)} %get-tuple-element.335.refs_2_, s32[1,384]{1,0:T(1,128)} %get-tuple-element.401.refs_3_), custom_call_target="tpu_custom_call" | custom-call | tf_op jit(solution)/shard_map/pallas_call | solution.py:76
  405.2 11.8 %all-to-all-done.part_ref = bf16[4,384,768]{2,1,0:T(8,128)(2,1)S(1)} async-done(((bf16[4,384,768]{2,1,0:T(8,128)(2,1)}), bf16[4,384,768]{2,1,0:T(8,128)(2,1)S(1)}, u32[]{:S(2)}, u32[]{:S(2)}) %all-to-all-start) | async-done | bytes 2359328 | tf_op jit(solution)/shard_map/all_to_all | solution.py:1429
  417.0 4.3 all-to-all-start.4
  421.8 8.2 %shard_map.307 = (bf16[384,768]{1,0:T(8,128)(2,1)}, bf16[3,1472,128]{2,1,0:T(8,128)(2,1)}, f32[1,1472]{1,0:T(1,128)}) custom-call(bf16[384,384]{1,0:T(8,128)(2,1)} %get-tuple-element.306.query_ref, bf16[4,384,768]{2,1,0:T(8,128)(2,1)} %copy-done.3, bf16[4,1472,384]{2,1,0:T(8,128)(2,1)} %get-tuple-element.209.wq_ref.wk_ref.wv_ref, ...), custom_call_target="tpu_custom_call" | custom-call | flops 1000 | bytes 1000 | tf_op jit(solution)/shard_map/pallas_call | solution.py:868
  431.7 6.7 %shard_map.310 = (bf16[4,4,208,384]{3,2,1,0:T(8,128)(2,1)}, bf16[4,4,208,384]{3,2,1,0:T(8,128)(2,1)}) custom-call(bf16[384,1472]{1,0:T(8,128)(2,1)} %get-tuple-element.315.normed_ref, bf16[384,384]{1,0:T(8,128)(2,1)} %get-tuple-element.306.query_ref, bf16[384,768]{1,0:T(8,128)(2,1)} %get-tuple-element.342.pair_ref, bf16[1472,384]{1,0:T(8,128)(2,1)} %reshape.261.out_grad_ref, ...), custom_call_target="tpu_custom_call" | custom-call | flops 1000 | bytes 1000 | tf_op jit(solution)/shard_map/pallas_call | solution.py:382
  438.5 3.3 add_convert_fusion
  441.9 9.2 %all-to-all-done.4 = bf16[4,176,896]{2,1,0:T(8,128)(2,1)} async-done(((bf16[4,176,896]{2,1,0:T(8,128)(2,1)}), bf16[4,176,896]{2,1,0:T(8,128)(2,1)}, u32[]{:S(2)}, u32[]{:S(2)}) %all-to-all-start.4) | async-done | bytes 1261600 | tf_op jit(solution)/shard_map/all_to_all | solution.py:1429
  451.1 4.6 all-to-all-start.2
  464.0 24.0 %all-to-all-done.2 = bf16[4,192,896]{2,1,0:T(8,128)(2,1)} async-done(((bf16[4,192,896]{2,1,0:T(8,128)(2,1)}), bf16[4,192,896]{2,1,0:T(8,128)(2,1)}, u32[]{:S(2)}, u32[]{:S(2)}) %all-to-all-start.2) | async-done | bytes 1376288 | tf_op jit(solution)/shard_map/all_to_all | solution.py:1429
  495.5 4.8 all-to-all-start.3
  500.3 14.2 %all-to-all-done.3 = bf16[4,208,384]{2,1,0:T(8,128)(2,1)S(1)} async-done(((bf16[4,208,384]{2,1,0:T(8,128)(2,1)}), bf16[4,208,384]{2,1,0:T(8,128)(2,1)S(1)}, u32[]{:S(2)}, u32[]{:S(2)}) %all-to-all-start.3) | async-done | bytes 639008 | tf_op jit(solution)/shard_map/all_to_all | solution.py:1429
  526.3 7.6 %collective-permute-done.54.refs_3_ = bf16[288,896]{1,0:T(8,128)(2,1)} collective-permute-done((bf16[288,896]{1,0:T(8,128)(2,1)}, bf16[288,896]{1,0:T(8,128)(2,1)}, u32[]{:S(2)}, u32[]{:S(2)}) %collective-permute-start.54) | collective-permute-done | bytes 516128 | tf_op jit(solution)/shard_map/ppermute | solution.py:1021
  537.8 9.5 %shard_map.312 = (f32[368,3584]{1,0:T(8,128)}, f32[368,3584]{1,0:T(8,128)}, f32[1472,896]{1,0:T(8,128)}) custom-call(bf16[592,896]{1,0:T(8,128)(2,1)} %copy-done.11, bf16[592,896]{1,0:T(8,128)(2,1)} %collective-permute-done.49.refs_1_, bf16[592,896]{1,0:T(8,128)(2,1)} %collective-permute-done.50.refs_2_, bf16[288,896]{1,0:T(8,128)(2,1)} %collective-permute-done.54.refs_3_, ...), custom_call_target="tpu_custom_call" | custom-call | tf_op jit(solution)/shard_map/pallas_call | solution.py:574
  (322 shorter events, 168.9 us)
Async XLA Ops:
  7.7 14.0 %collective-permute-start.2 = (bf16[208,384]{1,0:T(8,128)(2,1)}, bf16[208,384]{1,0:T(8,128)(2,1)}, u32[]{:S(2)}, u32[]{:S(2)}) collective-permute-start(bf16[208,384]{1,0:T(8,128)(2,1)} %pad_maximum_fusion.11), channel_id=1, source_target_pairs={{0,3},{1,0},{2,1},{3,2},{4,7},{5,4},{6,5},{7,6},{8,11},{9,8},{10,9... | collective-permute-start | bytes 479240 | tf_op jit(solution)/shard_map/ppermute | solution.py:1024
  12.8 13.8 %collective-permute-start.1 = (bf16[208,384]{1,0:T(8,128)(2,1)}, bf16[208,384]{1,0:T(8,128)(2,1)}, u32[]{:S(2)}, u32[]{:S(2)}) collective-permute-start(bf16[208,384]{1,0:T(8,128)(2,1)} %pad_maximum_fusion.11), channel_id=1, source_target_pairs={{0,2},{1,3},{2,0},{3,1},{4,6},{5,7},{6,4},{7,5},{8,10},{9,11},{10,... | collective-permute-start | bytes 479240 | tf_op jit(solution)/shard_map/ppermute | solution.py:1024
  12.8 14.8 %collective-permute-start = (bf16[208,384]{1,0:T(8,128)(2,1)}, bf16[208,384]{1,0:T(8,128)(2,1)S(1)}, u32[]{:S(2)}, u32[]{:S(2)}) collective-permute-start(bf16[208,384]{1,0:T(8,128)(2,1)} %pad_maximum_fusion.11), channel_id=1, source_target_pairs={{0,1},{1,2},{2,3},{3,0},{4,5},{5,6},{6,7},{7,4},{8,9},{9,10},{10,1... | collective-permute-start | bytes 479240 | tf_op jit(solution)/shard_map/ppermute | solution.py:1024
  27.7 28.0 %collective-permute-start.6 = (bf16[592,896]{1,0:T(8,128)(2,1)}, bf16[592,896]{1,0:T(8,128)(2,1)}, u32[]{:S(2)}, u32[]{:S(2)}) collective-permute-start(bf16[592,896]{1,0:T(8,128)(2,1)} %pad_maximum_fusion.7), channel_id=1, source_target_pairs={{0,1},{1,2},{2,3},{3,0},{4,5},{5,6},{6,7},{7,4},{8,9},{9,10},{10,1... | collective-permute-start | bytes 3182600 | tf_op jit(solution)/shard_map/ppermute | solution.py:1024
  32.0 14.1 %collective-permute-start.5 = (bf16[3,192,384]{2,1,0:T(8,128)(2,1)S(1)}, bf16[3,192,384]{2,1,0:T(8,128)(2,1)S(1)}, u32[]{:S(2)}, u32[]{:S(2)}) collective-permute-start(bf16[3,192,384]{2,1,0:T(8,128)(2,1)S(1)} %pad_maximum_fusion.10), channel_id=1, source_target_pairs={{0,24},{4,28},{8,16},{12,20},{16,8},{20,12},{24,0},{28,4},{1,25},{... | collective-permute-start | bytes 1327112 | tf_op jit(solution)/shard_map/ppermute | solution.py:1021
  33.6 20.4 %collective-permute-start.4 = (bf16[3,192,384]{2,1,0:T(8,128)(2,1)S(1)}, bf16[3,192,384]{2,1,0:T(8,128)(2,1)S(1)}, u32[]{:S(2)}, u32[]{:S(2)}) collective-permute-start(bf16[3,192,384]{2,1,0:T(8,128)(2,1)S(1)} %pad_maximum_fusion.10), channel_id=1, source_target_pairs={{0,16},{4,20},{8,24},{12,28},{16,0},{20,4},{24,8},{28,12},{1,17},{... | collective-permute-start | bytes 1327112 | tf_op jit(solution)/shard_map/ppermute | solution.py:1021
  35.0 19.1 %collective-permute-start.3 = (bf16[3,192,384]{2,1,0:T(8,128)(2,1)S(1)}, bf16[3,192,384]{2,1,0:T(8,128)(2,1)S(1)}, u32[]{:S(2)}, u32[]{:S(2)}) collective-permute-start(bf16[3,192,384]{2,1,0:T(8,128)(2,1)S(1)} %pad_maximum_fusion.10), channel_id=1, source_target_pairs={{0,8},{4,12},{8,0},{12,4},{16,24},{20,28},{24,16},{28,20},{1,9},{5... | collective-permute-start | bytes 1327112 | tf_op jit(solution)/shard_map/ppermute | solution.py:1021
  56.3 28.0 %collective-permute-start.8 = (bf16[592,896]{1,0:T(8,128)(2,1)}, bf16[592,896]{1,0:T(8,128)(2,1)}, u32[]{:S(2)}, u32[]{:S(2)}) collective-permute-start(bf16[592,896]{1,0:T(8,128)(2,1)} %collective-permute-done.6.rest_1_), channel_id=1, source_target_pairs={{0,1},{1,2},{2,3},{3,0},{4,5},{5,6},{6,7},{7,4},{8,9},{9,10},{10,1... | collective-permute-start | bytes 3182600 | tf_op jit(solution)/shard_map/ppermute | solution.py:1024
  58.0 34.2 %collective-permute-start.10 = (bf16[592,896]{1,0:T(8,128)(2,1)}, bf16[592,896]{1,0:T(8,128)(2,1)}, u32[]{:S(2)}, u32[]{:S(2)}) collective-permute-start(bf16[592,896]{1,0:T(8,128)(2,1)} %collective-permute-done.6.rest_1_), channel_id=1, source_target_pairs={{0,8},{4,12},{8,0},{12,4},{16,24},{20,28},{24,16},{28,20},{1,9},{5... | collective-permute-start | bytes 3182600 | tf_op jit(solution)/shard_map/ppermute | solution.py:1021
  59.4 32.8 %collective-permute-start.11 = (bf16[592,896]{1,0:T(8,128)(2,1)}, bf16[592,896]{1,0:T(8,128)(2,1)}, u32[]{:S(2)}, u32[]{:S(2)}) collective-permute-start(bf16[592,896]{1,0:T(8,128)(2,1)} %collective-permute-done.6.rest_1_), channel_id=1, source_target_pairs={{0,16},{4,20},{8,24},{12,28},{16,0},{20,4},{24,8},{28,12},{1,17},{... | collective-permute-start | bytes 3182600 | tf_op jit(solution)/shard_map/ppermute | solution.py:1021
  84.2 16.9 %collective-permute-start.9 = (bf16[384,768]{1,0:T(8,128)(2,1)}, bf16[384,768]{1,0:T(8,128)(2,1)S(1)}, u32[]{:S(2)}, u32[]{:S(2)}) collective-permute-start(bf16[384,768]{1,0:T(8,128)(2,1)} %get-tuple-element.205.rest_0_), channel_id=1, source_target_pairs={{0,1},{1,2},{2,3},{3,0},{4,5},{5,6},{6,7},{7,4},{8,9},{9,10},{10,1... | collective-permute-start | bytes 1769480 | tf_op jit(solution)/shard_map/ppermute | solution.py:1024
  101.2 18.9 %collective-permute-start.12 = (bf16[384,768]{1,0:T(8,128)(2,1)S(1)}, bf16[384,768]{1,0:T(8,128)(2,1)}, u32[]{:S(2)}, u32[]{:S(2)}) collective-permute-start(bf16[384,768]{1,0:T(8,128)(2,1)S(1)} %collective-permute-done.9.rest_1_), channel_id=1, source_target_pairs={{0,1},{1,2},{2,3},{3,0},{4,5},{5,6},{6,7},{7,4},{8,9},{9,10},{10,1... | collective-permute-start | bytes 1769480 | tf_op jit(solution)/shard_map/ppermute | solution.py:1024
  103.3 16.8 %collective-permute-start.13 = (bf16[288,896]{1,0:T(8,128)(2,1)}, bf16[288,896]{1,0:T(8,128)(2,1)}, u32[]{:S(2)}, u32[]{:S(2)}) collective-permute-start(bf16[288,896]{1,0:T(8,128)(2,1)} %slice.225), channel_id=1, source_target_pairs={{0,8},{4,12},{8,0},{12,4},{16,24},{20,28},{24,16},{28,20},{1,9},{5... | collective-permute-start | bytes 1548296 | tf_op jit(solution)/shard_map/ppermute | solution.py:1021
  106.4 13.7 %collective-permute-start.14 = (bf16[304,896]{1,0:T(8,128)(2,1)}, bf16[304,896]{1,0:T(8,128)(2,1)}, u32[]{:S(2)}, u32[]{:S(2)}) collective-permute-start(bf16[304,896]{1,0:T(8,128)(2,1)} %slice.226), channel_id=1, source_target_pairs={{0,16},{4,20},{8,24},{12,28},{16,0},{20,4},{24,8},{28,12},{1,17},{... | collective-permute-start | bytes 1634312 | tf_op jit(solution)/shard_map/ppermute | solution.py:1021
  120.1 31.7 %collective-permute-start.16 = (bf16[592,896]{1,0:T(8,128)(2,1)}, bf16[592,896]{1,0:T(8,128)(2,1)S(1)}, u32[]{:S(2)}, u32[]{:S(2)}) collective-permute-start(bf16[592,896]{1,0:T(8,128)(2,1)} %collective-permute-done.8.rest_6_.rest_5_), channel_id=1, source_target_pairs={{0,8},{4,12},{8,0},{12,4},{16,24},{20,28},{24,16},{28,20},{1,9},{5... | collective-permute-start | bytes 3182600 | tf_op jit(solution)/shard_map/ppermute | solution.py:1021
  121.6 30.2 %collective-permute-start.17 = (bf16[592,896]{1,0:T(8,128)(2,1)}, bf16[592,896]{1,0:T(8,128)(2,1)S(1)}, u32[]{:S(2)}, u32[]{:S(2)}) collective-permute-start(bf16[592,896]{1,0:T(8,128)(2,1)} %collective-permute-done.8.rest_6_.rest_5_), channel_id=1, source_target_pairs={{0,16},{4,20},{8,24},{12,28},{16,0},{20,4},{24,8},{28,12},{1,17},{... | collective-permute-start | bytes 3182600 | tf_op jit(solution)/shard_map/ppermute | solution.py:1021
  122.3 14.9 %collective-permute-start.15 = (bf16[384,768]{1,0:T(8,128)(2,1)}, bf16[384,768]{1,0:T(8,128)(2,1)S(1)}, u32[]{:S(2)}, u32[]{:S(2)}) collective-permute-start(bf16[384,768]{1,0:T(8,128)(2,1)} %collective-permute-done.12.rest_2_), channel_id=1, source_target_pairs={{0,1},{1,2},{2,3},{3,0},{4,5},{5,6},{6,7},{7,4},{8,9},{9,10},{10,1... | collective-permute-start | bytes 1769480 | tf_op jit(solution)/shard_map/ppermute | solution.py:1024
  139.5 20.5 %collective-permute-start.18 = (bf16[368,896]{1,0:T(8,128)(2,1)}, bf16[368,896]{1,0:T(8,128)(2,1)}, u32[]{:S(2)}, u32[]{:S(2)}) collective-permute-start(bf16[368,896]{1,0:T(8,128)(2,1)} %slice.244), channel_id=1, source_target_pairs={{0,1},{1,2},{2,3},{3,0},{4,5},{5,6},{6,7},{7,4},{8,9},{9,10},{10,1... | collective-permute-start | bytes 1978376 | tf_op jit(solution)/shard_map/ppermute | solution.py:1024
  165.3 13.2 %collective-permute-start.21 = (bf16[368,896]{1,0:T(8,128)(2,1)}, bf16[368,896]{1,0:T(8,128)(2,1)S(1)}, u32[]{:S(2)}, u32[]{:S(2)}) collective-permute-start(bf16[368,896]{1,0:T(8,128)(2,1)} %collective-permute-done.18.rest_11_), channel_id=1, source_target_pairs={{0,8},{4,12},{8,0},{12,4},{16,24},{20,28},{24,16},{28,20},{1,9},{5... | collective-permute-start | bytes 1978376 | tf_op jit(solution)/shard_map/ppermute | solution.py:1021
  190.5 21.6 %collective-permute-start.27 = (bf16[224,896]{1,0:T(8,128)(2,1)}, bf16[224,896]{1,0:T(8,128)(2,1)S(1)}, u32[]{:S(2)}, u32[]{:S(2)}) collective-permute-start(bf16[224,896]{1,0:T(8,128)(2,1)} %copy-done.32), channel_id=1, source_target_pairs={{0,8},{4,12},{8,0},{12,4},{16,24},{20,28},{24,16},{28,20},{1,9},{5... | collective-permute-start | bytes 1204232 | tf_op jit(solution)/shard_map/ppermute | solution.py:1021
  191.4 20.8 %collective-permute-start.28 = (bf16[224,896]{1,0:T(8,128)(2,1)}, bf16[224,896]{1,0:T(8,128)(2,1)}, u32[]{:S(2)}, u32[]{:S(2)}) collective-permute-start(bf16[224,896]{1,0:T(8,128)(2,1)} %copy-done.32), channel_id=1, source_target_pairs={{0,16},{4,20},{8,24},{12,28},{16,0},{20,4},{24,8},{28,12},{1,17},{... | collective-permute-start | bytes 1204232 | tf_op jit(solution)/shard_map/ppermute | solution.py:1021
  192.6 19.6 %collective-permute-start.29 = (bf16[224,896]{1,0:T(8,128)(2,1)}, bf16[224,896]{1,0:T(8,128)(2,1)}, u32[]{:S(2)}, u32[]{:S(2)}) collective-permute-start(bf16[224,896]{1,0:T(8,128)(2,1)} %copy-done.32), channel_id=1, source_target_pairs={{0,24},{4,28},{8,16},{12,20},{16,8},{20,12},{24,0},{28,4},{1,25},{... | collective-permute-start | bytes 1204232 | tf_op jit(solution)/shard_map/ppermute | solution.py:1021
  250.9 19.9 %collective-permute-start.33 = (bf16[4,64,1472]{2,1,0:T(8,128)(2,1)}, bf16[4,64,1472]{2,1,0:T(8,128)(2,1)S(1)}, u32[]{:S(2)}, u32[]{:S(2)}) collective-permute-start(bf16[4,64,1472]{2,1,0:T(8,128)(2,1)} %get-tuple-element.262), channel_id=1, source_target_pairs={{0,16},{4,20},{8,24},{12,28},{16,0},{20,4},{24,8},{28,12},{1,17},{... | collective-permute-start | bytes 2261000 | tf_op jit(solution)/shard_map/ppermute | solution.py:1021
  252.2 15.3 %collective-permute-start.32 = (bf16[4,48,1472]{2,1,0:T(8,128)(2,1)}, bf16[4,48,1472]{2,1,0:T(8,128)(2,1)S(1)}, u32[]{:S(2)}, u32[]{:S(2)}) collective-permute-start(bf16[4,48,1472]{2,1,0:T(8,128)(2,1)} %get-tuple-element.261), channel_id=1, source_target_pairs={{0,8},{4,12},{8,0},{12,4},{16,24},{20,28},{24,16},{28,20},{1,9},{5... | collective-permute-start | bytes 1695752 | tf_op jit(solution)/shard_map/ppermute | solution.py:1021
  274.2 31.7 %collective-permute-start.34 = (bf16[4,112,1472]{2,1,0:T(8,128)(2,1)}, bf16[4,112,1472]{2,1,0:T(8,128)(2,1)}, u32[]{:S(2)}, u32[]{:S(2)}) collective-permute-start(bf16[4,112,1472]{2,1,0:T(8,128)(2,1)} %pad_maximum_fusion.1), channel_id=1, source_target_pairs={{0,16},{4,20},{8,24},{12,28},{16,0},{20,4},{24,8},{28,12},{1,17},{... | collective-permute-start | bytes 3956744 | tf_op jit(solution)/shard_map/ppermute | solution.py:1021
  276.9 31.4 %collective-permute-start.35 = (bf16[4,112,1472]{2,1,0:T(8,128)(2,1)}, bf16[4,112,1472]{2,1,0:T(8,128)(2,1)}, u32[]{:S(2)}, u32[]{:S(2)}) collective-permute-start(bf16[4,112,1472]{2,1,0:T(8,128)(2,1)} %pad_maximum_fusion.2), channel_id=1, source_target_pairs={{0,8},{4,12},{8,0},{12,4},{16,24},{20,28},{24,16},{28,20},{1,9},{5... | collective-permute-start | bytes 3956744 | tf_op jit(solution)/shard_map/ppermute | solution.py:1021
  311.7 46.6 %all-to-all-start.1 = ((bf16[4,112,1472]{2,1,0:T(8,128)(2,1)}), bf16[4,112,1472]{2,1,0:T(8,128)(2,1)S(1)}, u32[]{:S(2)}, u32[]{:S(2)}) async-start(bf16[4,112,1472]{2,1,0:T(8,128)(2,1)} %add_convert_fusion.1), calls=%async_computation.1 | async-start | bytes 2752512 | tf_op jit(solution)/shard_map/all_to_all | solution.py:1429
  315.5 18.0 %collective-permute-start.38 = (bf16[4,96,896]{2,1,0:T(8,128)(2,1)}, bf16[4,96,896]{2,1,0:T(8,128)(2,1)}, u32[]{:S(2)}, u32[]{:S(2)}) collective-permute-start(bf16[4,96,896]{2,1,0:T(8,128)(2,1)} %get-tuple-element.291), channel_id=1, source_target_pairs={{0,16},{4,20},{8,24},{12,28},{16,0},{20,4},{24,8},{28,12},{1,17},{... | collective-permute-start | bytes 2064392 | tf_op jit(solution)/shard_map/ppermute | solution.py:1021
  316.5 15.1 %collective-permute-start.37 = (bf16[4,80,896]{2,1,0:T(8,128)(2,1)}, bf16[4,80,896]{2,1,0:T(8,128)(2,1)S(1)}, u32[]{:S(2)}, u32[]{:S(2)}) collective-permute-start(bf16[4,80,896]{2,1,0:T(8,128)(2,1)} %get-tuple-element.290), channel_id=1, source_target_pairs={{0,8},{4,12},{8,0},{12,4},{16,24},{20,28},{24,16},{28,20},{1,9},{5... | collective-permute-start | bytes 1720328 | tf_op jit(solution)/shard_map/ppermute | solution.py:1021
  337.0 40.0 %collective-permute-start.39 = (bf16[4,176,896]{2,1,0:T(8,128)(2,1)}, bf16[4,176,896]{2,1,0:T(8,128)(2,1)}, u32[]{:S(2)}, u32[]{:S(2)}) collective-permute-start(bf16[4,176,896]{2,1,0:T(8,128)(2,1)} %pad_maximum_fusion.5), channel_id=1, source_target_pairs={{0,16},{4,20},{8,24},{12,28},{16,0},{20,4},{24,8},{28,12},{1,17},{... | collective-permute-start | bytes 3784712 | tf_op jit(solution)/shard_map/ppermute | solution.py:1021
  340.5 36.5 %collective-permute-start.40 = (bf16[4,176,896]{2,1,0:T(8,128)(2,1)}, bf16[4,176,896]{2,1,0:T(8,128)(2,1)}, u32[]{:S(2)}, u32[]{:S(2)}) collective-permute-start(bf16[4,176,896]{2,1,0:T(8,128)(2,1)} %pad_maximum_fusion.6), channel_id=1, source_target_pairs={{0,8},{4,12},{8,0},{12,4},{16,24},{20,28},{24,16},{28,20},{1,9},{5... | collective-permute-start | bytes 3784712 | tf_op jit(solution)/shard_map/ppermute | solution.py:1021
  359.4 57.5 %all-to-all-start = ((bf16[4,384,768]{2,1,0:T(8,128)(2,1)}), bf16[4,384,768]{2,1,0:T(8,128)(2,1)S(1)}, u32[]{:S(2)}, u32[]{:S(2)}) async-start(bf16[4,384,768]{2,1,0:T(8,128)(2,1)} %get-tuple-element.308), calls=%async_computation | async-start | bytes 4718592 | tf_op jit(solution)/shard_map/all_to_all | solution.py:1429
  377.0 16.0 %collective-permute-start.41 = (bf16[4,96,896]{2,1,0:T(8,128)(2,1)}, bf16[4,96,896]{2,1,0:T(8,128)(2,1)}, u32[]{:S(2)}, u32[]{:S(2)}) collective-permute-start(bf16[4,96,896]{2,1,0:T(8,128)(2,1)} %get-tuple-element.331), channel_id=1, source_target_pairs={{0,8},{4,12},{8,0},{12,4},{16,24},{20,28},{24,16},{28,20},{1,9},{5... | collective-permute-start | bytes 2064392 | tf_op jit(solution)/shard_map/ppermute | solution.py:1021
  378.1 15.6 %collective-permute-start.42 = (bf16[4,96,896]{2,1,0:T(8,128)(2,1)}, bf16[4,96,896]{2,1,0:T(8,128)(2,1)}, u32[]{:S(2)}, u32[]{:S(2)}) collective-permute-start(bf16[4,96,896]{2,1,0:T(8,128)(2,1)} %get-tuple-element.332), channel_id=1, source_target_pairs={{0,16},{4,20},{8,24},{12,28},{16,0},{20,4},{24,8},{28,12},{1,17},{... | collective-permute-start | bytes 2064392 | tf_op jit(solution)/shard_map/ppermute | solution.py:1021
  397.4 32.7 %collective-permute-start.43 = (bf16[4,192,896]{2,1,0:T(8,128)(2,1)}, bf16[4,192,896]{2,1,0:T(8,128)(2,1)}, u32[]{:S(2)}, u32[]{:S(2)}) collective-permute-start(bf16[4,192,896]{2,1,0:T(8,128)(2,1)} %pad_maximum_fusion.3), channel_id=1, source_target_pairs={{0,16},{4,20},{8,24},{12,28},{16,0},{20,4},{24,8},{28,12},{1,17},{... | collective-permute-start | bytes 4128776 | tf_op jit(solution)/shard_map/ppermute | solution.py:1021
  400.9 29.2 %collective-permute-start.44 = (bf16[4,192,896]{2,1,0:T(8,128)(2,1)}, bf16[4,192,896]{2,1,0:T(8,128)(2,1)}, u32[]{:S(2)}, u32[]{:S(2)}) collective-permute-start(bf16[4,192,896]{2,1,0:T(8,128)(2,1)} %pad_maximum_fusion.4), channel_id=1, source_target_pairs={{0,8},{4,12},{8,0},{12,4},{16,24},{20,28},{24,16},{28,20},{1,9},{5... | collective-permute-start | bytes 4128776 | tf_op jit(solution)/shard_map/ppermute | solution.py:1021
  417.0 34.1 %all-to-all-start.4 = ((bf16[4,176,896]{2,1,0:T(8,128)(2,1)}), bf16[4,176,896]{2,1,0:T(8,128)(2,1)}, u32[]{:S(2)}, u32[]{:S(2)}) async-start(bf16[4,176,896]{2,1,0:T(8,128)(2,1)} %add_convert_fusion.2), calls=%async_computation.4 | async-start | bytes 2523136 | tf_op jit(solution)/shard_map/all_to_all | solution.py:1429
  438.4 17.2 %collective-permute-start.45 = (bf16[4,4,208,384]{3,2,1,0:T(8,128)(2,1)}, bf16[4,4,208,384]{3,2,1,0:T(8,128)(2,1)}, u32[]{:S(2)}, u32[]{:S(2)}) collective-permute-start(bf16[4,4,208,384]{3,2,1,0:T(8,128)(2,1)} %get-tuple-element.350), channel_id=1, source_target_pairs={{0,4},{4,0},{8,12},{12,8},{16,20},{20,16},{24,28},{28,24},{1,5},{5... | collective-permute-start | bytes 7667720 | tf_op jit(solution)/shard_map/ppermute | solution.py:1021
  451.1 36.9 %all-to-all-start.2 = ((bf16[4,192,896]{2,1,0:T(8,128)(2,1)}), bf16[4,192,896]{2,1,0:T(8,128)(2,1)}, u32[]{:S(2)}, u32[]{:S(2)}) async-start(bf16[4,192,896]{2,1,0:T(8,128)(2,1)} %add_convert_fusion), calls=%async_computation.2 | async-start | bytes 2752512 | tf_op jit(solution)/shard_map/all_to_all | solution.py:1429
  458.7 29.3 %collective-permute-start.46 = (bf16[4,208,384]{2,1,0:T(8,128)(2,1)}, bf16[4,208,384]{2,1,0:T(8,128)(2,1)S(1)}, u32[]{:S(2)}, u32[]{:S(2)}) collective-permute-start(bf16[4,208,384]{2,1,0:T(8,128)(2,1)} %get-tuple-element.385), channel_id=1, source_target_pairs={{0,8},{4,12},{8,0},{12,4},{16,24},{20,28},{24,16},{28,20},{1,9},{5... | collective-permute-start | bytes 1916936 | tf_op jit(solution)/shard_map/ppermute | solution.py:1021
  459.7 29.1 %collective-permute-start.47 = (bf16[4,208,384]{2,1,0:T(8,128)(2,1)}, bf16[4,208,384]{2,1,0:T(8,128)(2,1)}, u32[]{:S(2)}, u32[]{:S(2)}) collective-permute-start(bf16[4,208,384]{2,1,0:T(8,128)(2,1)} %get-tuple-element.384), channel_id=1, source_target_pairs={{0,16},{4,20},{8,24},{12,28},{16,0},{20,4},{24,8},{28,12},{1,17},{... | collective-permute-start | bytes 1916936 | tf_op jit(solution)/shard_map/ppermute | solution.py:1021
  460.7 28.0 %collective-permute-start.48 = (bf16[4,208,384]{2,1,0:T(8,128)(2,1)}, bf16[4,208,384]{2,1,0:T(8,128)(2,1)}, u32[]{:S(2)}, u32[]{:S(2)}) collective-permute-start(bf16[4,208,384]{2,1,0:T(8,128)(2,1)} %get-tuple-element.383), channel_id=1, source_target_pairs={{0,24},{4,28},{8,16},{12,20},{16,8},{20,12},{24,0},{28,4},{1,25},{... | collective-permute-start | bytes 1916936 | tf_op jit(solution)/shard_map/ppermute | solution.py:1021
  490.5 24.1 %collective-permute-start.49 = (bf16[592,896]{1,0:T(8,128)(2,1)S(1)}, bf16[592,896]{1,0:T(8,128)(2,1)}, u32[]{:S(2)}, u32[]{:S(2)}) collective-permute-start(bf16[592,896]{1,0:T(8,128)(2,1)S(1)} %pad_maximum_fusion.8.refs_0_), channel_id=1, source_target_pairs={{0,8},{4,12},{8,0},{12,4},{16,24},{20,28},{24,16},{28,20},{1,9},{5... | collective-permute-start | bytes 3182600 | tf_op jit(solution)/shard_map/ppermute | solution.py:1021
  491.6 23.4 %collective-permute-start.50 = (bf16[592,896]{1,0:T(8,128)(2,1)S(1)}, bf16[592,896]{1,0:T(8,128)(2,1)}, u32[]{:S(2)}, u32[]{:S(2)}) collective-permute-start(bf16[592,896]{1,0:T(8,128)(2,1)S(1)} %pad_maximum_fusion.8.refs_0_), channel_id=1, source_target_pairs={{0,16},{4,20},{8,24},{12,28},{16,0},{20,4},{24,8},{28,12},{1,17},{... | collective-permute-start | bytes 3182600 | tf_op jit(solution)/shard_map/ppermute | solution.py:1021
  495.5 19.0 %all-to-all-start.3 = ((bf16[4,208,384]{2,1,0:T(8,128)(2,1)}), bf16[4,208,384]{2,1,0:T(8,128)(2,1)S(1)}, u32[]{:S(2)}, u32[]{:S(2)}) async-start(bf16[4,208,384]{2,1,0:T(8,128)(2,1)} %fusion.2), calls=%async_computation.3 | async-start | bytes 1277952 | tf_op jit(solution)/shard_map/all_to_all | solution.py:1429
  500.3 34.2 %collective-permute-start.57 = (bf16[592,896]{1,0:T(8,128)(2,1)S(1)}, bf16[592,896]{1,0:T(8,128)(2,1)}, u32[]{:S(2)}, u32[]{:S(2)}) collective-permute-start(bf16[592,896]{1,0:T(8,128)(2,1)S(1)} %pad_maximum_fusion.8.refs_0_), channel_id=1, source_target_pairs={{0,4},{4,0},{8,12},{12,8},{16,20},{20,16},{24,28},{28,24},{1,5},{5... | collective-permute-start | bytes 3182600 | tf_op jit(solution)/shard_map/ppermute | solution.py:1021
  519.6 14.2 %collective-permute-start.55 = (bf16[304,896]{1,0:T(8,128)(2,1)S(1)}, bf16[304,896]{1,0:T(8,128)(2,1)S(1)}, u32[]{:S(2)}, u32[]{:S(2)}) collective-permute-start(bf16[304,896]{1,0:T(8,128)(2,1)S(1)} %slice.274), channel_id=1, source_target_pairs={{0,16},{4,20},{8,24},{12,28},{16,0},{20,4},{24,8},{28,12},{1,17},{... | collective-permute-start | bytes 1634312 | tf_op jit(solution)/shard_map/ppermute | solution.py:1021
  533.9 13.4 %collective-permute-start.56 = (bf16[4,192,384]{2,1,0:T(8,128)(2,1)S(1)}, bf16[4,192,384]{2,1,0:T(8,128)(2,1)}, u32[]{:S(2)}, u32[]{:S(2)}) collective-permute-start(bf16[4,192,384]{2,1,0:T(8,128)(2,1)S(1)} %pad_maximum_fusion.9.refs_0_), channel_id=1, source_target_pairs={{0,4},{4,0},{8,12},{12,8},{16,20},{20,16},{24,28},{28,24},{1,5},{5... | collective-permute-start | bytes 1769480 | tf_op jit(solution)/shard_map/ppermute | solution.py:1021
  (64 other events, 523.6 us)

commit v6 on v5

--- a/solution.py
+++ b/solution.py
@@ -1127,6 +1127,8 @@
     vector_pack = vector_pack.reshape(pack_rows, proj)
     attn_sent = jnp.concatenate([attn_piece, vector_pack])
     attn_arrived = [shift(attn_sent, step) for step in range(1, shards)]
+    token_rows = tokens.reshape(rows, width)
+    attn_arrived, (token_rows, attn_own) = tie(attn_arrived, (token_rows, attn_own))
     vectors = jnp.stack([vector_pack] + [part[attn_rows:] for part in attn_arrived])
     vectors = jnp.take(vectors, order, axis=0).reshape(shards, pack_rows * proj)
     attn_gain = vectors[:, :block].reshape(width).astype(F32)
@@ -1249,7 +1251,6 @@
     bias = bias_of_queries(bias_rows, own_slots.reshape(rows), group)
     first_len = seq_lengths[:, 0, 0]
 
-    token_rows = tokens.reshape(rows, width)
     normed_one, queries, own_pairs, attn_full = project_call(
         token_rows, attn_gain[None], attn_pieces, attn_places, block, proj
     )
@@ -1278,11 +1279,13 @@
             nears[2] = gather_near(ring[2])
     ring[-1], pairs[-1] = tie(ring[-1], pairs[-1])
     last = shift(ring[-1][:block])
+    pairs, nears[2] = tie(pairs, nears[2])
+    rests[2] = gather_rest(nears[2])
     context, probs, packed = [], [], []
     for micro in range(micro_count):
         if micro == micro_count - 1:
-            context, nears[2] = tie(context, nears[2])
-            rests[2] = gather_rest(nears[2])
+            context, (rests[2], last) = tie(context, (rests[2], last))
+            last_near = gather_near(last)
         *context, prob, pair = attention_call(
             micro,
             first_len[micro : micro + 1],
@@ -1299,9 +1302,10 @@
         ring[step], rests[step - 1] = tie(ring[step], rests[step - 1])
         nears[step] = gather_near(ring[step])
         rests[step] = gather_rest(nears[step])
-    context, (last, rests[shards - 2]) = tie(context, (last, rests[shards - 2]))
-    last_near = gather_near(last)
-    last_down = shift(ring[-1][block:])
+    if shards > 4:
+        context, rests[shards - 2] = tie(context, rests[shards - 2])
+    last_piece, last = tie(ring[-1][block:], last)
+    last_down = shift(last_piece)
     (context,) = context
     out_full, down_wide, cotangent_rows, gate_rows, gains, key_columns = early
     ffn_gain, delete_gain, delete_vec = gains

time: 564 us -> 557 us (0.988)
  waiting for transfers between devices: 175 us -> 161 us
    ppermute x10, waiting for transfers between devices: 47.6 us -> 34.9 us  [shift(): lax.ppermute(value, 'shard', [(i, (i + by) % shards) for i in range(shard...]
    unnamed x97 -> x91, local copies, waits for them, and re-layouts: 15 us -> 14.6 us
  transfers between devices with their start and end apart: 67 -> 67, of which waited for: 31 -> 31; matrix products, arithmetic and copies ran while one was open for 15% -> 16% of each run, Pallas kernels for 29% -> 30%
where the time goes in v6:
time: 557 us; the launch traced here: 546 us
  Pallas kernels  195 us (35%)
  waiting for transfers between devices  161 us (29%)
  starting transfers between devices  77.1 us (14%)
  local copies, waits for them, and re-layouts  67.3 us (12%)
  other arithmetic  42.4 us (8%)
    ppermute x52, waiting for transfers between devices, swap(): return lax.ppermute(value, 'rep', [(i, i ^ mask) for i in range(reps)])  67 us
    all_to_all x5, waiting for transfers between devices, exchange(): lax.all_to_all(value, 'shard', split_axis=0, concat_axis=0, tiled=True)  59.2 us
    ppermute x52, starting transfers between devices, swap(): return lax.ppermute(value, 'rep', [(i, i ^ mask) for i in range(reps)])  44.1 us
    pallas_call x3, Pallas kernels, weight_grad_call(): pl.pallas_call(kernel, in_specs=[ANY] * len(inputs), out_specs=[ANY] * co...  35.9 us
    ppermute x10, waiting for transfers between devices, shift(): lax.ppermute(value, 'shard', [(i, (i + by) % shards) for i in range(shard...  34.9 us
    all_to_all x5, starting transfers between devices, exchange(): lax.all_to_all(value, 'shard', split_axis=0, concat_axis=0, tiled=True)  23.7 us
    convert_element_type x11, other arithmetic, add(): return sum((value.astype(F32) for value in values)).astype(BF16)  22.3 us
    pallas_call x1, Pallas kernels, gate_up_call(): pl.pallas_call(kernel, in_specs=[ANY] * (2 + count), out_specs=[ANY] * 4,...  18 us
  transfers between devices with their start and end apart: 67, of which 31 were waited for; matrix products, arithmetic and copies ran while one was open for 16% of the time, Pallas kernels for 30%

profile of v6, /device:TPU:0, one launch (start us, length us, event | category | flops | bytes accessed | tf_op | source)
XLA Modules:
  0.0 546.0 jit_solution(10740163046845682777)
XLA Ops:
  8.9 3.0 collective-permute-start
  17.0 5.3 shard_map.289.rest_0_
  39.8 5.7 %collective-permute-done.5 = bf16[3,192,384]{2,1,0:T(8,128)(2,1)S(1)} collective-permute-done((bf16[3,192,384]{2,1,0:T(8,128)(2,1)S(1)}, bf16[3,192,384]{2,1,0:T(8,128)(2,1)S(1)}, u32[]{:S(2)}, u32[]{:S(2)}) %collective-permute-start.5) | collective-permute-done | bytes 442400 | tf_op jit(solution)/shard_map/ppermute | solution.py:1021
  45.5 8.3 %collective-permute-done.4 = bf16[3,192,384]{2,1,0:T(8,128)(2,1)} collective-permute-done((bf16[3,192,384]{2,1,0:T(8,128)(2,1)S(1)}, bf16[3,192,384]{2,1,0:T(8,128)(2,1)}, u32[]{:S(2)}, u32[]{:S(2)}) %collective-permute-start.4) | collective-permute-done | bytes 442400 | tf_op jit(solution)/shard_map/ppermute | solution.py:1021
  64.0 7.5 %shard_map.290 = (bf16[384,1472]{1,0:T(8,128)(2,1)}, bf16[384,384]{1,0:T(8,128)(2,1)}, bf16[384,768]{1,0:T(8,128)(2,1)}, bf16[4,1472,384]{2,1,0:T(8,128)(2,1)}) custom-call(bf16[384,1472]{1,0:T(8,128)(2,1)} %bitcast.85, f32[1,1472]{1,0:T(1,128)} %reshape.272.gain_ref, bf16[368,384]{1,0:T(8,128)(2,1)} %rest_0_.1, bf16[368,384]{1,0:T(8,128)(2,1)} %rest_1_.1, ...), custom_call_target="tpu_custom_call" | custom-call | flops 1000 | bytes 1000 | tf_op jit(solution)/shard_map/pallas_call | solution.py:326
  71.5 12.3 %collective-permute-done.8.rest_6_.rest_5_ = bf16[592,896]{1,0:T(8,128)(2,1)} collective-permute-done((bf16[592,896]{1,0:T(8,128)(2,1)}, bf16[592,896]{1,0:T(8,128)(2,1)}, u32[]{:S(2)}, u32[]{:S(2)}) %collective-permute-start.8) | collective-permute-done | bytes 1060896 | tf_op jit(solution)/shard_map/ppermute | solution.py:1024
  86.5 5.3 shard_map.291.rest_6_
  91.8 8.3 %collective-permute-done.9.rest_1_ = bf16[384,768]{1,0:T(8,128)(2,1)S(1)} collective-permute-done((bf16[384,768]{1,0:T(8,128)(2,1)}, bf16[384,768]{1,0:T(8,128)(2,1)S(1)}, u32[]{:S(2)}, u32[]{:S(2)}) %collective-permute-start.9) | collective-permute-done | bytes 589856 | tf_op jit(solution)/shard_map/ppermute | solution.py:1024
  121.2 14.3 %collective-permute-done.15.rest_3_ = bf16[384,768]{1,0:T(8,128)(2,1)S(1)} collective-permute-done((bf16[384,768]{1,0:T(8,128)(2,1)}, bf16[384,768]{1,0:T(8,128)(2,1)S(1)}, u32[]{:S(2)}, u32[]{:S(2)}) %collective-permute-start.15) | collective-permute-done | bytes 589856 | tf_op jit(solution)/shard_map/ppermute | solution.py:1024
  138.6 3.7 collective-permute-done.16.rest_7_.rest_6_
  147.8 5.4 shard_map.292
  153.2 5.4 shard_map.293
  162.1 5.4 shard_map.294
  167.5 4.8 shard_map.295
  174.4 8.9 %collective-permute-done.25.rest_14_ = bf16[176,896]{1,0:T(8,128)(2,1)S(1)} collective-permute-done((bf16[176,896]{1,0:T(8,128)(2,1)S(1)}, bf16[176,896]{1,0:T(8,128)(2,1)S(1)}, u32[]{:S(2)}, u32[]{:S(2)}) %collective-permute-start.25) | collective-permute-done | bytes 315424 | tf_op jit(solution)/shard_map/ppermute | solution.py:1021
  186.9 18.0 %shard_map.296 = (bf16[768,1792]{1,0:T(8,128)(2,1)}, bf16[768,1792]{1,0:T(8,128)(2,1)}, bf16[768,1792]{1,0:T(8,128)(2,1)}, bf16[1472,3584]{1,0:T(8,128)(2,1)}) custom-call(bf16[384,1536]{1,0:T(8,128)(2,1)} %get-tuple-element.249.own_ref.refs_0_, bf16[384,1536]{1,0:T(8,128)(2,1)} %copy-done.2, bf16[368,3584]{1,0:T(8,128)(2,1)} %shard_map.289.rest_0_, ...), custom_call_target="tpu_custom_call" | custom-call | flops 1000 | bytes 1000 | tf_op jit(solution)/shard_map/pallas_call | solution.py:455
  205.0 10.9 %shard_map.297 = (f32[384,1472]{1,0:T(8,128)}, bf16[384,1536]{1,0:T(8,128)(2,1)}, bf16[1792,1536]{1,0:T(8,128)(2,1)}) custom-call(bf16[768,1792]{1,0:T(8,128)(2,1)} %get-tuple-element.262.hidden_ref.refs_0_, bf16[448,1536]{1,0:T(8,128)(2,1)} %pad.30.rest_0_, bf16[592,896]{1,0:T(8,128)(2,1)} %collective-permute-done.6.rest_1_, ...), custom_call_target="tpu_custom_call" | custom-call | flops 1000 | bytes 1000 | tf_op jit(solution)/shard_map/pallas_call | solution.py:510
  220.1 7.7 %shard_map.298 = (f32[3,1472,128]{2,1,0:T(8,128)}, f32[384,1]{1,0:T(8,128)}, f32[384,1472]{1,0:T(8,128)}, bf16[384,1536]{1,0:T(8,128)(2,1)}, f32[1,1472]{1,0:T(1,128)}, /*index=5*/f32[1,1472]{1,0:T(1,128)}) custom-call(f32[384,1472]{1,0:T(8,128)} %get-tuple-element.245.hidden_ref, f32[384,1472]{1,0:T(8,128)} %get-tuple-element.265.part_ref, ...), custom_call_target="tpu_custom_call" | custom-call | flops 1000 | bytes 1000 | tf_op jit(solution)/shard_map/pallas_call | solution.py:773
  232.0 11.1 %shard_map.300 = (bf16[4,112,1472]{2,1,0:T(8,128)(2,1)}, bf16[4,112,1472]{2,1,0:T(8,128)(2,1)}, bf16[4,112,1472]{2,1,0:T(8,128)(2,1)}, bf16[4,48,1472]{2,1,0:T(8,128)(2,1)}, bf16[4,64,1472]{2,1,0:T(8,128)(2,1)}) custom-call(bf16[768,1792]{1,0:T(8,128)(2,1)} %get-tuple-element.262.hidden_ref.refs_0_, bf16[384,1536]{1,0:T(8,128)(2,1)} %get-tuple-element.273.own_ref.refs_1_, ...), custom_call_target="tpu_custom_call" | custom-call | flops 1000 | bytes 1000 | tf_op jit(solution)/shard_map/pallas_call | solution.py:958
  244.8 11.7 %shard_map.299 = (bf16[768,1792]{1,0:T(8,128)(2,1)}, bf16[768,1792]{1,0:T(8,128)(2,1)}) custom-call(bf16[384,1536]{1,0:T(8,128)(2,1)} %get-tuple-element.273.own_ref.refs_1_, bf16[384,1536]{1,0:T(8,128)(2,1)} %copy-done.10, bf16[1792,1536]{1,0:T(8,128)(2,1)} %get-tuple-element.274.down_ref, bf16[768,1792]{1,0:T(8,128)(2,1)} %get-tuple-element.275.slope_ref, ...), custom_call_target="tpu_custom_call" | custom-call | flops 1000 | bytes 1000 | tf_op jit(solution)/shard_map/pallas_call | solution.py:642
  259.3 3.6 collective-permute-done.33
  269.4 12.3 %shard_map.301 = (bf16[4,176,896]{2,1,0:T(8,128)(2,1)}, bf16[4,176,896]{2,1,0:T(8,128)(2,1)}, bf16[4,176,896]{2,1,0:T(8,128)(2,1)}, bf16[4,80,896]{2,1,0:T(8,128)(2,1)}, bf16[4,96,896]{2,1,0:T(8,128)(2,1)}) custom-call(bf16[384,1536]{1,0:T(8,128)(2,1)} %get-tuple-element.249.own_ref.refs_0_, bf16[384,1536]{1,0:T(8,128)(2,1)} %copy-done.2, ...), custom_call_target="tpu_custom_call" | custom-call | flops 1000 | bytes 1000 | tf_op jit(solution)/shard_map/pallas_call | solution.py:958
  281.7 14.2 %shard_map.302 = (f32[384,1472]{1,0:T(8,128)}, bf16[384,1536]{1,0:T(8,128)(2,1)}) custom-call(bf16[768,1792]{1,0:T(8,128)(2,1)} %get-tuple-element.337.refs_2_.gate_ref, bf16[768,1792]{1,0:T(8,128)(2,1)} %get-tuple-element.284.refs_3_.up_ref, bf16[1472,3584]{1,0:T(8,128)(2,1)} %get-tuple-element.291.low_ref.high_ref, ...), custom_call_target="tpu_custom_call" | custom-call | flops 1000 | bytes 1000 | tf_op jit(solution)/shard_map/pallas_call | solution.py:671
  300.2 3.4 add_convert_fusion.1
  303.6 5.0 all-to-all-start.1
  311.6 8.7 %shard_map.303 = (f32[384,1472]{1,0:T(8,128)}, bf16[384,384]{1,0:T(8,128)(2,1)}, bf16[384,1472]{1,0:T(8,128)(2,1)}, f32[1,1472]{1,0:T(1,128)}) custom-call(f32[384,1472]{1,0:T(8,128)} %get-tuple-element.292.part_ref, bf16[384,1536]{1,0:T(8,128)(2,1)} %copy-done.25, f32[384,1472]{1,0:T(8,128)} %get-tuple-element.305.grad_ref, ...), custom_call_target="tpu_custom_call" | custom-call | flops 1000 | bytes 1000 | tf_op jit(solution)/shard_map/pallas_call | solution.py:826
  320.4 4.3 collective-permute-done.37
  337.1 4.8 shard_map.304
  341.8 4.8 shard_map.305
  346.6 4.8 shard_map.306
  352.5 5.0 all-to-all-start
  357.5 12.5 %shard_map.308 = (bf16[4,192,896]{2,1,0:T(8,128)(2,1)}, bf16[4,192,896]{2,1,0:T(8,128)(2,1)}, bf16[4,192,896]{2,1,0:T(8,128)(2,1)}, bf16[4,96,896]{2,1,0:T(8,128)(2,1)}, bf16[4,96,896]{2,1,0:T(8,128)(2,1)}) custom-call(bf16[384,1536]{1,0:T(8,128)(2,1)} %get-tuple-element.249.own_ref.refs_0_, bf16[384,1536]{1,0:T(8,128)(2,1)} %copy-done.2, ...), custom_call_target="tpu_custom_call" | custom-call | flops 1000 | bytes 1000 | tf_op jit(solution)/shard_map/pallas_call | solution.py:958
  372.2 3.6 reshape.261.out_grad_ref
  375.8 6.8 %shard_map.309 = f32[6,1,1024]{2,1,0:T(1,128)} custom-call(bf16[6,128,512]{2,1,0:T(8,128)(2,1)} %get-tuple-element.353.refs_0_, bf16[6,128,512]{2,1,0:T(8,128)(2,1)} %get-tuple-element.354.refs_1_, bf16[6,128,512]{2,1,0:T(8,128)(2,1)} %get-tuple-element.355.refs_2_, s32[1,384]{1,0:T(1,128)} %get-tuple-element.421.refs_3_), custom_call_target="tpu_custom_call" | custom-call | tf_op jit(solution)/shard_map/pallas_call | solution.py:76
  395.0 3.2 add_convert_fusion.2
  398.2 11.8 %all-to-all-done.part_ref = bf16[4,384,768]{2,1,0:T(8,128)(2,1)S(1)} async-done(((bf16[4,384,768]{2,1,0:T(8,128)(2,1)}), bf16[4,384,768]{2,1,0:T(8,128)(2,1)S(1)}, u32[]{:S(2)}, u32[]{:S(2)}) %all-to-all-start) | async-done | bytes 2359328 | tf_op jit(solution)/shard_map/all_to_all | solution.py:1433
  410.0 4.3 all-to-all-start.4
  414.9 8.2 %shard_map.307 = (bf16[384,768]{1,0:T(8,128)(2,1)}, bf16[3,1472,128]{2,1,0:T(8,128)(2,1)}, f32[1,1472]{1,0:T(1,128)}) custom-call(bf16[384,384]{1,0:T(8,128)(2,1)} %get-tuple-element.326.query_ref, bf16[4,384,768]{2,1,0:T(8,128)(2,1)} %copy-done.3, bf16[4,1472,384]{2,1,0:T(8,128)(2,1)} %get-tuple-element.224.wq_ref.wk_ref.wv_ref, ...), custom_call_target="tpu_custom_call" | custom-call | flops 1000 | bytes 1000 | tf_op jit(solution)/shard_map/pallas_call | solution.py:868
  424.8 6.7 %shard_map.310 = (bf16[4,4,208,384]{3,2,1,0:T(8,128)(2,1)}, bf16[4,4,208,384]{3,2,1,0:T(8,128)(2,1)}) custom-call(bf16[384,1472]{1,0:T(8,128)(2,1)} %get-tuple-element.335.normed_ref, bf16[384,384]{1,0:T(8,128)(2,1)} %get-tuple-element.326.query_ref, bf16[384,768]{1,0:T(8,128)(2,1)} %get-tuple-element.362.pair_ref, bf16[1472,384]{1,0:T(8,128)(2,1)} %reshape.261.out_grad_ref, ...), custom_call_target="tpu_custom_call" | custom-call | flops 1000 | bytes 1000 | tf_op jit(solution)/shard_map/pallas_call | solution.py:382
  431.6 3.3 add_convert_fusion
  435.0 9.2 %all-to-all-done.4 = bf16[4,176,896]{2,1,0:T(8,128)(2,1)} async-done(((bf16[4,176,896]{2,1,0:T(8,128)(2,1)}), bf16[4,176,896]{2,1,0:T(8,128)(2,1)}, u32[]{:S(2)}, u32[]{:S(2)}) %all-to-all-start.4) | async-done | bytes 1261600 | tf_op jit(solution)/shard_map/all_to_all | solution.py:1433
  444.2 4.6 all-to-all-start.2
  448.8 3.0 fusion.6
  457.0 24.0 %all-to-all-done.2 = bf16[4,192,896]{2,1,0:T(8,128)(2,1)} async-done(((bf16[4,192,896]{2,1,0:T(8,128)(2,1)}), bf16[4,192,896]{2,1,0:T(8,128)(2,1)}, u32[]{:S(2)}, u32[]{:S(2)}) %all-to-all-start.2) | async-done | bytes 1376288 | tf_op jit(solution)/shard_map/all_to_all | solution.py:1433
  488.6 4.8 all-to-all-start.3
  493.4 14.2 %all-to-all-done.3 = bf16[4,208,384]{2,1,0:T(8,128)(2,1)S(1)} async-done(((bf16[4,208,384]{2,1,0:T(8,128)(2,1)}), bf16[4,208,384]{2,1,0:T(8,128)(2,1)S(1)}, u32[]{:S(2)}, u32[]{:S(2)}) %all-to-all-start.3) | async-done | bytes 639008 | tf_op jit(solution)/shard_map/all_to_all | solution.py:1433
  519.3 7.6 %collective-permute-done.54.refs_3_ = bf16[288,896]{1,0:T(8,128)(2,1)} collective-permute-done((bf16[288,896]{1,0:T(8,128)(2,1)}, bf16[288,896]{1,0:T(8,128)(2,1)}, u32[]{:S(2)}, u32[]{:S(2)}) %collective-permute-start.54) | collective-permute-done | bytes 516128 | tf_op jit(solution)/shard_map/ppermute | solution.py:1021
  530.9 9.5 %shard_map.312 = (f32[368,3584]{1,0:T(8,128)}, f32[368,3584]{1,0:T(8,128)}, f32[1472,896]{1,0:T(8,128)}) custom-call(bf16[592,896]{1,0:T(8,128)(2,1)} %copy-done.11, bf16[592,896]{1,0:T(8,128)(2,1)} %collective-permute-done.49.refs_1_, bf16[592,896]{1,0:T(8,128)(2,1)} %collective-permute-done.50.refs_2_, bf16[288,896]{1,0:T(8,128)(2,1)} %collective-permute-done.54.refs_3_, ...), custom_call_target="tpu_custom_call" | custom-call | tf_op jit(solution)/shard_map/pallas_call | solution.py:574
  (316 shorter events, 172.9 us)
Async XLA Ops:
  8.9 18.9 %collective-permute-start = (bf16[208,384]{1,0:T(8,128)(2,1)}, bf16[208,384]{1,0:T(8,128)(2,1)}, u32[]{:S(2)}, u32[]{:S(2)}) collective-permute-start(bf16[208,384]{1,0:T(8,128)(2,1)} %pad_maximum_fusion.12), channel_id=1, source_target_pairs={{0,1},{1,2},{2,3},{3,0},{4,5},{5,6},{6,7},{7,4},{8,9},{9,10},{10,1... | collective-permute-start | bytes 479240 | tf_op jit(solution)/shard_map/ppermute | solution.py:1024
  12.0 15.8 %collective-permute-start.1 = (bf16[208,384]{1,0:T(8,128)(2,1)}, bf16[208,384]{1,0:T(8,128)(2,1)}, u32[]{:S(2)}, u32[]{:S(2)}) collective-permute-start(bf16[208,384]{1,0:T(8,128)(2,1)} %pad_maximum_fusion.12), channel_id=1, source_target_pairs={{0,2},{1,3},{2,0},{3,1},{4,6},{5,7},{6,4},{7,5},{8,10},{9,11},{10,... | collective-permute-start | bytes 479240 | tf_op jit(solution)/shard_map/ppermute | solution.py:1024
  14.6 13.3 %collective-permute-start.2 = (bf16[208,384]{1,0:T(8,128)(2,1)}, bf16[208,384]{1,0:T(8,128)(2,1)}, u32[]{:S(2)}, u32[]{:S(2)}) collective-permute-start(bf16[208,384]{1,0:T(8,128)(2,1)} %pad_maximum_fusion.12), channel_id=1, source_target_pairs={{0,3},{1,0},{2,1},{3,2},{4,7},{5,4},{6,5},{7,6},{8,11},{9,8},{10,9... | collective-permute-start | bytes 479240 | tf_op jit(solution)/shard_map/ppermute | solution.py:1024
  29.8 26.6 %collective-permute-start.6 = (bf16[592,896]{1,0:T(8,128)(2,1)}, bf16[592,896]{1,0:T(8,128)(2,1)}, u32[]{:S(2)}, u32[]{:S(2)}) collective-permute-start(bf16[592,896]{1,0:T(8,128)(2,1)} %pad_maximum_fusion.8), channel_id=1, source_target_pairs={{0,1},{1,2},{2,3},{3,0},{4,5},{5,6},{6,7},{7,4},{8,9},{9,10},{10,1... | collective-permute-start | bytes 3182600 | tf_op jit(solution)/shard_map/ppermute | solution.py:1024
  31.4 14.1 %collective-permute-start.5 = (bf16[3,192,384]{2,1,0:T(8,128)(2,1)S(1)}, bf16[3,192,384]{2,1,0:T(8,128)(2,1)S(1)}, u32[]{:S(2)}, u32[]{:S(2)}) collective-permute-start(bf16[3,192,384]{2,1,0:T(8,128)(2,1)S(1)} %pad_maximum_fusion.11), channel_id=1, source_target_pairs={{0,24},{4,28},{8,16},{12,20},{16,8},{20,12},{24,0},{28,4},{1,25},{... | collective-permute-start | bytes 1327112 | tf_op jit(solution)/shard_map/ppermute | solution.py:1021
  33.9 19.8 %collective-permute-start.4 = (bf16[3,192,384]{2,1,0:T(8,128)(2,1)S(1)}, bf16[3,192,384]{2,1,0:T(8,128)(2,1)}, u32[]{:S(2)}, u32[]{:S(2)}) collective-permute-start(bf16[3,192,384]{2,1,0:T(8,128)(2,1)S(1)} %pad_maximum_fusion.11), channel_id=1, source_target_pairs={{0,16},{4,20},{8,24},{12,28},{16,0},{20,4},{24,8},{28,12},{1,17},{... | collective-permute-start | bytes 1327112 | tf_op jit(solution)/shard_map/ppermute | solution.py:1021
  34.4 19.4 %collective-permute-start.3 = (bf16[3,192,384]{2,1,0:T(8,128)(2,1)S(1)}, bf16[3,192,384]{2,1,0:T(8,128)(2,1)}, u32[]{:S(2)}, u32[]{:S(2)}) collective-permute-start(bf16[3,192,384]{2,1,0:T(8,128)(2,1)S(1)} %pad_maximum_fusion.11), channel_id=1, source_target_pairs={{0,8},{4,12},{8,0},{12,4},{16,24},{20,28},{24,16},{28,20},{1,9},{5... | collective-permute-start | bytes 1327112 | tf_op jit(solution)/shard_map/ppermute | solution.py:1021
  56.5 27.4 %collective-permute-start.8 = (bf16[592,896]{1,0:T(8,128)(2,1)}, bf16[592,896]{1,0:T(8,128)(2,1)}, u32[]{:S(2)}, u32[]{:S(2)}) collective-permute-start(bf16[592,896]{1,0:T(8,128)(2,1)} %collective-permute-done.6.rest_1_), channel_id=1, source_target_pairs={{0,1},{1,2},{2,3},{3,0},{4,5},{5,6},{6,7},{7,4},{8,9},{9,10},{10,1... | collective-permute-start | bytes 3182600 | tf_op jit(solution)/shard_map/ppermute | solution.py:1024
  57.0 34.8 %collective-permute-start.10 = (bf16[592,896]{1,0:T(8,128)(2,1)}, bf16[592,896]{1,0:T(8,128)(2,1)}, u32[]{:S(2)}, u32[]{:S(2)}) collective-permute-start(bf16[592,896]{1,0:T(8,128)(2,1)} %collective-permute-done.6.rest_1_), channel_id=1, source_target_pairs={{0,8},{4,12},{8,0},{12,4},{16,24},{20,28},{24,16},{28,20},{1,9},{5... | collective-permute-start | bytes 3182600 | tf_op jit(solution)/shard_map/ppermute | solution.py:1021
  58.5 33.3 %collective-permute-start.11 = (bf16[592,896]{1,0:T(8,128)(2,1)}, bf16[592,896]{1,0:T(8,128)(2,1)}, u32[]{:S(2)}, u32[]{:S(2)}) collective-permute-start(bf16[592,896]{1,0:T(8,128)(2,1)} %collective-permute-done.6.rest_1_), channel_id=1, source_target_pairs={{0,16},{4,20},{8,24},{12,28},{16,0},{20,4},{24,8},{28,12},{1,17},{... | collective-permute-start | bytes 3182600 | tf_op jit(solution)/shard_map/ppermute | solution.py:1021
  83.8 16.3 %collective-permute-start.9 = (bf16[384,768]{1,0:T(8,128)(2,1)}, bf16[384,768]{1,0:T(8,128)(2,1)S(1)}, u32[]{:S(2)}, u32[]{:S(2)}) collective-permute-start(bf16[384,768]{1,0:T(8,128)(2,1)} %get-tuple-element.231.rest_0_), channel_id=1, source_target_pairs={{0,1},{1,2},{2,3},{3,0},{4,5},{5,6},{6,7},{7,4},{8,9},{9,10},{10,1... | collective-permute-start | bytes 1769480 | tf_op jit(solution)/shard_map/ppermute | solution.py:1024
  100.1 18.6 %collective-permute-start.12 = (bf16[384,768]{1,0:T(8,128)(2,1)S(1)}, bf16[384,768]{1,0:T(8,128)(2,1)}, u32[]{:S(2)}, u32[]{:S(2)}) collective-permute-start(bf16[384,768]{1,0:T(8,128)(2,1)S(1)} %collective-permute-done.9.rest_1_), channel_id=1, source_target_pairs={{0,1},{1,2},{2,3},{3,0},{4,5},{5,6},{6,7},{7,4},{8,9},{9,10},{10,1... | collective-permute-start | bytes 1769480 | tf_op jit(solution)/shard_map/ppermute | solution.py:1024
  102.2 16.5 %collective-permute-start.13 = (bf16[288,896]{1,0:T(8,128)(2,1)}, bf16[288,896]{1,0:T(8,128)(2,1)}, u32[]{:S(2)}, u32[]{:S(2)}) collective-permute-start(bf16[288,896]{1,0:T(8,128)(2,1)} %slice.229), channel_id=1, source_target_pairs={{0,8},{4,12},{8,0},{12,4},{16,24},{20,28},{24,16},{28,20},{1,9},{5... | collective-permute-start | bytes 1548296 | tf_op jit(solution)/shard_map/ppermute | solution.py:1021
  118.8 23.6 %collective-permute-start.16 = (bf16[592,896]{1,0:T(8,128)(2,1)}, bf16[592,896]{1,0:T(8,128)(2,1)S(1)}, u32[]{:S(2)}, u32[]{:S(2)}) collective-permute-start(bf16[592,896]{1,0:T(8,128)(2,1)} %collective-permute-done.8.rest_6_.rest_5_), channel_id=1, source_target_pairs={{0,8},{4,12},{8,0},{12,4},{16,24},{20,28},{24,16},{28,20},{1,9},{5... | collective-permute-start | bytes 3182600 | tf_op jit(solution)/shard_map/ppermute | solution.py:1021
  120.8 23.0 %collective-permute-start.17 = (bf16[592,896]{1,0:T(8,128)(2,1)}, bf16[592,896]{1,0:T(8,128)(2,1)S(1)}, u32[]{:S(2)}, u32[]{:S(2)}) collective-permute-start(bf16[592,896]{1,0:T(8,128)(2,1)} %collective-permute-done.8.rest_6_.rest_5_), channel_id=1, source_target_pairs={{0,16},{4,20},{8,24},{12,28},{16,0},{20,4},{24,8},{28,12},{1,17},{... | collective-permute-start | bytes 3182600 | tf_op jit(solution)/shard_map/ppermute | solution.py:1021
  121.2 14.3 %collective-permute-start.15 = (bf16[384,768]{1,0:T(8,128)(2,1)}, bf16[384,768]{1,0:T(8,128)(2,1)S(1)}, u32[]{:S(2)}, u32[]{:S(2)}) collective-permute-start(bf16[384,768]{1,0:T(8,128)(2,1)} %collective-permute-done.12.rest_2_), channel_id=1, source_target_pairs={{0,1},{1,2},{2,3},{3,0},{4,5},{5,6},{6,7},{7,4},{8,9},{9,10},{10,1... | collective-permute-start | bytes 1769480 | tf_op jit(solution)/shard_map/ppermute | solution.py:1024
  137.7 20.9 %collective-permute-start.20 = (bf16[368,896]{1,0:T(8,128)(2,1)}, bf16[368,896]{1,0:T(8,128)(2,1)}, u32[]{:S(2)}, u32[]{:S(2)}) collective-permute-start(bf16[368,896]{1,0:T(8,128)(2,1)} %slice.250), channel_id=1, source_target_pairs={{0,1},{1,2},{2,3},{3,0},{4,5},{5,6},{6,7},{7,4},{8,9},{9,10},{10,1... | collective-permute-start | bytes 1978376 | tf_op jit(solution)/shard_map/ppermute | solution.py:1024
  143.9 14.7 %collective-permute-start.18 = (bf16[288,896]{1,0:T(8,128)(2,1)S(1)}, bf16[288,896]{1,0:T(8,128)(2,1)}, u32[]{:S(2)}, u32[]{:S(2)}) collective-permute-start(bf16[288,896]{1,0:T(8,128)(2,1)S(1)} %slice.248), channel_id=1, source_target_pairs={{0,8},{4,12},{8,0},{12,4},{16,24},{20,28},{24,16},{28,20},{1,9},{5... | collective-permute-start | bytes 1548296 | tf_op jit(solution)/shard_map/ppermute | solution.py:1021
  158.6 13.7 %collective-permute-start.21 = (bf16[368,896]{1,0:T(8,128)(2,1)}, bf16[368,896]{1,0:T(8,128)(2,1)S(1)}, u32[]{:S(2)}, u32[]{:S(2)}) collective-permute-start(bf16[368,896]{1,0:T(8,128)(2,1)} %collective-permute-done.20.rest_11_), channel_id=1, source_target_pairs={{0,8},{4,12},{8,0},{12,4},{16,24},{20,28},{24,16},{28,20},{1,9},{5... | collective-permute-start | bytes 1978376 | tf_op jit(solution)/shard_map/ppermute | solution.py:1021
  183.3 21.6 %collective-permute-start.27 = (bf16[224,896]{1,0:T(8,128)(2,1)S(1)}, bf16[224,896]{1,0:T(8,128)(2,1)}, u32[]{:S(2)}, u32[]{:S(2)}) collective-permute-start(bf16[224,896]{1,0:T(8,128)(2,1)S(1)} %collective-permute-done.23.rest_9_), channel_id=1, source_target_pairs={{0,8},{4,12},{8,0},{12,4},{16,24},{20,28},{24,16},{28,20},{1,9},{5... | collective-permute-start | bytes 1204232 | tf_op jit(solution)/shard_map/ppermute | solution.py:1021
  184.2 20.8 %collective-permute-start.28 = (bf16[224,896]{1,0:T(8,128)(2,1)S(1)}, bf16[224,896]{1,0:T(8,128)(2,1)}, u32[]{:S(2)}, u32[]{:S(2)}) collective-permute-start(bf16[224,896]{1,0:T(8,128)(2,1)S(1)} %collective-permute-done.23.rest_9_), channel_id=1, source_target_pairs={{0,16},{4,20},{8,24},{12,28},{16,0},{20,4},{24,8},{28,12},{1,17},{... | collective-permute-start | bytes 1204232 | tf_op jit(solution)/shard_map/ppermute | solution.py:1021
  185.1 19.9 %collective-permute-start.29 = (bf16[224,896]{1,0:T(8,128)(2,1)S(1)}, bf16[224,896]{1,0:T(8,128)(2,1)}, u32[]{:S(2)}, u32[]{:S(2)}) collective-permute-start(bf16[224,896]{1,0:T(8,128)(2,1)S(1)} %collective-permute-done.23.rest_9_), channel_id=1, source_target_pairs={{0,24},{4,28},{8,16},{12,20},{16,8},{20,12},{24,0},{28,4},{1,25},{... | collective-permute-start | bytes 1204232 | tf_op jit(solution)/shard_map/ppermute | solution.py:1021
  243.1 19.9 %collective-permute-start.33 = (bf16[4,64,1472]{2,1,0:T(8,128)(2,1)}, bf16[4,64,1472]{2,1,0:T(8,128)(2,1)S(1)}, u32[]{:S(2)}, u32[]{:S(2)}) collective-permute-start(bf16[4,64,1472]{2,1,0:T(8,128)(2,1)} %get-tuple-element.282), channel_id=1, source_target_pairs={{0,16},{4,20},{8,24},{12,28},{16,0},{20,4},{24,8},{28,12},{1,17},{... | collective-permute-start | bytes 2261000 | tf_op jit(solution)/shard_map/ppermute | solution.py:1021
  244.0 15.3 %collective-permute-start.32 = (bf16[4,48,1472]{2,1,0:T(8,128)(2,1)}, bf16[4,48,1472]{2,1,0:T(8,128)(2,1)S(1)}, u32[]{:S(2)}, u32[]{:S(2)}) collective-permute-start(bf16[4,48,1472]{2,1,0:T(8,128)(2,1)} %get-tuple-element.281), channel_id=1, source_target_pairs={{0,8},{4,12},{8,0},{12,4},{16,24},{20,28},{24,16},{28,20},{1,9},{5... | collective-permute-start | bytes 1695752 | tf_op jit(solution)/shard_map/ppermute | solution.py:1021
  266.3 31.7 %collective-permute-start.34 = (bf16[4,112,1472]{2,1,0:T(8,128)(2,1)}, bf16[4,112,1472]{2,1,0:T(8,128)(2,1)}, u32[]{:S(2)}, u32[]{:S(2)}) collective-permute-start(bf16[4,112,1472]{2,1,0:T(8,128)(2,1)} %pad_maximum_fusion.1), channel_id=1, source_target_pairs={{0,16},{4,20},{8,24},{12,28},{16,0},{20,4},{24,8},{28,12},{1,17},{... | collective-permute-start | bytes 3956744 | tf_op jit(solution)/shard_map/ppermute | solution.py:1021
  268.7 31.5 %collective-permute-start.35 = (bf16[4,112,1472]{2,1,0:T(8,128)(2,1)}, bf16[4,112,1472]{2,1,0:T(8,128)(2,1)}, u32[]{:S(2)}, u32[]{:S(2)}) collective-permute-start(bf16[4,112,1472]{2,1,0:T(8,128)(2,1)} %pad_maximum_fusion.2), channel_id=1, source_target_pairs={{0,8},{4,12},{8,0},{12,4},{16,24},{20,28},{24,16},{28,20},{1,9},{5... | collective-permute-start | bytes 3956744 | tf_op jit(solution)/shard_map/ppermute | solution.py:1021
  303.6 47.8 %all-to-all-start.1 = ((bf16[4,112,1472]{2,1,0:T(8,128)(2,1)}), bf16[4,112,1472]{2,1,0:T(8,128)(2,1)S(1)}, u32[]{:S(2)}, u32[]{:S(2)}) async-start(bf16[4,112,1472]{2,1,0:T(8,128)(2,1)} %add_convert_fusion.1), calls=%async_computation.1 | async-start | bytes 2752512 | tf_op jit(solution)/shard_map/all_to_all | solution.py:1433
  308.6 17.9 %collective-permute-start.38 = (bf16[4,96,896]{2,1,0:T(8,128)(2,1)}, bf16[4,96,896]{2,1,0:T(8,128)(2,1)}, u32[]{:S(2)}, u32[]{:S(2)}) collective-permute-start(bf16[4,96,896]{2,1,0:T(8,128)(2,1)} %get-tuple-element.311), channel_id=1, source_target_pairs={{0,16},{4,20},{8,24},{12,28},{16,0},{20,4},{24,8},{28,12},{1,17},{... | collective-permute-start | bytes 2064392 | tf_op jit(solution)/shard_map/ppermute | solution.py:1021
  309.7 15.0 %collective-permute-start.37 = (bf16[4,80,896]{2,1,0:T(8,128)(2,1)}, bf16[4,80,896]{2,1,0:T(8,128)(2,1)S(1)}, u32[]{:S(2)}, u32[]{:S(2)}) collective-permute-start(bf16[4,80,896]{2,1,0:T(8,128)(2,1)} %get-tuple-element.310), channel_id=1, source_target_pairs={{0,8},{4,12},{8,0},{12,4},{16,24},{20,28},{24,16},{28,20},{1,9},{5... | collective-permute-start | bytes 1720328 | tf_op jit(solution)/shard_map/ppermute | solution.py:1021
  330.1 40.0 %collective-permute-start.39 = (bf16[4,176,896]{2,1,0:T(8,128)(2,1)}, bf16[4,176,896]{2,1,0:T(8,128)(2,1)}, u32[]{:S(2)}, u32[]{:S(2)}) collective-permute-start(bf16[4,176,896]{2,1,0:T(8,128)(2,1)} %pad_maximum_fusion.5), channel_id=1, source_target_pairs={{0,16},{4,20},{8,24},{12,28},{16,0},{20,4},{24,8},{28,12},{1,17},{... | collective-permute-start | bytes 3784712 | tf_op jit(solution)/shard_map/ppermute | solution.py:1021
  333.6 36.5 %collective-permute-start.40 = (bf16[4,176,896]{2,1,0:T(8,128)(2,1)}, bf16[4,176,896]{2,1,0:T(8,128)(2,1)}, u32[]{:S(2)}, u32[]{:S(2)}) collective-permute-start(bf16[4,176,896]{2,1,0:T(8,128)(2,1)} %pad_maximum_fusion.6), channel_id=1, source_target_pairs={{0,8},{4,12},{8,0},{12,4},{16,24},{20,28},{24,16},{28,20},{1,9},{5... | collective-permute-start | bytes 3784712 | tf_op jit(solution)/shard_map/ppermute | solution.py:1021
  352.5 57.5 %all-to-all-start = ((bf16[4,384,768]{2,1,0:T(8,128)(2,1)}), bf16[4,384,768]{2,1,0:T(8,128)(2,1)S(1)}, u32[]{:S(2)}, u32[]{:S(2)}) async-start(bf16[4,384,768]{2,1,0:T(8,128)(2,1)} %get-tuple-element.328), calls=%async_computation | async-start | bytes 4718592 | tf_op jit(solution)/shard_map/all_to_all | solution.py:1433
  370.1 16.0 %collective-permute-start.41 = (bf16[4,96,896]{2,1,0:T(8,128)(2,1)}, bf16[4,96,896]{2,1,0:T(8,128)(2,1)}, u32[]{:S(2)}, u32[]{:S(2)}) collective-permute-start(bf16[4,96,896]{2,1,0:T(8,128)(2,1)} %get-tuple-element.351), channel_id=1, source_target_pairs={{0,8},{4,12},{8,0},{12,4},{16,24},{20,28},{24,16},{28,20},{1,9},{5... | collective-permute-start | bytes 2064392 | tf_op jit(solution)/shard_map/ppermute | solution.py:1021
  371.2 15.6 %collective-permute-start.42 = (bf16[4,96,896]{2,1,0:T(8,128)(2,1)}, bf16[4,96,896]{2,1,0:T(8,128)(2,1)}, u32[]{:S(2)}, u32[]{:S(2)}) collective-permute-start(bf16[4,96,896]{2,1,0:T(8,128)(2,1)} %get-tuple-element.352), channel_id=1, source_target_pairs={{0,16},{4,20},{8,24},{12,28},{16,0},{20,4},{24,8},{28,12},{1,17},{... | collective-permute-start | bytes 2064392 | tf_op jit(solution)/shard_map/ppermute | solution.py:1021
  390.5 32.7 %collective-permute-start.43 = (bf16[4,192,896]{2,1,0:T(8,128)(2,1)}, bf16[4,192,896]{2,1,0:T(8,128)(2,1)}, u32[]{:S(2)}, u32[]{:S(2)}) collective-permute-start(bf16[4,192,896]{2,1,0:T(8,128)(2,1)} %pad_maximum_fusion.3), channel_id=1, source_target_pairs={{0,16},{4,20},{8,24},{12,28},{16,0},{20,4},{24,8},{28,12},{1,17},{... | collective-permute-start | bytes 4128776 | tf_op jit(solution)/shard_map/ppermute | solution.py:1021
  394.1 29.2 %collective-permute-start.44 = (bf16[4,192,896]{2,1,0:T(8,128)(2,1)}, bf16[4,192,896]{2,1,0:T(8,128)(2,1)}, u32[]{:S(2)}, u32[]{:S(2)}) collective-permute-start(bf16[4,192,896]{2,1,0:T(8,128)(2,1)} %pad_maximum_fusion.4), channel_id=1, source_target_pairs={{0,8},{4,12},{8,0},{12,4},{16,24},{20,28},{24,16},{28,20},{1,9},{5... | collective-permute-start | bytes 4128776 | tf_op jit(solution)/shard_map/ppermute | solution.py:1021
  410.0 34.1 %all-to-all-start.4 = ((bf16[4,176,896]{2,1,0:T(8,128)(2,1)}), bf16[4,176,896]{2,1,0:T(8,128)(2,1)}, u32[]{:S(2)}, u32[]{:S(2)}) async-start(bf16[4,176,896]{2,1,0:T(8,128)(2,1)} %add_convert_fusion.2), calls=%async_computation.4 | async-start | bytes 2523136 | tf_op jit(solution)/shard_map/all_to_all | solution.py:1433
  431.6 17.2 %collective-permute-start.45 = (bf16[4,4,208,384]{3,2,1,0:T(8,128)(2,1)}, bf16[4,4,208,384]{3,2,1,0:T(8,128)(2,1)}, u32[]{:S(2)}, u32[]{:S(2)}) collective-permute-start(bf16[4,4,208,384]{3,2,1,0:T(8,128)(2,1)} %get-tuple-element.370), channel_id=1, source_target_pairs={{0,4},{4,0},{8,12},{12,8},{16,20},{20,16},{24,28},{28,24},{1,5},{5... | collective-permute-start | bytes 7667720 | tf_op jit(solution)/shard_map/ppermute | solution.py:1021
  444.2 36.9 %all-to-all-start.2 = ((bf16[4,192,896]{2,1,0:T(8,128)(2,1)}), bf16[4,192,896]{2,1,0:T(8,128)(2,1)}, u32[]{:S(2)}, u32[]{:S(2)}) async-start(bf16[4,192,896]{2,1,0:T(8,128)(2,1)} %add_convert_fusion), calls=%async_computation.2 | async-start | bytes 2752512 | tf_op jit(solution)/shard_map/all_to_all | solution.py:1433
  451.8 29.3 %collective-permute-start.46 = (bf16[4,208,384]{2,1,0:T(8,128)(2,1)}, bf16[4,208,384]{2,1,0:T(8,128)(2,1)S(1)}, u32[]{:S(2)}, u32[]{:S(2)}) collective-permute-start(bf16[4,208,384]{2,1,0:T(8,128)(2,1)} %get-tuple-element.405), channel_id=1, source_target_pairs={{0,8},{4,12},{8,0},{12,4},{16,24},{20,28},{24,16},{28,20},{1,9},{5... | collective-permute-start | bytes 1916936 | tf_op jit(solution)/shard_map/ppermute | solution.py:1021
  452.8 29.1 %collective-permute-start.47 = (bf16[4,208,384]{2,1,0:T(8,128)(2,1)}, bf16[4,208,384]{2,1,0:T(8,128)(2,1)}, u32[]{:S(2)}, u32[]{:S(2)}) collective-permute-start(bf16[4,208,384]{2,1,0:T(8,128)(2,1)} %get-tuple-element.404), channel_id=1, source_target_pairs={{0,16},{4,20},{8,24},{12,28},{16,0},{20,4},{24,8},{28,12},{1,17},{... | collective-permute-start | bytes 1916936 | tf_op jit(solution)/shard_map/ppermute | solution.py:1021
  453.9 28.1 %collective-permute-start.48 = (bf16[4,208,384]{2,1,0:T(8,128)(2,1)}, bf16[4,208,384]{2,1,0:T(8,128)(2,1)}, u32[]{:S(2)}, u32[]{:S(2)}) collective-permute-start(bf16[4,208,384]{2,1,0:T(8,128)(2,1)} %get-tuple-element.403), channel_id=1, source_target_pairs={{0,24},{4,28},{8,16},{12,20},{16,8},{20,12},{24,0},{28,4},{1,25},{... | collective-permute-start | bytes 1916936 | tf_op jit(solution)/shard_map/ppermute | solution.py:1021
  483.7 24.1 %collective-permute-start.49 = (bf16[592,896]{1,0:T(8,128)(2,1)S(1)}, bf16[592,896]{1,0:T(8,128)(2,1)}, u32[]{:S(2)}, u32[]{:S(2)}) collective-permute-start(bf16[592,896]{1,0:T(8,128)(2,1)S(1)} %pad_maximum_fusion.9.refs_0_), channel_id=1, source_target_pairs={{0,8},{4,12},{8,0},{12,4},{16,24},{20,28},{24,16},{28,20},{1,9},{5... | collective-permute-start | bytes 3182600 | tf_op jit(solution)/shard_map/ppermute | solution.py:1021
  484.7 23.5 %collective-permute-start.50 = (bf16[592,896]{1,0:T(8,128)(2,1)S(1)}, bf16[592,896]{1,0:T(8,128)(2,1)}, u32[]{:S(2)}, u32[]{:S(2)}) collective-permute-start(bf16[592,896]{1,0:T(8,128)(2,1)S(1)} %pad_maximum_fusion.9.refs_0_), channel_id=1, source_target_pairs={{0,16},{4,20},{8,24},{12,28},{16,0},{20,4},{24,8},{28,12},{1,17},{... | collective-permute-start | bytes 3182600 | tf_op jit(solution)/shard_map/ppermute | solution.py:1021
  488.6 19.0 %all-to-all-start.3 = ((bf16[4,208,384]{2,1,0:T(8,128)(2,1)}), bf16[4,208,384]{2,1,0:T(8,128)(2,1)S(1)}, u32[]{:S(2)}, u32[]{:S(2)}) async-start(bf16[4,208,384]{2,1,0:T(8,128)(2,1)} %fusion.2), calls=%async_computation.3 | async-start | bytes 1277952 | tf_op jit(solution)/shard_map/all_to_all | solution.py:1433
  493.4 34.2 %collective-permute-start.57 = (bf16[592,896]{1,0:T(8,128)(2,1)S(1)}, bf16[592,896]{1,0:T(8,128)(2,1)}, u32[]{:S(2)}, u32[]{:S(2)}) collective-permute-start(bf16[592,896]{1,0:T(8,128)(2,1)S(1)} %pad_maximum_fusion.9.refs_0_), channel_id=1, source_target_pairs={{0,4},{4,0},{8,12},{12,8},{16,20},{20,16},{24,28},{28,24},{1,5},{5... | collective-permute-start | bytes 3182600 | tf_op jit(solution)/shard_map/ppermute | solution.py:1021
  512.8 14.1 %collective-permute-start.55 = (bf16[304,896]{1,0:T(8,128)(2,1)S(1)}, bf16[304,896]{1,0:T(8,128)(2,1)S(1)}, u32[]{:S(2)}, u32[]{:S(2)}) collective-permute-start(bf16[304,896]{1,0:T(8,128)(2,1)S(1)} %slice.278), channel_id=1, source_target_pairs={{0,16},{4,20},{8,24},{12,28},{16,0},{20,4},{24,8},{28,12},{1,17},{... | collective-permute-start | bytes 1634312 | tf_op jit(solution)/shard_map/ppermute | solution.py:1021
  527.0 13.4 %collective-permute-start.56 = (bf16[4,192,384]{2,1,0:T(8,128)(2,1)S(1)}, bf16[4,192,384]{2,1,0:T(8,128)(2,1)}, u32[]{:S(2)}, u32[]{:S(2)}) collective-permute-start(bf16[4,192,384]{2,1,0:T(8,128)(2,1)S(1)} %pad_maximum_fusion.10.refs_0_), channel_id=1, source_target_pairs={{0,4},{4,0},{8,12},{12,8},{16,20},{20,16},{24,28},{28,24},{1,5},{5... | collective-permute-start | bytes 1769480 | tf_op jit(solution)/shard_map/ppermute | solution.py:1021
  (61 other events, 534.4 us)

commit v7 on v6

--- a/solution.py
+++ b/solution.py
@@ -57,8 +57,7 @@
 
 
 def bias_fold(score_grads, slots):
-    heads, local, group = score_grads[0].shape
-    count = len(score_grads)
+    count, heads, local, group = score_grads.shape
 
     def kernel(*refs):
         grad_refs, slots_ref, out_ref = refs[:count], refs[count], refs[count + 1]
@@ -67,7 +66,7 @@
             mine = slots_ref[:, index * local : (index + 1) * local]
             row = lax.broadcasted_iota(jnp.int32, (group, local), 0)
             place = (row == (group - 1) - mine).astype(BF16)
-            part = jnp.dot(place, ref[0], preferred_element_type=F32)
+            part = jnp.dot(place, ref[0, 0], preferred_element_type=F32)
             square = part if square is None else square + part
         wide = jnp.concatenate([square, jnp.zeros_like(square)], axis=1)
         rolled = pltpu.roll(wide, 0, 1, stride=1, stride_axis=0)
@@ -76,11 +75,13 @@
     return pl.pallas_call(
         kernel,
         grid=(heads,),
-        in_specs=[pl.BlockSpec((1, local, group), lambda h: (h, 0, 0))] * count
+        in_specs=[
+            pl.BlockSpec((1, 1, local, group), lambda h, m=m: (m, h, 0, 0)) for m in range(count)
+        ]
         + [pl.BlockSpec((1, count * local), lambda h: (0, 0))],
         out_specs=pl.BlockSpec((1, 1, 2 * group), lambda h: (h, 0, 0)),
         out_shape=jax.ShapeDtypeStruct((heads, 1, 2 * group), F32),
-    )(*score_grads, slots.reshape(1, count * local)).reshape(heads, 2 * group)
+    )(*[score_grads] * count, slots.reshape(1, count * local)).reshape(heads, 2 * group)
 
 
 def by_head(value, head, head_size):
@@ -95,7 +96,7 @@
     return lax.dot_general(left, right, (((1,), (1,)), ((), ())), preferred_element_type=F32)
 
 
-def attention_call(micro, lengths, queries, pairs, own_slots, key_slots, bias, context):
+def attention_call(micro, micro_count, lengths, queries, pairs, own_slots, key_slots, bias, into):
     heads, rows, group = bias.shape
     double = pairs[0].shape[1]
     count = len(pairs)
@@ -107,6 +108,7 @@
         pair_refs = rest[:count]
         own_ref, key_ref, bias_ref = rest[count : count + 3]
         context_ref, prob_ref, packed_ref, arrived = rest[-4:]
+        prob_ref, packed_ref = prob_ref.at[0], packed_ref.at[0]
         for index, ref in enumerate(pair_refs):
             arrived[index * local : (index + 1) * local] = ref[...]
         place = (
@@ -144,31 +146,32 @@
             pl.BlockSpec((1, group), lambda i: (0, 0)),
             pl.BlockSpec((heads, local, group), lambda i: (0, micro, 0)),
         ]
-        + [ANY] * len(context),
+        + [ANY] * len(into),
         out_specs=[
             pl.BlockSpec((local, proj), lambda i: (micro, 0)),
-            pl.BlockSpec((heads, local, group), lambda i: (0, 0, 0)),
-            pl.BlockSpec((group, double), lambda i: (0, 0)),
+            pl.BlockSpec((1, heads, local, group), lambda i: (micro, 0, 0, 0)),
+            pl.BlockSpec((1, group, double), lambda i: (micro, 0, 0)),
         ],
         out_shape=[
             jax.ShapeDtypeStruct(queries.shape, BF16),
-            jax.ShapeDtypeStruct((heads, local, group), BF16),
-            jax.ShapeDtypeStruct((group, double), BF16),
-        ],
-        input_output_aliases={count + 5: 0} if context else {},
+            jax.ShapeDtypeStruct((micro_count, heads, local, group), BF16),
+            jax.ShapeDtypeStruct((micro_count, group, double), BF16),
+        ],
+        input_output_aliases={count + 5 + i: i for i in range(len(into))},
         scratch_shapes=[pltpu.VMEM((group, double), BF16)],
         cost_estimate=LIGHT,
-    )(lengths, queries, *pairs, own_slots, key_slots, bias, *context)
-
-
-def attention_back_call(micro, queries, context_grad, probs, packed, key_slots, shards, sums):
-    heads, local, group = probs.shape
-    double = packed.shape[1]
+    )(lengths, queries, *pairs, own_slots, key_slots, bias, *into)
+
+
+def attention_back_call(queries, context_grad, probs, packed, key_slots, shards):
+    micro_count, heads, local, group = probs.shape
+    double = packed.shape[2]
     proj = double // 2
     head_size = proj // heads
 
     def kernel(query_ref, context_ref, prob_ref, packed_ref, key_ref, *rest):
-        score_ref, dq_ref, part_ref, sums = rest[-4:]
+        score_ref, dq_ref, part_ref, sums = rest
+        score_ref, prob_ref, packed_ref = score_ref.at[0], prob_ref.at[0], packed_ref.at[0]
         per_block = 128 // head_size
         for head in range(heads):
             context, start = by_head(context_ref[...], head, head_size)
@@ -199,31 +202,31 @@
             pick = (lax.broadcasted_iota(jnp.int32, (local, group), 1) == slots).astype(BF16)
             part_ref[index] = jnp.dot(pick, sums[...], preferred_element_type=F32).astype(BF16)
 
+    by_scores = pl.BlockSpec((1, heads, local, group), lambda i: (i, 0, 0, 0))
+    by_proj = pl.BlockSpec((local, proj), lambda i: (i, 0))
     return pl.pallas_call(
         kernel,
-        grid=(1,),
+        grid=(micro_count,),
         in_specs=[
-            pl.BlockSpec((local, proj), lambda i: (micro, 0)),
-            pl.BlockSpec((local, proj), lambda i: (micro, 0)),
-            pl.BlockSpec((heads, local, group), lambda i: (0, 0, 0)),
-            pl.BlockSpec((group, double), lambda i: (0, 0)),
-            pl.BlockSpec((group, 1), lambda i: (0, 0)),
-        ]
-        + [ANY] * len(sums),
+            by_proj,
+            by_proj,
+            by_scores,
+            pl.BlockSpec((1, group, double), lambda i: (i, 0, 0)),
+            pl.BlockSpec((group, 1), lambda i: (i, 0)),
+        ],
         out_specs=[
-            pl.BlockSpec((heads, local, group), lambda i: (0, 0, 0)),
-            pl.BlockSpec((local, proj), lambda i: (micro, 0)),
-            pl.BlockSpec((shards, local, double), lambda i: (0, micro, 0)),
+            by_scores,
+            by_proj,
+            pl.BlockSpec((shards, local, double), lambda i: (0, i, 0)),
         ],
         out_shape=[
-            jax.ShapeDtypeStruct((heads, local, group), BF16),
+            jax.ShapeDtypeStruct(probs.shape, BF16),
             jax.ShapeDtypeStruct(queries.shape, BF16),
             jax.ShapeDtypeStruct((shards, queries.shape[0], double), BF16),
         ],
-        input_output_aliases={5 + i: 1 + i for i in range(len(sums))},
         scratch_shapes=[pltpu.VMEM((group, double), BF16)],
         cost_estimate=LIGHT,
-    )(queries, context_grad, probs, packed, key_slots, *sums)
+    )(queries, context_grad, probs, packed, key_slots)
 
 
 def axis_ranks():
@@ -1265,7 +1268,7 @@
         cotangent.reshape(rows, width),
         gate_cotangent.reshape(rows, 1).astype(F32),
         [value[None] for value in (ffn_gain, delete_gain, delete_vec)],
-        [slots[micro].reshape(group, 1) for micro in range(micro_count)],
+        slots.reshape(micro_count * group, 1),
     )
     pairs = [own_pairs]
     for step in range(1, shards):
@@ -1281,23 +1284,23 @@
     last = shift(ring[-1][:block])
     pairs, nears[2] = tie(pairs, nears[2])
     rests[2] = gather_rest(nears[2])
-    context, probs, packed = [], [], []
+    made = []
     for micro in range(micro_count):
         if micro == micro_count - 1:
-            context, (rests[2], last) = tie(context, (rests[2], last))
+            made, (rests[2], last) = tie(made, (rests[2], last))
             last_near = gather_near(last)
-        *context, prob, pair = attention_call(
+        made = attention_call(
             micro,
+            micro_count,
             first_len[micro : micro + 1],
             queries,
             pairs,
             own_slots.reshape(rows, 1),
             key_slots[micro : micro + 1],
             bias,
-            context,
+            made,
         )
-        probs.append(prob)
-        packed.append(pair)
+    context, probs, packed = made
     for step in range(3, shards - 1):
         ring[step], rests[step - 1] = tie(ring[step], rests[step - 1])
         nears[step] = gather_near(ring[step])
@@ -1306,7 +1309,6 @@
         context, rests[shards - 2] = tie(context, rests[shards - 2])
     last_piece, last = tie(ring[-1][block:], last)
     last_down = shift(last_piece)
-    (context,) = context
     out_full, down_wide, cotangent_rows, gate_rows, gains, key_columns = early
     ffn_gain, delete_gain, delete_vec = gains
 
@@ -1488,20 +1490,9 @@
     )
     context_grad, gate_up_state = tie(context_grad, gate_up_state)
     gate_up_state = reduce_middle(gate_up_state, 1)
-    score_grads, sums = [], []
-    for micro in range(micro_count):
-        score_grad, *sums = attention_back_call(
-            micro,
-            queries,
-            context_grad,
-            probs[micro],
-            packed[micro],
-            key_columns[micro],
-            shards,
-            sums,
-        )
-        score_grads.append(score_grad)
-    query_grad, pair_parts = sums
+    score_grads, query_grad, pair_parts = attention_back_call(
+        queries, context_grad, probs, packed, key_columns, shards
+    )
     gate_grad, pair_parts = tie(gate_grad, pair_parts)
     pair_arrived = exchange(pair_parts)
     gate_up_buffers = gate_up_grads(

time: 557 us -> 554 us (level)
  starting transfers between devices: 77.1 us -> 88.6 us
    ppermute x10, starting transfers between devices: 9.34 us -> 21.3 us  [shift(): lax.ppermute(value, 'shard', [(i, (i + by) % shards) for i in range(shard...]
    pallas_call x4 -> x2, Pallas kernels: 21.1 us -> 16.5 us  [the longest x1 9.65 us: attention_back_call(): pl.pallas_call(kernel, grid=(micro_count,), in_specs=[by_proj, by_proj, b...]
  transfers between devices with their start and end apart: 67 -> 67, of which waited for: 31 -> 30; matrix products, arithmetic and copies ran while one was open for 16% -> 16% of each run, Pallas kernels for 30% -> 29%
where the time goes in v7:
time: 554 us; the launch traced here: 547 us
  Pallas kernels  190 us (34%)
  waiting for transfers between devices  157 us (28%)
  starting transfers between devices  88.6 us (16%)
  local copies, waits for them, and re-layouts  66 us (12%)
  other arithmetic  42.4 us (8%)
    ppermute x52, waiting for transfers between devices, swap(): return lax.ppermute(value, 'rep', [(i, i ^ mask) for i in range(reps)])  62.6 us
    all_to_all x5, waiting for transfers between devices, exchange(): lax.all_to_all(value, 'shard', split_axis=0, concat_axis=0, tiled=True)  59.2 us
    ppermute x52, starting transfers between devices, swap(): return lax.ppermute(value, 'rep', [(i, i ^ mask) for i in range(reps)])  43.5 us
    pallas_call x3, Pallas kernels, weight_grad_call(): pl.pallas_call(kernel, in_specs=[ANY] * len(inputs), out_specs=[ANY] * co...  35.9 us
    ppermute x10, waiting for transfers between devices, shift(): lax.ppermute(value, 'shard', [(i, (i + by) % shards) for i in range(shard...  34.9 us
    all_to_all x5, starting transfers between devices, exchange(): lax.all_to_all(value, 'shard', split_axis=0, concat_axis=0, tiled=True)  23.7 us
    convert_element_type x11, other arithmetic, add(): return sum((value.astype(F32) for value in values)).astype(BF16)  22.3 us
    ppermute x10, starting transfers between devices, shift(): lax.ppermute(value, 'shard', [(i, (i + by) % shards) for i in range(shard...  21.3 us
  transfers between devices with their start and end apart: 67, of which 30 were waited for; matrix products, arithmetic and copies ran while one was open for 16% of the time, Pallas kernels for 29%

profile of v7, /device:TPU:0, one launch (start us, length us, event | category | flops | bytes accessed | tf_op | source)
XLA Modules:
  0.0 547.1 jit_solution(15620837741936528716)
XLA Ops:
  8.9 3.0 collective-permute-start
  17.0 5.3 shard_map.289.rest_0_
  39.8 5.7 %collective-permute-done.5 = bf16[3,192,384]{2,1,0:T(8,128)(2,1)S(1)} collective-permute-done((bf16[3,192,384]{2,1,0:T(8,128)(2,1)S(1)}, bf16[3,192,384]{2,1,0:T(8,128)(2,1)S(1)}, u32[]{:S(2)}, u32[]{:S(2)}) %collective-permute-start.5) | collective-permute-done | bytes 442400 | tf_op jit(solution)/shard_map/ppermute | solution.py:1024
  45.5 8.3 %collective-permute-done.4 = bf16[3,192,384]{2,1,0:T(8,128)(2,1)} collective-permute-done((bf16[3,192,384]{2,1,0:T(8,128)(2,1)S(1)}, bf16[3,192,384]{2,1,0:T(8,128)(2,1)}, u32[]{:S(2)}, u32[]{:S(2)}) %collective-permute-start.4) | collective-permute-done | bytes 442400 | tf_op jit(solution)/shard_map/ppermute | solution.py:1024
  64.0 7.5 %shard_map.290 = (bf16[384,1472]{1,0:T(8,128)(2,1)}, bf16[384,384]{1,0:T(8,128)(2,1)}, bf16[384,768]{1,0:T(8,128)(2,1)}, bf16[4,1472,384]{2,1,0:T(8,128)(2,1)}) custom-call(bf16[384,1472]{1,0:T(8,128)(2,1)} %bitcast.80, f32[1,1472]{1,0:T(1,128)} %reshape.266.gain_ref, bf16[368,384]{1,0:T(8,128)(2,1)} %rest_0_.1, bf16[368,384]{1,0:T(8,128)(2,1)} %rest_1_.1, ...), custom_call_target="tpu_custom_call" | custom-call | flops 1000 | bytes 1000 | tf_op jit(solution)/shard_map/pallas_call | solution.py:329
  71.5 12.3 %collective-permute-done.8.rest_6_.rest_5_ = bf16[592,896]{1,0:T(8,128)(2,1)} collective-permute-done((bf16[592,896]{1,0:T(8,128)(2,1)}, bf16[592,896]{1,0:T(8,128)(2,1)}, u32[]{:S(2)}, u32[]{:S(2)}) %collective-permute-start.8) | collective-permute-done | bytes 1060896 | tf_op jit(solution)/shard_map/ppermute | solution.py:1027
  86.5 5.3 shard_map.291.rest_6_
  91.8 8.3 %collective-permute-done.9.rest_1_ = bf16[384,768]{1,0:T(8,128)(2,1)S(1)} collective-permute-done((bf16[384,768]{1,0:T(8,128)(2,1)}, bf16[384,768]{1,0:T(8,128)(2,1)S(1)}, u32[]{:S(2)}, u32[]{:S(2)}) %collective-permute-start.9) | collective-permute-done | bytes 589856 | tf_op jit(solution)/shard_map/ppermute | solution.py:1027
  121.3 14.3 %collective-permute-done.15.rest_3_ = bf16[384,768]{1,0:T(8,128)(2,1)S(1)} collective-permute-done((bf16[384,768]{1,0:T(8,128)(2,1)}, bf16[384,768]{1,0:T(8,128)(2,1)S(1)}, u32[]{:S(2)}, u32[]{:S(2)}) %collective-permute-start.15) | collective-permute-done | bytes 589856 | tf_op jit(solution)/shard_map/ppermute | solution.py:1027
  137.8 12.1 %collective-permute-start.20 = (bf16[368,896]{1,0:T(8,128)(2,1)}, bf16[368,896]{1,0:T(8,128)(2,1)}, u32[]{:S(2)}, u32[]{:S(2)}) collective-permute-start(bf16[368,896]{1,0:T(8,128)(2,1)} %slice.235), channel_id=1, source_target_pairs={{0,1},{1,2},{2,3},{3,0},{4,5},{5,6},{6,7},{7,4},{8,9},{9,10},{10,1... | collective-permute-start | bytes 1978376 | tf_op jit(solution)/shard_map/ppermute | solution.py:1027
  154.9 5.4 shard_map.292
  160.4 5.4 shard_map.293
  169.0 5.4 shard_map.294
  174.4 4.8 shard_map.295
  181.8 9.1 %collective-permute-done.25.rest_14_ = bf16[176,896]{1,0:T(8,128)(2,1)S(1)} collective-permute-done((bf16[176,896]{1,0:T(8,128)(2,1)S(1)}, bf16[176,896]{1,0:T(8,128)(2,1)S(1)}, u32[]{:S(2)}, u32[]{:S(2)}) %collective-permute-start.25) | collective-permute-done | bytes 315424 | tf_op jit(solution)/shard_map/ppermute | solution.py:1024
  194.5 18.0 %shard_map.296 = (bf16[768,1792]{1,0:T(8,128)(2,1)}, bf16[768,1792]{1,0:T(8,128)(2,1)}, bf16[768,1792]{1,0:T(8,128)(2,1)}, bf16[1472,3584]{1,0:T(8,128)(2,1)}) custom-call(bf16[384,1536]{1,0:T(8,128)(2,1)} %get-tuple-element.249.own_ref.refs_0_, bf16[384,1536]{1,0:T(8,128)(2,1)} %copy-done.2, bf16[368,3584]{1,0:T(8,128)(2,1)} %shard_map.289.rest_0_, ...), custom_call_target="tpu_custom_call" | custom-call | flops 1000 | bytes 1000 | tf_op jit(solution)/shard_map/pallas_call | solution.py:458
  212.6 10.8 %shard_map.297 = (f32[384,1472]{1,0:T(8,128)}, bf16[384,1536]{1,0:T(8,128)(2,1)}, bf16[1792,1536]{1,0:T(8,128)(2,1)}) custom-call(bf16[768,1792]{1,0:T(8,128)(2,1)} %get-tuple-element.262.hidden_ref.refs_0_, bf16[448,1536]{1,0:T(8,128)(2,1)} %pad.30.rest_0_, bf16[592,896]{1,0:T(8,128)(2,1)} %collective-permute-done.6.rest_1_, ...), custom_call_target="tpu_custom_call" | custom-call | flops 1000 | bytes 1000 | tf_op jit(solution)/shard_map/pallas_call | solution.py:513
  227.5 7.7 %shard_map.298 = (f32[3,1472,128]{2,1,0:T(8,128)}, f32[384,1]{1,0:T(8,128)}, f32[384,1472]{1,0:T(8,128)}, bf16[384,1536]{1,0:T(8,128)(2,1)}, f32[1,1472]{1,0:T(1,128)}, /*index=5*/f32[1,1472]{1,0:T(1,128)}) custom-call(f32[384,1472]{1,0:T(8,128)} %get-tuple-element.245.hidden_ref, f32[384,1472]{1,0:T(8,128)} %get-tuple-element.265.part_ref, ...), custom_call_target="tpu_custom_call" | custom-call | flops 1000 | bytes 1000 | tf_op jit(solution)/shard_map/pallas_call | solution.py:776
  235.4 2.9 collective-permute-done.31.other_ref.refs_2_
  239.3 11.1 %shard_map.300 = (bf16[4,112,1472]{2,1,0:T(8,128)(2,1)}, bf16[4,112,1472]{2,1,0:T(8,128)(2,1)}, bf16[4,112,1472]{2,1,0:T(8,128)(2,1)}, bf16[4,48,1472]{2,1,0:T(8,128)(2,1)}, bf16[4,64,1472]{2,1,0:T(8,128)(2,1)}) custom-call(bf16[768,1792]{1,0:T(8,128)(2,1)} %get-tuple-element.262.hidden_ref.refs_0_, bf16[384,1536]{1,0:T(8,128)(2,1)} %get-tuple-element.273.own_ref.refs_1_, ...), custom_call_target="tpu_custom_call" | custom-call | flops 1000 | bytes 1000 | tf_op jit(solution)/shard_map/pallas_call | solution.py:961
  252.3 11.7 %shard_map.299 = (bf16[768,1792]{1,0:T(8,128)(2,1)}, bf16[768,1792]{1,0:T(8,128)(2,1)}) custom-call(bf16[384,1536]{1,0:T(8,128)(2,1)} %get-tuple-element.273.own_ref.refs_1_, bf16[384,1536]{1,0:T(8,128)(2,1)} %copy-done.10, bf16[1792,1536]{1,0:T(8,128)(2,1)} %get-tuple-element.274.down_ref, bf16[768,1792]{1,0:T(8,128)(2,1)} %get-tuple-element.275.slope_ref, ...), custom_call_target="tpu_custom_call" | custom-call | flops 1000 | bytes 1000 | tf_op jit(solution)/shard_map/pallas_call | solution.py:645
  266.6 3.7 collective-permute-done.33
  276.9 12.2 %shard_map.301 = (bf16[4,176,896]{2,1,0:T(8,128)(2,1)}, bf16[4,176,896]{2,1,0:T(8,128)(2,1)}, bf16[4,176,896]{2,1,0:T(8,128)(2,1)}, bf16[4,80,896]{2,1,0:T(8,128)(2,1)}, bf16[4,96,896]{2,1,0:T(8,128)(2,1)}) custom-call(bf16[384,1536]{1,0:T(8,128)(2,1)} %get-tuple-element.249.own_ref.refs_0_, bf16[384,1536]{1,0:T(8,128)(2,1)} %copy-done.2, ...), custom_call_target="tpu_custom_call" | custom-call | flops 1000 | bytes 1000 | tf_op jit(solution)/shard_map/pallas_call | solution.py:961
  289.1 14.3 %shard_map.302 = (f32[384,1472]{1,0:T(8,128)}, bf16[384,1536]{1,0:T(8,128)(2,1)}) custom-call(bf16[768,1792]{1,0:T(8,128)(2,1)} %get-tuple-element.327.refs_2_.gate_ref, bf16[768,1792]{1,0:T(8,128)(2,1)} %get-tuple-element.284.refs_3_.up_ref, bf16[1472,3584]{1,0:T(8,128)(2,1)} %get-tuple-element.291.low_ref.high_ref, ...), custom_call_target="tpu_custom_call" | custom-call | flops 1000 | bytes 1000 | tf_op jit(solution)/shard_map/pallas_call | solution.py:674
  307.6 3.4 add_convert_fusion.1
  311.0 5.4 all-to-all-start.1
  319.2 8.8 %shard_map.303 = (f32[384,1472]{1,0:T(8,128)}, bf16[384,384]{1,0:T(8,128)(2,1)}, bf16[384,1472]{1,0:T(8,128)(2,1)}, f32[1,1472]{1,0:T(1,128)}) custom-call(f32[384,1472]{1,0:T(8,128)} %get-tuple-element.292.part_ref, bf16[384,1536]{1,0:T(8,128)(2,1)} %copy-done.25, f32[384,1472]{1,0:T(8,128)} %get-tuple-element.305.grad_ref, ...), custom_call_target="tpu_custom_call" | custom-call | flops 1000 | bytes 1000 | tf_op jit(solution)/shard_map/pallas_call | solution.py:829
  327.9 4.5 collective-permute-done.37
  343.2 9.6 %shard_map.304 = (bf16[3,6,128,512]{3,2,1,0:T(8,128)(2,1)}, bf16[384,384]{1,0:T(8,128)(2,1)}, bf16[4,384,768]{2,1,0:T(8,128)(2,1)}) custom-call(bf16[384,384]{1,0:T(8,128)(2,1)} %get-tuple-element.211.query_ref, bf16[384,384]{1,0:T(8,128)(2,1)} %get-tuple-element.312.context_ref, bf16[3,6,128,512]{3,2,1,0:T(8,128)(2,1)} %get-tuple-element.313.prob_ref, ...), custom_call_target="tpu_custom_call" | custom-call | flops 1000 | bytes 1000 | tf_op jit(solution)/shard_map/pallas_call | solution.py:207
  354.0 4.8 all-to-all-start
  358.8 12.6 %shard_map.306 = (bf16[4,192,896]{2,1,0:T(8,128)(2,1)}, bf16[4,192,896]{2,1,0:T(8,128)(2,1)}, bf16[4,192,896]{2,1,0:T(8,128)(2,1)}, bf16[4,96,896]{2,1,0:T(8,128)(2,1)}, bf16[4,96,896]{2,1,0:T(8,128)(2,1)}) custom-call(bf16[384,1536]{1,0:T(8,128)(2,1)} %get-tuple-element.249.own_ref.refs_0_, bf16[384,1536]{1,0:T(8,128)(2,1)} %copy-done.2, ...), custom_call_target="tpu_custom_call" | custom-call | flops 1000 | bytes 1000 | tf_op jit(solution)/shard_map/pallas_call | solution.py:961
  373.8 3.6 reshape.255.out_grad_ref
  377.4 6.8 %shard_map.307 = f32[6,1,1024]{2,1,0:T(1,128)} custom-call(bf16[3,6,128,512]{3,2,1,0:T(8,128)(2,1)} %get-tuple-element.343.refs_0_.refs_1_.refs_2_, bf16[3,6,128,512]{3,2,1,0:T(8,128)(2,1)} %get-tuple-element.343.refs_0_.refs_1_.refs_2_, bf16[3,6,128,512]{3,2,1,0:T(8,128)(2,1)} %get-tuple-element.343.refs_0_.refs_1_.refs_2_, s32[1,384]{1,0:T(1,128)} %get-tuple-element.409.refs_3_), custom_call_target="tpu_custom_call" | custom-call | tf_op jit(solution)/shard_map/pallas_call | solution.py:75
  396.4 3.2 add_convert_fusion.2
  399.6 11.7 %all-to-all-done.part_ref = bf16[4,384,768]{2,1,0:T(8,128)(2,1)S(1)} async-done(((bf16[4,384,768]{2,1,0:T(8,128)(2,1)}), bf16[4,384,768]{2,1,0:T(8,128)(2,1)S(1)}, u32[]{:S(2)}, u32[]{:S(2)}) %all-to-all-start) | async-done | bytes 2359328 | tf_op jit(solution)/shard_map/all_to_all | solution.py:1435
  411.3 4.5 all-to-all-start.4
  416.4 8.2 %shard_map.305 = (bf16[384,768]{1,0:T(8,128)(2,1)}, bf16[3,1472,128]{2,1,0:T(8,128)(2,1)}, f32[1,1472]{1,0:T(1,128)}) custom-call(bf16[384,384]{1,0:T(8,128)(2,1)} %get-tuple-element.316.query_ref, bf16[4,384,768]{2,1,0:T(8,128)(2,1)} %copy-done.3, bf16[4,1472,384]{2,1,0:T(8,128)(2,1)} %get-tuple-element.218.wq_ref.wk_ref.wv_ref, ...), custom_call_target="tpu_custom_call" | custom-call | flops 1000 | bytes 1000 | tf_op jit(solution)/shard_map/pallas_call | solution.py:871
  426.4 6.7 %shard_map.308 = (bf16[4,4,208,384]{3,2,1,0:T(8,128)(2,1)}, bf16[4,4,208,384]{3,2,1,0:T(8,128)(2,1)}) custom-call(bf16[384,1472]{1,0:T(8,128)(2,1)} %get-tuple-element.325.normed_ref, bf16[384,384]{1,0:T(8,128)(2,1)} %get-tuple-element.316.query_ref, bf16[384,768]{1,0:T(8,128)(2,1)} %get-tuple-element.350.pair_ref, bf16[1472,384]{1,0:T(8,128)(2,1)} %reshape.255.out_grad_ref, ...), custom_call_target="tpu_custom_call" | custom-call | flops 1000 | bytes 1000 | tf_op jit(solution)/shard_map/pallas_call | solution.py:385
  433.2 3.3 add_convert_fusion
  436.6 9.1 %all-to-all-done.4 = bf16[4,176,896]{2,1,0:T(8,128)(2,1)} async-done(((bf16[4,176,896]{2,1,0:T(8,128)(2,1)}), bf16[4,176,896]{2,1,0:T(8,128)(2,1)}, u32[]{:S(2)}, u32[]{:S(2)}) %all-to-all-start.4) | async-done | bytes 1261600 | tf_op jit(solution)/shard_map/all_to_all | solution.py:1435
  445.6 4.3 all-to-all-start.2
  450.0 3.0 fusion.6
  458.2 24.0 %all-to-all-done.2 = bf16[4,192,896]{2,1,0:T(8,128)(2,1)} async-done(((bf16[4,192,896]{2,1,0:T(8,128)(2,1)}), bf16[4,192,896]{2,1,0:T(8,128)(2,1)}, u32[]{:S(2)}, u32[]{:S(2)}) %all-to-all-start.2) | async-done | bytes 1376288 | tf_op jit(solution)/shard_map/all_to_all | solution.py:1435
  489.8 4.8 all-to-all-start.3
  494.6 14.4 %all-to-all-done.3 = bf16[4,208,384]{2,1,0:T(8,128)(2,1)S(1)} async-done(((bf16[4,208,384]{2,1,0:T(8,128)(2,1)}), bf16[4,208,384]{2,1,0:T(8,128)(2,1)S(1)}, u32[]{:S(2)}, u32[]{:S(2)}) %all-to-all-start.3) | async-done | bytes 639008 | tf_op jit(solution)/shard_map/all_to_all | solution.py:1435
  520.5 7.6 %collective-permute-done.54.refs_3_ = bf16[288,896]{1,0:T(8,128)(2,1)} collective-permute-done((bf16[288,896]{1,0:T(8,128)(2,1)}, bf16[288,896]{1,0:T(8,128)(2,1)}, u32[]{:S(2)}, u32[]{:S(2)}) %collective-permute-start.54) | collective-permute-done | bytes 516128 | tf_op jit(solution)/shard_map/ppermute | solution.py:1024
  532.2 9.5 %shard_map.310 = (f32[368,3584]{1,0:T(8,128)}, f32[368,3584]{1,0:T(8,128)}, f32[1472,896]{1,0:T(8,128)}) custom-call(bf16[592,896]{1,0:T(8,128)(2,1)} %copy-done.11, bf16[592,896]{1,0:T(8,128)(2,1)} %collective-permute-done.49.refs_1_, bf16[592,896]{1,0:T(8,128)(2,1)} %collective-permute-done.50.refs_2_, bf16[288,896]{1,0:T(8,128)(2,1)} %collective-permute-done.54.refs_3_, ...), custom_call_target="tpu_custom_call" | custom-call | tf_op jit(solution)/shard_map/pallas_call | solution.py:577
  541.7 3.0 shard_map.309
  (311 shorter events, 163.9 us)
Async XLA Ops:
  8.9 18.9 %collective-permute-start = (bf16[208,384]{1,0:T(8,128)(2,1)}, bf16[208,384]{1,0:T(8,128)(2,1)}, u32[]{:S(2)}, u32[]{:S(2)}) collective-permute-start(bf16[208,384]{1,0:T(8,128)(2,1)} %pad_maximum_fusion.12), channel_id=1, source_target_pairs={{0,1},{1,2},{2,3},{3,0},{4,5},{5,6},{6,7},{7,4},{8,9},{9,10},{10,1... | collective-permute-start | bytes 479240 | tf_op jit(solution)/shard_map/ppermute | solution.py:1027
  12.0 15.9 %collective-permute-start.1 = (bf16[208,384]{1,0:T(8,128)(2,1)}, bf16[208,384]{1,0:T(8,128)(2,1)}, u32[]{:S(2)}, u32[]{:S(2)}) collective-permute-start(bf16[208,384]{1,0:T(8,128)(2,1)} %pad_maximum_fusion.12), channel_id=1, source_target_pairs={{0,2},{1,3},{2,0},{3,1},{4,6},{5,7},{6,4},{7,5},{8,10},{9,11},{10,... | collective-permute-start | bytes 479240 | tf_op jit(solution)/shard_map/ppermute | solution.py:1027
  14.6 13.3 %collective-permute-start.2 = (bf16[208,384]{1,0:T(8,128)(2,1)}, bf16[208,384]{1,0:T(8,128)(2,1)}, u32[]{:S(2)}, u32[]{:S(2)}) collective-permute-start(bf16[208,384]{1,0:T(8,128)(2,1)} %pad_maximum_fusion.12), channel_id=1, source_target_pairs={{0,3},{1,0},{2,1},{3,2},{4,7},{5,4},{6,5},{7,6},{8,11},{9,8},{10,9... | collective-permute-start | bytes 479240 | tf_op jit(solution)/shard_map/ppermute | solution.py:1027
  29.8 26.6 %collective-permute-start.6 = (bf16[592,896]{1,0:T(8,128)(2,1)}, bf16[592,896]{1,0:T(8,128)(2,1)}, u32[]{:S(2)}, u32[]{:S(2)}) collective-permute-start(bf16[592,896]{1,0:T(8,128)(2,1)} %pad_maximum_fusion.8), channel_id=1, source_target_pairs={{0,1},{1,2},{2,3},{3,0},{4,5},{5,6},{6,7},{7,4},{8,9},{9,10},{10,1... | collective-permute-start | bytes 3182600 | tf_op jit(solution)/shard_map/ppermute | solution.py:1027
  31.4 14.1 %collective-permute-start.5 = (bf16[3,192,384]{2,1,0:T(8,128)(2,1)S(1)}, bf16[3,192,384]{2,1,0:T(8,128)(2,1)S(1)}, u32[]{:S(2)}, u32[]{:S(2)}) collective-permute-start(bf16[3,192,384]{2,1,0:T(8,128)(2,1)S(1)} %pad_maximum_fusion.11), channel_id=1, source_target_pairs={{0,24},{4,28},{8,16},{12,20},{16,8},{20,12},{24,0},{28,4},{1,25},{... | collective-permute-start | bytes 1327112 | tf_op jit(solution)/shard_map/ppermute | solution.py:1024
  33.9 19.8 %collective-permute-start.4 = (bf16[3,192,384]{2,1,0:T(8,128)(2,1)S(1)}, bf16[3,192,384]{2,1,0:T(8,128)(2,1)}, u32[]{:S(2)}, u32[]{:S(2)}) collective-permute-start(bf16[3,192,384]{2,1,0:T(8,128)(2,1)S(1)} %pad_maximum_fusion.11), channel_id=1, source_target_pairs={{0,16},{4,20},{8,24},{12,28},{16,0},{20,4},{24,8},{28,12},{1,17},{... | collective-permute-start | bytes 1327112 | tf_op jit(solution)/shard_map/ppermute | solution.py:1024
  34.4 19.4 %collective-permute-start.3 = (bf16[3,192,384]{2,1,0:T(8,128)(2,1)S(1)}, bf16[3,192,384]{2,1,0:T(8,128)(2,1)}, u32[]{:S(2)}, u32[]{:S(2)}) collective-permute-start(bf16[3,192,384]{2,1,0:T(8,128)(2,1)S(1)} %pad_maximum_fusion.11), channel_id=1, source_target_pairs={{0,8},{4,12},{8,0},{12,4},{16,24},{20,28},{24,16},{28,20},{1,9},{5... | collective-permute-start | bytes 1327112 | tf_op jit(solution)/shard_map/ppermute | solution.py:1024
  56.5 27.4 %collective-permute-start.8 = (bf16[592,896]{1,0:T(8,128)(2,1)}, bf16[592,896]{1,0:T(8,128)(2,1)}, u32[]{:S(2)}, u32[]{:S(2)}) collective-permute-start(bf16[592,896]{1,0:T(8,128)(2,1)} %collective-permute-done.6.rest_1_), channel_id=1, source_target_pairs={{0,1},{1,2},{2,3},{3,0},{4,5},{5,6},{6,7},{7,4},{8,9},{9,10},{10,1... | collective-permute-start | bytes 3182600 | tf_op jit(solution)/shard_map/ppermute | solution.py:1027
  57.0 34.8 %collective-permute-start.10 = (bf16[592,896]{1,0:T(8,128)(2,1)}, bf16[592,896]{1,0:T(8,128)(2,1)}, u32[]{:S(2)}, u32[]{:S(2)}) collective-permute-start(bf16[592,896]{1,0:T(8,128)(2,1)} %collective-permute-done.6.rest_1_), channel_id=1, source_target_pairs={{0,8},{4,12},{8,0},{12,4},{16,24},{20,28},{24,16},{28,20},{1,9},{5... | collective-permute-start | bytes 3182600 | tf_op jit(solution)/shard_map/ppermute | solution.py:1024
  58.5 33.3 %collective-permute-start.11 = (bf16[592,896]{1,0:T(8,128)(2,1)}, bf16[592,896]{1,0:T(8,128)(2,1)}, u32[]{:S(2)}, u32[]{:S(2)}) collective-permute-start(bf16[592,896]{1,0:T(8,128)(2,1)} %collective-permute-done.6.rest_1_), channel_id=1, source_target_pairs={{0,16},{4,20},{8,24},{12,28},{16,0},{20,4},{24,8},{28,12},{1,17},{... | collective-permute-start | bytes 3182600 | tf_op jit(solution)/shard_map/ppermute | solution.py:1024
  83.8 16.3 %collective-permute-start.9 = (bf16[384,768]{1,0:T(8,128)(2,1)}, bf16[384,768]{1,0:T(8,128)(2,1)S(1)}, u32[]{:S(2)}, u32[]{:S(2)}) collective-permute-start(bf16[384,768]{1,0:T(8,128)(2,1)} %get-tuple-element.225.rest_0_), channel_id=1, source_target_pairs={{0,1},{1,2},{2,3},{3,0},{4,5},{5,6},{6,7},{7,4},{8,9},{9,10},{10,1... | collective-permute-start | bytes 1769480 | tf_op jit(solution)/shard_map/ppermute | solution.py:1027
  100.1 18.7 %collective-permute-start.12 = (bf16[384,768]{1,0:T(8,128)(2,1)S(1)}, bf16[384,768]{1,0:T(8,128)(2,1)}, u32[]{:S(2)}, u32[]{:S(2)}) collective-permute-start(bf16[384,768]{1,0:T(8,128)(2,1)S(1)} %collective-permute-done.9.rest_1_), channel_id=1, source_target_pairs={{0,1},{1,2},{2,3},{3,0},{4,5},{5,6},{6,7},{7,4},{8,9},{9,10},{10,1... | collective-permute-start | bytes 1769480 | tf_op jit(solution)/shard_map/ppermute | solution.py:1027
  102.2 16.5 %collective-permute-start.14 = (bf16[304,896]{1,0:T(8,128)(2,1)}, bf16[304,896]{1,0:T(8,128)(2,1)}, u32[]{:S(2)}, u32[]{:S(2)}) collective-permute-start(bf16[304,896]{1,0:T(8,128)(2,1)} %slice.218), channel_id=1, source_target_pairs={{0,16},{4,20},{8,24},{12,28},{16,0},{20,4},{24,8},{28,12},{1,17},{... | collective-permute-start | bytes 1634312 | tf_op jit(solution)/shard_map/ppermute | solution.py:1024
  118.8 31.6 %collective-permute-start.16 = (bf16[592,896]{1,0:T(8,128)(2,1)}, bf16[592,896]{1,0:T(8,128)(2,1)S(1)}, u32[]{:S(2)}, u32[]{:S(2)}) collective-permute-start(bf16[592,896]{1,0:T(8,128)(2,1)} %collective-permute-done.8.rest_6_.rest_5_), channel_id=1, source_target_pairs={{0,8},{4,12},{8,0},{12,4},{16,24},{20,28},{24,16},{28,20},{1,9},{5... | collective-permute-start | bytes 3182600 | tf_op jit(solution)/shard_map/ppermute | solution.py:1024
  120.9 29.6 %collective-permute-start.17 = (bf16[592,896]{1,0:T(8,128)(2,1)}, bf16[592,896]{1,0:T(8,128)(2,1)S(1)}, u32[]{:S(2)}, u32[]{:S(2)}) collective-permute-start(bf16[592,896]{1,0:T(8,128)(2,1)} %collective-permute-done.8.rest_6_.rest_5_), channel_id=1, source_target_pairs={{0,16},{4,20},{8,24},{12,28},{16,0},{20,4},{24,8},{28,12},{1,17},{... | collective-permute-start | bytes 3182600 | tf_op jit(solution)/shard_map/ppermute | solution.py:1024
  121.3 14.3 %collective-permute-start.15 = (bf16[384,768]{1,0:T(8,128)(2,1)}, bf16[384,768]{1,0:T(8,128)(2,1)S(1)}, u32[]{:S(2)}, u32[]{:S(2)}) collective-permute-start(bf16[384,768]{1,0:T(8,128)(2,1)} %collective-permute-done.12.rest_2_), channel_id=1, source_target_pairs={{0,1},{1,2},{2,3},{3,0},{4,5},{5,6},{6,7},{7,4},{8,9},{9,10},{10,1... | collective-permute-start | bytes 1769480 | tf_op jit(solution)/shard_map/ppermute | solution.py:1027
  137.8 28.0 %collective-permute-start.20 = (bf16[368,896]{1,0:T(8,128)(2,1)}, bf16[368,896]{1,0:T(8,128)(2,1)}, u32[]{:S(2)}, u32[]{:S(2)}) collective-permute-start(bf16[368,896]{1,0:T(8,128)(2,1)} %slice.235), channel_id=1, source_target_pairs={{0,1},{1,2},{2,3},{3,0},{4,5},{5,6},{6,7},{7,4},{8,9},{9,10},{10,1... | collective-permute-start | bytes 1978376 | tf_op jit(solution)/shard_map/ppermute | solution.py:1027
  150.5 15.2 %collective-permute-start.18 = (bf16[288,896]{1,0:T(8,128)(2,1)S(1)}, bf16[288,896]{1,0:T(8,128)(2,1)}, u32[]{:S(2)}, u32[]{:S(2)}) collective-permute-start(bf16[288,896]{1,0:T(8,128)(2,1)S(1)} %slice.233), channel_id=1, source_target_pairs={{0,8},{4,12},{8,0},{12,4},{16,24},{20,28},{24,16},{28,20},{1,9},{5... | collective-permute-start | bytes 1548296 | tf_op jit(solution)/shard_map/ppermute | solution.py:1024
  165.8 13.5 %collective-permute-start.21 = (bf16[368,896]{1,0:T(8,128)(2,1)}, bf16[368,896]{1,0:T(8,128)(2,1)S(1)}, u32[]{:S(2)}, u32[]{:S(2)}) collective-permute-start(bf16[368,896]{1,0:T(8,128)(2,1)} %collective-permute-done.20.rest_11_), channel_id=1, source_target_pairs={{0,8},{4,12},{8,0},{12,4},{16,24},{20,28},{24,16},{28,20},{1,9},{5... | collective-permute-start | bytes 1978376 | tf_op jit(solution)/shard_map/ppermute | solution.py:1024
  190.9 21.6 %collective-permute-start.27 = (bf16[224,896]{1,0:T(8,128)(2,1)S(1)}, bf16[224,896]{1,0:T(8,128)(2,1)}, u32[]{:S(2)}, u32[]{:S(2)}) collective-permute-start(bf16[224,896]{1,0:T(8,128)(2,1)S(1)} %collective-permute-done.23.rest_9_), channel_id=1, source_target_pairs={{0,8},{4,12},{8,0},{12,4},{16,24},{20,28},{24,16},{28,20},{1,9},{5... | collective-permute-start | bytes 1204232 | tf_op jit(solution)/shard_map/ppermute | solution.py:1024
  191.7 20.8 %collective-permute-start.28 = (bf16[224,896]{1,0:T(8,128)(2,1)S(1)}, bf16[224,896]{1,0:T(8,128)(2,1)}, u32[]{:S(2)}, u32[]{:S(2)}) collective-permute-start(bf16[224,896]{1,0:T(8,128)(2,1)S(1)} %collective-permute-done.23.rest_9_), channel_id=1, source_target_pairs={{0,16},{4,20},{8,24},{12,28},{16,0},{20,4},{24,8},{28,12},{1,17},{... | collective-permute-start | bytes 1204232 | tf_op jit(solution)/shard_map/ppermute | solution.py:1024
  192.7 19.8 %collective-permute-start.29 = (bf16[224,896]{1,0:T(8,128)(2,1)S(1)}, bf16[224,896]{1,0:T(8,128)(2,1)}, u32[]{:S(2)}, u32[]{:S(2)}) collective-permute-start(bf16[224,896]{1,0:T(8,128)(2,1)S(1)} %collective-permute-done.23.rest_9_), channel_id=1, source_target_pairs={{0,24},{4,28},{8,16},{12,20},{16,8},{20,12},{24,0},{28,4},{1,25},{... | collective-permute-start | bytes 1204232 | tf_op jit(solution)/shard_map/ppermute | solution.py:1024
  250.4 19.9 %collective-permute-start.33 = (bf16[4,64,1472]{2,1,0:T(8,128)(2,1)}, bf16[4,64,1472]{2,1,0:T(8,128)(2,1)S(1)}, u32[]{:S(2)}, u32[]{:S(2)}) collective-permute-start(bf16[4,64,1472]{2,1,0:T(8,128)(2,1)} %get-tuple-element.282), channel_id=1, source_target_pairs={{0,16},{4,20},{8,24},{12,28},{16,0},{20,4},{24,8},{28,12},{1,17},{... | collective-permute-start | bytes 2261000 | tf_op jit(solution)/shard_map/ppermute | solution.py:1024
  251.3 15.3 %collective-permute-start.32 = (bf16[4,48,1472]{2,1,0:T(8,128)(2,1)}, bf16[4,48,1472]{2,1,0:T(8,128)(2,1)S(1)}, u32[]{:S(2)}, u32[]{:S(2)}) collective-permute-start(bf16[4,48,1472]{2,1,0:T(8,128)(2,1)} %get-tuple-element.281), channel_id=1, source_target_pairs={{0,8},{4,12},{8,0},{12,4},{16,24},{20,28},{24,16},{28,20},{1,9},{5... | collective-permute-start | bytes 1695752 | tf_op jit(solution)/shard_map/ppermute | solution.py:1024
  273.7 31.7 %collective-permute-start.34 = (bf16[4,112,1472]{2,1,0:T(8,128)(2,1)}, bf16[4,112,1472]{2,1,0:T(8,128)(2,1)}, u32[]{:S(2)}, u32[]{:S(2)}) collective-permute-start(bf16[4,112,1472]{2,1,0:T(8,128)(2,1)} %pad_maximum_fusion.1), channel_id=1, source_target_pairs={{0,16},{4,20},{8,24},{12,28},{16,0},{20,4},{24,8},{28,12},{1,17},{... | collective-permute-start | bytes 3956744 | tf_op jit(solution)/shard_map/ppermute | solution.py:1024
  276.0 31.7 %collective-permute-start.35 = (bf16[4,112,1472]{2,1,0:T(8,128)(2,1)}, bf16[4,112,1472]{2,1,0:T(8,128)(2,1)}, u32[]{:S(2)}, u32[]{:S(2)}) collective-permute-start(bf16[4,112,1472]{2,1,0:T(8,128)(2,1)} %pad_maximum_fusion.2), channel_id=1, source_target_pairs={{0,8},{4,12},{8,0},{12,4},{16,24},{20,28},{24,16},{28,20},{1,9},{5... | collective-permute-start | bytes 3956744 | tf_op jit(solution)/shard_map/ppermute | solution.py:1024
  311.0 41.9 %all-to-all-start.1 = ((bf16[4,112,1472]{2,1,0:T(8,128)(2,1)}), bf16[4,112,1472]{2,1,0:T(8,128)(2,1)S(1)}, u32[]{:S(2)}, u32[]{:S(2)}) async-start(bf16[4,112,1472]{2,1,0:T(8,128)(2,1)} %add_convert_fusion.1), calls=%async_computation.1 | async-start | bytes 2752512 | tf_op jit(solution)/shard_map/all_to_all | solution.py:1435
  316.4 17.9 %collective-permute-start.38 = (bf16[4,96,896]{2,1,0:T(8,128)(2,1)}, bf16[4,96,896]{2,1,0:T(8,128)(2,1)}, u32[]{:S(2)}, u32[]{:S(2)}) collective-permute-start(bf16[4,96,896]{2,1,0:T(8,128)(2,1)} %get-tuple-element.311), channel_id=1, source_target_pairs={{0,16},{4,20},{8,24},{12,28},{16,0},{20,4},{24,8},{28,12},{1,17},{... | collective-permute-start | bytes 2064392 | tf_op jit(solution)/shard_map/ppermute | solution.py:1024
  317.4 15.0 %collective-permute-start.37 = (bf16[4,80,896]{2,1,0:T(8,128)(2,1)}, bf16[4,80,896]{2,1,0:T(8,128)(2,1)S(1)}, u32[]{:S(2)}, u32[]{:S(2)}) collective-permute-start(bf16[4,80,896]{2,1,0:T(8,128)(2,1)} %get-tuple-element.310), channel_id=1, source_target_pairs={{0,8},{4,12},{8,0},{12,4},{16,24},{20,28},{24,16},{28,20},{1,9},{5... | collective-permute-start | bytes 1720328 | tf_op jit(solution)/shard_map/ppermute | solution.py:1024
  337.8 33.6 %collective-permute-start.39 = (bf16[4,176,896]{2,1,0:T(8,128)(2,1)}, bf16[4,176,896]{2,1,0:T(8,128)(2,1)}, u32[]{:S(2)}, u32[]{:S(2)}) collective-permute-start(bf16[4,176,896]{2,1,0:T(8,128)(2,1)} %pad_maximum_fusion.5), channel_id=1, source_target_pairs={{0,16},{4,20},{8,24},{12,28},{16,0},{20,4},{24,8},{28,12},{1,17},{... | collective-permute-start | bytes 3784712 | tf_op jit(solution)/shard_map/ppermute | solution.py:1024
  341.3 30.1 %collective-permute-start.40 = (bf16[4,176,896]{2,1,0:T(8,128)(2,1)}, bf16[4,176,896]{2,1,0:T(8,128)(2,1)}, u32[]{:S(2)}, u32[]{:S(2)}) collective-permute-start(bf16[4,176,896]{2,1,0:T(8,128)(2,1)} %pad_maximum_fusion.6), channel_id=1, source_target_pairs={{0,8},{4,12},{8,0},{12,4},{16,24},{20,28},{24,16},{28,20},{1,9},{5... | collective-permute-start | bytes 3784712 | tf_op jit(solution)/shard_map/ppermute | solution.py:1024
  354.0 57.3 %all-to-all-start = ((bf16[4,384,768]{2,1,0:T(8,128)(2,1)}), bf16[4,384,768]{2,1,0:T(8,128)(2,1)S(1)}, u32[]{:S(2)}, u32[]{:S(2)}) async-start(bf16[4,384,768]{2,1,0:T(8,128)(2,1)} %get-tuple-element.318), calls=%async_computation | async-start | bytes 4718592 | tf_op jit(solution)/shard_map/all_to_all | solution.py:1435
  371.4 16.0 %collective-permute-start.41 = (bf16[4,96,896]{2,1,0:T(8,128)(2,1)}, bf16[4,96,896]{2,1,0:T(8,128)(2,1)}, u32[]{:S(2)}, u32[]{:S(2)}) collective-permute-start(bf16[4,96,896]{2,1,0:T(8,128)(2,1)} %get-tuple-element.341), channel_id=1, source_target_pairs={{0,8},{4,12},{8,0},{12,4},{16,24},{20,28},{24,16},{28,20},{1,9},{5... | collective-permute-start | bytes 2064392 | tf_op jit(solution)/shard_map/ppermute | solution.py:1024
  372.8 15.6 %collective-permute-start.42 = (bf16[4,96,896]{2,1,0:T(8,128)(2,1)}, bf16[4,96,896]{2,1,0:T(8,128)(2,1)}, u32[]{:S(2)}, u32[]{:S(2)}) collective-permute-start(bf16[4,96,896]{2,1,0:T(8,128)(2,1)} %get-tuple-element.342), channel_id=1, source_target_pairs={{0,16},{4,20},{8,24},{12,28},{16,0},{20,4},{24,8},{28,12},{1,17},{... | collective-permute-start | bytes 2064392 | tf_op jit(solution)/shard_map/ppermute | solution.py:1024
  392.0 32.6 %collective-permute-start.43 = (bf16[4,192,896]{2,1,0:T(8,128)(2,1)}, bf16[4,192,896]{2,1,0:T(8,128)(2,1)}, u32[]{:S(2)}, u32[]{:S(2)}) collective-permute-start(bf16[4,192,896]{2,1,0:T(8,128)(2,1)} %pad_maximum_fusion.3), channel_id=1, source_target_pairs={{0,16},{4,20},{8,24},{12,28},{16,0},{20,4},{24,8},{28,12},{1,17},{... | collective-permute-start | bytes 4128776 | tf_op jit(solution)/shard_map/ppermute | solution.py:1024
  395.6 29.2 %collective-permute-start.44 = (bf16[4,192,896]{2,1,0:T(8,128)(2,1)}, bf16[4,192,896]{2,1,0:T(8,128)(2,1)}, u32[]{:S(2)}, u32[]{:S(2)}) collective-permute-start(bf16[4,192,896]{2,1,0:T(8,128)(2,1)} %pad_maximum_fusion.4), channel_id=1, source_target_pairs={{0,8},{4,12},{8,0},{12,4},{16,24},{20,28},{24,16},{28,20},{1,9},{5... | collective-permute-start | bytes 4128776 | tf_op jit(solution)/shard_map/ppermute | solution.py:1024
  411.3 34.3 %all-to-all-start.4 = ((bf16[4,176,896]{2,1,0:T(8,128)(2,1)}), bf16[4,176,896]{2,1,0:T(8,128)(2,1)}, u32[]{:S(2)}, u32[]{:S(2)}) async-start(bf16[4,176,896]{2,1,0:T(8,128)(2,1)} %add_convert_fusion.2), calls=%async_computation.4 | async-start | bytes 2523136 | tf_op jit(solution)/shard_map/all_to_all | solution.py:1435
  433.1 16.8 %collective-permute-start.45 = (bf16[4,4,208,384]{3,2,1,0:T(8,128)(2,1)}, bf16[4,4,208,384]{3,2,1,0:T(8,128)(2,1)}, u32[]{:S(2)}, u32[]{:S(2)}) collective-permute-start(bf16[4,4,208,384]{3,2,1,0:T(8,128)(2,1)} %get-tuple-element.358), channel_id=1, source_target_pairs={{0,4},{4,0},{8,12},{12,8},{16,20},{20,16},{24,28},{28,24},{1,5},{5... | collective-permute-start | bytes 7667720 | tf_op jit(solution)/shard_map/ppermute | solution.py:1024
  445.6 36.6 %all-to-all-start.2 = ((bf16[4,192,896]{2,1,0:T(8,128)(2,1)}), bf16[4,192,896]{2,1,0:T(8,128)(2,1)}, u32[]{:S(2)}, u32[]{:S(2)}) async-start(bf16[4,192,896]{2,1,0:T(8,128)(2,1)} %add_convert_fusion), calls=%async_computation.2 | async-start | bytes 2752512 | tf_op jit(solution)/shard_map/all_to_all | solution.py:1435
  453.0 29.3 %collective-permute-start.46 = (bf16[4,208,384]{2,1,0:T(8,128)(2,1)}, bf16[4,208,384]{2,1,0:T(8,128)(2,1)S(1)}, u32[]{:S(2)}, u32[]{:S(2)}) collective-permute-start(bf16[4,208,384]{2,1,0:T(8,128)(2,1)} %get-tuple-element.393), channel_id=1, source_target_pairs={{0,8},{4,12},{8,0},{12,4},{16,24},{20,28},{24,16},{28,20},{1,9},{5... | collective-permute-start | bytes 1916936 | tf_op jit(solution)/shard_map/ppermute | solution.py:1024
  454.3 29.1 %collective-permute-start.47 = (bf16[4,208,384]{2,1,0:T(8,128)(2,1)}, bf16[4,208,384]{2,1,0:T(8,128)(2,1)}, u32[]{:S(2)}, u32[]{:S(2)}) collective-permute-start(bf16[4,208,384]{2,1,0:T(8,128)(2,1)} %get-tuple-element.392), channel_id=1, source_target_pairs={{0,16},{4,20},{8,24},{12,28},{16,0},{20,4},{24,8},{28,12},{1,17},{... | collective-permute-start | bytes 1916936 | tf_op jit(solution)/shard_map/ppermute | solution.py:1024
  455.3 28.1 %collective-permute-start.48 = (bf16[4,208,384]{2,1,0:T(8,128)(2,1)}, bf16[4,208,384]{2,1,0:T(8,128)(2,1)}, u32[]{:S(2)}, u32[]{:S(2)}) collective-permute-start(bf16[4,208,384]{2,1,0:T(8,128)(2,1)} %get-tuple-element.391), channel_id=1, source_target_pairs={{0,24},{4,28},{8,16},{12,20},{16,8},{20,12},{24,0},{28,4},{1,25},{... | collective-permute-start | bytes 1916936 | tf_op jit(solution)/shard_map/ppermute | solution.py:1024
  485.1 24.0 %collective-permute-start.49 = (bf16[592,896]{1,0:T(8,128)(2,1)S(1)}, bf16[592,896]{1,0:T(8,128)(2,1)}, u32[]{:S(2)}, u32[]{:S(2)}) collective-permute-start(bf16[592,896]{1,0:T(8,128)(2,1)S(1)} %pad_maximum_fusion.9.refs_0_), channel_id=1, source_target_pairs={{0,8},{4,12},{8,0},{12,4},{16,24},{20,28},{24,16},{28,20},{1,9},{5... | collective-permute-start | bytes 3182600 | tf_op jit(solution)/shard_map/ppermute | solution.py:1024
  485.9 23.7 %collective-permute-start.50 = (bf16[592,896]{1,0:T(8,128)(2,1)S(1)}, bf16[592,896]{1,0:T(8,128)(2,1)}, u32[]{:S(2)}, u32[]{:S(2)}) collective-permute-start(bf16[592,896]{1,0:T(8,128)(2,1)S(1)} %pad_maximum_fusion.9.refs_0_), channel_id=1, source_target_pairs={{0,16},{4,20},{8,24},{12,28},{16,0},{20,4},{24,8},{28,12},{1,17},{... | collective-permute-start | bytes 3182600 | tf_op jit(solution)/shard_map/ppermute | solution.py:1024
  489.8 19.1 %all-to-all-start.3 = ((bf16[4,208,384]{2,1,0:T(8,128)(2,1)}), bf16[4,208,384]{2,1,0:T(8,128)(2,1)S(1)}, u32[]{:S(2)}, u32[]{:S(2)}) async-start(bf16[4,208,384]{2,1,0:T(8,128)(2,1)} %fusion.2), calls=%async_computation.3 | async-start | bytes 1277952 | tf_op jit(solution)/shard_map/all_to_all | solution.py:1435
  494.6 34.3 %collective-permute-start.57 = (bf16[592,896]{1,0:T(8,128)(2,1)S(1)}, bf16[592,896]{1,0:T(8,128)(2,1)}, u32[]{:S(2)}, u32[]{:S(2)}) collective-permute-start(bf16[592,896]{1,0:T(8,128)(2,1)S(1)} %pad_maximum_fusion.9.refs_0_), channel_id=1, source_target_pairs={{0,4},{4,0},{8,12},{12,8},{16,20},{20,16},{24,28},{28,24},{1,5},{5... | collective-permute-start | bytes 3182600 | tf_op jit(solution)/shard_map/ppermute | solution.py:1024
  514.2 14.0 %collective-permute-start.55 = (bf16[304,896]{1,0:T(8,128)(2,1)S(1)}, bf16[304,896]{1,0:T(8,128)(2,1)S(1)}, u32[]{:S(2)}, u32[]{:S(2)}) collective-permute-start(bf16[304,896]{1,0:T(8,128)(2,1)S(1)} %slice.263), channel_id=1, source_target_pairs={{0,16},{4,20},{8,24},{12,28},{16,0},{20,4},{24,8},{28,12},{1,17},{... | collective-permute-start | bytes 1634312 | tf_op jit(solution)/shard_map/ppermute | solution.py:1024
  528.3 13.4 %collective-permute-start.56 = (bf16[4,192,384]{2,1,0:T(8,128)(2,1)S(1)}, bf16[4,192,384]{2,1,0:T(8,128)(2,1)}, u32[]{:S(2)}, u32[]{:S(2)}) collective-permute-start(bf16[4,192,384]{2,1,0:T(8,128)(2,1)S(1)} %pad_maximum_fusion.10.refs_0_), channel_id=1, source_target_pairs={{0,4},{4,0},{8,12},{12,8},{16,20},{20,16},{24,28},{28,24},{1,5},{5... | collective-permute-start | bytes 1769480 | tf_op jit(solution)/shard_map/ppermute | solution.py:1024
  (61 other events, 549.2 us)
